TPU v7x, 32 devices: a whole 2x2x4 slice. The times are simulated.
32 devices in a mesh: gx: 2 (over x), gy: 16 (over z, y, core).
Axes of the slice: x: 2, y: 2, z: 4, core: 2. Of those that a mesh axis runs over, the one named last changes fastest.
Arguments:
- features: bfloat16 [4, 128, 16, 8, 256], P('gx', 'gy'), may hold values from -6 to 6
- fractions: bfloat16 [4, 128, 16, 8, 3], P('gx', 'gy'), may hold values from 0 to 1
- counts: int32 [4, 128, 16], P('gx', 'gy'), may hold values from 2 to 8
- k_index: int32 [1024, 3], replicated, may hold values from -112 to 112, as said below
- w_short: bfloat16 [8, 256, 256], replicated, may hold values from -0.375 to 0.375
- w_charge: bfloat16 [256, 256], replicated, may hold values from -0.375 to 0.375
- w_out: bfloat16 [256, 256], replicated, may hold values from -0.75 to 0.75
Outputs:
- updated: bfloat16 [4, 128, 16, 8, 256], P('gx', 'gy')
Inputs may be any that keep to these rules, and one draw needn't show every extreme that they name: No two rows of k_index are equal, and no row is all zeros.
All inputs are finite; a program needn't handle non-finite values.
Results may differ from a plain program's by a relative error of at most 0.007.
Values may be sent and summed in bfloat16 or wider, within the bound.
No kernel may reach another device: no remote copies, remote signals or barrier semaphores. Data moves between devices by JAX's collectives and lax.ppermute only.
A program may use at most 128 MiB of HBM per device.

v0:
```python
import functools
import math

import jax
import jax.numpy as jnp
from jax import lax
from jax.experimental import pallas as pl
from jax.experimental.pallas import tpu as pltpu
from jax.sharding import PartitionSpec as P

TWO_PI = 2.0 * math.pi
SHARPNESS = 600.0
CENTER_LOW = 0.2
CENTER_SPAN = 0.5
SCREEN = 16.0
FAR = 8.0
BF16 = jnp.bfloat16
F32 = jnp.float32
AXES = ("gx", "gy")
KTILE = 256

COS = (
    0.9999992215641686,
    -19.738982514492687,
    64.92872654701725,
    -85.27239608425373,
    58.794033945704726,
    -21.076773632203547,
)
SIN = (
    6.28318281853067,
    -41.34142139672705,
    81.59618382164335,
    -76.58009998806374,
    41.205392442366964,
    -12.271258434551658,
)
NT = (((1,), (1,)), ((), ()))


def horner(coefs, s):
    value = coefs[-1] * s + coefs[-2]
    for c in coefs[-3::-1]:
        value = value * s + c
    return value


def factor_kernel(grid_all, scale_all, pos, kmat, kall, feat, wc_t, mask, ph, fac, charges, kw):
    step = pl.program_id(0)
    atoms = pos.shape[0]
    basis_k = kall.shape[1]

    @pl.when(step == 0)
    def _():
        for j in range(0, atoms, 256):
            c = lax.dot_general(
                wc_t[...], feat[j : j + 256, :], NT, preferred_element_type=F32
            )
            charges[:, j : j + 256] = (c * mask[0:1, j : j + 256]).astype(BF16)
        k_sq = jnp.zeros((1, basis_k), F32)
        for d in range(3):
            wave = TWO_PI * kall[d : d + 1, :].astype(F32)
            k_sq = k_sq + wave * wave
        screened = jnp.exp(-k_sq / (4.0 * SCREEN)) / k_sq
        total = jnp.sum(screened, axis=1, keepdims=True)
        row = screened / total * scale_all
        for j in range(0, basis_k, KTILE):
            kw[j // KTILE] = jnp.broadcast_to(row[:, j : j + KTILE], (8, KTILE))

    for j in range(0, atoms, 256):
        t = jnp.dot(pos[j : j + 256, :], kmat[...], preferred_element_type=F32)
        r = t - jnp.round(t)
        s = r * r
        ph[0, j : j + 256, :] = horner(COS, s).astype(BF16)
        ph[1, j : j + 256, :] = (horner(SIN, s) * r).astype(BF16)
    weight = kw[step][0:1, :]
    rows = charges.shape[0]
    for p in range(2):
        part = jnp.dot(charges[...], ph[p], preferred_element_type=F32)
        fac[p * rows : (p + 1) * rows, :] = part * weight


def factor_call(pos, kmat, feat, wc_t, mask, grid_all, scale_all):
    atoms, width = feat.shape
    vectors = kmat.shape[1]
    steps = vectors // KTILE
    lanes = pos.shape[1]
    return pl.pallas_call(
        functools.partial(factor_kernel, grid_all, scale_all),
        grid=(steps,),
        in_specs=[
            pl.BlockSpec((atoms, lanes), lambda i: (0, 0)),
            pl.BlockSpec((lanes, KTILE), lambda i: (0, i)),
            pl.BlockSpec((lanes, vectors), lambda i: (0, 0)),
            pl.BlockSpec((atoms, width), lambda i: (0, 0)),
            pl.BlockSpec((width, width), lambda i: (0, 0)),
            pl.BlockSpec((1, atoms), lambda i: (0, 0)),
        ],
        out_specs=[
            pl.BlockSpec((2, atoms, KTILE), lambda i: (0, 0, i)),
            pl.BlockSpec((2 * width, KTILE), lambda i: (i, 0)),
        ],
        out_shape=[
            jax.ShapeDtypeStruct((2, atoms, vectors), BF16),
            jax.ShapeDtypeStruct((steps * 2 * width, KTILE), F32),
        ],
        scratch_shapes=[
            pltpu.VMEM((width, atoms), BF16),
            pltpu.VMEM((steps, 8, KTILE), F32),
        ],
        compiler_params=pltpu.CompilerParams(
            dimension_semantics=("arbitrary",), vmem_limit_bytes=40 << 20
        ),
        cost_estimate=pl.CostEstimate(
            flops=6 * atoms * vectors * width, bytes_accessed=16 << 20, transcendentals=0
        ),
        name="factor",
    )(pos, kmat, kmat, feat, wc_t, mask)


def short_kernel(slots, basis, lo, mid, hi, own, feat, w, out, agg):
    xi = pl.program_id(1)
    rows = feat.shape[2]
    width = feat.shape[3]
    pairs = rows // (2 * slots)
    two = 2 * slots
    window = 4 * slots
    sub = lax.broadcasted_iota(jnp.int32, (8, 128), 0)
    lane = lax.broadcasted_iota(jnp.int32, (8, 128), 1)
    lane_block = lane // window
    cell_in_window = (lane % window) // slots
    z_off = jnp.where(sub == 2, (cell_in_window - 1).astype(F32), 0.0)
    refs = (lo, mid, hi)
    columns = [(dx, dy) for dx in (-1, 0, 1) for dy in (-1, 0, 1) if (dx, dy) != (0, 0)]
    columns.append((0, 0))
    placed = []
    for dx, dy in columns:
        coords = refs[dy + 1][xi + 1 + dx, 0, rows : rows + 16, 0:128].astype(F32)[0:8]
        shift = jnp.where(sub == 0, float(dx), jnp.where(sub == 1, float(dy), 0.0))
        placed.append(coords + shift)
    select = jnp.where(
        lax.broadcasted_iota(jnp.int32, (16, 384), 0)
        == lax.broadcasted_iota(jnp.int32, (16, 384), 1) // 128,
        1.0,
        0.0,
    ).astype(BF16)
    own_all = jnp.dot(own[xi, 0], select, preferred_element_type=F32)
    stretch = math.sqrt(SHARPNESS * math.log2(math.e))
    centers = [stretch * (CENTER_LOW + b * (CENTER_SPAN / (basis - 1))) for b in range(basis)]

    for p in range(pairs):
        packed = []
        for h in range(3):
            merged = None
            for c in range(4 * h, min(4 * h + 4, 9)):
                amount = (window * (c % 4) - two * p) % 128
                moved = pltpu.roll(placed[c], amount, axis=1) if amount else placed[c]
                merged = moved if merged is None else jnp.where(lane_block == c % 4, moved, merged)
            merged = merged + z_off
            if h == 2:
                merged = jnp.where(lane_block == 0, merged, FAR)
            packed.append([jnp.broadcast_to(merged[d : d + 1, :], (8, 128)) for d in range(3)])
        parts = [[None, None] for _ in range(3)]
        for h in range(3):
            for q in range(2):
                r0 = two * p + slots * q
                d2 = None
                for d in range(3):
                    mine = own_all[r0 : r0 + slots, 128 * d : 128 * d + 128]
                    if d == 2 and q == 1:
                        mine = mine + 1.0
                    delta = packed[h][d] - mine
                    d2 = delta * delta if d2 is None else d2 + delta * delta
                env = jnp.maximum(1.0 - d2, 0.0)
                env = env * env
                if h == 2:
                    env = jnp.where(lane == sub + slots * (1 + q), 0.0, env)
                ar = jnp.sqrt(d2) * stretch
                values = []
                for b in range(basis):
                    u = ar - centers[b]
                    values.append(jnp.exp2(u * (centers[b] - ar)) * env)
                parts[h][q] = values
        lhs = []
        for h in range(3):
            lhs.append(
                jnp.concatenate(
                    [
                        jnp.concatenate([parts[h][0][b], parts[h][1][b]], axis=0).astype(BF16)
                        for b in range(basis)
                    ],
                    axis=0,
                )
            )
        near = []
        for dx, dy in columns:
            ref = refs[dy + 1]
            near.append(ref[xi + 1 + dx, 0, two * p : two * p + two, :])
            nxt = two * ((p + 1) % pairs)
            near.append(ref[xi + 1 + dx, 0, nxt : nxt + two, :])
        pad = jnp.zeros((384 - 9 * window, width), BF16)
        total = jnp.dot(
            jnp.concatenate(lhs, axis=1),
            jnp.concatenate(near + [pad], axis=0),
            preferred_element_type=F32,
        ).astype(BF16)
        for b in range(basis):
            agg[xi, two * p : two * p + two, width * b : width * (b + 1)] = total[
                two * b : two * b + two
            ]

    @pl.when(xi == pl.num_programs(1) - 1)
    def _():
        planes = feat.shape[0]
        value = jnp.dot(
            agg[...].reshape(planes * rows, basis * width), w[...], preferred_element_type=F32
        )
        value = jax.nn.silu(value).reshape(planes, rows, width)
        out[:, 0] = feat[:, 0].astype(F32) + value


def short_call(ext, own, feat, w_flat, slots, basis, first, count):
    planes, cols, rows, width = feat.shape
    ext_rows = ext.shape[2]
    lanes = own.shape[3]
    window = lambda off: pl.BlockSpec(
        (planes + 2, 1, ext_rows, width), lambda y, x: (0, y + first + off, 0, 0)
    )
    return pl.pallas_call(
        functools.partial(short_kernel, slots, basis),
        grid=(count, planes),
        in_specs=[
            window(0),
            window(1),
            window(2),
            pl.BlockSpec((planes, 1, rows, lanes), lambda y, x: (0, y + first, 0, 0)),
            pl.BlockSpec((planes, 1, rows, width), lambda y, x: (0, y + first, 0, 0)),
            pl.BlockSpec((basis * width, width), lambda y, x: (0, 0)),
        ],
        out_specs=pl.BlockSpec((planes, 1, rows, width), lambda y, x: (0, y, 0, 0)),
        out_shape=jax.ShapeDtypeStruct((planes, count, rows, width), F32),
        scratch_shapes=[pltpu.VMEM((planes, rows, basis * width), BF16)],
        compiler_params=pltpu.CompilerParams(
            dimension_semantics=("arbitrary", "arbitrary"), vmem_limit_bytes=40 << 20
        ),
        cost_estimate=pl.CostEstimate(
            flops=count * planes * rows * width * 2 * (basis * 384 + basis * width),
            bytes_accessed=8 << 20,
            transcendentals=count * planes * rows * 384 * (basis + 1),
        ),
        name="short",
    )(ext, ext, ext, own, feat, w_flat)


def field_kernel(ph, weighted, w_out, base, mask, out):
    tiles = weighted.shape[0]
    lhs = jnp.concatenate(
        [ph[t % 2, :, KTILE * (t // 2) : KTILE * (t // 2 + 1)] for t in range(tiles)], axis=1
    )
    rhs = jnp.concatenate([weighted[t] for t in range(tiles)], axis=1)
    recip = lax.dot_general(lhs, rhs, NT, preferred_element_type=F32)
    far = jnp.dot(recip.astype(BF16), w_out[...], preferred_element_type=F32)
    value = base[...] + far
    out[...] = jnp.where(mask[...] > 0.0, value, 0.0).astype(BF16)


def field_call(ph, weighted, w_out, base, mask, tile=256):
    _, atoms, vectors = ph.shape
    tiles, width, _ = weighted.shape
    return pl.pallas_call(
        field_kernel,
        grid=(atoms // tile,),
        in_specs=[
            pl.BlockSpec((2, tile, vectors), lambda i: (0, i, 0)),
            pl.BlockSpec((tiles, width, KTILE), lambda i: (0, 0, 0)),
            pl.BlockSpec((width, width), lambda i: (0, 0)),
            pl.BlockSpec((tile, width), lambda i: (i, 0)),
            pl.BlockSpec((tile, 1), lambda i: (i, 0)),
        ],
        out_specs=pl.BlockSpec((tile, width), lambda i: (i, 0)),
        out_shape=jax.ShapeDtypeStruct((atoms, width), BF16),
        compiler_params=pltpu.CompilerParams(
            dimension_semantics=("arbitrary",), vmem_limit_bytes=40 << 20
        ),
        cost_estimate=pl.CostEstimate(
            flops=4 * atoms * vectors * width, bytes_accessed=16 << 20, transcendentals=0
        ),
        name="field",
    )(ph, weighted, w_out, base, mask)


def my_index():
    return lax.axis_index("gx") * lax.axis_size("gy") + lax.axis_index("gy")


def swap(value, bit):
    count = lax.axis_size("gx") * lax.axis_size("gy")
    return lax.ppermute(value, AXES, [(i, i ^ bit) for i in range(count)])


def reduce_halving(value, bits):
    for bit in bits:
        half = value.shape[0] // 2
        mine = (my_index() // bit) % 2
        keep = lax.dynamic_slice_in_dim(value, mine * half, half, 0)
        give = lax.dynamic_slice_in_dim(value, (1 - mine) * half, half, 0).astype(BF16)
        value = keep + swap(give, bit).astype(F32)
    return value


def gather_doubling(value, bits):
    for bit in bits:
        mine = (my_index() // bit) % 2
        other = swap(value, bit)
        value = jnp.where(
            mine == 0, jnp.concatenate([value, other]), jnp.concatenate([other, value])
        )
    return value


def with_halo(cells, axis, dim):
    count = lax.axis_size(axis)
    size = cells.shape[dim]
    if count == 2 and size == 2:
        other = lax.ppermute(cells, axis, [(0, 1), (1, 0)])
        left = lax.slice_in_dim(other, 1, 2, axis=dim)
        right = lax.slice_in_dim(other, 0, 1, axis=dim)
    else:
        head = lax.slice_in_dim(cells, 0, 1, axis=dim)
        tail = lax.slice_in_dim(cells, size - 1, size, axis=dim)
        left = lax.ppermute(tail, axis, [(i, (i + 1) % count) for i in range(count)])
        right = lax.ppermute(head, axis, [((i + 1) % count, i) for i in range(count)])
    return jnp.concatenate([left, cells, right], axis=dim)


def on_device(features, fractions, counts, k_index, w_short, w_charge, w_out):
    planes, cols, depth, slots, width = features.shape
    basis = w_short.shape[0]
    vectors = k_index.shape[0]
    rows = depth * slots
    atoms = planes * cols * rows
    grid_all = (planes * lax.axis_size("gx"), cols * lax.axis_size("gy"), depth)
    assert rows == 128 and slots == 8 and vectors % KTILE == 0 and width % 128 == 0
    for extent in grid_all:
        assert extent & (extent - 1) == 0 and extent <= 256
    scale_all = math.sqrt(vectors / (grid_all[0] * grid_all[1] * grid_all[2] * slots))

    occupied = jnp.arange(slots, dtype=jnp.int32) < counts[..., None]
    feat = features.reshape(planes, cols, rows, width)

    placed = jnp.where(occupied[..., None], fractions, jnp.asarray(FAR, BF16))
    placed = jnp.roll(placed.reshape(planes, cols, rows, 3), slots, axis=2)
    placed = jnp.swapaxes(placed, 2, 3)
    placed = jnp.pad(placed, ((0, 0), (0, 0), (0, 13), (0, width - rows)))
    block = jnp.concatenate([feat[:, :, rows - slots :], feat[:, :, : rows - slots], placed], axis=2)
    ext = with_halo(with_halo(block, "gx", 0), "gy", 1)

    start_x = lax.axis_index("gx") * planes
    start_y = lax.axis_index("gy") * cols
    shape = (planes, cols, depth, slots)
    cells = [
        jnp.broadcast_to((start_x + jnp.arange(planes))[:, None, None, None], shape),
        jnp.broadcast_to((start_y + jnp.arange(cols))[None, :, None, None], shape),
        jnp.broadcast_to(jnp.arange(depth)[None, None, :, None], shape),
    ]
    cells = jnp.stack(cells, axis=-1).astype(BF16)
    pos = jnp.concatenate([fractions, cells, jnp.zeros(shape + (10,), BF16)], axis=-1)
    pos = pos.reshape(planes, cols, rows, 16)
    scaled = k_index.astype(F32) / jnp.array(grid_all, F32)
    kmat = jnp.pad(jnp.concatenate([scaled, scaled], axis=1).T, ((0, 10), (0, 0))).astype(BF16)

    flat = feat.reshape(atoms, width)
    mask = occupied.reshape(1, atoms).astype(F32)
    ph, partial = factor_call(
        pos.reshape(atoms, 16), kmat, flat, w_charge.T, mask, grid_all, scale_all
    )

    count = lax.axis_size("gx") * lax.axis_size("gy")
    bits = [1 << i for i in range(count.bit_length() - 1)]
    reduced = reduce_halving(partial, bits).astype(BF16)
    weighted = gather_doubling(reduced, bits[::-1])
    weighted = weighted.reshape(2 * vectors // KTILE, width, KTILE)

    w_flat = w_short.reshape(basis * width, width)
    step = max(cols // 4, 1)
    bases = [
        short_call(ext, pos, feat, w_flat, slots, basis, first, step)
        for first in range(0, cols, step)
    ]
    base = jnp.concatenate(bases, axis=1).reshape(atoms, width)
    out = field_call(ph, weighted, w_out, base, occupied.reshape(atoms, 1).astype(F32))
    return out.reshape(features.shape)


def solution(mesh):
    return jax.shard_map(
        on_device,
        mesh=mesh,
        in_specs=(
            P("gx", "gy", None, None, None),
            P("gx", "gy", None, None, None),
            P("gx", "gy", None),
            P(),
            P(),
            P(),
            P(),
        ),
        out_specs=P("gx", "gy", None, None, None),
        check_vma=False,
    )
```

profile of v0, /device:TPU:0, one launch (start us, length us, event | category | flops | bytes accessed | tf_op | source)
XLA Modules:
  0.0 122.2 jit_solution(17029233577352020718)
XLA Ops:
  1.5 1.7 %copy.13 = bf16[2,8,16,8,3]{4,3,2,1,0:T(8,128)(2,1)S(1)} copy(bf16[2,8,16,8,3]{2,3,4,1,0:T(8,128)(2,1)} %param.9) | data formatting | bytes 24576 | tf_op args[1]
  7.3 2.8 %concatenate.54 = bf16[2,8,16,8,16]{4,3,2,1,0:T(8,128)(2,1)S(1)} concatenate(bf16[2,8,16,8,3]{4,3,2,1,0:T(8,128)(2,1)S(1)} %copy.13, bf16[2,8,16,8,1]{4,3,2,1,0:T(8,128)(2,1)S(1)} %stack_broadcast_in_dim.6, bf16[2,8,16,8,1]{4,3,2,1,0:T(8,128)(2,1)} %stack_broadcast_in_dim.7, bf16[2,8,16,8,1]{4,3,2,1,0:T(8,128)(2,1)S(1)} %iota_convert_fusion, ...), dimensions={4} | concatenate | bytes 131072 | tf_op jit(solution)/shard_map/concatenate | solution.py:367
  10.1 10.5 %factor.1 = (bf16[2,2048,1024]{2,1,0:T(8,128)(2,1)S(1)}, f32[2048,256]{1,0:T(8,128)S(1)}) custom-call(bf16[2048,16]{1,0:T(8,128)(2,1)S(1)} %bitcast.33, bf16[16,1024]{1,0:T(8,128)(2,1)S(1)} %pad.9.kmat.kall, bf16[16,1024]{1,0:T(8,128)(2,1)S(1)} %pad.9.kmat.kall, bf16[2048,256]{1,0:T(8,128)(2,1)S(1)} %bitcast.22, bf16[256,256]{1,0:T(8,128)(2,1)S(1)} %bitcast.42, ...), custom_call_target="tpu_custom_call" | custom-call | flops 3221225472 | bytes 16777216 | tf_op jit(solution)/shard_map/factor/pallas_call | solution.py:88
  20.7 3.3 %copy-done.2 = bf16[2,2048,1024]{2,1,0:T(8,128)(2,1)} copy-done((bf16[2,2048,1024]{2,1,0:T(8,128)(2,1)}, bf16[2,2048,1024]{2,1,0:T(8,128)(2,1)S(1)}, u32[]{:S(2)}) %copy-start.2) | copy-done | bytes 8388632
  27.5 2.5 %convert_add_fusion = f32[1024,256]{1,0:T(8,128)} fusion(bf16[1024,256]{1,0:T(8,128)(2,1)} %collective-permute-done, f32[2048,256]{1,0:T(8,128)} %copy-done.3, s32[]{:T(128)S(6)} %select_n.144), kind=kLoop, calls=%fused_computation.4 | loop fusion | flops 524288 | bytes 2621444 | tf_op jit(solution)/shard_map/add | solution.py:307
  31.0 2.9 %collective-permute-start.1 = (bf16[512,256]{1,0:T(8,128)(2,1)S(1)}, bf16[512,256]{1,0:T(8,128)(2,1)}, u32[]{:S(2)}, u32[]{:S(2)}) collective-permute-start(bf16[512,256]{1,0:T(8,128)(2,1)S(1)} %dynamic-slice_convert_fusion.1), channel_id=1, source_target_pairs={{0,2},{1,3},{2,0},{3,1},{4,6},{5,7},{6,4},{7,5},{8,10},{9,11},{10,... | collective-permute-start | bytes 786440 | tf_op jit(solution)/shard_map/ppermute | solution.py:298
  34.6 6.1 %collective-permute-done.1 = bf16[512,256]{1,0:T(8,128)(2,1)} collective-permute-done((bf16[512,256]{1,0:T(8,128)(2,1)S(1)}, bf16[512,256]{1,0:T(8,128)(2,1)}, u32[]{:S(2)}, u32[]{:S(2)}) %collective-permute-start.1) | collective-permute-done | bytes 262176 | tf_op jit(solution)/shard_map/ppermute | solution.py:298
  41.9 1.9 %collective-permute-start.2 = (bf16[256,256]{1,0:T(8,128)(2,1)S(1)}, bf16[256,256]{1,0:T(8,128)(2,1)}, u32[]{:S(2)}, u32[]{:S(2)}) collective-permute-start(bf16[256,256]{1,0:T(8,128)(2,1)S(1)} %dynamic-slice_convert_fusion.2), channel_id=1, source_target_pairs={{0,4},{1,5},{2,6},{3,7},{4,0},{5,1},{6,2},{7,3},{8,12},{9,13},{10,... | collective-permute-start | bytes 393224 | tf_op jit(solution)/shard_map/ppermute | solution.py:298
  44.9 1.5 %collective-permute-start.10 = (bf16[2,8,144,256]{3,2,1,0:T(8,128)(2,1)}, bf16[2,8,144,256]{3,2,1,0:T(8,128)(2,1)}, u32[]{:S(2)}, u32[]{:S(2)}) collective-permute-start(bf16[2,8,144,256]{3,2,1,0:T(8,128)(2,1)} %pad_maximum_fusion.2), channel_id=1, source_target_pairs={{0,16},{16,0},{1,17},{17,1},{2,18},{18,2},{3,19},{19,3},{4,20},{20... | collective-permute-start | bytes 3538952 | tf_op jit(solution)/shard_map/ppermute | solution.py:325
  48.7 2.8 %collective-permute-start.3 = (bf16[128,256]{1,0:T(8,128)(2,1)S(1)}, bf16[128,256]{1,0:T(8,128)(2,1)S(1)}, u32[]{:S(2)}, u32[]{:S(2)}) collective-permute-start(bf16[128,256]{1,0:T(8,128)(2,1)S(1)} %dynamic-slice_convert_fusion.3), channel_id=1, source_target_pairs={{0,8},{1,9},{2,10},{3,11},{4,12},{5,13},{6,14},{7,15},{8,0},{9,1},... | collective-permute-start | bytes 196616 | tf_op jit(solution)/shard_map/ppermute | solution.py:298
  51.6 2.4 %collective-permute-done.3 = bf16[128,256]{1,0:T(8,128)(2,1)S(1)} collective-permute-done((bf16[128,256]{1,0:T(8,128)(2,1)S(1)}, bf16[128,256]{1,0:T(8,128)(2,1)S(1)}, u32[]{:S(2)}, u32[]{:S(2)}) %collective-permute-start.3) | collective-permute-done | bytes 65568 | tf_op jit(solution)/shard_map/ppermute | solution.py:298
  54.9 1.7 %collective-permute-start.4 = (bf16[64,256]{1,0:T(8,128)(2,1)S(1)}, bf16[64,256]{1,0:T(8,128)(2,1)S(1)}, u32[]{:S(2)}, u32[]{:S(2)}) collective-permute-start(bf16[64,256]{1,0:T(8,128)(2,1)S(1)} %dynamic-slice_convert_fusion.4), channel_id=1, source_target_pairs={{0,16},{1,17},{2,18},{3,19},{4,20},{5,21},{6,22},{7,23},{8,24},{9,... | collective-permute-start | bytes 98312 | tf_op jit(solution)/shard_map/ppermute | solution.py:298
  56.6 16.1 %collective-permute-done.4 = bf16[64,256]{1,0:T(8,128)(2,1)S(1)} collective-permute-done((bf16[64,256]{1,0:T(8,128)(2,1)S(1)}, bf16[64,256]{1,0:T(8,128)(2,1)S(1)}, u32[]{:S(2)}, u32[]{:S(2)}) %collective-permute-start.4) | collective-permute-done | bytes 32800 | tf_op jit(solution)/shard_map/ppermute | solution.py:298
  72.7 1.5 %collective-permute-start.5 = (bf16[64,256]{1,0:T(8,128)(2,1)S(1)}, bf16[64,256]{1,0:T(8,128)(2,1)S(1)}, u32[]{:S(2)}, u32[]{:S(2)}) collective-permute-start(bf16[64,256]{1,0:T(8,128)(2,1)S(1)} %add_convert_fusion), channel_id=1, source_target_pairs={{0,16},{1,17},{2,18},{3,19},{4,20},{5,21},{6,22},{7,23},{8,24},{9,... | collective-permute-start | bytes 98312 | tf_op jit(solution)/shard_map/ppermute | solution.py:298
  74.3 2.4 %collective-permute-done.5 = bf16[64,256]{1,0:T(8,128)(2,1)S(1)} collective-permute-done((bf16[64,256]{1,0:T(8,128)(2,1)S(1)}, bf16[64,256]{1,0:T(8,128)(2,1)S(1)}, u32[]{:S(2)}, u32[]{:S(2)}) %collective-permute-start.5) | collective-permute-done | bytes 32800 | tf_op jit(solution)/shard_map/ppermute | solution.py:298
  76.7 2.6 %collective-permute-start.6 = (bf16[128,256]{1,0:T(8,128)(2,1)S(1)}, bf16[128,256]{1,0:T(8,128)(2,1)S(1)}, u32[]{:S(2)}, u32[]{:S(2)}) collective-permute-start(bf16[128,256]{1,0:T(8,128)(2,1)S(1)} %maximum_select_fusion.4), channel_id=1, source_target_pairs={{0,8},{1,9},{2,10},{3,11},{4,12},{5,13},{6,14},{7,15},{8,0},{9,1},... | collective-permute-start | bytes 196616 | tf_op jit(solution)/shard_map/ppermute | solution.py:298
  81.7 4.4 %collective-permute-start.12 = (bf16[4,1,144,256]{3,2,1,0:T(8,128)(2,1)}, bf16[4,1,144,256]{3,2,1,0:T(8,128)(2,1)}, u32[]{:S(2)}, u32[]{:S(2)}) collective-permute-start(bf16[4,1,144,256]{3,2,1,0:T(8,128)(2,1)} %get-tuple-element.10), channel_id=1, source_target_pairs={{1,0},{2,1},{3,2},{4,3},{5,4},{6,5},{7,6},{8,7},{9,8},{10,9},{11,1... | collective-permute-start | bytes 884744 | tf_op jit(solution)/shard_map/ppermute | solution.py:332
  87.2 5.5 %collective-permute-done.7 = bf16[256,256]{1,0:T(8,128)(2,1)} collective-permute-done((bf16[256,256]{1,0:T(8,128)(2,1)}, bf16[256,256]{1,0:T(8,128)(2,1)}, u32[]{:S(2)}, u32[]{:S(2)}) %collective-permute-start.7) | collective-permute-done | bytes 131104 | tf_op jit(solution)/shard_map/ppermute | solution.py:298
  94.6 1.9 %pad_maximum_fusion.lo.mid.hi = bf16[4,10,144,256]{3,2,1,0:T(8,128)(2,1)S(1)} fusion(bf16[4,1,144,256]{3,2,1,0:T(8,128)(2,1)} %collective-permute-done.12, bf16[1,8,144,256]{3,2,1,0:T(8,128)(2,1)} %copy-done.6, bf16[2,8,16,256]{3,2,1,0:T(8,128)(2,1)S(1)} %pad.10, bf16[2,8,120,256]{3,2,1,0:T(8,128)(2,1)} %copy-done.5, bf16[2,8,8,256]{3,2,1,0:T(8,128)(2,1)S(1)} %slice.34, ...), kind=kLoop, calls=%fused_computation | loop fusion | flops 20643840 | bytes 5898240 | tf_op jit(solution)/shard_map/concatenate | solution.py:333
  96.5 4.5 %short.4 = f32[2,2,128,256]{3,2,1,0:T(8,128)S(1)} custom-call(bf16[4,10,144,256]{3,2,1,0:T(8,128)(2,1)S(1)} %pad_maximum_fusion.lo.mid.hi, bf16[4,10,144,256]{3,2,1,0:T(8,128)(2,1)S(1)} %pad_maximum_fusion.lo.mid.hi, bf16[4,10,144,256]{3,2,1,0:T(8,128)(2,1)S(1)} %pad_maximum_fusion.lo.mid.hi, bf16[2,8,128,16]{3,2,1,0:T(8,128)(2,1)S(1)} %bitcast.34, ...), custom_call_target="tpu_custom_call" | custom-call | flops 1342177280 | bytes 8388608 | tf_op jit(solution)/shard_map/short/pallas_call | solution.py:229
  101.3 4.5 %short.5 = f32[2,2,128,256]{3,2,1,0:T(8,128)S(1)} custom-call(bf16[4,10,144,256]{3,2,1,0:T(8,128)(2,1)S(1)} %pad_maximum_fusion.lo.mid.hi, bf16[4,10,144,256]{3,2,1,0:T(8,128)(2,1)S(1)} %pad_maximum_fusion.lo.mid.hi, bf16[4,10,144,256]{3,2,1,0:T(8,128)(2,1)S(1)} %pad_maximum_fusion.lo.mid.hi, bf16[2,8,128,16]{3,2,1,0:T(8,128)(2,1)S(1)} %bitcast.35, ...), custom_call_target="tpu_custom_call" | custom-call | flops 1342177280 | bytes 8388608 | tf_op jit(solution)/shard_map/short/pallas_call | solution.py:229
  105.7 4.5 %short.6 = f32[2,2,128,256]{3,2,1,0:T(8,128)S(1)} custom-call(bf16[4,10,144,256]{3,2,1,0:T(8,128)(2,1)S(1)} %pad_maximum_fusion.lo.mid.hi, bf16[4,10,144,256]{3,2,1,0:T(8,128)(2,1)S(1)} %pad_maximum_fusion.lo.mid.hi, bf16[4,10,144,256]{3,2,1,0:T(8,128)(2,1)S(1)} %pad_maximum_fusion.lo.mid.hi, bf16[2,8,128,16]{3,2,1,0:T(8,128)(2,1)S(1)} %bitcast.36, ...), custom_call_target="tpu_custom_call" | custom-call | flops 1342177280 | bytes 8388608 | tf_op jit(solution)/shard_map/short/pallas_call | solution.py:229
  110.2 4.5 %short.7 = f32[2,2,128,256]{3,2,1,0:T(8,128)S(1)} custom-call(bf16[4,10,144,256]{3,2,1,0:T(8,128)(2,1)S(1)} %pad_maximum_fusion.lo.mid.hi, bf16[4,10,144,256]{3,2,1,0:T(8,128)(2,1)S(1)} %pad_maximum_fusion.lo.mid.hi, bf16[4,10,144,256]{3,2,1,0:T(8,128)(2,1)S(1)} %pad_maximum_fusion.lo.mid.hi, bf16[2,8,128,16]{3,2,1,0:T(8,128)(2,1)S(1)} %bitcast.37, ...), custom_call_target="tpu_custom_call" | custom-call | flops 1342177280 | bytes 8388608 | tf_op jit(solution)/shard_map/short/pallas_call | solution.py:229
  115.6 6.6 %field.1 = bf16[2048,256]{1,0:T(8,128)(2,1)} custom-call(bf16[2,2048,1024]{2,1,0:T(8,128)(2,1)S(1)} %bitcast.39, bf16[8,256,256]{2,1,0:T(8,128)(2,1)S(1)} %bitcast.41, bf16[256,256]{1,0:T(8,128)(2,1)S(1)} %copy-done.4, f32[2048,256]{1,0:T(8,128)S(1)} %bitcast.40, f32[2048,1]{1,0:T(8,128)S(1)} %reshape.106.mask), custom_call_target="tpu_custom_call" | custom-call | flops 2147483648 | bytes 16777216 | tf_op jit(solution)/shard_map/field/pallas_call | solution.py:270
  (77 shorter events, 22.6 us)
Async XLA Ops:
  5.3 4.8 %copy-start = (bf16[2,8,16,8,256]{4,3,2,1,0:T(8,128)(2,1)S(1)}, bf16[2,8,16,8,256]{4,3,2,1,0:T(8,128)(2,1)}, u32[]{:S(2)}) copy-start(bf16[2,8,16,8,256]{4,3,2,1,0:T(8,128)(2,1)} %param.8) | copy-start | bytes 3145732
  20.6 3.3 %copy-start.2 = (bf16[2,2048,1024]{2,1,0:T(8,128)(2,1)}, bf16[2,2048,1024]{2,1,0:T(8,128)(2,1)S(1)}, u32[]{:S(2)}) copy-start(bf16[2,2048,1024]{2,1,0:T(8,128)(2,1)S(1)} %get-tuple-element.7.ph) | copy-start | bytes 25165828
  23.9 1.3 %copy-start.3 = (f32[2048,256]{1,0:T(8,128)}, f32[2048,256]{1,0:T(8,128)S(1)}, u32[]{:S(2)}) copy-start(f32[2048,256]{1,0:T(8,128)S(1)} %get-tuple-element.8) | copy-start | bytes 6291460
  23.9 2.1 %copy-start.9 = (pred[2,8,16,8]{3,2,1,0:T(8,128)(4,1)S(1)}, pred[2,8,16,8]{3,2,1,0:T(8,128)(4,1)}, u32[]{:S(2)}) copy-start(pred[2,8,16,8]{3,2,1,0:T(8,128)(4,1)} %get-tuple-element.13) | copy-start | bytes 6148
  25.3 2.2 %collective-permute-start = (bf16[1024,256]{1,0:T(8,128)(2,1)S(1)}, bf16[1024,256]{1,0:T(8,128)(2,1)}, u32[]{:S(2)}, u32[]{:S(2)}) collective-permute-start(bf16[1024,256]{1,0:T(8,128)(2,1)S(1)} %dynamic-slice_convert_fusion), channel_id=1, source_target_pairs={{0,1},{1,0},{2,3},{3,2},{4,5},{5,4},{6,7},{7,6},{8,9},{9,8},{10,11... | collective-permute-start | bytes 1572872 | tf_op jit(solution)/shard_map/ppermute | solution.py:298
  25.8 8.1 %copy-start.8 = (bf16[2,8,16,8,3]{2,3,4,1,0:T(8,128)(2,1)S(1)}, bf16[2,8,16,8,3]{2,3,4,1,0:T(8,128)(2,1)}, u32[]{:S(2)}) copy-start(bf16[2,8,16,8,3]{2,3,4,1,0:T(8,128)(2,1)} %param.9) | copy-start | bytes 36868
  25.9 54.8 %copy-start.5 = (bf16[2,8,120,256]{3,2,1,0:T(8,128)(2,1)}, bf16[2,8,120,256]{3,2,1,0:T(8,128)(2,1)S(1)}, u32[]{:S(2)}) copy-start(bf16[2,8,120,256]{3,2,1,0:T(8,128)(2,1)S(1)} %slice.35) | copy-start | bytes 2949124
  31.0 9.7 %collective-permute-start.1 = (bf16[512,256]{1,0:T(8,128)(2,1)S(1)}, bf16[512,256]{1,0:T(8,128)(2,1)}, u32[]{:S(2)}, u32[]{:S(2)}) collective-permute-start(bf16[512,256]{1,0:T(8,128)(2,1)S(1)} %dynamic-slice_convert_fusion.1), channel_id=1, source_target_pairs={{0,2},{1,3},{2,0},{3,1},{4,6},{5,7},{6,4},{7,5},{8,10},{9,11},{10,... | collective-permute-start | bytes 786440 | tf_op jit(solution)/shard_map/ppermute | solution.py:298
  41.9 5.2 %collective-permute-start.2 = (bf16[256,256]{1,0:T(8,128)(2,1)S(1)}, bf16[256,256]{1,0:T(8,128)(2,1)}, u32[]{:S(2)}, u32[]{:S(2)}) collective-permute-start(bf16[256,256]{1,0:T(8,128)(2,1)S(1)} %dynamic-slice_convert_fusion.2), channel_id=1, source_target_pairs={{0,4},{1,5},{2,6},{3,7},{4,0},{5,1},{6,2},{7,3},{8,12},{9,13},{10,... | collective-permute-start | bytes 393224 | tf_op jit(solution)/shard_map/ppermute | solution.py:298
  44.9 34.5 %collective-permute-start.10 = (bf16[2,8,144,256]{3,2,1,0:T(8,128)(2,1)}, bf16[2,8,144,256]{3,2,1,0:T(8,128)(2,1)}, u32[]{:S(2)}, u32[]{:S(2)}) collective-permute-start(bf16[2,8,144,256]{3,2,1,0:T(8,128)(2,1)} %pad_maximum_fusion.2), channel_id=1, source_target_pairs={{0,16},{16,0},{1,17},{17,1},{2,18},{18,2},{3,19},{19,3},{4,20},{20... | collective-permute-start | bytes 3538952 | tf_op jit(solution)/shard_map/ppermute | solution.py:325
  48.7 5.2 %collective-permute-start.3 = (bf16[128,256]{1,0:T(8,128)(2,1)S(1)}, bf16[128,256]{1,0:T(8,128)(2,1)S(1)}, u32[]{:S(2)}, u32[]{:S(2)}) collective-permute-start(bf16[128,256]{1,0:T(8,128)(2,1)S(1)} %dynamic-slice_convert_fusion.3), channel_id=1, source_target_pairs={{0,8},{1,9},{2,10},{3,11},{4,12},{5,13},{6,14},{7,15},{8,0},{9,1},... | collective-permute-start | bytes 196616 | tf_op jit(solution)/shard_map/ppermute | solution.py:298
  54.9 17.8 %collective-permute-start.4 = (bf16[64,256]{1,0:T(8,128)(2,1)S(1)}, bf16[64,256]{1,0:T(8,128)(2,1)S(1)}, u32[]{:S(2)}, u32[]{:S(2)}) collective-permute-start(bf16[64,256]{1,0:T(8,128)(2,1)S(1)} %dynamic-slice_convert_fusion.4), channel_id=1, source_target_pairs={{0,16},{1,17},{2,18},{3,19},{4,20},{5,21},{6,22},{7,23},{8,24},{9,... | collective-permute-start | bytes 98312 | tf_op jit(solution)/shard_map/ppermute | solution.py:298
  72.7 4.0 %collective-permute-start.5 = (bf16[64,256]{1,0:T(8,128)(2,1)S(1)}, bf16[64,256]{1,0:T(8,128)(2,1)S(1)}, u32[]{:S(2)}, u32[]{:S(2)}) collective-permute-start(bf16[64,256]{1,0:T(8,128)(2,1)S(1)} %add_convert_fusion), channel_id=1, source_target_pairs={{0,16},{1,17},{2,18},{3,19},{4,20},{5,21},{6,22},{7,23},{8,24},{9,... | collective-permute-start | bytes 98312 | tf_op jit(solution)/shard_map/ppermute | solution.py:298
  76.7 9.4 %collective-permute-start.6 = (bf16[128,256]{1,0:T(8,128)(2,1)S(1)}, bf16[128,256]{1,0:T(8,128)(2,1)S(1)}, u32[]{:S(2)}, u32[]{:S(2)}) collective-permute-start(bf16[128,256]{1,0:T(8,128)(2,1)S(1)} %maximum_select_fusion.4), channel_id=1, source_target_pairs={{0,8},{1,9},{2,10},{3,11},{4,12},{5,13},{6,14},{7,15},{8,0},{9,1},... | collective-permute-start | bytes 196616 | tf_op jit(solution)/shard_map/ppermute | solution.py:298
  80.7 1.0 copy-start.6
  81.7 12.9 %collective-permute-start.11 = (bf16[4,1,144,256]{3,2,1,0:T(8,128)(2,1)}, bf16[4,1,144,256]{3,2,1,0:T(8,128)(2,1)}, u32[]{:S(2)}, u32[]{:S(2)}) collective-permute-start(bf16[4,1,144,256]{3,2,1,0:T(8,128)(2,1)} %get-tuple-element.9), channel_id=1, source_target_pairs={{0,1},{1,2},{2,3},{3,4},{4,5},{5,6},{6,7},{7,8},{8,9},{9,10},{10,1... | collective-permute-start | bytes 884744 | tf_op jit(solution)/shard_map/ppermute | solution.py:331
  81.7 12.9 %collective-permute-start.12 = (bf16[4,1,144,256]{3,2,1,0:T(8,128)(2,1)}, bf16[4,1,144,256]{3,2,1,0:T(8,128)(2,1)}, u32[]{:S(2)}, u32[]{:S(2)}) collective-permute-start(bf16[4,1,144,256]{3,2,1,0:T(8,128)(2,1)} %get-tuple-element.10), channel_id=1, source_target_pairs={{1,0},{2,1},{3,2},{4,3},{5,4},{6,5},{7,6},{8,7},{9,8},{10,9},{11,1... | collective-permute-start | bytes 884744 | tf_op jit(solution)/shard_map/ppermute | solution.py:332
  86.8 5.8 %collective-permute-start.7 = (bf16[256,256]{1,0:T(8,128)(2,1)}, bf16[256,256]{1,0:T(8,128)(2,1)}, u32[]{:S(2)}, u32[]{:S(2)}) collective-permute-start(bf16[256,256]{1,0:T(8,128)(2,1)} %maximum_select_fusion.3), channel_id=1, source_target_pairs={{0,4},{1,5},{2,6},{3,7},{4,0},{5,1},{6,2},{7,3},{8,12},{9,13},{10,... | collective-permute-start | bytes 393224 | tf_op jit(solution)/shard_map/ppermute | solution.py:298
  93.8 2.7 %copy-start.1 = (bf16[8,256,256]{2,1,0:T(8,128)(2,1)S(1)}, bf16[8,256,256]{2,1,0:T(8,128)(2,1)}, u32[]{:S(2)}) copy-start(bf16[8,256,256]{2,1,0:T(8,128)(2,1)} %param.12) | copy-start | bytes 3145732
  93.8 7.1 %collective-permute-start.8 = (bf16[512,256]{1,0:T(8,128)(2,1)S(1)}, bf16[512,256]{1,0:T(8,128)(2,1)S(1)}, u32[]{:S(2)}, u32[]{:S(2)}) collective-permute-start(bf16[512,256]{1,0:T(8,128)(2,1)S(1)} %maximum_select_fusion.2), channel_id=1, source_target_pairs={{0,2},{1,3},{2,0},{3,1},{4,6},{5,7},{6,4},{7,5},{8,10},{9,11},{10,... | collective-permute-start | bytes 786440 | tf_op jit(solution)/shard_map/ppermute | solution.py:298
  101.2 13.8 %collective-permute-start.9 = (bf16[1024,256]{1,0:T(8,128)(2,1)S(1)}, bf16[1024,256]{1,0:T(8,128)(2,1)S(1)}, u32[]{:S(2)}, u32[]{:S(2)}) collective-permute-start(bf16[1024,256]{1,0:T(8,128)(2,1)S(1)} %maximum_select_fusion.1), channel_id=1, source_target_pairs={{0,1},{1,0},{2,3},{3,2},{4,5},{5,4},{6,7},{7,6},{8,9},{9,8},{10,11... | collective-permute-start | bytes 1572872 | tf_op jit(solution)/shard_map/ppermute | solution.py:298
  105.7 9.5 %slice-start = ((s8[8388608]{0:T(1024)(128)(4,1)}), s8[4194304]{0:T(1024)(128)(4,1)S(1)}, s32[]{:S(2)}) async-start(s8[8388608]{0:T(1024)(128)(4,1)} %bitcast.38), calls=%async_computation | async-start | bytes 8388608
  110.2 5.0 %slice-start.1 = ((s8[8388608]{0:T(1024)(128)(4,1)}), s8[4194304]{0:T(1024)(128)(4,1)S(1)}, s32[]{:S(2)}) async-start(s8[8388608]{0:T(1024)(128)(4,1)} %bitcast.38), calls=%async_computation.1 | async-start | bytes 8388608
  114.7 0.9 copy-start.4
  (1 other events, 0.7 us)
where the time goes:
time: 123 us; the launch traced here: 122 us
  Pallas kernels  35 us (28%)
  waiting for transfers between devices  34.6 us (28%)
  starting transfers between devices  20.8 us (17%)
  local copies, waits for them, and re-layouts  16.9 us (14%)
  other arithmetic  14.4 us (12%)
    ppermute x10, waiting for transfers between devices, swap(): return lax.ppermute(value, AXES, [(i, i ^ bit) for i in range(count)])  34.6 us
    pallas_call x4, Pallas kernels, short_call(): pl.pallas_call(functools.partial(short_kernel, slots, basis), grid=(count...  17.9 us
    ppermute x10, starting transfers between devices, swap(): return lax.ppermute(value, AXES, [(i, i ^ bit) for i in range(count)])  14.9 us
    pallas_call x1, Pallas kernels, factor_call(): pl.pallas_call(functools.partial(factor_kernel, grid_all, scale_all), gri...  10.5 us
    unnamed x26, local copies, waits for them, and re-layouts  8.53 us
    pallas_call x1, Pallas kernels, field_call(): pl.pallas_call(field_kernel, grid=(atoms // tile,), in_specs=[pl.BlockSpe...  6.59 us
    add x4, other arithmetic, reduce_halving(): value = keep + swap(give, bit).astype(F32)  5.48 us
    ppermute x1, starting transfers between devices, with_halo(): lax.ppermute(head, axis, [((i + 1) % count, i) for i in range(count)])  4.44 us
  transfers between devices with their start and end apart: 13, of which 7 were waited for; matrix products, arithmetic and copies ran while one was open for 8% of the time, Pallas kernels for 15%

commit v1 on v0

v1 whole, which is shorter than its diff:
```python
import functools
import math

import jax
import jax.numpy as jnp
from jax import lax
from jax.experimental import pallas as pl
from jax.experimental.pallas import tpu as pltpu
from jax.sharding import PartitionSpec as P

TWO_PI = 2.0 * math.pi
SHARPNESS = 600.0
CENTER_LOW = 0.2
CENTER_SPAN = 0.5
SCREEN = 16.0
FAR = 8.0
BF16 = jnp.bfloat16
F32 = jnp.float32
AXES = ("gx", "gy")
KTILE = 256

HALF_COS = (
    1.4142134965644628,
    -6.978850988150233,
    5.739461168545313,
    -1.8835629713129327,
    0.3106981552009573,
)
HALF_SIN = (4.442867902918289, -7.307443416752583, 3.594788034903934, -0.7843739144750123)
NT = (((1,), (1,)), ((), ()))
TN = (((0,), (0,)), ((), ()))
TT = (((0,), (1,)), ((), ()))
OCC_ROW = 3
CELL_ROW = 4
POS_ROWS = 16
VMEM = pltpu.VMEM


def horner(coefs, s):
    value = coefs[-1] * s + coefs[-2]
    for c in coefs[-3::-1]:
        value = value * s + c
    return value


def factor_kernel(grid_all, scale_all, pos, kidx, feat, wc, ph, fac, charges, kmat, kw):
    step = pl.program_id(0)
    planes, cols, _, rows = pos.shape
    atoms = planes * cols * rows
    vectors = kidx.shape[1]

    @pl.when(step == 0)
    def _():
        sub = lax.broadcasted_iota(jnp.int32, (POS_ROWS, KTILE), 0)
        parts = []
        for j in range(0, vectors, KTILE):
            waves = [
                kidx[d : d + 1, j : j + KTILE].astype(F32) * (1.0 / grid_all[d]) for d in range(3)
            ]
            value = jnp.zeros((POS_ROWS, KTILE), F32)
            k_sq = jnp.zeros((1, KTILE), F32)
            for d in range(3):
                hit = (sub == d) | (sub == CELL_ROW + d)
                value = jnp.where(hit, jnp.broadcast_to(waves[d], value.shape), value)
                wave = TWO_PI * waves[d]
                k_sq = k_sq + wave * wave
            kmat[j // KTILE] = value.astype(BF16)
            parts.append(jnp.exp(-k_sq / (4.0 * SCREEN)) / k_sq)
        total = sum(jnp.sum(part, axis=1, keepdims=True) for part in parts)
        for j, part in enumerate(parts):
            kw[j] = jnp.broadcast_to(part / total * scale_all, (8, KTILE))
        for x in range(planes):
            for y in range(cols):
                j = (x * cols + y) * rows
                c = lax.dot_general(wc[...], feat[j : j + rows, :], TT, preferred_element_type=F32)
                occ = pos[x, y, OCC_ROW : OCC_ROW + 1, :].astype(F32)
                charges[:, j : j + rows] = (c * occ).astype(BF16)

    sub = lax.broadcasted_iota(jnp.int32, (POS_ROWS, rows), 0)
    depth = (lax.broadcasted_iota(jnp.int32, (POS_ROWS, rows), 1) // 8).astype(F32)
    x0 = (lax.axis_index("gx") * planes).astype(F32)
    y0 = (lax.axis_index("gy") * cols).astype(F32)
    for x in range(planes):
        for y in range(cols):
            j = (x * cols + y) * rows
            tile = pos[x, y].astype(F32)
            tile = jnp.where(sub == CELL_ROW, x0 + float(x), tile)
            tile = jnp.where(sub == CELL_ROW + 1, y0 + float(y), tile)
            tile = jnp.where(sub == CELL_ROW + 2, depth, tile)
            t = lax.dot_general(tile.astype(BF16), kmat[step], TN, preferred_element_type=F32)
            r = t - jnp.round(t)
            s = r * r
            half_c = horner(HALF_COS, s)
            half_s = horner(HALF_SIN, s) * r
            ph[0, j : j + rows, :] = (1.0 - half_s * half_s).astype(BF16)
            ph[1, j : j + rows, :] = (half_s * half_c).astype(BF16)
    weight = kw[step][0:1, :]
    width = charges.shape[0]
    for p in range(2):
        part = jnp.dot(charges[...], ph[p], preferred_element_type=F32)
        fac[p * width : (p + 1) * width, :] = part * weight


def factor_call(pos, kidx, feat, wc, grid_all, scale_all):
    planes, cols, _, rows = pos.shape
    atoms, width = feat.shape
    vectors = kidx.shape[1]
    steps = vectors // KTILE
    return pl.pallas_call(
        functools.partial(factor_kernel, grid_all, scale_all),
        grid=(steps,),
        in_specs=[
            pl.BlockSpec(pos.shape, lambda i: (0, 0, 0, 0)),
            pl.BlockSpec(kidx.shape, lambda i: (0, 0)),
            pl.BlockSpec((atoms, width), lambda i: (0, 0)),
            pl.BlockSpec((width, width), lambda i: (0, 0)),
        ],
        out_specs=[
            pl.BlockSpec((2, atoms, KTILE), lambda i: (0, 0, i)),
            pl.BlockSpec((2 * width, KTILE), lambda i: (i, 0)),
        ],
        out_shape=[
            jax.ShapeDtypeStruct((2, atoms, vectors), BF16),
            jax.ShapeDtypeStruct((steps * 2 * width, KTILE), F32),
        ],
        scratch_shapes=[
            VMEM((width, atoms), BF16),
            VMEM((steps, POS_ROWS, KTILE), BF16),
            VMEM((steps, 8, KTILE), F32),
        ],
        compiler_params=pltpu.CompilerParams(
            dimension_semantics=("arbitrary",), vmem_limit_bytes=20 << 20
        ),
        cost_estimate=pl.CostEstimate(
            flops=24 * atoms * vectors * width, bytes_accessed=16 << 20, transcendentals=0
        ),
        name="factor",
    )(pos, kidx, feat, wc)


def short_rows(slots, basis, planes, rows, width, near_feat, near_pos, own_pos, own_feat, w, out, agg):
    pairs = rows // (2 * slots)
    two = 2 * slots
    window = 4 * slots
    sub = lax.broadcasted_iota(jnp.int32, (8, 128), 0)
    lane = lax.broadcasted_iota(jnp.int32, (8, 128), 1)
    lane_block = lane // window
    cell_in_window = (lane % window) // slots
    z_off = jnp.where(sub == 2, (cell_in_window - 1).astype(F32), 0.0)
    columns = [(dx, dy) for dx in (-1, 0, 1) for dy in (-1, 0, 1) if (dx, dy) != (0, 0)]
    columns.append((0, 0))
    select = jnp.where(
        lax.broadcasted_iota(jnp.int32, (POS_ROWS, 384), 0)
        == lax.broadcasted_iota(jnp.int32, (POS_ROWS, 384), 1) // 128,
        1.0,
        0.0,
    ).astype(BF16)
    stretch = math.sqrt(SHARPNESS * math.log2(math.e))
    centers = [stretch * (CENTER_LOW + b * (CENTER_SPAN / (basis - 1))) for b in range(basis)]

    for xi in range(planes):
        placed = []
        for dx, dy in columns:
            coords = near_pos(xi + dx, dy).astype(F32)[0:8]
            occ = jnp.broadcast_to(coords[OCC_ROW : OCC_ROW + 1, :], coords.shape)
            shift = jnp.where(sub == 0, float(dx), jnp.where(sub == 1, float(dy), 0.0))
            placed.append(jnp.where(occ > 0.0, coords + shift, FAR))
        own_all = lax.dot_general(own_pos(xi), select, TN, preferred_element_type=F32)
        for p in range(pairs):
            packed = []
            for h in range(3):
                merged = None
                for c in range(4 * h, min(4 * h + 4, 9)):
                    amount = (window * (c % 4) - two * p) % 128
                    moved = pltpu.roll(placed[c], amount, axis=1) if amount else placed[c]
                    merged = (
                        moved if merged is None else jnp.where(lane_block == c % 4, moved, merged)
                    )
                merged = merged + z_off
                if h == 2:
                    merged = jnp.where(lane_block == 0, merged, FAR)
                packed.append([jnp.broadcast_to(merged[d : d + 1, :], (8, 128)) for d in range(3)])
            parts = [[None, None] for _ in range(3)]
            for h in range(3):
                for q in range(2):
                    r0 = (two * p + slots * (1 + q)) % rows
                    d2 = None
                    for d in range(3):
                        mine = own_all[r0 : r0 + slots, 128 * d : 128 * d + 128]
                        if d == 2 and q == 1:
                            mine = mine + 1.0
                        delta = packed[h][d] - mine
                        d2 = delta * delta if d2 is None else d2 + delta * delta
                    env = jnp.maximum(1.0 - d2, 0.0)
                    env = env * env
                    if h == 2:
                        env = jnp.where(lane == sub + slots * (1 + q), 0.0, env)
                    ar = jnp.sqrt(d2) * stretch
                    values = []
                    for b in range(basis):
                        u = ar - centers[b]
                        values.append(jnp.exp2(u * (centers[b] - ar)) * env)
                    parts[h][q] = values
            lhs = []
            for h in range(3):
                lhs.append(
                    jnp.concatenate(
                        [
                            jnp.concatenate([parts[h][0][b], parts[h][1][b]], axis=0).astype(BF16)
                            for b in range(basis)
                        ],
                        axis=0,
                    )
                )
            near = []
            nxt = two * ((p + 1) % pairs)
            for dx, dy in columns:
                near.append(near_feat(xi + dx, dy, two * p, two))
                near.append(near_feat(xi + dx, dy, nxt, two))
            pad = jnp.zeros((384 - 9 * window, width), BF16)
            total = jnp.dot(
                jnp.concatenate(lhs, axis=1),
                jnp.concatenate(near + [pad], axis=0),
                preferred_element_type=F32,
            ).astype(BF16)
            for b in range(basis):
                agg[xi, two * p : two * p + two, width * b : width * (b + 1)] = total[
                    two * b : two * b + two
                ]
    value = jnp.dot(
        agg[...].reshape(planes * rows, basis * width), w[...], preferred_element_type=F32
    )
    value = jax.nn.silu(value).reshape(planes, rows, width)
    for xi in range(planes):
        turned = jnp.concatenate([value[xi, rows - slots :], value[xi, : rows - slots]], axis=0)
        out(xi, own_feat(xi).astype(F32) + turned)


def inner_kernel(slots, basis, first, count, feat, pos, side_feat, side_pos, w, out, agg):
    planes, _, rows, width = feat.shape

    def body(i, carry):
        y = first + i

        def pick(ref, side, x):
            if 0 <= x < planes:
                return ref, x
            return side, (0 if x == planes else 1)

        def near_feat(x, dy, start, size):
            ref, i = pick(feat, side_feat, x)
            return ref[i, y + dy, start : start + size, :]

        def near_pos(x, dy):
            ref, i = pick(pos, side_pos, x)
            return ref[i, y + dy]

        def write(x, value):
            out[i, x] = value

        short_rows(
            slots, basis, planes, rows, width, near_feat, near_pos,
            lambda x: pos[x, y], lambda x: feat[x, y], w, write, agg,
        )
        return carry

    lax.fori_loop(0, count, body, 0)


def edge_kernel(slots, basis, y, halo_dy, feat, pos, side_feat, side_pos, halo, w, out, agg):
    planes, _, rows, width = feat.shape

    def pick(ref, side, x):
        if 0 <= x < planes:
            return ref, x
        return side, (0 if x == planes else 1)

    def near_feat(x, dy, start, size):
        if dy == halo_dy:
            return halo[x + 1, 0, start : start + size, :]
        ref, i = pick(feat, side_feat, x)
        return ref[i, y + dy, start : start + size, :]

    def near_pos(x, dy):
        if dy == halo_dy:
            return halo[x + 1, 0, rows : rows + POS_ROWS, 0:128]
        ref, i = pick(pos, side_pos, x)
        return ref[i, y + dy]

    def write(x, value):
        out[0, x] = value

    short_rows(
        slots, basis, planes, rows, width, near_feat, near_pos,
        lambda x: pos[x, y], lambda x: feat[x, y], w, write, agg,
    )


def short_call(kernel, name, count, basis, *args):
    planes, _, rows, width = args[0].shape
    whole = pl.BlockSpec(memory_space=VMEM)
    return pl.pallas_call(
        kernel,
        in_specs=[whole] * len(args),
        out_specs=whole,
        out_shape=jax.ShapeDtypeStruct((count, planes, rows, width), F32),
        scratch_shapes=[VMEM((planes, rows, basis * width), BF16)],
        compiler_params=pltpu.CompilerParams(vmem_limit_bytes=16 << 20),
        cost_estimate=pl.CostEstimate(
            flops=count * planes * rows * width * 8 * (basis * 384 + basis * width),
            bytes_accessed=4 << 20,
            transcendentals=count * planes * rows * 384 * (basis + 1),
        ),
        name=name,
    )(*args)


def field_kernel(ph, weighted, w_out, base, pos, out):
    tiles, width, _ = weighted.shape
    lhs = jnp.concatenate(
        [ph[t % 2, :, KTILE * (t // 2) : KTILE * (t // 2 + 1)] for t in range(tiles)], axis=1
    )
    rhs = jnp.concatenate([weighted[t] for t in range(tiles)], axis=1)
    recip = lax.dot_general(lhs, rhs, NT, preferred_element_type=F32)
    far = jnp.dot(recip.astype(BF16), w_out[...], preferred_element_type=F32)
    sub = lax.broadcasted_iota(jnp.int32, (POS_ROWS, width), 0)
    select = jnp.where(sub == OCC_ROW, 1.0, 0.0).astype(BF16)
    rows = base.shape[2]
    for y in range(base.shape[0]):
        occ = lax.dot_general(pos[0, y], select, TN, preferred_element_type=F32)
        value = base[y, 0] + far[rows * y : rows * (y + 1)]
        out[rows * y : rows * (y + 1), :] = jnp.where(occ > 0.0, value, 0.0).astype(BF16)


def field_call(ph, weighted, w_out, base, pos, group=2):
    _, atoms, vectors = ph.shape
    tiles, width, _ = weighted.shape
    cols, planes, rows, _ = base.shape
    tile = group * rows
    groups = cols // group
    return pl.pallas_call(
        field_kernel,
        grid=(atoms // tile,),
        in_specs=[
            pl.BlockSpec((2, tile, vectors), lambda i: (0, i, 0)),
            pl.BlockSpec((tiles, width, KTILE), lambda i: (0, 0, 0)),
            pl.BlockSpec((width, width), lambda i: (0, 0)),
            pl.BlockSpec((group, 1, rows, width), lambda i: (i % groups, i // groups, 0, 0)),
            pl.BlockSpec((1, group, POS_ROWS, rows), lambda i: (i // groups, i % groups, 0, 0)),
        ],
        out_specs=pl.BlockSpec((tile, width), lambda i: (i, 0)),
        out_shape=jax.ShapeDtypeStruct((atoms, width), BF16),
        compiler_params=pltpu.CompilerParams(
            dimension_semantics=("arbitrary",), vmem_limit_bytes=16 << 20
        ),
        cost_estimate=pl.CostEstimate(
            flops=4 * atoms * vectors * width, bytes_accessed=16 << 20, transcendentals=0
        ),
        name="field",
    )(ph, weighted, w_out, base, pos)


def my_index():
    return lax.axis_index("gx") * lax.axis_size("gy") + lax.axis_index("gy")


def swap(value, mask):
    count = lax.axis_size("gx") * lax.axis_size("gy")
    return lax.ppermute(value, AXES, [(i, i ^ mask) for i in range(count)])


def tied(*values):
    return lax.optimization_barrier(values)


def no_work():
    return ()


class Exchange:
    def __init__(self):
        size_y = lax.axis_size("gy")
        count = lax.axis_size("gx") * size_y
        bits = [1 << i for i in range(count.bit_length() - 1)]
        low = [b for b in bits if b < size_y]
        self.halved = low[:2]
        self.direct = low[2:4]
        self.whole = low[4:] + [b for b in bits if b >= size_y]
        self.masks = [0]
        for b in self.direct:
            self.masks = self.masks + [m ^ b for m in self.masks]

    def place(self):
        return sum(((my_index() // b) % 2) << k for k, b in enumerate(self.direct))

    def halve(self, value, bit, work=no_work, arrived=()):
        half = value.shape[0] // 2
        mine = (my_index() // bit) % 2
        keep = lax.dynamic_slice_in_dim(value, mine * half, half, 0)
        give = lax.dynamic_slice_in_dim(value, (1 - mine) * half, half, 0).astype(BF16)
        got, arrived = tied(swap(give, bit), arrived)
        return keep + got.astype(F32), arrived

    def spread_sum(self, value, work):
        count = len(self.masks)
        value = value.reshape((count, -1) + value.shape[1:])
        me = self.place()
        keep = lax.dynamic_index_in_dim(value, me, 0, False)
        gives = [
            lax.dynamic_index_in_dim(value, me ^ j, 0, False).astype(BF16) for j in range(1, count)
        ]
        gives, done = run_under(gives, self.masks[1:], work)
        for got in gives:
            keep = keep + got.astype(F32)
        return keep, done

    def whole_sum(self, value, bit, work=no_work):
        (got,), done = run_under([value.astype(BF16)], [bit], work)
        return value + got.astype(F32), done

    def spread(self, value, work):
        count = len(self.masks)
        got, done = run_under([value] * (count - 1), self.masks[1:], work)
        parts = jnp.stack([value] + got)
        me = self.place()
        for k in range(len(self.direct)):
            b = 1 << k
            cut = parts.reshape((count // (2 * b), 2, b) + value.shape)
            parts = jnp.where((me >> k) & 1 == 0, cut, cut[:, ::-1]).reshape(parts.shape)
        return parts.reshape((-1,) + value.shape[1:]), done

    def double(self, value, bit, work=no_work):
        mine = (my_index() // bit) % 2
        (other,), done = run_under([value], [bit], work)
        return (
            jnp.where(
                mine == 0, jnp.concatenate([value, other]), jnp.concatenate([other, value])
            ),
            done,
        )


def run_under(gives, masks, work):
    inputs = work.inputs if work is not no_work else ()
    gives, inputs = tied(list(gives), inputs)
    got = [swap(give, mask) for give, mask in zip(gives, masks)]
    done = work(*inputs) if work is not no_work else ()
    return tied(got, done)


class Work:
    def __init__(self, call, *inputs):
        self.call = call
        self.inputs = inputs

    def __call__(self, *inputs):
        return self.call(*inputs)


def side_planes(cells):
    count = lax.axis_size("gx")
    size = cells.shape[0]
    if count == 2 and size == 2:
        return lax.ppermute(cells, "gx", [(0, 1), (1, 0)])
    after = lax.ppermute(cells[:1], "gx", [((i + 1) % count, i) for i in range(count)])
    before = lax.ppermute(cells[size - 1 :], "gx", [(i, (i + 1) % count) for i in range(count)])
    return jnp.concatenate([after, before], axis=0)


def edge_rows(feat, pos, side_feat, side_pos, y):
    width = feat.shape[3]
    parts = []
    for f, q in ((side_feat[1:2], side_pos[1:2]), (feat, pos), (side_feat[0:1], side_pos[0:1])):
        q = jnp.pad(q[:, y : y + 1], ((0, 0), (0, 0), (0, 0), (0, width - q.shape[3])))
        parts.append(jnp.concatenate([f[:, y : y + 1], q], axis=2))
    return jnp.concatenate(parts, axis=0)


def on_device(features, fractions, counts, k_index, w_short, w_charge, w_out):
    planes, cols, depth, slots, width = features.shape
    basis = w_short.shape[0]
    vectors = k_index.shape[0]
    rows = depth * slots
    atoms = planes * cols * rows
    size_x, size_y = lax.axis_size("gx"), lax.axis_size("gy")
    grid_all = (planes * size_x, cols * size_y, depth)
    assert rows == 128 and slots == 8 and planes == 2 and cols == 8 and width == KTILE
    assert vectors % KTILE == 0
    for extent in grid_all:
        assert extent & (extent - 1) == 0 and extent <= 256
    scale_all = math.sqrt(vectors / (grid_all[0] * grid_all[1] * grid_all[2] * slots))

    feat = features.reshape(planes, cols, rows, width)
    side_feat = side_planes(feat)

    occupied = (jnp.arange(slots, dtype=jnp.int32) < counts[..., None]).astype(BF16)
    frac = jnp.transpose(fractions, (0, 1, 4, 2, 3)).reshape(planes, cols, 3, rows)
    pos = jnp.concatenate(
        [
            frac,
            occupied.reshape(planes, cols, 1, rows),
            jnp.zeros((planes, cols, POS_ROWS - 4, rows), BF16),
        ],
        axis=2,
    )
    side_pos = side_planes(pos)

    ph, partial = factor_call(
        pos, k_index.T, feat.reshape(atoms, width), w_charge, grid_all, scale_all
    )

    w_flat = w_short.reshape(basis * width, width)
    exchange = Exchange()

    def inner(first, count):
        kernel = functools.partial(inner_kernel, slots, basis, first, count)
        return lambda *args: short_call(kernel, "short", count, basis, *args)

    def edges(*args):
        *common, low, high, w = args
        first = short_call(
            functools.partial(edge_kernel, slots, basis, 0, -1), "low", 1, basis, *common, low, w
        )
        last = short_call(
            functools.partial(edge_kernel, slots, basis, cols - 1, 1),
            "high", 1, basis, *common, high, w,
        )
        return first, last

    value, _ = exchange.halve(partial, exchange.halved[0])
    value, (side_feat, side_pos) = exchange.halve(
        value, exchange.halved[1], arrived=(side_feat, side_pos)
    )
    near = (feat, pos, side_feat, side_pos)
    up = [(i, (i + 1) % size_y) for i in range(size_y)]
    down = [((i + 1) % size_y, i) for i in range(size_y)]
    low = lax.ppermute(edge_rows(*near, cols - 1), "gy", up)
    high = lax.ppermute(edge_rows(*near, 0), "gy", down)

    value, rows_a = exchange.spread_sum(value, Work(inner(1, 2), *near, w_flat))
    rows_b = None
    for i, bit in enumerate(exchange.whole):
        if i == 0:
            value, rows_b = exchange.whole_sum(value, bit, Work(inner(3, 2), *near, w_flat))
        else:
            value, _ = exchange.whole_sum(value, bit)
    value = value.astype(BF16)
    value, rows_c = exchange.spread(value, Work(inner(5, 2), *near, w_flat))
    value, (row_first, row_last) = exchange.double(
        value, exchange.halved[1], Work(edges, *near, low, high, w_flat)
    )
    value, _ = exchange.double(value, exchange.halved[0])
    weighted = value.reshape(2 * vectors // KTILE, width, KTILE)
    base = jnp.concatenate([row_first, rows_a, rows_b, rows_c, row_last], axis=0)
    out = field_call(ph, weighted, w_out, base, pos)
    return out.reshape(features.shape)


def solution(mesh):
    return jax.shard_map(
        on_device,
        mesh=mesh,
        in_specs=(
            P("gx", "gy", None, None, None),
            P("gx", "gy", None, None, None),
            P("gx", "gy", None),
            P(),
            P(),
            P(),
            P(),
        ),
        out_specs=P("gx", "gy", None, None, None),
        check_vma=False,
    )
```

time: 123 us -> 99.3 us (0.81)
  waiting for transfers between devices: 34.6 us -> 20.7 us
  other arithmetic: 14.4 us -> 4.09 us
  local copies, waits for them, and re-layouts: 16.9 us -> 10.3 us
  Pallas kernels: 35 us -> 40.9 us
  starting transfers between devices: 20.8 us -> 22.2 us
    ppermute x13 -> x15, waiting for transfers between devices: 34.6 us -> 20.7 us  [the longest x2 18.8 us: side_planes(): return lax.ppermute(cells, 'gx', [(0, 1), (1, 0)])]
    unnamed x26 -> x18, local copies, waits for them, and re-layouts: 8.53 us -> 5.04 us
    pallas_call x4 -> x5, Pallas kernels: 17.9 us -> 21.1 us  [short_call(): pl.pallas_call(kernel, in_specs=[whole] * len(args), out_specs=whole, out...]
    concatenate x3, other arithmetic: 3.17 us -> 0.13 us  [the longest x1 0.09 us: on_device(): jnp.concatenate([frac, occupied.reshape(planes, cols, 1, rows), jnp.zeros...]
    concatenate x1 -> x2, local copies, waits for them, and re-layouts: 2.82 us -> 0.1 us  [the longest x1 0.08 us: on_device(): jnp.concatenate([frac, occupied.reshape(planes, cols, 1, rows), jnp.zeros...]
    add x4 -> x2, other arithmetic: 5.48 us -> 3.21 us  [halve(): return (keep + got.astype(F32), arrived)]
    select_n x6 -> x3, other arithmetic: 2.36 us -> 0.56 us  [the longest x2 0.51 us: double(): jnp.where(mine == 0, jnp.concatenate([value, other]), jnp.concatenate([ot...]
    pallas_call x1, Pallas kernels: 10.5 us -> 12.3 us  [factor_call(): pl.pallas_call(functools.partial(factor_kernel, grid_all, scale_all), gri...]
  transfers between devices with their start and end apart: 13 -> 15, of which waited for: 7 -> 3; matrix products, arithmetic and copies ran while one was open for 8% -> 6% of each run, Pallas kernels for 15% -> 21%
where the time goes in v1:
time: 99.3 us; the launch traced here: 98.7 us
  Pallas kernels  40.9 us (41%)
  starting transfers between devices  22.2 us (22%)
  waiting for transfers between devices  20.7 us (21%)
  local copies, waits for them, and re-layouts  10.3 us (10%)
  other arithmetic  4.09 us (4%)
    pallas_call x5, Pallas kernels, short_call(): pl.pallas_call(kernel, in_specs=[whole] * len(args), out_specs=whole, out...  21.1 us
    ppermute x2, waiting for transfers between devices, side_planes(): return lax.ppermute(cells, 'gx', [(0, 1), (1, 0)])  18.8 us
    ppermute x11, starting transfers between devices, swap(): return lax.ppermute(value, AXES, [(i, i ^ mask) for i in range(count)])  15.3 us
    pallas_call x1, Pallas kernels, factor_call(): pl.pallas_call(functools.partial(factor_kernel, grid_all, scale_all), gri...  12.3 us
    pallas_call x1, Pallas kernels, field_call(): pl.pallas_call(field_kernel, grid=(atoms // tile,), in_specs=[pl.BlockSpe...  7.46 us
    unnamed x18, local copies, waits for them, and re-layouts  5.04 us
    ppermute x1, starting transfers between devices, on_device(): high = lax.ppermute(edge_rows(*near, 0), 'gy', down)  4.19 us
    add x2, other arithmetic, halve(): return (keep + got.astype(F32), arrived)  3.21 us
  transfers between devices with their start and end apart: 15, of which 3 were waited for; matrix products, arithmetic and copies ran while one was open for 6% of the time, Pallas kernels for 21%

profile of v1, /device:TPU:0, one launch (start us, length us, event | category | flops | bytes accessed | tf_op | source)
XLA Modules:
  0.0 98.7 jit_solution(1255232214315381834)
XLA Ops:
  0.0 1.0 %copy.16 = bf16[2,8,3,16,8]{4,3,2,1,0:T(8,128)(2,1)S(1)} copy(bf16[2,8,3,16,8]{3,4,2,1,0:T(8,128)(2,1)} %bitcast.54) | data formatting | bytes 24576 | tf_op jit(solution)/shard_map/reshape | solution.py:497
  4.1 12.3 %factor.1 = (bf16[2,2048,1024]{2,1,0:T(8,128)(2,1)S(1)}, f32[2048,256]{1,0:T(8,128)S(1)}) custom-call(bf16[2,8,16,128]{3,2,1,0:T(8,128)(2,1)S(1)} %maximum_maximum_fusion.pos, s32[3,1024]{1,0:T(4,128)S(1)} %bitcast.46, bf16[2048,256]{1,0:T(8,128)(2,1)} %bitcast.4.feat, bf16[256,256]{1,0:T(8,128)(2,1)S(1)} %copy-done.3), custom_call_target="tpu_custom_call" | custom-call | flops 12884901888 | bytes 16777216 | tf_op jit(solution)/shard_map/factor/pallas_call | solution.py:109
  16.5 3.3 %copy-done = bf16[2,2048,1024]{2,1,0:T(8,128)(2,1)} copy-done((bf16[2,2048,1024]{2,1,0:T(8,128)(2,1)}, bf16[2,2048,1024]{2,1,0:T(8,128)(2,1)S(1)}, u32[]{:S(2)}) %copy-start) | copy-done | bytes 8388632
  21.0 2.5 %collective-permute-start.2 = (bf16[2,8,128,256]{3,2,1,0:T(8,128)(2,1)}, bf16[2,8,128,256]{3,2,1,0:T(8,128)(2,1)S(1)}, u32[]{:S(2)}, u32[]{:S(2)}) collective-permute-start(bf16[2,8,128,256]{3,2,1,0:T(8,128)(2,1)} %bitcast.5.feat), channel_id=1, source_target_pairs={{0,16},{16,0},{1,17},{17,1},{2,18},{18,2},{3,19},{19,3},{4,20},{20... | collective-permute-start | bytes 3145736 | tf_op jit(solution)/shard_map/ppermute | solution.py:464
  23.5 2.1 %convert_add_fusion = f32[1024,256]{1,0:T(8,128)} fusion(bf16[1024,256]{1,0:T(8,128)(2,1)} %collective-permute-done, f32[2048,256]{1,0:T(8,128)S(1)} %get-tuple-element.54, s32[]{:T(128)S(6)} %select_n.114), kind=kLoop, calls=%fused_computation.1 | loop fusion | flops 524288 | bytes 2621444 | tf_op jit(solution)/shard_map/add | solution.py:402
  25.7 1.1 %dynamic-slice_convert_fusion.1 = bf16[512,256]{1,0:T(8,128)(2,1)S(1)} fusion(f32[1024,256]{1,0:T(8,128)} %convert_add_fusion, s32[]{:T(128)S(6)} %select_n.117), kind=kLoop, calls=%fused_computation.18 | loop fusion | bytes 524292 | tf_op jit(solution)/shard_map/convert_element_type | solution.py:400
  26.7 2.3 %collective-permute-start.1 = (bf16[512,256]{1,0:T(8,128)(2,1)S(1)}, bf16[512,256]{1,0:T(8,128)(2,1)S(1)}, u32[]{:S(2)}, u32[]{:S(2)}) collective-permute-start(bf16[512,256]{1,0:T(8,128)(2,1)S(1)} %dynamic-slice_convert_fusion.1), channel_id=1, source_target_pairs={{0,2},{1,3},{2,0},{3,1},{4,6},{5,7},{6,4},{7,5},{8,10},{9,11},{10,... | collective-permute-start | bytes 786440 | tf_op jit(solution)/shard_map/ppermute | solution.py:369
  29.1 1.0 fusion.34
  30.1 18.8 %collective-permute-done.3.side_pos = bf16[2,8,16,128]{3,2,1,0:T(8,128)(2,1)S(1)} collective-permute-done((bf16[2,8,16,128]{3,2,1,0:T(8,128)(2,1)S(1)}, bf16[2,8,16,128]{3,2,1,0:T(8,128)(2,1)S(1)}, u32[]{:S(2)}, u32[]{:S(2)}) %collective-permute-start.3) | collective-permute-done | bytes 65568 | tf_op jit(solution)/shard_map/ppermute | solution.py:464
  49.0 4.2 %collective-permute-start.12 = (bf16[4,1,144,256]{3,2,1,0:T(8,128)(2,1)S(1)}, bf16[4,1,144,256]{3,2,1,0:T(8,128)(2,1)S(1)}, u32[]{:S(2)}, u32[]{:S(2)}) collective-permute-start(bf16[4,1,144,256]{3,2,1,0:T(8,128)(2,1)S(1)} %fusion.21), channel_id=1, source_target_pairs={{1,0},{2,1},{3,2},{4,3},{5,4},{6,5},{7,6},{8,7},{9,8},{10,9},{11,1... | collective-permute-start | bytes 884744 | tf_op jit(solution)/shard_map/ppermute | solution.py:538
  53.5 1.1 %convert_add_fusion.1 = f32[512,256]{1,0:T(8,128)S(1)} fusion(bf16[512,256]{1,0:T(8,128)(2,1)S(1)} %collective-permute-done.1, f32[1024,256]{1,0:T(8,128)} %convert_add_fusion, s32[]{:T(128)S(6)} %select_n.116), kind=kLoop, calls=%fused_computation.17 | loop fusion | flops 262144 | bytes 1310724 | tf_op jit(solution)/shard_map/add | solution.py:402
  54.7 1.0 %collective-permute-start.5 = (bf16[128,256]{1,0:T(8,128)(2,1)S(1)}, bf16[128,256]{1,0:T(8,128)(2,1)S(1)}, u32[]{:S(2)}, u32[]{:S(2)}) collective-permute-start(bf16[128,256]{1,0:T(8,128)(2,1)S(1)} %get-tuple-element.59), channel_id=1, source_target_pairs={{0,8},{1,9},{2,10},{3,11},{4,12},{5,13},{6,14},{7,15},{8,0},{9,1},... | collective-permute-start | bytes 196616 | tf_op jit(solution)/shard_map/ppermute | solution.py:369
  55.7 3.4 %collective-permute-start.6 = (bf16[128,256]{1,0:T(8,128)(2,1)S(1)}, bf16[128,256]{1,0:T(8,128)(2,1)S(1)}, u32[]{:S(2)}, u32[]{:S(2)}) collective-permute-start(bf16[128,256]{1,0:T(8,128)(2,1)S(1)} %get-tuple-element.60), channel_id=1, source_target_pairs={{0,12},{1,13},{2,14},{3,15},{4,8},{5,9},{6,10},{7,11},{8,4},{9,5},... | collective-permute-start | bytes 196616 | tf_op jit(solution)/shard_map/ppermute | solution.py:369
  59.1 4.9 %short.3 = f32[2,2,128,256]{3,2,1,0:T(8,128)S(1)} custom-call(bf16[2,8,128,256]{3,2,1,0:T(8,128)(2,1)} %bitcast.5.feat, bf16[2,8,16,128]{3,2,1,0:T(8,128)(2,1)S(1)} %maximum_maximum_fusion.pos, bf16[2,8,128,256]{3,2,1,0:T(8,128)(2,1)S(1)} %collective-permute-done.2.side_feat, bf16[2,8,16,128]{3,2,1,0:T(8,128)(2,1)S(1)} %collective-permute-done.3.side_pos, ...), custom_call_target="tpu_custom_call" | custom-call | flops 5368709120 | bytes 4194304 | tf_op jit(solution)/shard_map/short/pallas_call | solution.py:302
  64.1 1.6 %collective-permute-start.7 = (bf16[128,256]{1,0:T(8,128)(2,1)S(1)}, bf16[128,256]{1,0:T(8,128)(2,1)S(1)}, u32[]{:S(2)}, u32[]{:S(2)}) collective-permute-start(bf16[128,256]{1,0:T(8,128)(2,1)S(1)} %fusion.32), channel_id=1, source_target_pairs={{0,16},{1,17},{2,18},{3,19},{4,20},{5,21},{6,22},{7,23},{8,24},{9,... | collective-permute-start | bytes 196616 | tf_op jit(solution)/shard_map/ppermute | solution.py:369
  65.6 4.9 %short.4 = f32[2,2,128,256]{3,2,1,0:T(8,128)S(1)} custom-call(bf16[2,8,128,256]{3,2,1,0:T(8,128)(2,1)} %bitcast.5.feat, bf16[2,8,16,128]{3,2,1,0:T(8,128)(2,1)S(1)} %maximum_maximum_fusion.pos, bf16[2,8,128,256]{3,2,1,0:T(8,128)(2,1)S(1)} %collective-permute-done.2.side_feat, bf16[2,8,16,128]{3,2,1,0:T(8,128)(2,1)S(1)} %collective-permute-done.3.side_pos, ...), custom_call_target="tpu_custom_call" | custom-call | flops 5368709120 | bytes 4194304 | tf_op jit(solution)/shard_map/short/pallas_call | solution.py:302
  70.6 2.7 %collective-permute-start.10 = (bf16[128,256]{1,0:T(8,128)(2,1)S(1)}, bf16[128,256]{1,0:T(8,128)(2,1)S(1)}, u32[]{:S(2)}, u32[]{:S(2)}) collective-permute-start(bf16[128,256]{1,0:T(8,128)(2,1)S(1)} %add_convert_fusion), channel_id=1, source_target_pairs={{0,12},{1,13},{2,14},{3,15},{4,8},{5,9},{6,10},{7,11},{8,4},{9,5},... | collective-permute-start | bytes 196616 | tf_op jit(solution)/shard_map/ppermute | solution.py:369
  73.2 1.0 collective-permute-start.8
  75.0 4.9 %short.5 = f32[2,2,128,256]{3,2,1,0:T(8,128)S(1)} custom-call(bf16[2,8,128,256]{3,2,1,0:T(8,128)(2,1)} %bitcast.5.feat, bf16[2,8,16,128]{3,2,1,0:T(8,128)(2,1)S(1)} %maximum_maximum_fusion.pos, bf16[2,8,128,256]{3,2,1,0:T(8,128)(2,1)S(1)} %collective-permute-done.2.side_feat, bf16[2,8,16,128]{3,2,1,0:T(8,128)(2,1)S(1)} %collective-permute-done.3.side_pos, ...), custom_call_target="tpu_custom_call" | custom-call | flops 5368709120 | bytes 4194304 | tf_op jit(solution)/shard_map/short/pallas_call | solution.py:302
  80.3 2.0 %collective-permute-start.13 = (bf16[512,256]{1,0:T(8,128)(2,1)S(1)}, bf16[512,256]{1,0:T(8,128)(2,1)S(1)}, u32[]{:S(2)}, u32[]{:S(2)}) collective-permute-start(bf16[512,256]{1,0:T(8,128)(2,1)S(1)} %bitcast.51), channel_id=1, source_target_pairs={{0,2},{1,3},{2,0},{3,1},{4,6},{5,7},{6,4},{7,5},{8,10},{9,11},{10,... | collective-permute-start | bytes 786440 | tf_op jit(solution)/shard_map/ppermute | solution.py:369
  82.2 3.2 %high.1 = f32[1,2,128,256]{3,2,1,0:T(8,128)S(1)} custom-call(bf16[2,8,128,256]{3,2,1,0:T(8,128)(2,1)} %bitcast.5.feat, bf16[2,8,16,128]{3,2,1,0:T(8,128)(2,1)S(1)} %maximum_maximum_fusion.pos, bf16[2,8,128,256]{3,2,1,0:T(8,128)(2,1)S(1)} %collective-permute-done.2.side_feat, bf16[2,8,16,128]{3,2,1,0:T(8,128)(2,1)S(1)} %collective-permute-done.3.side_pos, ...), custom_call_target="tpu_custom_call" | custom-call | flops 2684354560 | bytes 4194304 | tf_op jit(solution)/shard_map/high/pallas_call | solution.py:302
  85.5 3.2 %low.1 = f32[1,2,128,256]{3,2,1,0:T(8,128)S(1)} custom-call(bf16[2,8,128,256]{3,2,1,0:T(8,128)(2,1)} %bitcast.5.feat, bf16[2,8,16,128]{3,2,1,0:T(8,128)(2,1)S(1)} %maximum_maximum_fusion.pos, bf16[2,8,128,256]{3,2,1,0:T(8,128)(2,1)S(1)} %collective-permute-done.2.side_feat, bf16[2,8,16,128]{3,2,1,0:T(8,128)(2,1)S(1)} %collective-permute-done.3.side_pos, ...), custom_call_target="tpu_custom_call" | custom-call | flops 2684354560 | bytes 4194304 | tf_op jit(solution)/shard_map/low/pallas_call | solution.py:302
  89.2 1.7 %collective-permute-done.14 = bf16[1024,256]{1,0:T(8,128)(2,1)S(1)} collective-permute-done((bf16[1024,256]{1,0:T(8,128)(2,1)S(1)}, bf16[1024,256]{1,0:T(8,128)(2,1)S(1)}, u32[]{:S(2)}, u32[]{:S(2)}) %collective-permute-start.14) | collective-permute-done | bytes 524320 | tf_op jit(solution)/shard_map/ppermute | solution.py:369
  91.2 7.5 %field.1 = bf16[2048,256]{1,0:T(8,128)(2,1)} custom-call(bf16[2,2048,1024]{2,1,0:T(8,128)(2,1)S(1)} %bitcast.39, bf16[8,256,256]{2,1,0:T(8,128)(2,1)S(1)} %bitcast.40, bf16[256,256]{1,0:T(8,128)(2,1)S(1)} %copy-done.1, f32[8,2,128,256]{3,2,1,0:T(8,128)S(1)} %constant_dynamic-update-slice_fusion.base, bf16[2,8,16,128]{3,2,1,0:T(8,128)(2,1)S(1)} %maximum_maximum_fusion.pos), custom_call_target="tpu_custom_call" | custom-call | flops 2147483648 | bytes 16777216 | tf_op jit(solution)/shard_map/field/pallas_call | solution.py:341
  (62 shorter events, 6.7 us)
Async XLA Ops:
  2.5 0.9 copy-start.3
  3.4 0.7 copy-start.4
  16.4 3.3 %copy-start = (bf16[2,2048,1024]{2,1,0:T(8,128)(2,1)}, bf16[2,2048,1024]{2,1,0:T(8,128)(2,1)S(1)}, u32[]{:S(2)}) copy-start(bf16[2,2048,1024]{2,1,0:T(8,128)(2,1)S(1)} %get-tuple-element.53.ph) | copy-start | bytes 25165828
  20.6 3.0 %collective-permute-start = (bf16[1024,256]{1,0:T(8,128)(2,1)}, bf16[1024,256]{1,0:T(8,128)(2,1)}, u32[]{:S(2)}, u32[]{:S(2)}) collective-permute-start(bf16[1024,256]{1,0:T(8,128)(2,1)} %dynamic-slice_convert_fusion), channel_id=1, source_target_pairs={{0,1},{1,0},{2,3},{3,2},{4,5},{5,4},{6,7},{7,6},{8,9},{9,8},{10,11... | collective-permute-start | bytes 1572872 | tf_op jit(solution)/shard_map/ppermute | solution.py:369
  21.0 27.9 %collective-permute-start.2 = (bf16[2,8,128,256]{3,2,1,0:T(8,128)(2,1)}, bf16[2,8,128,256]{3,2,1,0:T(8,128)(2,1)S(1)}, u32[]{:S(2)}, u32[]{:S(2)}) collective-permute-start(bf16[2,8,128,256]{3,2,1,0:T(8,128)(2,1)} %bitcast.5.feat), channel_id=1, source_target_pairs={{0,16},{16,0},{1,17},{17,1},{2,18},{18,2},{3,19},{19,3},{4,20},{20... | collective-permute-start | bytes 3145736 | tf_op jit(solution)/shard_map/ppermute | solution.py:464
  23.5 25.4 %collective-permute-start.3 = (bf16[2,8,16,128]{3,2,1,0:T(8,128)(2,1)S(1)}, bf16[2,8,16,128]{3,2,1,0:T(8,128)(2,1)S(1)}, u32[]{:S(2)}, u32[]{:S(2)}) collective-permute-start(bf16[2,8,16,128]{3,2,1,0:T(8,128)(2,1)S(1)} %maximum_maximum_fusion.pos), channel_id=1, source_target_pairs={{0,16},{16,0},{1,17},{17,1},{2,18},{18,2},{3,19},{19,3},{4,20},{20... | collective-permute-start | bytes 196616 | tf_op jit(solution)/shard_map/ppermute | solution.py:464
  26.7 32.4 %copy-start.2 = (bf16[8,256,256]{2,1,0:T(8,128)(2,1)S(1)}, bf16[8,256,256]{2,1,0:T(8,128)(2,1)}, u32[]{:S(2)}) copy-start(bf16[8,256,256]{2,1,0:T(8,128)(2,1)} %param.11) | copy-start | bytes 3145732
  26.7 22.2 %collective-permute-start.1 = (bf16[512,256]{1,0:T(8,128)(2,1)S(1)}, bf16[512,256]{1,0:T(8,128)(2,1)S(1)}, u32[]{:S(2)}, u32[]{:S(2)}) collective-permute-start(bf16[512,256]{1,0:T(8,128)(2,1)S(1)} %dynamic-slice_convert_fusion.1), channel_id=1, source_target_pairs={{0,2},{1,3},{2,0},{3,1},{4,6},{5,7},{6,4},{7,5},{8,10},{9,11},{10,... | collective-permute-start | bytes 786440 | tf_op jit(solution)/shard_map/ppermute | solution.py:369
  49.0 31.2 %collective-permute-start.12 = (bf16[4,1,144,256]{3,2,1,0:T(8,128)(2,1)S(1)}, bf16[4,1,144,256]{3,2,1,0:T(8,128)(2,1)S(1)}, u32[]{:S(2)}, u32[]{:S(2)}) collective-permute-start(bf16[4,1,144,256]{3,2,1,0:T(8,128)(2,1)S(1)} %fusion.21), channel_id=1, source_target_pairs={{1,0},{2,1},{3,2},{4,3},{5,4},{6,5},{7,6},{8,7},{9,8},{10,9},{11,1... | collective-permute-start | bytes 884744 | tf_op jit(solution)/shard_map/ppermute | solution.py:538
  53.2 27.0 %collective-permute-start.11 = (bf16[4,1,144,256]{3,2,1,0:T(8,128)(2,1)S(1)}, bf16[4,1,144,256]{3,2,1,0:T(8,128)(2,1)S(1)}, u32[]{:S(2)}, u32[]{:S(2)}) collective-permute-start(bf16[4,1,144,256]{3,2,1,0:T(8,128)(2,1)S(1)} %fusion.17), channel_id=1, source_target_pairs={{0,1},{1,2},{2,3},{3,4},{4,5},{5,6},{6,7},{7,8},{8,9},{9,10},{10,1... | collective-permute-start | bytes 884744 | tf_op jit(solution)/shard_map/ppermute | solution.py:537
  54.6 9.4 %collective-permute-start.4 = (bf16[128,256]{1,0:T(8,128)(2,1)S(1)}, bf16[128,256]{1,0:T(8,128)(2,1)S(1)}, u32[]{:S(2)}, u32[]{:S(2)}) collective-permute-start(bf16[128,256]{1,0:T(8,128)(2,1)S(1)} %get-tuple-element.58), channel_id=1, source_target_pairs={{0,4},{1,5},{2,6},{3,7},{4,0},{5,1},{6,2},{7,3},{8,12},{9,13},{10,... | collective-permute-start | bytes 196616 | tf_op jit(solution)/shard_map/ppermute | solution.py:369
  54.7 9.3 %collective-permute-start.5 = (bf16[128,256]{1,0:T(8,128)(2,1)S(1)}, bf16[128,256]{1,0:T(8,128)(2,1)S(1)}, u32[]{:S(2)}, u32[]{:S(2)}) collective-permute-start(bf16[128,256]{1,0:T(8,128)(2,1)S(1)} %get-tuple-element.59), channel_id=1, source_target_pairs={{0,8},{1,9},{2,10},{3,11},{4,12},{5,13},{6,14},{7,15},{8,0},{9,1},... | collective-permute-start | bytes 196616 | tf_op jit(solution)/shard_map/ppermute | solution.py:369
  55.7 8.3 %collective-permute-start.6 = (bf16[128,256]{1,0:T(8,128)(2,1)S(1)}, bf16[128,256]{1,0:T(8,128)(2,1)S(1)}, u32[]{:S(2)}, u32[]{:S(2)}) collective-permute-start(bf16[128,256]{1,0:T(8,128)(2,1)S(1)} %get-tuple-element.60), channel_id=1, source_target_pairs={{0,12},{1,13},{2,14},{3,15},{4,8},{5,9},{6,10},{7,11},{8,4},{9,5},... | collective-permute-start | bytes 196616 | tf_op jit(solution)/shard_map/ppermute | solution.py:369
  64.1 6.5 %collective-permute-start.7 = (bf16[128,256]{1,0:T(8,128)(2,1)S(1)}, bf16[128,256]{1,0:T(8,128)(2,1)S(1)}, u32[]{:S(2)}, u32[]{:S(2)}) collective-permute-start(bf16[128,256]{1,0:T(8,128)(2,1)S(1)} %fusion.32), channel_id=1, source_target_pairs={{0,16},{1,17},{2,18},{3,19},{4,20},{5,21},{6,22},{7,23},{8,24},{9,... | collective-permute-start | bytes 196616 | tf_op jit(solution)/shard_map/ppermute | solution.py:369
  70.6 9.4 %collective-permute-start.10 = (bf16[128,256]{1,0:T(8,128)(2,1)S(1)}, bf16[128,256]{1,0:T(8,128)(2,1)S(1)}, u32[]{:S(2)}, u32[]{:S(2)}) collective-permute-start(bf16[128,256]{1,0:T(8,128)(2,1)S(1)} %add_convert_fusion), channel_id=1, source_target_pairs={{0,12},{1,13},{2,14},{3,15},{4,8},{5,9},{6,10},{7,11},{8,4},{9,5},... | collective-permute-start | bytes 196616 | tf_op jit(solution)/shard_map/ppermute | solution.py:369
  73.2 6.7 %collective-permute-start.8 = (bf16[128,256]{1,0:T(8,128)(2,1)S(1)}, bf16[128,256]{1,0:T(8,128)(2,1)S(1)}, u32[]{:S(2)}, u32[]{:S(2)}) collective-permute-start(bf16[128,256]{1,0:T(8,128)(2,1)S(1)} %add_convert_fusion), channel_id=1, source_target_pairs={{0,4},{1,5},{2,6},{3,7},{4,0},{5,1},{6,2},{7,3},{8,12},{9,13},{10,... | collective-permute-start | bytes 196616 | tf_op jit(solution)/shard_map/ppermute | solution.py:369
  74.2 5.9 %collective-permute-start.9 = (bf16[128,256]{1,0:T(8,128)(2,1)S(1)}, bf16[128,256]{1,0:T(8,128)(2,1)S(1)}, u32[]{:S(2)}, u32[]{:S(2)}) collective-permute-start(bf16[128,256]{1,0:T(8,128)(2,1)S(1)} %add_convert_fusion), channel_id=1, source_target_pairs={{0,8},{1,9},{2,10},{3,11},{4,12},{5,13},{6,14},{7,15},{8,0},{9,1},... | collective-permute-start | bytes 196616 | tf_op jit(solution)/shard_map/ppermute | solution.py:369
  80.3 8.4 %collective-permute-start.13 = (bf16[512,256]{1,0:T(8,128)(2,1)S(1)}, bf16[512,256]{1,0:T(8,128)(2,1)S(1)}, u32[]{:S(2)}, u32[]{:S(2)}) collective-permute-start(bf16[512,256]{1,0:T(8,128)(2,1)S(1)} %bitcast.51), channel_id=1, source_target_pairs={{0,2},{1,3},{2,0},{3,1},{4,6},{5,7},{6,4},{7,5},{8,10},{9,11},{10,... | collective-permute-start | bytes 786440 | tf_op jit(solution)/shard_map/ppermute | solution.py:369
  82.2 8.9 %slice-start = ((s8[8388608]{0:T(1024)(128)(4,1)}), s8[4194304]{0:T(1024)(128)(4,1)S(1)}, s32[]{:S(2)}) async-start(s8[8388608]{0:T(1024)(128)(4,1)} %bitcast.38), calls=%async_computation | async-start | bytes 8388608
  85.5 5.7 %slice-start.1 = ((s8[8388608]{0:T(1024)(128)(4,1)}), s8[4194304]{0:T(1024)(128)(4,1)S(1)}, s32[]{:S(2)}) async-start(s8[8388608]{0:T(1024)(128)(4,1)} %bitcast.38), calls=%async_computation.1 | async-start | bytes 8388608
  88.9 2.0 %collective-permute-start.14 = (bf16[1024,256]{1,0:T(8,128)(2,1)S(1)}, bf16[1024,256]{1,0:T(8,128)(2,1)S(1)}, u32[]{:S(2)}, u32[]{:S(2)}) collective-permute-start(bf16[1024,256]{1,0:T(8,128)(2,1)S(1)} %maximum_select_fusion.1), channel_id=1, source_target_pairs={{0,1},{1,0},{2,3},{3,2},{4,5},{5,4},{6,7},{7,6},{8,9},{9,8},{10,11... | collective-permute-start | bytes 1572872 | tf_op jit(solution)/shard_map/ppermute | solution.py:369
  89.1 2.1 %copy-start.1 = (bf16[256,256]{1,0:T(8,128)(2,1)S(1)}, bf16[256,256]{1,0:T(8,128)(2,1)}, u32[]{:S(2)}) copy-start(bf16[256,256]{1,0:T(8,128)(2,1)} %w_out.1) | copy-start | bytes 393220

commit v2 on v1

v2 whole, which is shorter than its diff:
```python
import functools
import math

import jax
import jax.numpy as jnp
from jax import lax
from jax.experimental import pallas as pl
from jax.experimental.pallas import tpu as pltpu
from jax.sharding import PartitionSpec as P

TWO_PI = 2.0 * math.pi
SHARPNESS = 600.0
CENTER_LOW = 0.2
CENTER_SPAN = 0.5
SCREEN = 16.0
FAR = 8.0
BF16 = jnp.bfloat16
F32 = jnp.float32
AXES = ("gx", "gy")
KTILE = 256

HALF_COS = (
    1.4142134965644628,
    -6.978850988150233,
    5.739461168545313,
    -1.8835629713129327,
    0.3106981552009573,
)
HALF_SIN = (4.442867902918289, -7.307443416752583, 3.594788034903934, -0.7843739144750123)
NT = (((1,), (1,)), ((), ()))
TN = (((0,), (0,)), ((), ()))
TT = (((0,), (1,)), ((), ()))
OCC_ROW = 3
CELL_ROW = 4
POS_ROWS = 16
VMEM = pltpu.VMEM


def horner(coefs, s):
    value = coefs[-1] * s + coefs[-2]
    for c in coefs[-3::-1]:
        value = value * s + c
    return value


def factor_kernel(grid_all, scale_all, pos, kidx, feat, wc, ph, fac, charges, where_at, kmat, kw):
    step = pl.program_id(0)
    planes, cols, _, rows = pos.shape
    vectors = kidx.shape[1]
    atoms, width = feat.shape

    @pl.when(step == 0)
    def _():
        sub = lax.broadcasted_iota(jnp.int32, (POS_ROWS, KTILE), 0)
        parts = []
        for j in range(0, vectors, KTILE):
            waves = [
                kidx[d : d + 1, j : j + KTILE].astype(F32) * (1.0 / grid_all[d]) for d in range(3)
            ]
            value = jnp.zeros((POS_ROWS, KTILE), F32)
            k_sq = jnp.zeros((1, KTILE), F32)
            for d in range(3):
                hit = (sub == d) | (sub == CELL_ROW + d)
                value = jnp.where(hit, jnp.broadcast_to(waves[d], value.shape), value)
                wave = TWO_PI * waves[d]
                k_sq = k_sq + wave * wave
            kmat[j // KTILE] = value.astype(BF16)
            parts.append(jnp.exp(-k_sq / (4.0 * SCREEN)) / k_sq)
        total = sum(jnp.sum(part, axis=1, keepdims=True) for part in parts)
        for j, part in enumerate(parts):
            kw[j] = jnp.broadcast_to(part / total * scale_all, (8, KTILE))
        sub = lax.broadcasted_iota(jnp.int32, (POS_ROWS, rows), 0)
        depth = (lax.broadcasted_iota(jnp.int32, (POS_ROWS, rows), 1) // 8).astype(F32)
        x0 = (lax.axis_index("gx") * planes).astype(F32)
        y0 = (lax.axis_index("gy") * cols).astype(F32)
        turned = wc[...].T
        for x in range(planes):
            for y in range(cols):
                j = (x * cols + y) * rows
                c = lax.dot_general(turned, feat[j : j + rows, :], NT, preferred_element_type=F32)
                tile = pos[x, y].astype(F32)
                charges[:, j : j + rows] = (c * tile[OCC_ROW : OCC_ROW + 1, :]).astype(BF16)
                tile = jnp.where(sub == CELL_ROW, x0 + float(x), tile)
                tile = jnp.where(sub == CELL_ROW + 1, y0 + float(y), tile)
                tile = jnp.where(sub == CELL_ROW + 2, depth, tile)
                where_at[j : j + rows, :] = tile.T.astype(BF16)

    for j in range(0, atoms, 256):
        t_all = jnp.dot(where_at[j : j + 256, :], kmat[step], preferred_element_type=F32)
        for i in range(0, 256, 16):
            t = t_all[i : i + 16]
            r = t - jnp.round(t)
            s = r * r
            half_c = horner(HALF_COS, s)
            half_s = horner(HALF_SIN, s) * r
            ph[0, j + i : j + i + 16, :] = (1.0 - half_s * half_s).astype(BF16)
            ph[1, j + i : j + i + 16, :] = (half_s * half_c).astype(BF16)
    weight = kw[step][0:1, :]
    for p in range(2):
        part = jnp.dot(charges[...], ph[p], preferred_element_type=F32)
        fac[p * width : (p + 1) * width, :] = part * weight


def factor_call(pos, kidx, feat, wc, grid_all, scale_all):
    atoms, width = feat.shape
    vectors = kidx.shape[1]
    steps = vectors // KTILE
    return pl.pallas_call(
        functools.partial(factor_kernel, grid_all, scale_all),
        grid=(steps,),
        in_specs=[
            pl.BlockSpec(pos.shape, lambda i: (0, 0, 0, 0)),
            pl.BlockSpec(kidx.shape, lambda i: (0, 0)),
            pl.BlockSpec((atoms, width), lambda i: (0, 0)),
            pl.BlockSpec((width, width), lambda i: (0, 0)),
        ],
        out_specs=[
            pl.BlockSpec((2, atoms, KTILE), lambda i: (0, 0, i)),
            pl.BlockSpec((2 * width, KTILE), lambda i: (i, 0)),
        ],
        out_shape=[
            jax.ShapeDtypeStruct((2, atoms, vectors), BF16),
            jax.ShapeDtypeStruct((steps * 2 * width, KTILE), F32),
        ],
        scratch_shapes=[
            VMEM((width, atoms), BF16),
            VMEM((atoms, POS_ROWS), BF16),
            VMEM((steps, POS_ROWS, KTILE), BF16),
            VMEM((steps, 8, KTILE), F32),
        ],
        compiler_params=pltpu.CompilerParams(
            dimension_semantics=("arbitrary",), vmem_limit_bytes=56 << 20
        ),
        cost_estimate=pl.CostEstimate(
            flops=24 * atoms * vectors * width, bytes_accessed=16 << 20, transcendentals=0
        ),
        name="factor",
    )(pos, kidx, feat, wc)


def aggregate_row(slots, basis, near_feat, near_pos, own_pos, write):
    rows = 128
    pairs = rows // (2 * slots)
    two = 2 * slots
    window = 4 * slots
    sub = lax.broadcasted_iota(jnp.int32, (8, 128), 0)
    lane = lax.broadcasted_iota(jnp.int32, (8, 128), 1)
    lane_block = lane // window
    cell_in_window = (lane % window) // slots
    z_off = jnp.where(sub == 2, (cell_in_window - 1).astype(F32), 0.0)
    columns = [(dx, dy) for dx in (-1, 0, 1) for dy in (-1, 0, 1) if (dx, dy) != (0, 0)]
    columns.append((0, 0))
    select = jnp.where(
        lax.broadcasted_iota(jnp.int32, (POS_ROWS, 384), 0)
        == lax.broadcasted_iota(jnp.int32, (POS_ROWS, 384), 1) // 128,
        1.0,
        0.0,
    ).astype(BF16)
    stretch = math.sqrt(SHARPNESS)
    centers = [stretch * (CENTER_LOW + b * (CENTER_SPAN / (basis - 1))) for b in range(basis)]

    placed = []
    for dx, dy in columns:
        coords = near_pos(dx, dy).astype(F32)[0:8]
        occ = jnp.broadcast_to(coords[OCC_ROW : OCC_ROW + 1, :], coords.shape)
        shift = jnp.where(sub == 0, float(dx), jnp.where(sub == 1, float(dy), 0.0))
        placed.append(jnp.where(occ > 0.0, coords + shift, FAR))
    own_all = lax.dot_general(own_pos, select, TN, preferred_element_type=F32)
    for p in range(pairs):
        packed = []
        for h in range(3):
            merged = None
            for c in range(4 * h, min(4 * h + 4, 9)):
                amount = (window * (c % 4) - two * p) % 128
                moved = pltpu.roll(placed[c], amount, axis=1) if amount else placed[c]
                merged = moved if merged is None else jnp.where(lane_block == c % 4, moved, merged)
            merged = merged + z_off
            if h == 2:
                merged = jnp.where(lane_block == 0, merged, FAR)
            packed.append([jnp.broadcast_to(merged[d : d + 1, :], (8, 128)) for d in range(3)])
        parts = [[None, None] for _ in range(3)]
        for h in range(3):
            for q in range(2):
                r0 = (two * p + slots * (1 + q)) % rows
                d2 = None
                for d in range(3):
                    mine = own_all[r0 : r0 + slots, 128 * d : 128 * d + 128]
                    if d == 2 and q == 1:
                        mine = mine + 1.0
                    delta = packed[h][d] - mine
                    d2 = delta * delta if d2 is None else d2 + delta * delta
                env = jnp.maximum(1.0 - d2, 0.0)
                env = env * env
                if h == 2:
                    env = jnp.where(lane == sub + slots * (1 + q), 0.0, env)
                ar = (d2 * stretch) * lax.rsqrt(jnp.maximum(d2, 1e-30))
                values = []
                for b in range(basis):
                    u = ar - centers[b]
                    values.append(jnp.exp(u * (centers[b] - ar)) * env)
                parts[h][q] = values
        lhs = []
        for h in range(3):
            lhs.append(
                jnp.concatenate(
                    [
                        jnp.concatenate([parts[h][0][b], parts[h][1][b]], axis=0).astype(BF16)
                        for b in range(basis)
                    ],
                    axis=0,
                )
            )
        near = []
        nxt = two * ((p + 1) % pairs)
        for dx, dy in columns:
            near.append(near_feat(dx, dy, two * p, two))
            near.append(near_feat(dx, dy, nxt, two))
        near.append(jnp.zeros((384 - 9 * window, near[0].shape[1]), BF16))
        total = jnp.dot(
            jnp.concatenate(lhs, axis=1),
            jnp.concatenate(near, axis=0),
            preferred_element_type=F32,
        ).astype(BF16)
        for b in range(basis):
            write(two * p, two, b, total[two * b : two * b + two])


def turn(value, slots):
    return jnp.concatenate([value[128 - slots :], value[: 128 - slots]], axis=0)


def plane_kernel(slots, basis, plane, first, count, feat, pos, side_feat, side_pos, w, *rest):
    out, agg = rest[-2:]
    planes, _, rows, width = feat.shape

    def pick(ref, side, dx):
        x = plane + dx
        return (ref, x) if 0 <= x < planes else (side, 0)

    def body(i, carry):
        y = first + i

        def near_feat(dx, dy, start, size):
            ref, x = pick(feat, side_feat, dx)
            return ref[x, y + dy, start : start + size, :]

        def near_pos(dx, dy):
            ref, x = pick(pos, side_pos, dx)
            return ref[x, y + dy]

        def write(start, size, b, value):
            agg[i, start : start + size, width * b : width * (b + 1)] = value

        aggregate_row(slots, basis, near_feat, near_pos, pos[plane, y], write)
        return carry

    lax.fori_loop(0, count, body, 0)
    value = jnp.dot(
        agg[...].reshape(count * rows, basis * width), w[...], preferred_element_type=F32
    )
    value = jax.nn.silu(value).reshape(count, rows, width)
    for i in range(count):
        out[first + i, plane] = feat[plane, first + i].astype(F32) + turn(value[i], slots)


def edge_kernel(
    slots, basis, y, halo_dy, feat, pos, before, pos_before, after, pos_after, halo, w, *rest
):
    out, agg = rest[-2:]
    planes, _, rows, width = feat.shape
    for plane in range(planes):

        def near_feat(dx, dy, start, size):
            x = plane + dx
            if dy == halo_dy:
                return halo[x + 1, 0, start : start + size, :]
            if 0 <= x < planes:
                return feat[x, y + dy, start : start + size, :]
            return (before if x < 0 else after)[0, y + dy, start : start + size, :]

        def near_pos(dx, dy):
            x = plane + dx
            if dy == halo_dy:
                return halo[x + 1, 0, rows : rows + POS_ROWS, 0:128]
            if 0 <= x < planes:
                return pos[x, y + dy]
            return (pos_before if x < 0 else pos_after)[0, y + dy]

        def write(start, size, b, value):
            agg[plane, start : start + size, width * b : width * (b + 1)] = value

        aggregate_row(slots, basis, near_feat, near_pos, pos[plane, y], write)
    value = jnp.dot(
        agg[...].reshape(planes * rows, basis * width), w[...], preferred_element_type=F32
    )
    value = jax.nn.silu(value).reshape(planes, rows, width)
    for plane in range(planes):
        out[y, plane] = feat[plane, y].astype(F32) + turn(value[plane], slots)


def short_call(kernel, name, lines, basis, args, base):
    planes, cols, rows, width = args[0].shape
    whole = pl.BlockSpec(memory_space=VMEM)
    aliases = {}
    if base is not None:
        aliases = {len(args): 0}
        args = (*args, base)
    return pl.pallas_call(
        kernel,
        in_specs=[whole] * len(args),
        out_specs=whole,
        out_shape=jax.ShapeDtypeStruct((cols, planes, rows, width), F32),
        scratch_shapes=[VMEM((lines, rows, basis * width), BF16)],
        input_output_aliases=aliases,
        compiler_params=pltpu.CompilerParams(vmem_limit_bytes=16 << 20),
        cost_estimate=pl.CostEstimate(
            flops=lines * rows * width * 8 * (basis * 384 + basis * width),
            bytes_accessed=4 << 20,
            transcendentals=lines * rows * 384 * (basis + 1),
        ),
        name=name,
    )(*args)


def field_kernel(ph, weighted, w_out, base, pos, out, rhs):
    tiles, width, _ = weighted.shape

    @pl.when(pl.program_id(0) == 0)
    def _():
        for t in range(tiles):
            rhs[t * KTILE : (t + 1) * KTILE, :] = weighted[t].T

    lhs = jnp.concatenate(
        [ph[t % 2, :, KTILE * (t // 2) : KTILE * (t // 2 + 1)] for t in range(tiles)], axis=1
    )
    recip = jnp.dot(lhs, rhs[...], preferred_element_type=F32)
    far = jnp.dot(recip.astype(BF16), w_out[...], preferred_element_type=F32)
    sub = lax.broadcasted_iota(jnp.int32, (POS_ROWS, width), 0)
    select = jnp.where(sub == OCC_ROW, 1.0, 0.0).astype(BF16)
    rows = base.shape[2]
    for y in range(base.shape[0]):
        occ = lax.dot_general(pos[0, y], select, TN, preferred_element_type=F32)
        value = base[y, 0] + far[rows * y : rows * (y + 1)]
        out[rows * y : rows * (y + 1), :] = jnp.where(occ > 0.0, value, 0.0).astype(BF16)


def field_call(ph, weighted, w_out, base, pos, group=2):
    _, atoms, vectors = ph.shape
    tiles, width, _ = weighted.shape
    cols, planes, rows, _ = base.shape
    tile = group * rows
    groups = cols // group
    return pl.pallas_call(
        field_kernel,
        grid=(atoms // tile,),
        in_specs=[
            pl.BlockSpec((2, tile, vectors), lambda i: (0, i, 0)),
            pl.BlockSpec((tiles, width, KTILE), lambda i: (0, 0, 0)),
            pl.BlockSpec((width, width), lambda i: (0, 0)),
            pl.BlockSpec((group, 1, rows, width), lambda i: (i % groups, i // groups, 0, 0)),
            pl.BlockSpec((1, group, POS_ROWS, rows), lambda i: (i // groups, i % groups, 0, 0)),
        ],
        out_specs=pl.BlockSpec((tile, width), lambda i: (i, 0)),
        out_shape=jax.ShapeDtypeStruct((atoms, width), BF16),
        scratch_shapes=[VMEM((tiles * KTILE, width), BF16)],
        compiler_params=pltpu.CompilerParams(
            dimension_semantics=("arbitrary",), vmem_limit_bytes=54 << 20
        ),
        cost_estimate=pl.CostEstimate(
            flops=4 * atoms * vectors * width, bytes_accessed=16 << 20, transcendentals=0
        ),
        name="field",
    )(ph, weighted, w_out, base, pos)


def my_index():
    return lax.axis_index("gx") * lax.axis_size("gy") + lax.axis_index("gy")


def swap(value, mask):
    count = lax.axis_size("gx") * lax.axis_size("gy")
    return lax.ppermute(value, AXES, [(i, i ^ mask) for i in range(count)])


def tied(*values):
    return lax.optimization_barrier(values)


def no_work():
    return ()


class Exchange:
    def __init__(self):
        size_y = lax.axis_size("gy")
        count = lax.axis_size("gx") * size_y
        bits = [1 << i for i in range(count.bit_length() - 1)]
        low = [b for b in bits if b < size_y]
        self.halved = low[:2]
        self.direct = low[2:4]
        self.whole = low[4:] + [b for b in bits if b >= size_y]
        self.masks = [0]
        for b in self.direct:
            self.masks = self.masks + [m ^ b for m in self.masks]

    def place(self):
        return sum(((my_index() // b) % 2) << k for k, b in enumerate(self.direct))

    def halve(self, value, bit, work=no_work):
        half = value.shape[0] // 2
        mine = (my_index() // bit) % 2
        keep = lax.dynamic_slice_in_dim(value, mine * half, half, 0)
        give = lax.dynamic_slice_in_dim(value, (1 - mine) * half, half, 0).astype(BF16)
        (got,), done = run_under([give], [bit], work)
        return keep + got.astype(F32), done

    def spread_sum(self, value, work):
        count = len(self.masks)
        value = value.reshape((count, -1) + value.shape[1:])
        me = self.place()
        keep = lax.dynamic_index_in_dim(value, me, 0, False)
        gives = [
            lax.dynamic_index_in_dim(value, me ^ j, 0, False).astype(BF16) for j in range(1, count)
        ]
        gives, done = run_under(gives, self.masks[1:], work)
        for got in gives:
            keep = keep + got.astype(F32)
        return keep, done

    def whole_sum(self, value, bit, work=no_work):
        (got,), done = run_under([value.astype(BF16)], [bit], work)
        return value + got.astype(F32), done

    def spread(self, value, work):
        count = len(self.masks)
        got, done = run_under([value] * (count - 1), self.masks[1:], work)
        parts = jnp.stack([value] + got)
        me = self.place()
        for k in range(len(self.direct)):
            b = 1 << k
            cut = parts.reshape((count // (2 * b), 2, b) + value.shape)
            parts = jnp.where((me >> k) & 1 == 0, cut, cut[:, ::-1]).reshape(parts.shape)
        return parts.reshape((-1,) + value.shape[1:]), done

    def double(self, value, bit, work=no_work):
        mine = (my_index() // bit) % 2
        (other,), done = run_under([value], [bit], work)
        return (
            jnp.where(
                mine == 0, jnp.concatenate([value, other]), jnp.concatenate([other, value])
            ),
            done,
        )


def run_under(gives, masks, work):
    inputs = work.inputs if work is not no_work else ()
    gives, inputs = tied(list(gives), inputs)
    got = [swap(give, mask) for give, mask in zip(gives, masks)]
    done = work(*inputs) if work is not no_work else ()
    return tied(got, done)


class Work:
    def __init__(self, call, *inputs):
        self.call = call
        self.inputs = inputs

    def __call__(self, *inputs):
        return self.call(*inputs)


def from_before(cells, axis, dim):
    count = lax.axis_size(axis)
    size = cells.shape[dim]
    tail = lax.slice_in_dim(cells, size - 1, size, axis=dim)
    return lax.ppermute(tail, axis, [(i, (i + 1) % count) for i in range(count)])


def from_after(cells, axis, dim):
    count = lax.axis_size(axis)
    head = lax.slice_in_dim(cells, 0, 1, axis=dim)
    return lax.ppermute(head, axis, [((i + 1) % count, i) for i in range(count)])


def edge_rows(feat_planes, pos_planes, y):
    parts = []
    for f, q in zip(feat_planes, pos_planes):
        q = jnp.pad(q[:, y : y + 1], ((0, 0), (0, 0), (0, 0), (0, f.shape[3] - q.shape[3])))
        parts.append(jnp.concatenate([f[:, y : y + 1], q], axis=2))
    return jnp.concatenate(parts, axis=0)


def on_device(features, fractions, counts, k_index, w_short, w_charge, w_out):
    planes, cols, depth, slots, width = features.shape
    basis = w_short.shape[0]
    vectors = k_index.shape[0]
    rows = depth * slots
    atoms = planes * cols * rows
    size_x, size_y = lax.axis_size("gx"), lax.axis_size("gy")
    grid_all = (planes * size_x, cols * size_y, depth)
    assert rows == 128 and slots == 8 and planes == 2 and cols == 8 and width == KTILE
    assert vectors % KTILE == 0
    for extent in grid_all:
        assert extent & (extent - 1) == 0 and extent <= 256
    scale_all = math.sqrt(vectors / (grid_all[0] * grid_all[1] * grid_all[2] * slots))

    feat = features.reshape(planes, cols, rows, width)
    before = from_before(feat, "gx", 0)

    occupied = (jnp.arange(slots, dtype=jnp.int32) < counts[..., None]).astype(BF16)
    frac = jnp.transpose(fractions, (0, 1, 4, 2, 3)).reshape(planes, cols, 3, rows)
    pos = jnp.concatenate(
        [
            frac,
            occupied.reshape(planes, cols, 1, rows),
            jnp.zeros((planes, cols, POS_ROWS - 4, rows), BF16),
        ],
        axis=2,
    )
    pos_before = from_before(pos, "gx", 0)
    pos_after = from_after(pos, "gx", 0)

    ph, partial = factor_call(
        pos, k_index.T, feat.reshape(atoms, width), w_charge, grid_all, scale_all
    )
    ph, partial, before, pos_before, pos_after = tied(ph, partial, before, pos_before, pos_after)
    after = from_after(feat, "gx", 0)

    w_flat = w_short.reshape(basis * width, width)
    exchange = Exchange()

    def plane_work(plane, first, count, base, *sides):
        kernel = functools.partial(plane_kernel, slots, basis, plane, first, count)
        call = lambda *args: short_call(
            kernel, "plane", count, basis, args[:5], args[5] if len(args) > 5 else None
        )
        inputs = (feat, pos, *sides, w_flat) + (() if base is None else (base,))
        return Work(call, *inputs)

    def edges(*args):
        feat, pos, before, pos_before, after, pos_after, low, high, w, base = args
        common = (feat, pos, before, pos_before, after, pos_after)
        for name, y, dy, halo in (("low", 0, -1, low), ("high", cols - 1, 1, high)):
            kernel = functools.partial(edge_kernel, slots, basis, y, dy)
            base = short_call(kernel, name, planes, basis, (*common, halo, w), base)
        return base

    value, _ = exchange.halve(partial, exchange.halved[0])
    value, base = exchange.halve(
        value, exchange.halved[1], plane_work(0, 1, 3, None, before, pos_before)
    )
    value, base = exchange.spread_sum(value, plane_work(0, 4, 3, base, before, pos_before))
    value, base, after = tied(value, base, after)
    feat_planes = (before, feat, after)
    pos_planes = (pos_before, pos, pos_after)
    low = from_before(edge_rows(feat_planes, pos_planes, cols - 1), "gy", 1)
    high = from_after(edge_rows(feat_planes, pos_planes, 0), "gy", 1)
    for i, bit in enumerate(exchange.whole):
        if i == 0:
            value, base = exchange.whole_sum(
                value, bit, plane_work(1, 1, 3, base, after, pos_after)
            )
        else:
            value, _ = exchange.whole_sum(value, bit)
    value = value.astype(BF16)
    value, base = exchange.spread(value, plane_work(1, 4, 3, base, after, pos_after))
    value, base = exchange.double(
        value,
        exchange.halved[1],
        Work(edges, feat, pos, before, pos_before, after, pos_after, low, high, w_flat, base),
    )
    value, _ = exchange.double(value, exchange.halved[0])
    weighted = value.reshape(2 * vectors // KTILE, width, KTILE)
    out = field_call(ph, weighted, w_out, base, pos)
    return out.reshape(features.shape)


def solution(mesh):
    return jax.shard_map(
        on_device,
        mesh=mesh,
        in_specs=(
            P("gx", "gy", None, None, None),
            P("gx", "gy", None, None, None),
            P("gx", "gy", None),
            P(),
            P(),
            P(),
            P(),
        ),
        out_specs=P("gx", "gy", None, None, None),
        check_vma=False,
    )
```

time: 99.3 us -> 86 us (0.87)
  waiting for transfers between devices: 20.7 us -> 9.54 us
  starting transfers between devices: 22.2 us -> 20 us
  Pallas kernels: 40.9 us -> 42.1 us
    ppermute x4 -> x6, waiting for transfers between devices: 18.8 us -> 0.36 us  [the longest x3 0.35 us: from_before(): lax.ppermute(tail, axis, [(i, (i + 1) % count) for i in range(count)])]
    ppermute x11, waiting for transfers between devices: 1.87 us -> 9.18 us  [swap(): return lax.ppermute(value, AXES, [(i, i ^ mask) for i in range(count)])]
    pallas_call x1, Pallas kernels: 7.46 us -> 10.5 us  [field_call(): pl.pallas_call(field_kernel, grid=(atoms // tile,), in_specs=[pl.BlockSpe...]
    unnamed x18 -> x14, local copies, waits for them, and re-layouts: 5.04 us -> 2.29 us
    slice x0 -> x2, local copies, waits for them, and re-layouts: none -> 2.08 us  [from_after(): head = lax.slice_in_dim(cells, 0, 1, axis=dim)]
    pallas_call x5 -> x6, Pallas kernels: 21.1 us -> 19.3 us  [short_call(): pl.pallas_call(kernel, in_specs=[whole] * len(args), out_specs=whole, out...]
    add x2 -> x3, other arithmetic: 3.21 us -> 1.41 us  [the longest x2 1.38 us: halve(): return (keep + got.astype(F32), done)]
    ppermute x11, starting transfers between devices: 15.3 us -> 14.2 us  [swap(): return lax.ppermute(value, AXES, [(i, i ^ mask) for i in range(count)])]
  transfers between devices with their start and end apart: 15 -> 17, of which waited for: 3 -> 8; matrix products, arithmetic and copies ran while one was open for 6% -> 7% of each run, Pallas kernels for 21% -> 37%
where the time goes in v2:
time: 86 us; the launch traced here: 85.1 us
  Pallas kernels  42.1 us (49%)
  starting transfers between devices  20 us (23%)
  local copies, waits for them, and re-layouts  9.85 us (11%)
  waiting for transfers between devices  9.54 us (11%)
  other arithmetic  3.18 us (4%)
    pallas_call x6, Pallas kernels, short_call(): pl.pallas_call(kernel, in_specs=[whole] * len(args), out_specs=whole, out...  19.3 us
    ppermute x11, starting transfers between devices, swap(): return lax.ppermute(value, AXES, [(i, i ^ mask) for i in range(count)])  14.2 us
    pallas_call x1, Pallas kernels, factor_call(): pl.pallas_call(functools.partial(factor_kernel, grid_all, scale_all), gri...  12.4 us
    pallas_call x1, Pallas kernels, field_call(): pl.pallas_call(field_kernel, grid=(atoms // tile,), in_specs=[pl.BlockSpe...  10.5 us
    ppermute x11, waiting for transfers between devices, swap(): return lax.ppermute(value, AXES, [(i, i ^ mask) for i in range(count)])  9.18 us
    ppermute x3, starting transfers between devices, from_before(): lax.ppermute(tail, axis, [(i, (i + 1) % count) for i in range(count)])  5.67 us
    unnamed x14, local copies, waits for them, and re-layouts  2.29 us
    slice x2, local copies, waits for them, and re-layouts, from_after(): head = lax.slice_in_dim(cells, 0, 1, axis=dim)  2.08 us
  transfers between devices with their start and end apart: 17, of which 8 were waited for; matrix products, arithmetic and copies ran while one was open for 7% of the time, Pallas kernels for 37%

profile of v2, /device:TPU:0, one launch (start us, length us, event | category | flops | bytes accessed | tf_op | source)
XLA Modules:
  0.0 85.1 jit_solution(9512496229964406298)
XLA Ops:
  2.5 3.0 %collective-permute-start.1 = (bf16[1,8,16,128]{3,2,1,0:T(8,128)(2,1)S(1)}, bf16[1,8,16,128]{3,2,1,0:T(8,128)(2,1)S(1)}, u32[]{:S(2)}, u32[]{:S(2)}) collective-permute-start(bf16[1,8,16,128]{3,2,1,0:T(8,128)(2,1)S(1)} %get-tuple-element.151), channel_id=1, source_target_pairs={{0,16},{16,0},{1,17},{17,1},{2,18},{18,2},{3,19},{19,3},{4,20},{20... | collective-permute-start | bytes 98312 | tf_op jit(solution)/shard_map/ppermute | solution.py:477
  5.6 2.1 %slice_bitcast_fusion = (bf16[1,8,128,256]{3,2,1,0:T(8,128)(2,1)}, bf16[1,8,128,256]{3,2,1,0:T(8,128)(2,1)S(1)}) fusion(bf16[2,8,16,8,256]{4,3,2,1,0:T(8,128)(2,1)} %param.7), kind=kLoop, calls=%fused_computation.17 | loop fusion | bytes 2097152 | tf_op jit(solution)/shard_map/slice | solution.py:482
  7.7 1.9 %collective-permute-start = (bf16[1,8,128,256]{3,2,1,0:T(8,128)(2,1)S(1)}, bf16[1,8,128,256]{3,2,1,0:T(8,128)(2,1)S(1)}, u32[]{:S(2)}, u32[]{:S(2)}) collective-permute-start(bf16[1,8,128,256]{3,2,1,0:T(8,128)(2,1)S(1)} %get-tuple-element.140), channel_id=1, source_target_pairs={{0,16},{16,0},{1,17},{17,1},{2,18},{18,2},{3,19},{19,3},{4,20},{20... | collective-permute-start | bytes 1572872 | tf_op jit(solution)/shard_map/ppermute | solution.py:477
  9.7 12.4 %factor.1 = (bf16[2,2048,1024]{2,1,0:T(8,128)(2,1)}, f32[2048,256]{1,0:T(8,128)}) custom-call(bf16[2,8,16,128]{3,2,1,0:T(8,128)(2,1)} %copy-done.2, s32[3,1024]{1,0:T(4,128)} %bitcast.65, bf16[2048,256]{1,0:T(8,128)(2,1)} %bitcast.38, bf16[256,256]{1,0:T(8,128)(2,1)} %wc.1), custom_call_target="tpu_custom_call" | custom-call | flops 12884901888 | bytes 16777216 | tf_op jit(solution)/shard_map/factor/pallas_call | solution.py:108
  22.5 1.5 %dynamic-slice_convert_fusion = bf16[1024,256]{1,0:T(8,128)(2,1)S(1)} fusion(f32[2048,256]{1,0:T(8,128)} %get-tuple-element.74, s32[]{:T(128)S(6)} %select_n.115), kind=kLoop, calls=%fused_computation.2 | loop fusion | bytes 1048580 | tf_op jit(solution)/shard_map/convert_element_type | solution.py:413
  26.0 1.3 %convert_add_fusion = f32[1024,256]{1,0:T(8,128)S(1)} fusion(bf16[1024,256]{1,0:T(8,128)(2,1)S(1)} %collective-permute-done.3, f32[2048,256]{1,0:T(8,128)} %get-tuple-element.74, s32[]{:T(128)S(6)} %select_n.114), kind=kLoop, calls=%fused_computation.1 | loop fusion | flops 524288 | bytes 2621444 | tf_op jit(solution)/shard_map/add | solution.py:415
  27.4 2.1 %collective-permute-start.4 = (bf16[512,256]{1,0:T(8,128)(2,1)S(1)}, bf16[512,256]{1,0:T(8,128)(2,1)S(1)}, u32[]{:S(2)}, u32[]{:S(2)}) collective-permute-start(bf16[512,256]{1,0:T(8,128)(2,1)S(1)} %dynamic-slice_convert_fusion.1), channel_id=1, source_target_pairs={{0,2},{1,3},{2,0},{3,1},{4,6},{5,7},{6,4},{7,5},{8,10},{9,11},{10,... | collective-permute-start | bytes 786440 | tf_op jit(solution)/shard_map/ppermute | solution.py:382
  31.7 2.9 %plane.4.rest_0_ = f32[8,2,128,256]{3,2,1,0:T(8,128)S(1)} custom-call(bf16[2,8,128,256]{3,2,1,0:T(8,128)(2,1)S(1)} %bitcast.40, bf16[2,8,16,128]{3,2,1,0:T(8,128)(2,1)S(1)} %copy-done.3, bf16[1,8,128,256]{3,2,1,0:T(8,128)(2,1)S(1)} %copy-done.5, bf16[1,8,16,128]{3,2,1,0:T(8,128)(2,1)S(1)} %collective-permute-done.1.side_pos.pos_before, ...), custom_call_target="tpu_custom_call" | custom-call | flops 4026531840 | bytes 4194304 | tf_op jit(solution)/shard_map/plane/pallas_call | solution.py:308
  34.6 1.4 %collective-permute-done.4 = bf16[512,256]{1,0:T(8,128)(2,1)S(1)} collective-permute-done((bf16[512,256]{1,0:T(8,128)(2,1)S(1)}, bf16[512,256]{1,0:T(8,128)(2,1)S(1)}, u32[]{:S(2)}, u32[]{:S(2)}) %collective-permute-start.4) | collective-permute-done | bytes 262176 | tf_op jit(solution)/shard_map/ppermute | solution.py:382
  36.1 1.9 %collective-permute-start.5 = (bf16[128,256]{1,0:T(8,128)(2,1)S(1)}, bf16[128,256]{1,0:T(8,128)(2,1)S(1)}, u32[]{:S(2)}, u32[]{:S(2)}) collective-permute-start(bf16[128,256]{1,0:T(8,128)(2,1)S(1)} %get-tuple-element.85), channel_id=1, source_target_pairs={{0,4},{1,5},{2,6},{3,7},{4,0},{5,1},{6,2},{7,3},{8,12},{9,13},{10,... | collective-permute-start | bytes 196616 | tf_op jit(solution)/shard_map/ppermute | solution.py:382
  38.0 2.6 %collective-permute-start.6 = (bf16[128,256]{1,0:T(8,128)(2,1)S(1)}, bf16[128,256]{1,0:T(8,128)(2,1)S(1)}, u32[]{:S(2)}, u32[]{:S(2)}) collective-permute-start(bf16[128,256]{1,0:T(8,128)(2,1)S(1)} %get-tuple-element.86), channel_id=1, source_target_pairs={{0,8},{1,9},{2,10},{3,11},{4,12},{5,13},{6,14},{7,15},{8,0},{9,1},... | collective-permute-start | bytes 196616 | tf_op jit(solution)/shard_map/ppermute | solution.py:382
  40.6 2.9 %plane.5.rest_0_ = f32[8,2,128,256]{3,2,1,0:T(8,128)S(1)} custom-call(bf16[2,8,128,256]{3,2,1,0:T(8,128)(2,1)S(1)} %bitcast.41, bf16[2,8,16,128]{3,2,1,0:T(8,128)(2,1)S(1)} %copy-done.3, bf16[1,8,128,256]{3,2,1,0:T(8,128)(2,1)S(1)} %copy-done.5, ...), custom_call_target="tpu_custom_call", output_to_operand_aliasing={{}: (5, {})} | custom-call | flops 4026531840 | bytes 4194304 | tf_op jit(solution)/shard_map/plane/pallas_call | solution.py:308
  44.7 1.9 %collective-permute-done.7 = bf16[128,256]{1,0:T(8,128)(2,1)S(1)} collective-permute-done((bf16[128,256]{1,0:T(8,128)(2,1)S(1)}, bf16[128,256]{1,0:T(8,128)(2,1)S(1)}, u32[]{:S(2)}, u32[]{:S(2)}) %collective-permute-start.7) | collective-permute-done | bytes 65568 | tf_op jit(solution)/shard_map/ppermute | solution.py:382
  48.4 1.6 %collective-permute-start.9 = (bf16[128,256]{1,0:T(8,128)(2,1)S(1)}, bf16[128,256]{1,0:T(8,128)(2,1)S(1)}, u32[]{:S(2)}, u32[]{:S(2)}) collective-permute-start(bf16[128,256]{1,0:T(8,128)(2,1)S(1)} %convert_element_type.80), channel_id=1, source_target_pairs={{0,16},{1,17},{2,18},{3,19},{4,20},{5,21},{6,22},{7,23},{8,24},{9,... | collective-permute-start | bytes 196616 | tf_op jit(solution)/shard_map/ppermute | solution.py:382
  50.0 4.0 %plane.6.rest_0_ = f32[8,2,128,256]{3,2,1,0:T(8,128)S(1)} custom-call(bf16[2,8,128,256]{3,2,1,0:T(8,128)(2,1)S(1)} %bitcast.42, bf16[2,8,16,128]{3,2,1,0:T(8,128)(2,1)S(1)} %copy-done.3, bf16[1,8,128,256]{3,2,1,0:T(8,128)(2,1)} %collective-permute-done.8.side_feat.after, ...), custom_call_target="tpu_custom_call", output_to_operand_aliasing={{}: (5, {})} | custom-call | flops 4026531840 | bytes 4194304 | tf_op jit(solution)/shard_map/plane/pallas_call | solution.py:308
  54.1 1.8 %collective-permute-start.11 = (bf16[128,256]{1,0:T(8,128)(2,1)S(1)}, bf16[128,256]{1,0:T(8,128)(2,1)S(1)}, u32[]{:S(2)}, u32[]{:S(2)}) collective-permute-start(bf16[128,256]{1,0:T(8,128)(2,1)S(1)} %add_convert_fusion), channel_id=1, source_target_pairs={{0,8},{1,9},{2,10},{3,11},{4,12},{5,13},{6,14},{7,15},{8,0},{9,1},... | collective-permute-start | bytes 196616 | tf_op jit(solution)/shard_map/ppermute | solution.py:382
  55.9 2.6 %collective-permute-start.12 = (bf16[128,256]{1,0:T(8,128)(2,1)S(1)}, bf16[128,256]{1,0:T(8,128)(2,1)S(1)}, u32[]{:S(2)}, u32[]{:S(2)}) collective-permute-start(bf16[128,256]{1,0:T(8,128)(2,1)S(1)} %add_convert_fusion), channel_id=1, source_target_pairs={{0,12},{1,13},{2,14},{3,15},{4,8},{5,9},{6,10},{7,11},{8,4},{9,5},... | collective-permute-start | bytes 196616 | tf_op jit(solution)/shard_map/ppermute | solution.py:382
  58.4 4.0 %plane.7.rest_0_ = f32[8,2,128,256]{3,2,1,0:T(8,128)S(1)} custom-call(bf16[2,8,128,256]{3,2,1,0:T(8,128)(2,1)S(1)} %bitcast.43, bf16[2,8,16,128]{3,2,1,0:T(8,128)(2,1)S(1)} %copy-done.3, bf16[1,8,128,256]{3,2,1,0:T(8,128)(2,1)} %collective-permute-done.8.side_feat.after, ...), custom_call_target="tpu_custom_call", output_to_operand_aliasing={{}: (5, {})} | custom-call | flops 4026531840 | bytes 4194304 | tf_op jit(solution)/shard_map/plane/pallas_call | solution.py:308
  63.0 1.5 %collective-permute-start.15 = (bf16[512,256]{1,0:T(8,128)(2,1)S(1)}, bf16[512,256]{1,0:T(8,128)(2,1)S(1)}, u32[]{:S(2)}, u32[]{:S(2)}) collective-permute-start(bf16[512,256]{1,0:T(8,128)(2,1)S(1)} %bitcast.56), channel_id=1, source_target_pairs={{0,2},{1,3},{2,0},{3,1},{4,6},{5,7},{6,4},{7,5},{8,10},{9,11},{10,... | collective-permute-start | bytes 786440 | tf_op jit(solution)/shard_map/ppermute | solution.py:382
  64.5 2.7 %low.1.rest_0_ = f32[8,2,128,256]{3,2,1,0:T(8,128)S(1)} custom-call(bf16[2,8,128,256]{3,2,1,0:T(8,128)(2,1)S(1)} %bitcast.44, bf16[2,8,16,128]{3,2,1,0:T(8,128)(2,1)S(1)} %copy-done.3, bf16[1,8,128,256]{3,2,1,0:T(8,128)(2,1)S(1)} %copy-done.5, bf16[1,8,16,128]{3,2,1,0:T(8,128)(2,1)S(1)} %collective-permute-done.1.side_pos.pos_before, ...), custom_call_target="tpu_custom_call", output_to_operand_aliasing={{}: (8, {})} | custom-call | flops 2684354560 | bytes 4194304 | tf_op jit(solution)/shard_map/low/pallas_call | solution.py:308
  67.3 2.8 %high.1.base = f32[8,2,128,256]{3,2,1,0:T(8,128)S(1)} custom-call(bf16[2,8,128,256]{3,2,1,0:T(8,128)(2,1)S(1)} %bitcast.45, bf16[2,8,16,128]{3,2,1,0:T(8,128)(2,1)S(1)} %copy-done.3, bf16[1,8,128,256]{3,2,1,0:T(8,128)(2,1)S(1)} %copy-done.5, bf16[1,8,16,128]{3,2,1,0:T(8,128)(2,1)S(1)} %collective-permute-done.1.side_pos.pos_before, ...), custom_call_target="tpu_custom_call", output_to_operand_aliasing={{}: (8, {})} | custom-call | flops 2684354560 | bytes 4194304 | tf_op jit(solution)/shard_map/high/pallas_call | solution.py:308
  71.5 1.9 %collective-permute-done.16 = bf16[1024,256]{1,0:T(8,128)(2,1)S(1)} collective-permute-done((bf16[1024,256]{1,0:T(8,128)(2,1)S(1)}, bf16[1024,256]{1,0:T(8,128)(2,1)S(1)}, u32[]{:S(2)}, u32[]{:S(2)}) %collective-permute-start.16) | collective-permute-done | bytes 524320 | tf_op jit(solution)/shard_map/ppermute | solution.py:382
  73.4 1.2 %maximum_select_fusion = bf16[2048,256]{1,0:T(8,128)(2,1)} fusion(bf16[1024,256]{1,0:T(8,128)(2,1)S(1)} %collective-permute-done.16, bf16[1024,256]{1,0:T(8,128)(2,1)S(1)} %maximum_select_fusion.1, pred[]{:T(512)S(6)} %eq.21), kind=kLoop, calls=%fused_computation | loop fusion | flops 4718592 | bytes 2097153 | tf_op jit(solution)/shard_map/jit(_where)/select_n | solution.py:449
  74.6 10.5 %field.1 = bf16[2048,256]{1,0:T(8,128)(2,1)} custom-call(bf16[2,2048,1024]{2,1,0:T(8,128)(2,1)} %get-tuple-element.73.ph, bf16[8,256,256]{2,1,0:T(8,128)(2,1)} %bitcast.52, bf16[256,256]{1,0:T(8,128)(2,1)} %w_out.1, f32[8,2,128,256]{3,2,1,0:T(8,128)} %copy-done, bf16[2,8,16,128]{3,2,1,0:T(8,128)(2,1)} %copy-done.2), custom_call_target="tpu_custom_call" | custom-call | flops 2147483648 | bytes 16777216 | tf_op jit(solution)/shard_map/field/pallas_call | solution.py:353
  (65 shorter events, 12.4 us)
Async XLA Ops:
  2.5 7.2 %copy-start.2 = (bf16[2,8,16,128]{3,2,1,0:T(8,128)(2,1)}, bf16[2,8,16,128]{3,2,1,0:T(8,128)(2,1)S(1)}, u32[]{:S(2)}) copy-start(bf16[2,8,16,128]{3,2,1,0:T(8,128)(2,1)S(1)} %maximum_maximum_fusion.pos) | copy-start | bytes 196612
  2.5 19.6 %collective-permute-start.1 = (bf16[1,8,16,128]{3,2,1,0:T(8,128)(2,1)S(1)}, bf16[1,8,16,128]{3,2,1,0:T(8,128)(2,1)S(1)}, u32[]{:S(2)}, u32[]{:S(2)}) collective-permute-start(bf16[1,8,16,128]{3,2,1,0:T(8,128)(2,1)S(1)} %get-tuple-element.151), channel_id=1, source_target_pairs={{0,16},{16,0},{1,17},{17,1},{2,18},{18,2},{3,19},{19,3},{4,20},{20... | collective-permute-start | bytes 98312 | tf_op jit(solution)/shard_map/ppermute | solution.py:477
  5.5 16.7 %collective-permute-start.2 = (bf16[1,8,16,128]{3,2,1,0:T(8,128)(2,1)S(1)}, bf16[1,8,16,128]{3,2,1,0:T(8,128)(2,1)S(1)}, u32[]{:S(2)}, u32[]{:S(2)}) collective-permute-start(bf16[1,8,16,128]{3,2,1,0:T(8,128)(2,1)S(1)} %get-tuple-element.150), channel_id=1, source_target_pairs={{16,0},{0,16},{17,1},{1,17},{18,2},{2,18},{19,3},{3,19},{20,4},{4,... | collective-permute-start | bytes 98312 | tf_op jit(solution)/shard_map/ppermute | solution.py:483
  7.7 14.8 %collective-permute-start = (bf16[1,8,128,256]{3,2,1,0:T(8,128)(2,1)S(1)}, bf16[1,8,128,256]{3,2,1,0:T(8,128)(2,1)S(1)}, u32[]{:S(2)}, u32[]{:S(2)}) collective-permute-start(bf16[1,8,128,256]{3,2,1,0:T(8,128)(2,1)S(1)} %get-tuple-element.140), channel_id=1, source_target_pairs={{0,16},{16,0},{1,17},{17,1},{2,18},{18,2},{3,19},{19,3},{4,20},{20... | collective-permute-start | bytes 1572872 | tf_op jit(solution)/shard_map/ppermute | solution.py:477
  9.6 37.1 %collective-permute-start.8 = (bf16[1,8,128,256]{3,2,1,0:T(8,128)(2,1)}, bf16[1,8,128,256]{3,2,1,0:T(8,128)(2,1)}, u32[]{:S(2)}, u32[]{:S(2)}) collective-permute-start(bf16[1,8,128,256]{3,2,1,0:T(8,128)(2,1)} %get-tuple-element.139), channel_id=1, source_target_pairs={{16,0},{0,16},{17,1},{1,17},{18,2},{2,18},{19,3},{3,19},{20,4},{4,... | collective-permute-start | bytes 1572872 | tf_op jit(solution)/shard_map/ppermute | solution.py:483
  9.7 12.4 %copy-start.1 = (bf16[2,8,16,8,256]{4,3,2,1,0:T(8,128)(2,1)S(1)}, bf16[2,8,16,8,256]{4,3,2,1,0:T(8,128)(2,1)}, u32[]{:S(2)}) copy-start(bf16[2,8,16,8,256]{4,3,2,1,0:T(8,128)(2,1)} %param.7) | copy-start | bytes 3145732
  22.5 4.8 %copy-start.4 = (bf16[1,8,128,256]{3,2,1,0:T(8,128)(2,1)}, bf16[1,8,128,256]{3,2,1,0:T(8,128)(2,1)S(1)}, u32[]{:S(2)}) copy-start(bf16[1,8,128,256]{3,2,1,0:T(8,128)(2,1)S(1)} %collective-permute-done.side_feat.before) | copy-start | bytes 1572868
  24.0 5.4 %copy-start.3 = (bf16[2,8,16,128]{3,2,1,0:T(8,128)(2,1)S(1)}, bf16[2,8,16,128]{3,2,1,0:T(8,128)(2,1)}, u32[]{:S(2)}) copy-start(bf16[2,8,16,128]{3,2,1,0:T(8,128)(2,1)} %copy-done.2) | copy-start | bytes 196612
  24.0 2.0 %collective-permute-start.3 = (bf16[1024,256]{1,0:T(8,128)(2,1)S(1)}, bf16[1024,256]{1,0:T(8,128)(2,1)S(1)}, u32[]{:S(2)}, u32[]{:S(2)}) collective-permute-start(bf16[1024,256]{1,0:T(8,128)(2,1)S(1)} %dynamic-slice_convert_fusion), channel_id=1, source_target_pairs={{0,1},{1,0},{2,3},{3,2},{4,5},{5,4},{6,7},{7,6},{8,9},{9,8},{10,11... | collective-permute-start | bytes 1572872 | tf_op jit(solution)/shard_map/ppermute | solution.py:382
  27.4 8.7 %collective-permute-start.4 = (bf16[512,256]{1,0:T(8,128)(2,1)S(1)}, bf16[512,256]{1,0:T(8,128)(2,1)S(1)}, u32[]{:S(2)}, u32[]{:S(2)}) collective-permute-start(bf16[512,256]{1,0:T(8,128)(2,1)S(1)} %dynamic-slice_convert_fusion.1), channel_id=1, source_target_pairs={{0,2},{1,3},{2,0},{3,1},{4,6},{5,7},{6,4},{7,5},{8,10},{9,11},{10,... | collective-permute-start | bytes 786440 | tf_op jit(solution)/shard_map/ppermute | solution.py:382
  29.4 1.0 %copy-start.5 = (bf16[1,8,128,256]{3,2,1,0:T(8,128)(2,1)S(1)}, bf16[1,8,128,256]{3,2,1,0:T(8,128)(2,1)}, u32[]{:S(2)}) copy-start(bf16[1,8,128,256]{3,2,1,0:T(8,128)(2,1)} %copy-done.4) | copy-start | bytes 1572868
  30.5 1.2 %copy-start.6 = (bf16[8,256,256]{2,1,0:T(8,128)(2,1)S(1)}, bf16[8,256,256]{2,1,0:T(8,128)(2,1)}, u32[]{:S(2)}) copy-start(bf16[8,256,256]{2,1,0:T(8,128)(2,1)} %param.11) | copy-start | bytes 3145732
  36.1 7.4 %collective-permute-start.5 = (bf16[128,256]{1,0:T(8,128)(2,1)S(1)}, bf16[128,256]{1,0:T(8,128)(2,1)S(1)}, u32[]{:S(2)}, u32[]{:S(2)}) collective-permute-start(bf16[128,256]{1,0:T(8,128)(2,1)S(1)} %get-tuple-element.85), channel_id=1, source_target_pairs={{0,4},{1,5},{2,6},{3,7},{4,0},{5,1},{6,2},{7,3},{8,12},{9,13},{10,... | collective-permute-start | bytes 196616 | tf_op jit(solution)/shard_map/ppermute | solution.py:382
  38.0 6.7 %collective-permute-start.6 = (bf16[128,256]{1,0:T(8,128)(2,1)S(1)}, bf16[128,256]{1,0:T(8,128)(2,1)S(1)}, u32[]{:S(2)}, u32[]{:S(2)}) collective-permute-start(bf16[128,256]{1,0:T(8,128)(2,1)S(1)} %get-tuple-element.86), channel_id=1, source_target_pairs={{0,8},{1,9},{2,10},{3,11},{4,12},{5,13},{6,14},{7,15},{8,0},{9,1},... | collective-permute-start | bytes 196616 | tf_op jit(solution)/shard_map/ppermute | solution.py:382
  40.6 6.1 %collective-permute-start.7 = (bf16[128,256]{1,0:T(8,128)(2,1)S(1)}, bf16[128,256]{1,0:T(8,128)(2,1)S(1)}, u32[]{:S(2)}, u32[]{:S(2)}) collective-permute-start(bf16[128,256]{1,0:T(8,128)(2,1)S(1)} %get-tuple-element.87), channel_id=1, source_target_pairs={{0,12},{1,13},{2,14},{3,15},{4,8},{5,9},{6,10},{7,11},{8,4},{9,5},... | collective-permute-start | bytes 196616 | tf_op jit(solution)/shard_map/ppermute | solution.py:382
  47.6 15.4 %collective-permute-start.14 = (bf16[4,1,144,256]{3,2,1,0:T(8,128)(2,1)S(1)}, bf16[4,1,144,256]{3,2,1,0:T(8,128)(2,1)S(1)}, u32[]{:S(2)}, u32[]{:S(2)}) collective-permute-start(bf16[4,1,144,256]{3,2,1,0:T(8,128)(2,1)S(1)} %fusion.21), channel_id=1, source_target_pairs={{1,0},{2,1},{3,2},{4,3},{5,4},{6,5},{7,6},{8,7},{9,8},{10,9},{11,1... | collective-permute-start | bytes 884744 | tf_op jit(solution)/shard_map/ppermute | solution.py:483
  47.7 15.3 %collective-permute-start.13 = (bf16[4,1,144,256]{3,2,1,0:T(8,128)(2,1)S(1)}, bf16[4,1,144,256]{3,2,1,0:T(8,128)(2,1)S(1)}, u32[]{:S(2)}, u32[]{:S(2)}) collective-permute-start(bf16[4,1,144,256]{3,2,1,0:T(8,128)(2,1)S(1)} %fusion.17), channel_id=1, source_target_pairs={{0,1},{1,2},{2,3},{3,4},{4,5},{5,6},{6,7},{7,8},{8,9},{9,10},{10,1... | collective-permute-start | bytes 884744 | tf_op jit(solution)/shard_map/ppermute | solution.py:477
  48.4 5.5 %collective-permute-start.9 = (bf16[128,256]{1,0:T(8,128)(2,1)S(1)}, bf16[128,256]{1,0:T(8,128)(2,1)S(1)}, u32[]{:S(2)}, u32[]{:S(2)}) collective-permute-start(bf16[128,256]{1,0:T(8,128)(2,1)S(1)} %convert_element_type.80), channel_id=1, source_target_pairs={{0,16},{1,17},{2,18},{3,19},{4,20},{5,21},{6,22},{7,23},{8,24},{9,... | collective-permute-start | bytes 196616 | tf_op jit(solution)/shard_map/ppermute | solution.py:382
  54.0 8.4 %collective-permute-start.10 = (bf16[128,256]{1,0:T(8,128)(2,1)S(1)}, bf16[128,256]{1,0:T(8,128)(2,1)S(1)}, u32[]{:S(2)}, u32[]{:S(2)}) collective-permute-start(bf16[128,256]{1,0:T(8,128)(2,1)S(1)} %add_convert_fusion), channel_id=1, source_target_pairs={{0,4},{1,5},{2,6},{3,7},{4,0},{5,1},{6,2},{7,3},{8,12},{9,13},{10,... | collective-permute-start | bytes 196616 | tf_op jit(solution)/shard_map/ppermute | solution.py:382
  54.1 8.8 %collective-permute-start.11 = (bf16[128,256]{1,0:T(8,128)(2,1)S(1)}, bf16[128,256]{1,0:T(8,128)(2,1)S(1)}, u32[]{:S(2)}, u32[]{:S(2)}) collective-permute-start(bf16[128,256]{1,0:T(8,128)(2,1)S(1)} %add_convert_fusion), channel_id=1, source_target_pairs={{0,8},{1,9},{2,10},{3,11},{4,12},{5,13},{6,14},{7,15},{8,0},{9,1},... | collective-permute-start | bytes 196616 | tf_op jit(solution)/shard_map/ppermute | solution.py:382
  55.9 7.0 %collective-permute-start.12 = (bf16[128,256]{1,0:T(8,128)(2,1)S(1)}, bf16[128,256]{1,0:T(8,128)(2,1)S(1)}, u32[]{:S(2)}, u32[]{:S(2)}) collective-permute-start(bf16[128,256]{1,0:T(8,128)(2,1)S(1)} %add_convert_fusion), channel_id=1, source_target_pairs={{0,12},{1,13},{2,14},{3,15},{4,8},{5,9},{6,10},{7,11},{8,4},{9,5},... | collective-permute-start | bytes 196616 | tf_op jit(solution)/shard_map/ppermute | solution.py:382
  63.0 8.2 %collective-permute-start.15 = (bf16[512,256]{1,0:T(8,128)(2,1)S(1)}, bf16[512,256]{1,0:T(8,128)(2,1)S(1)}, u32[]{:S(2)}, u32[]{:S(2)}) collective-permute-start(bf16[512,256]{1,0:T(8,128)(2,1)S(1)} %bitcast.56), channel_id=1, source_target_pairs={{0,2},{1,3},{2,0},{3,1},{4,6},{5,7},{6,4},{7,5},{8,10},{9,11},{10,... | collective-permute-start | bytes 786440 | tf_op jit(solution)/shard_map/ppermute | solution.py:382
  70.0 4.6 %copy-start = (f32[8,2,128,256]{3,2,1,0:T(8,128)}, f32[8,2,128,256]{3,2,1,0:T(8,128)S(1)}, u32[]{:S(2)}) copy-start(f32[8,2,128,256]{3,2,1,0:T(8,128)S(1)} %high.1.base) | copy-start | bytes 6291460
  71.4 2.0 %collective-permute-start.16 = (bf16[1024,256]{1,0:T(8,128)(2,1)S(1)}, bf16[1024,256]{1,0:T(8,128)(2,1)S(1)}, u32[]{:S(2)}, u32[]{:S(2)}) collective-permute-start(bf16[1024,256]{1,0:T(8,128)(2,1)S(1)} %maximum_select_fusion.1), channel_id=1, source_target_pairs={{0,1},{1,0},{2,3},{3,2},{4,5},{5,4},{6,7},{7,6},{8,9},{9,8},{10,11... | collective-permute-start | bytes 1572872 | tf_op jit(solution)/shard_map/ppermute | solution.py:382

commit v3 on v2

--- a/solution.py
+++ b/solution.py
@@ -43,96 +43,107 @@
     return value
 
 
-def factor_kernel(grid_all, scale_all, pos, kidx, feat, wc, ph, fac, charges, where_at, kmat, kw):
-    step = pl.program_id(0)
+def factor_kernel(grid_all, scale_all, pos, kidx, feat, wc, ph_out, fac, ph, charges, where_at, sems):
     planes, cols, _, rows = pos.shape
-    vectors = kidx.shape[1]
+    copies = []
+    steps = ph.shape[0]
     atoms, width = feat.shape
 
-    @pl.when(step == 0)
-    def _():
-        sub = lax.broadcasted_iota(jnp.int32, (POS_ROWS, KTILE), 0)
-        parts = []
-        for j in range(0, vectors, KTILE):
-            waves = [
-                kidx[d : d + 1, j : j + KTILE].astype(F32) * (1.0 / grid_all[d]) for d in range(3)
-            ]
-            value = jnp.zeros((POS_ROWS, KTILE), F32)
-            k_sq = jnp.zeros((1, KTILE), F32)
-            for d in range(3):
-                hit = (sub == d) | (sub == CELL_ROW + d)
-                value = jnp.where(hit, jnp.broadcast_to(waves[d], value.shape), value)
-                wave = TWO_PI * waves[d]
-                k_sq = k_sq + wave * wave
-            kmat[j // KTILE] = value.astype(BF16)
-            parts.append(jnp.exp(-k_sq / (4.0 * SCREEN)) / k_sq)
-        total = sum(jnp.sum(part, axis=1, keepdims=True) for part in parts)
-        for j, part in enumerate(parts):
-            kw[j] = jnp.broadcast_to(part / total * scale_all, (8, KTILE))
-        sub = lax.broadcasted_iota(jnp.int32, (POS_ROWS, rows), 0)
-        depth = (lax.broadcasted_iota(jnp.int32, (POS_ROWS, rows), 1) // 8).astype(F32)
-        x0 = (lax.axis_index("gx") * planes).astype(F32)
-        y0 = (lax.axis_index("gy") * cols).astype(F32)
-        turned = wc[...].T
-        for x in range(planes):
-            for y in range(cols):
-                j = (x * cols + y) * rows
-                c = lax.dot_general(turned, feat[j : j + rows, :], NT, preferred_element_type=F32)
-                tile = pos[x, y].astype(F32)
-                charges[:, j : j + rows] = (c * tile[OCC_ROW : OCC_ROW + 1, :]).astype(BF16)
-                tile = jnp.where(sub == CELL_ROW, x0 + float(x), tile)
-                tile = jnp.where(sub == CELL_ROW + 1, y0 + float(y), tile)
-                tile = jnp.where(sub == CELL_ROW + 2, depth, tile)
-                where_at[j : j + rows, :] = tile.T.astype(BF16)
-
-    for j in range(0, atoms, 256):
-        t_all = jnp.dot(where_at[j : j + 256, :], kmat[step], preferred_element_type=F32)
-        for i in range(0, 256, 16):
-            t = t_all[i : i + 16]
-            r = t - jnp.round(t)
-            s = r * r
-            half_c = horner(HALF_COS, s)
-            half_s = horner(HALF_SIN, s) * r
-            ph[0, j + i : j + i + 16, :] = (1.0 - half_s * half_s).astype(BF16)
-            ph[1, j + i : j + i + 16, :] = (half_s * half_c).astype(BF16)
-    weight = kw[step][0:1, :]
-    for p in range(2):
-        part = jnp.dot(charges[...], ph[p], preferred_element_type=F32)
-        fac[p * width : (p + 1) * width, :] = part * weight
+    sub = lax.broadcasted_iota(jnp.int32, (POS_ROWS, KTILE), 0)
+    kmat, screened = [], []
+    for step in range(steps):
+        value = jnp.zeros((POS_ROWS, KTILE), F32)
+        k_sq = jnp.zeros((1, KTILE), F32)
+        for d in range(3):
+            k = kidx[d : d + 1, step * KTILE : (step + 1) * KTILE].astype(F32) * (1.0 / grid_all[d])
+            hit = (sub == d) | (sub == CELL_ROW + d)
+            value = jnp.where(hit, jnp.broadcast_to(k, value.shape), value)
+            k_sq = k_sq + (TWO_PI * k) * (TWO_PI * k)
+        kmat.append(value.astype(BF16))
+        screened.append(jnp.exp(-k_sq / (4.0 * SCREEN)) / k_sq)
+    total = sum(jnp.sum(part, axis=1, keepdims=True) for part in screened)
+
+    sub = lax.broadcasted_iota(jnp.int32, (POS_ROWS, rows), 0)
+    depth = (lax.broadcasted_iota(jnp.int32, (POS_ROWS, rows), 1) // 8).astype(F32)
+    x0 = (lax.axis_index("gx") * planes).astype(F32)
+    y0 = (lax.axis_index("gy") * cols).astype(F32)
+    for x in range(planes):
+        for y in range(cols):
+            j = (x * cols + y) * rows
+            tile = pos[x, y].astype(F32)
+            tile = jnp.where(sub == CELL_ROW, x0 + float(x), tile)
+            tile = jnp.where(sub == CELL_ROW + 1, y0 + float(y), tile)
+            tile = jnp.where(sub == CELL_ROW + 2, depth, tile)
+            where_at[j : j + rows, :] = tile.T.astype(BF16)
+    turned = wc[...].T
+
+    size = 2 * rows
+    for step in range(steps + 1):
+        sums = [None, None]
+        for j in range(0, atoms, size):
+            if step < steps:
+                t_all = jnp.dot(
+                    where_at[j : j + size, :], kmat[step], preferred_element_type=F32
+                )
+                for i in range(0, size, 16):
+                    t = t_all[i : i + 16]
+                    r = t - jnp.round(t)
+                    s = r * r
+                    half_c = horner(HALF_COS, s)
+                    half_s = horner(HALF_SIN, s) * r
+                    ph[step, 0, j + i : j + i + 16, :] = (1.0 - half_s * half_s).astype(BF16)
+                    ph[step, 1, j + i : j + i + 16, :] = (half_s * half_c).astype(BF16)
+            if step == 0:
+                c = lax.dot_general(turned, feat[j : j + size, :], NT, preferred_element_type=F32)
+                line = j // rows
+                occ = [
+                    pos[n // cols, n % cols, OCC_ROW : OCC_ROW + 1, :].astype(F32)
+                    for n in range(line, line + 2)
+                ]
+                charges[:, j : j + size] = (c * jnp.concatenate(occ, axis=1)).astype(BF16)
+            if step > 0:
+                for p in range(2):
+                    part = jnp.dot(
+                        charges[:, j : j + size],
+                        ph[step - 1, p, j : j + size, :],
+                        preferred_element_type=F32,
+                    )
+                    sums[p] = part if sums[p] is None else sums[p] + part
+        if step < steps:
+            copy = pltpu.make_async_copy(ph.at[step], ph_out.at[step], sems.at[step])
+            copy.start()
+            copies.append(copy)
+        if step > 0:
+            weight = screened[step - 1] / total * scale_all
+            for p in range(2):
+                row = (2 * (step - 1) + p) * width
+                fac[row : row + width, :] = sums[p] * weight
+    for copy in copies:
+        copy.wait()
 
 
 def factor_call(pos, kidx, feat, wc, grid_all, scale_all):
     atoms, width = feat.shape
     vectors = kidx.shape[1]
     steps = vectors // KTILE
+    whole = pl.BlockSpec(memory_space=VMEM)
     return pl.pallas_call(
         functools.partial(factor_kernel, grid_all, scale_all),
-        grid=(steps,),
-        in_specs=[
-            pl.BlockSpec(pos.shape, lambda i: (0, 0, 0, 0)),
-            pl.BlockSpec(kidx.shape, lambda i: (0, 0)),
-            pl.BlockSpec((atoms, width), lambda i: (0, 0)),
-            pl.BlockSpec((width, width), lambda i: (0, 0)),
-        ],
-        out_specs=[
-            pl.BlockSpec((2, atoms, KTILE), lambda i: (0, 0, i)),
-            pl.BlockSpec((2 * width, KTILE), lambda i: (i, 0)),
-        ],
+        in_specs=[whole] * 4,
+        out_specs=[pl.BlockSpec(memory_space=pltpu.HBM), whole],
         out_shape=[
-            jax.ShapeDtypeStruct((2, atoms, vectors), BF16),
+            pltpu.HBM((steps, 2, atoms, KTILE), BF16),
             jax.ShapeDtypeStruct((steps * 2 * width, KTILE), F32),
         ],
         scratch_shapes=[
+            VMEM((steps, 2, atoms, KTILE), BF16),
             VMEM((width, atoms), BF16),
             VMEM((atoms, POS_ROWS), BF16),
-            VMEM((steps, POS_ROWS, KTILE), BF16),
-            VMEM((steps, 8, KTILE), F32),
+            pltpu.SemaphoreType.DMA((steps,)),
         ],
-        compiler_params=pltpu.CompilerParams(
-            dimension_semantics=("arbitrary",), vmem_limit_bytes=56 << 20
-        ),
+        compiler_params=pltpu.CompilerParams(vmem_limit_bytes=24 << 20),
         cost_estimate=pl.CostEstimate(
-            flops=24 * atoms * vectors * width, bytes_accessed=16 << 20, transcendentals=0
+            flops=24 * atoms * vectors * width, bytes_accessed=4 << 20, transcendentals=0
         ),
         name="factor",
     )(pos, kidx, feat, wc)
@@ -322,55 +333,67 @@
     )(*args)
 
 
-def field_kernel(ph, weighted, w_out, base, pos, out, rhs):
+def field_kernel(ph_all, weighted, w_out, base, pos, out, ph, rhs, held, in_sems, out_sems):
     tiles, width, _ = weighted.shape
-
-    @pl.when(pl.program_id(0) == 0)
-    def _():
-        for t in range(tiles):
-            rhs[t * KTILE : (t + 1) * KTILE, :] = weighted[t].T
-
-    lhs = jnp.concatenate(
-        [ph[t % 2, :, KTILE * (t // 2) : KTILE * (t // 2 + 1)] for t in range(tiles)], axis=1
-    )
-    recip = jnp.dot(lhs, rhs[...], preferred_element_type=F32)
-    far = jnp.dot(recip.astype(BF16), w_out[...], preferred_element_type=F32)
+    cols, planes, rows, _ = base.shape
+    count, size, _ = held.shape
+    lines = size // rows
+    loads = []
+    for i in range(count):
+        part = pl.ds(size * i, size)
+        load = pltpu.make_async_copy(
+            ph_all.at[:, :, part, :], ph.at[:, :, part, :], in_sems.at[i]
+        )
+        load.start()
+        loads.append(load)
+    for t in range(tiles):
+        rhs[t * KTILE : (t + 1) * KTILE, :] = weighted[t].T
     sub = lax.broadcasted_iota(jnp.int32, (POS_ROWS, width), 0)
     select = jnp.where(sub == OCC_ROW, 1.0, 0.0).astype(BF16)
-    rows = base.shape[2]
-    for y in range(base.shape[0]):
-        occ = lax.dot_general(pos[0, y], select, TN, preferred_element_type=F32)
-        value = base[y, 0] + far[rows * y : rows * (y + 1)]
-        out[rows * y : rows * (y + 1), :] = jnp.where(occ > 0.0, value, 0.0).astype(BF16)
-
-
-def field_call(ph, weighted, w_out, base, pos, group=2):
-    _, atoms, vectors = ph.shape
+    stores = []
+    for i in range(count):
+        loads[i].wait()
+        lhs = jnp.concatenate(
+            [ph[t // 2, t % 2, size * i : size * (i + 1), :] for t in range(tiles)], axis=1
+        )
+        recip = jnp.dot(lhs, rhs[...], preferred_element_type=F32)
+        far = jnp.dot(recip.astype(BF16), w_out[...], preferred_element_type=F32)
+        for j in range(lines):
+            x, y = divmod(lines * i + j, cols)
+            occ = lax.dot_general(pos[x, y], select, TN, preferred_element_type=F32)
+            value = base[y, x] + far[rows * j : rows * (j + 1)]
+            held[i, rows * j : rows * (j + 1), :] = jnp.where(occ > 0.0, value, 0.0).astype(BF16)
+        store = pltpu.make_async_copy(held.at[i], out.at[pl.ds(size * i, size), :], out_sems.at[i])
+        store.start()
+        stores.append(store)
+    for store in stores:
+        store.wait()
+
+
+def field_call(ph, weighted, w_out, base, pos, lines=4):
+    atoms = ph.shape[2]
     tiles, width, _ = weighted.shape
     cols, planes, rows, _ = base.shape
-    tile = group * rows
-    groups = cols // group
+    count = planes * cols // lines
+    whole = pl.BlockSpec(memory_space=VMEM)
     return pl.pallas_call(
         field_kernel,
-        grid=(atoms // tile,),
-        in_specs=[
-            pl.BlockSpec((2, tile, vectors), lambda i: (0, i, 0)),
-            pl.BlockSpec((tiles, width, KTILE), lambda i: (0, 0, 0)),
-            pl.BlockSpec((width, width), lambda i: (0, 0)),
-            pl.BlockSpec((group, 1, rows, width), lambda i: (i % groups, i // groups, 0, 0)),
-            pl.BlockSpec((1, group, POS_ROWS, rows), lambda i: (i // groups, i % groups, 0, 0)),
+        in_specs=[pl.BlockSpec(memory_space=pltpu.HBM)] + [whole] * 4,
+        out_specs=pl.BlockSpec(memory_space=pltpu.HBM),
+        out_shape=jax.ShapeDtypeStruct((atoms, width), BF16),
+        scratch_shapes=[
+            VMEM(ph.shape, BF16),
+            VMEM((tiles * KTILE, width), BF16),
+            VMEM((count, lines * rows, width), BF16),
+            pltpu.SemaphoreType.DMA((count,)),
+            pltpu.SemaphoreType.DMA((count,)),
         ],
-        out_specs=pl.BlockSpec((tile, width), lambda i: (i, 0)),
-        out_shape=jax.ShapeDtypeStruct((atoms, width), BF16),
-        scratch_shapes=[VMEM((tiles * KTILE, width), BF16)],
-        compiler_params=pltpu.CompilerParams(
-            dimension_semantics=("arbitrary",), vmem_limit_bytes=54 << 20
-        ),
+        compiler_params=pltpu.CompilerParams(vmem_limit_bytes=24 << 20),
         cost_estimate=pl.CostEstimate(
-            flops=4 * atoms * vectors * width, bytes_accessed=16 << 20, transcendentals=0
+            flops=2 * atoms * tiles * KTILE * width, bytes_accessed=4 << 20, transcendentals=0
         ),
         name="field",
-    )(ph, weighted, w_out, base, pos)
+    )(pltpu.with_memory_space_constraint(ph, pltpu.HBM), weighted, w_out, base, pos)
 
 
 def my_index():
@@ -524,7 +547,7 @@
     ph, partial = factor_call(
         pos, k_index.T, feat.reshape(atoms, width), w_charge, grid_all, scale_all
     )
-    ph, partial, before, pos_before, pos_after = tied(ph, partial, before, pos_before, pos_after)
+    partial, before, pos_before, pos_after = tied(partial, before, pos_before, pos_after)
     after = from_after(feat, "gx", 0)
 
     w_flat = w_short.reshape(basis * width, width)

time: 86 us -> 84.8 us (0.986)
  waiting for transfers between devices: 9.54 us -> 14.1 us
  Pallas kernels: 42.1 us -> 38.3 us
  local copies, waits for them, and re-layouts: 9.85 us -> 8.1 us
    pallas_call x2, Pallas kernels: 22.9 us -> 16.7 us  [the longest x1 8.34 us: factor_call(): pl.pallas_call(functools.partial(factor_kernel, grid_all, scale_all), in_...]
    ppermute x3, waiting for transfers between devices: 0.35 us -> 4.7 us  [from_before(): lax.ppermute(tail, axis, [(i, (i + 1) % count) for i in range(count)])]
    pallas_call x6, Pallas kernels: 19.3 us -> 21.7 us  [short_call(): pl.pallas_call(kernel, in_specs=[whole] * len(args), out_specs=whole, out...]
    unnamed x14 -> x10, local copies, waits for them, and re-layouts: 2.29 us -> 0.02 us
    slice x3, local copies, waits for them, and re-layouts: 0.91 us -> 1.87 us  [edge_rows(): parts.append(jnp.concatenate([f[:, y:y + 1], q], axis=2))]
  transfers between devices with their start and end apart: 17 -> 17, of which waited for: 8 -> 8; matrix products, arithmetic and copies ran while one was open for 7% -> 7% of each run, Pallas kernels for 37% -> 36%
where the time goes in v3:
time: 84.8 us; the launch traced here: 84.3 us
  Pallas kernels  38.3 us (45%)
  starting transfers between devices  20 us (24%)
  waiting for transfers between devices  14.1 us (17%)
  local copies, waits for them, and re-layouts  8.1 us (10%)
  other arithmetic  3.29 us (4%)
    pallas_call x6, Pallas kernels, short_call(): pl.pallas_call(kernel, in_specs=[whole] * len(args), out_specs=whole, out...  21.7 us
    ppermute x11, starting transfers between devices, swap(): return lax.ppermute(value, AXES, [(i, i ^ mask) for i in range(count)])  13.9 us
    ppermute x11, waiting for transfers between devices, swap(): return lax.ppermute(value, AXES, [(i, i ^ mask) for i in range(count)])  9.34 us
    pallas_call x1, Pallas kernels, factor_call(): pl.pallas_call(functools.partial(factor_kernel, grid_all, scale_all), in_...  8.34 us
    pallas_call x1, Pallas kernels, field_call(): pl.pallas_call(field_kernel, in_specs=[pl.BlockSpec(memory_space=pltpu.HB...  8.33 us
    ppermute x3, starting transfers between devices, from_before(): lax.ppermute(tail, axis, [(i, (i + 1) % count) for i in range(count)])  5.17 us
    ppermute x3, waiting for transfers between devices, from_before(): lax.ppermute(tail, axis, [(i, (i + 1) % count) for i in range(count)])  4.7 us
    slice x2, local copies, waits for them, and re-layouts, from_after(): head = lax.slice_in_dim(cells, 0, 1, axis=dim)  2.88 us
  transfers between devices with their start and end apart: 17, of which 8 were waited for; matrix products, arithmetic and copies ran while one was open for 7% of the time, Pallas kernels for 36%

profile of v3, /device:TPU:0, one launch (start us, length us, event | category | flops | bytes accessed | tf_op | source)
XLA Modules:
  0.0 84.3 jit_solution(3087727479699574735)
XLA Ops:
  3.2 2.9 %collective-permute-start.1 = (bf16[1,8,16,128]{3,2,1,0:T(8,128)(2,1)}, bf16[1,8,16,128]{3,2,1,0:T(8,128)(2,1)S(1)}, u32[]{:S(2)}, u32[]{:S(2)}) collective-permute-start(bf16[1,8,16,128]{3,2,1,0:T(8,128)(2,1)} %get-tuple-element.149), channel_id=1, source_target_pairs={{0,16},{16,0},{1,17},{17,1},{2,18},{18,2},{3,19},{19,3},{4,20},{20... | collective-permute-start | bytes 98312 | tf_op jit(solution)/shard_map/ppermute | solution.py:500
  6.2 2.3 %slice_bitcast_fusion = (bf16[1,8,128,256]{3,2,1,0:T(8,128)(2,1)}, bf16[1,8,128,256]{3,2,1,0:T(8,128)(2,1)}) fusion(bf16[2,8,16,8,256]{4,3,2,1,0:T(8,128)(2,1)} %param.7), kind=kLoop, calls=%fused_computation.17 | loop fusion | bytes 2097152 | tf_op jit(solution)/shard_map/slice | solution.py:505
  8.4 2.0 %collective-permute-start = (bf16[1,8,128,256]{3,2,1,0:T(8,128)(2,1)}, bf16[1,8,128,256]{3,2,1,0:T(8,128)(2,1)}, u32[]{:S(2)}, u32[]{:S(2)}) collective-permute-start(bf16[1,8,128,256]{3,2,1,0:T(8,128)(2,1)} %get-tuple-element.138), channel_id=1, source_target_pairs={{0,16},{16,0},{1,17},{17,1},{2,18},{18,2},{3,19},{19,3},{4,20},{20... | collective-permute-start | bytes 1572872 | tf_op jit(solution)/shard_map/ppermute | solution.py:500
  10.5 8.3 %factor.1 = (bf16[4,2,2048,256]{3,2,1,0:T(8,128)(2,1)}, f32[2048,256]{1,0:T(8,128)S(1)}) custom-call(bf16[2,8,16,128]{3,2,1,0:T(8,128)(2,1)S(1)} %maximum_maximum_fusion.pos, s32[3,1024]{1,0:T(4,128)S(1)} %bitcast.53, bf16[2048,256]{1,0:T(8,128)(2,1)S(1)} %bitcast.39, bf16[256,256]{1,0:T(8,128)(2,1)S(1)} %copy-done.3), custom_call_target="tpu_custom_call" | custom-call | flops 12884901888 | bytes 4194304 | tf_op jit(solution)/shard_map/factor/pallas_call | solution.py:130
  18.9 4.7 %collective-permute-done.side_feat.before = bf16[1,8,128,256]{3,2,1,0:T(8,128)(2,1)} collective-permute-done((bf16[1,8,128,256]{3,2,1,0:T(8,128)(2,1)}, bf16[1,8,128,256]{3,2,1,0:T(8,128)(2,1)}, u32[]{:S(2)}, u32[]{:S(2)}) %collective-permute-start) | collective-permute-done | bytes 524320 | tf_op jit(solution)/shard_map/ppermute | solution.py:500
  25.4 1.3 %collective-permute-done.3 = bf16[1024,256]{1,0:T(8,128)(2,1)} collective-permute-done((bf16[1024,256]{1,0:T(8,128)(2,1)}, bf16[1024,256]{1,0:T(8,128)(2,1)}, u32[]{:S(2)}, u32[]{:S(2)}) %collective-permute-start.3) | collective-permute-done | bytes 524320 | tf_op jit(solution)/shard_map/ppermute | solution.py:405
  27.9 2.1 %collective-permute-start.4 = (bf16[512,256]{1,0:T(8,128)(2,1)S(1)}, bf16[512,256]{1,0:T(8,128)(2,1)S(1)}, u32[]{:S(2)}, u32[]{:S(2)}) collective-permute-start(bf16[512,256]{1,0:T(8,128)(2,1)S(1)} %dynamic-slice_convert_fusion.1), channel_id=1, source_target_pairs={{0,2},{1,3},{2,0},{3,1},{4,6},{5,7},{6,4},{7,5},{8,10},{9,11},{10,... | collective-permute-start | bytes 786440 | tf_op jit(solution)/shard_map/ppermute | solution.py:405
  30.0 4.0 %plane.4.rest_0_ = f32[8,2,128,256]{3,2,1,0:T(8,128)S(1)} custom-call(bf16[2,8,128,256]{3,2,1,0:T(8,128)(2,1)S(1)} %bitcast.41, bf16[2,8,16,128]{3,2,1,0:T(8,128)(2,1)S(1)} %maximum_maximum_fusion.pos, bf16[1,8,128,256]{3,2,1,0:T(8,128)(2,1)} %collective-permute-done.side_feat.before, bf16[1,8,16,128]{3,2,1,0:T(8,128)(2,1)S(1)} %collective-permute-done.1.side_pos.pos_before, ...), custom_call_target="tpu_custom_call" | custom-call | flops 4026531840 | bytes 4194304 | tf_op jit(solution)/shard_map/plane/pallas_call | solution.py:319
  34.0 2.6 %collective-permute-done.4 = bf16[512,256]{1,0:T(8,128)(2,1)S(1)} collective-permute-done((bf16[512,256]{1,0:T(8,128)(2,1)S(1)}, bf16[512,256]{1,0:T(8,128)(2,1)S(1)}, u32[]{:S(2)}, u32[]{:S(2)}) %collective-permute-start.4) | collective-permute-done | bytes 262176 | tf_op jit(solution)/shard_map/ppermute | solution.py:405
  36.7 1.9 %collective-permute-start.5 = (bf16[128,256]{1,0:T(8,128)(2,1)S(1)}, bf16[128,256]{1,0:T(8,128)(2,1)S(1)}, u32[]{:S(2)}, u32[]{:S(2)}) collective-permute-start(bf16[128,256]{1,0:T(8,128)(2,1)S(1)} %get-tuple-element.83), channel_id=1, source_target_pairs={{0,4},{1,5},{2,6},{3,7},{4,0},{5,1},{6,2},{7,3},{8,12},{9,13},{10,... | collective-permute-start | bytes 196616 | tf_op jit(solution)/shard_map/ppermute | solution.py:405
  38.6 2.6 %collective-permute-start.6 = (bf16[128,256]{1,0:T(8,128)(2,1)S(1)}, bf16[128,256]{1,0:T(8,128)(2,1)S(1)}, u32[]{:S(2)}, u32[]{:S(2)}) collective-permute-start(bf16[128,256]{1,0:T(8,128)(2,1)S(1)} %get-tuple-element.84), channel_id=1, source_target_pairs={{0,8},{1,9},{2,10},{3,11},{4,12},{5,13},{6,14},{7,15},{8,0},{9,1},... | collective-permute-start | bytes 196616 | tf_op jit(solution)/shard_map/ppermute | solution.py:405
  41.2 4.0 %plane.5.rest_0_ = f32[8,2,128,256]{3,2,1,0:T(8,128)S(1)} custom-call(bf16[2,8,128,256]{3,2,1,0:T(8,128)(2,1)S(1)} %bitcast.42, bf16[2,8,16,128]{3,2,1,0:T(8,128)(2,1)S(1)} %maximum_maximum_fusion.pos, bf16[1,8,128,256]{3,2,1,0:T(8,128)(2,1)} %collective-permute-done.side_feat.before, ...), custom_call_target="tpu_custom_call", output_to_operand_aliasing={{}: (5, {})} | custom-call | flops 4026531840 | bytes 4194304 | tf_op jit(solution)/shard_map/plane/pallas_call | solution.py:319
  45.3 1.9 %collective-permute-done.7 = bf16[128,256]{1,0:T(8,128)(2,1)S(1)} collective-permute-done((bf16[128,256]{1,0:T(8,128)(2,1)S(1)}, bf16[128,256]{1,0:T(8,128)(2,1)S(1)}, u32[]{:S(2)}, u32[]{:S(2)}) %collective-permute-start.7) | collective-permute-done | bytes 65568 | tf_op jit(solution)/shard_map/ppermute | solution.py:405
  49.3 1.6 %collective-permute-start.9 = (bf16[128,256]{1,0:T(8,128)(2,1)S(1)}, bf16[128,256]{1,0:T(8,128)(2,1)S(1)}, u32[]{:S(2)}, u32[]{:S(2)}) collective-permute-start(bf16[128,256]{1,0:T(8,128)(2,1)S(1)} %convert_element_type.80), channel_id=1, source_target_pairs={{0,16},{1,17},{2,18},{3,19},{4,20},{5,21},{6,22},{7,23},{8,24},{9,... | collective-permute-start | bytes 196616 | tf_op jit(solution)/shard_map/ppermute | solution.py:405
  50.9 4.0 %plane.6.rest_0_ = f32[8,2,128,256]{3,2,1,0:T(8,128)S(1)} custom-call(bf16[2,8,128,256]{3,2,1,0:T(8,128)(2,1)S(1)} %bitcast.43, bf16[2,8,16,128]{3,2,1,0:T(8,128)(2,1)S(1)} %maximum_maximum_fusion.pos, bf16[1,8,128,256]{3,2,1,0:T(8,128)(2,1)} %collective-permute-done.8.side_feat.after, ...), custom_call_target="tpu_custom_call", output_to_operand_aliasing={{}: (5, {})} | custom-call | flops 4026531840 | bytes 4194304 | tf_op jit(solution)/shard_map/plane/pallas_call | solution.py:319
  55.0 2.0 %collective-permute-start.11 = (bf16[128,256]{1,0:T(8,128)(2,1)S(1)}, bf16[128,256]{1,0:T(8,128)(2,1)S(1)}, u32[]{:S(2)}, u32[]{:S(2)}) collective-permute-start(bf16[128,256]{1,0:T(8,128)(2,1)S(1)} %add_convert_fusion), channel_id=1, source_target_pairs={{0,8},{1,9},{2,10},{3,11},{4,12},{5,13},{6,14},{7,15},{8,0},{9,1},... | collective-permute-start | bytes 196616 | tf_op jit(solution)/shard_map/ppermute | solution.py:405
  57.0 2.4 %collective-permute-start.12 = (bf16[128,256]{1,0:T(8,128)(2,1)S(1)}, bf16[128,256]{1,0:T(8,128)(2,1)S(1)}, u32[]{:S(2)}, u32[]{:S(2)}) collective-permute-start(bf16[128,256]{1,0:T(8,128)(2,1)S(1)} %add_convert_fusion), channel_id=1, source_target_pairs={{0,12},{1,13},{2,14},{3,15},{4,8},{5,9},{6,10},{7,11},{8,4},{9,5},... | collective-permute-start | bytes 196616 | tf_op jit(solution)/shard_map/ppermute | solution.py:405
  59.3 4.0 %plane.7.rest_0_ = f32[8,2,128,256]{3,2,1,0:T(8,128)S(1)} custom-call(bf16[2,8,128,256]{3,2,1,0:T(8,128)(2,1)S(1)} %bitcast.44, bf16[2,8,16,128]{3,2,1,0:T(8,128)(2,1)S(1)} %maximum_maximum_fusion.pos, bf16[1,8,128,256]{3,2,1,0:T(8,128)(2,1)} %collective-permute-done.8.side_feat.after, ...), custom_call_target="tpu_custom_call", output_to_operand_aliasing={{}: (5, {})} | custom-call | flops 4026531840 | bytes 4194304 | tf_op jit(solution)/shard_map/plane/pallas_call | solution.py:319
  63.8 1.2 %collective-permute-start.15 = (bf16[512,256]{1,0:T(8,128)(2,1)S(1)}, bf16[512,256]{1,0:T(8,128)(2,1)S(1)}, u32[]{:S(2)}, u32[]{:S(2)}) collective-permute-start(bf16[512,256]{1,0:T(8,128)(2,1)S(1)} %bitcast.57), channel_id=1, source_target_pairs={{0,2},{1,3},{2,0},{3,1},{4,6},{5,7},{6,4},{7,5},{8,10},{9,11},{10,... | collective-permute-start | bytes 786440 | tf_op jit(solution)/shard_map/ppermute | solution.py:405
  65.1 2.9 %low.1.rest_0_ = f32[8,2,128,256]{3,2,1,0:T(8,128)S(1)} custom-call(bf16[2,8,128,256]{3,2,1,0:T(8,128)(2,1)S(1)} %bitcast.45, bf16[2,8,16,128]{3,2,1,0:T(8,128)(2,1)S(1)} %maximum_maximum_fusion.pos, bf16[1,8,128,256]{3,2,1,0:T(8,128)(2,1)} %collective-permute-done.side_feat.before, ...), custom_call_target="tpu_custom_call", output_to_operand_aliasing={{}: (8, {})} | custom-call | flops 2684354560 | bytes 4194304 | tf_op jit(solution)/shard_map/low/pallas_call | solution.py:319
  68.0 2.9 %high.1.base = f32[8,2,128,256]{3,2,1,0:T(8,128)S(1)} custom-call(bf16[2,8,128,256]{3,2,1,0:T(8,128)(2,1)S(1)} %bitcast.46, bf16[2,8,16,128]{3,2,1,0:T(8,128)(2,1)S(1)} %maximum_maximum_fusion.pos, bf16[1,8,128,256]{3,2,1,0:T(8,128)(2,1)} %collective-permute-done.side_feat.before, ...), custom_call_target="tpu_custom_call", output_to_operand_aliasing={{}: (8, {})} | custom-call | flops 2684354560 | bytes 4194304 | tf_op jit(solution)/shard_map/high/pallas_call | solution.py:319
  72.2 2.0 %collective-permute-done.16 = bf16[1024,256]{1,0:T(8,128)(2,1)} collective-permute-done((bf16[1024,256]{1,0:T(8,128)(2,1)S(1)}, bf16[1024,256]{1,0:T(8,128)(2,1)}, u32[]{:S(2)}, u32[]{:S(2)}) %collective-permute-start.16) | collective-permute-done | bytes 524320 | tf_op jit(solution)/shard_map/ppermute | solution.py:405
  74.2 1.5 %maximum_select_fusion = bf16[2048,256]{1,0:T(8,128)(2,1)S(1)} fusion(bf16[1024,256]{1,0:T(8,128)(2,1)} %collective-permute-done.16, bf16[1024,256]{1,0:T(8,128)(2,1)S(1)} %maximum_select_fusion.1, pred[]{:T(512)S(6)} %eq.21), kind=kLoop, calls=%fused_computation | loop fusion | flops 4718592 | bytes 2097153 | tf_op jit(solution)/shard_map/jit(_where)/select_n | solution.py:472
  75.8 8.3 %field.1 = bf16[2048,256]{1,0:T(8,128)(2,1)} custom-call(bf16[4,2,2048,256]{3,2,1,0:T(8,128)(2,1)} %get-tuple-element.70.ph_all, bf16[8,256,256]{2,1,0:T(8,128)(2,1)S(1)} %bitcast.38, bf16[256,256]{1,0:T(8,128)(2,1)S(1)} %copy-done.1, f32[8,2,128,256]{3,2,1,0:T(8,128)S(1)} %high.1.base, bf16[2,8,16,128]{3,2,1,0:T(8,128)(2,1)S(1)} %maximum_maximum_fusion.pos), custom_call_target="tpu_custom_call" | custom-call | flops 2147483648 | bytes 4194304 | tf_op jit(solution)/shard_map/field/pallas_call | solution.py:379
  (61 shorter events, 10.4 us)
Async XLA Ops:
  0.0 10.5 %copy-start = (bf16[2,8,16,8,256]{4,3,2,1,0:T(8,128)(2,1)S(1)}, bf16[2,8,16,8,256]{4,3,2,1,0:T(8,128)(2,1)}, u32[]{:S(2)}) copy-start(bf16[2,8,16,8,256]{4,3,2,1,0:T(8,128)(2,1)} %param.7) | copy-start | bytes 3145732
  0.0 10.5 %copy-start.4 = (s32[1024,3]{0,1:T(4,128)S(1)}, s32[1024,3]{0,1:T(4,128)}, u32[]{:S(2)}) copy-start(s32[1024,3]{0,1:T(4,128)} %param.10) | copy-start | bytes 36868
  0.0 10.5 %copy-start.3 = (bf16[256,256]{1,0:T(8,128)(2,1)S(1)}, bf16[256,256]{1,0:T(8,128)(2,1)}, u32[]{:S(2)}) copy-start(bf16[256,256]{1,0:T(8,128)(2,1)} %wc.1) | copy-start | bytes 393220
  3.2 15.7 %collective-permute-start.1 = (bf16[1,8,16,128]{3,2,1,0:T(8,128)(2,1)}, bf16[1,8,16,128]{3,2,1,0:T(8,128)(2,1)S(1)}, u32[]{:S(2)}, u32[]{:S(2)}) collective-permute-start(bf16[1,8,16,128]{3,2,1,0:T(8,128)(2,1)} %get-tuple-element.149), channel_id=1, source_target_pairs={{0,16},{16,0},{1,17},{17,1},{2,18},{18,2},{3,19},{19,3},{4,20},{20... | collective-permute-start | bytes 98312 | tf_op jit(solution)/shard_map/ppermute | solution.py:500
  6.1 12.7 %collective-permute-start.2 = (bf16[1,8,16,128]{3,2,1,0:T(8,128)(2,1)}, bf16[1,8,16,128]{3,2,1,0:T(8,128)(2,1)S(1)}, u32[]{:S(2)}, u32[]{:S(2)}) collective-permute-start(bf16[1,8,16,128]{3,2,1,0:T(8,128)(2,1)} %get-tuple-element.148), channel_id=1, source_target_pairs={{16,0},{0,16},{17,1},{1,17},{18,2},{2,18},{19,3},{3,19},{20,4},{4,... | collective-permute-start | bytes 98312 | tf_op jit(solution)/shard_map/ppermute | solution.py:506
  8.4 15.2 %collective-permute-start = (bf16[1,8,128,256]{3,2,1,0:T(8,128)(2,1)}, bf16[1,8,128,256]{3,2,1,0:T(8,128)(2,1)}, u32[]{:S(2)}, u32[]{:S(2)}) collective-permute-start(bf16[1,8,128,256]{3,2,1,0:T(8,128)(2,1)} %get-tuple-element.138), channel_id=1, source_target_pairs={{0,16},{16,0},{1,17},{17,1},{2,18},{18,2},{3,19},{19,3},{4,20},{20... | collective-permute-start | bytes 1572872 | tf_op jit(solution)/shard_map/ppermute | solution.py:500
  10.4 36.8 %collective-permute-start.8 = (bf16[1,8,128,256]{3,2,1,0:T(8,128)(2,1)}, bf16[1,8,128,256]{3,2,1,0:T(8,128)(2,1)}, u32[]{:S(2)}, u32[]{:S(2)}) collective-permute-start(bf16[1,8,128,256]{3,2,1,0:T(8,128)(2,1)} %get-tuple-element.137), channel_id=1, source_target_pairs={{16,0},{0,16},{17,1},{1,17},{18,2},{2,18},{19,3},{3,19},{20,4},{4,... | collective-permute-start | bytes 1572872 | tf_op jit(solution)/shard_map/ppermute | solution.py:506
  24.4 2.3 %collective-permute-start.3 = (bf16[1024,256]{1,0:T(8,128)(2,1)}, bf16[1024,256]{1,0:T(8,128)(2,1)}, u32[]{:S(2)}, u32[]{:S(2)}) collective-permute-start(bf16[1024,256]{1,0:T(8,128)(2,1)} %dynamic-slice_convert_fusion), channel_id=1, source_target_pairs={{0,1},{1,0},{2,3},{3,2},{4,5},{5,4},{6,7},{7,6},{8,9},{9,8},{10,11... | collective-permute-start | bytes 1572872 | tf_op jit(solution)/shard_map/ppermute | solution.py:405
  24.5 5.5 %copy-start.2 = (bf16[8,256,256]{2,1,0:T(8,128)(2,1)S(1)}, bf16[8,256,256]{2,1,0:T(8,128)(2,1)}, u32[]{:S(2)}) copy-start(bf16[8,256,256]{2,1,0:T(8,128)(2,1)} %param.11) | copy-start | bytes 3145732
  27.9 8.7 %collective-permute-start.4 = (bf16[512,256]{1,0:T(8,128)(2,1)S(1)}, bf16[512,256]{1,0:T(8,128)(2,1)S(1)}, u32[]{:S(2)}, u32[]{:S(2)}) collective-permute-start(bf16[512,256]{1,0:T(8,128)(2,1)S(1)} %dynamic-slice_convert_fusion.1), channel_id=1, source_target_pairs={{0,2},{1,3},{2,0},{3,1},{4,6},{5,7},{6,4},{7,5},{8,10},{9,11},{10,... | collective-permute-start | bytes 786440 | tf_op jit(solution)/shard_map/ppermute | solution.py:405
  36.7 8.4 %collective-permute-start.5 = (bf16[128,256]{1,0:T(8,128)(2,1)S(1)}, bf16[128,256]{1,0:T(8,128)(2,1)S(1)}, u32[]{:S(2)}, u32[]{:S(2)}) collective-permute-start(bf16[128,256]{1,0:T(8,128)(2,1)S(1)} %get-tuple-element.83), channel_id=1, source_target_pairs={{0,4},{1,5},{2,6},{3,7},{4,0},{5,1},{6,2},{7,3},{8,12},{9,13},{10,... | collective-permute-start | bytes 196616 | tf_op jit(solution)/shard_map/ppermute | solution.py:405
  38.6 6.7 %collective-permute-start.6 = (bf16[128,256]{1,0:T(8,128)(2,1)S(1)}, bf16[128,256]{1,0:T(8,128)(2,1)S(1)}, u32[]{:S(2)}, u32[]{:S(2)}) collective-permute-start(bf16[128,256]{1,0:T(8,128)(2,1)S(1)} %get-tuple-element.84), channel_id=1, source_target_pairs={{0,8},{1,9},{2,10},{3,11},{4,12},{5,13},{6,14},{7,15},{8,0},{9,1},... | collective-permute-start | bytes 196616 | tf_op jit(solution)/shard_map/ppermute | solution.py:405
  41.2 6.1 %collective-permute-start.7 = (bf16[128,256]{1,0:T(8,128)(2,1)S(1)}, bf16[128,256]{1,0:T(8,128)(2,1)S(1)}, u32[]{:S(2)}, u32[]{:S(2)}) collective-permute-start(bf16[128,256]{1,0:T(8,128)(2,1)S(1)} %get-tuple-element.85), channel_id=1, source_target_pairs={{0,12},{1,13},{2,14},{3,15},{4,8},{5,9},{6,10},{7,11},{8,4},{9,5},... | collective-permute-start | bytes 196616 | tf_op jit(solution)/shard_map/ppermute | solution.py:405
  48.2 15.6 %collective-permute-start.14 = (bf16[4,1,144,256]{3,2,1,0:T(8,128)(2,1)S(1)}, bf16[4,1,144,256]{3,2,1,0:T(8,128)(2,1)S(1)}, u32[]{:S(2)}, u32[]{:S(2)}) collective-permute-start(bf16[4,1,144,256]{3,2,1,0:T(8,128)(2,1)S(1)} %fusion.21), channel_id=1, source_target_pairs={{1,0},{2,1},{3,2},{4,3},{5,4},{6,5},{7,6},{8,7},{9,8},{10,9},{11,1... | collective-permute-start | bytes 884744 | tf_op jit(solution)/shard_map/ppermute | solution.py:506
  49.1 14.8 %collective-permute-start.13 = (bf16[4,1,144,256]{3,2,1,0:T(8,128)(2,1)S(1)}, bf16[4,1,144,256]{3,2,1,0:T(8,128)(2,1)S(1)}, u32[]{:S(2)}, u32[]{:S(2)}) collective-permute-start(bf16[4,1,144,256]{3,2,1,0:T(8,128)(2,1)S(1)} %fusion.17), channel_id=1, source_target_pairs={{0,1},{1,2},{2,3},{3,4},{4,5},{5,6},{6,7},{7,8},{8,9},{9,10},{10,1... | collective-permute-start | bytes 884744 | tf_op jit(solution)/shard_map/ppermute | solution.py:500
  49.3 5.5 %collective-permute-start.9 = (bf16[128,256]{1,0:T(8,128)(2,1)S(1)}, bf16[128,256]{1,0:T(8,128)(2,1)S(1)}, u32[]{:S(2)}, u32[]{:S(2)}) collective-permute-start(bf16[128,256]{1,0:T(8,128)(2,1)S(1)} %convert_element_type.80), channel_id=1, source_target_pairs={{0,16},{1,17},{2,18},{3,19},{4,20},{5,21},{6,22},{7,23},{8,24},{9,... | collective-permute-start | bytes 196616 | tf_op jit(solution)/shard_map/ppermute | solution.py:405
  54.9 8.4 %collective-permute-start.10 = (bf16[128,256]{1,0:T(8,128)(2,1)S(1)}, bf16[128,256]{1,0:T(8,128)(2,1)S(1)}, u32[]{:S(2)}, u32[]{:S(2)}) collective-permute-start(bf16[128,256]{1,0:T(8,128)(2,1)S(1)} %add_convert_fusion), channel_id=1, source_target_pairs={{0,4},{1,5},{2,6},{3,7},{4,0},{5,1},{6,2},{7,3},{8,12},{9,13},{10,... | collective-permute-start | bytes 196616 | tf_op jit(solution)/shard_map/ppermute | solution.py:405
  55.0 8.7 %collective-permute-start.11 = (bf16[128,256]{1,0:T(8,128)(2,1)S(1)}, bf16[128,256]{1,0:T(8,128)(2,1)S(1)}, u32[]{:S(2)}, u32[]{:S(2)}) collective-permute-start(bf16[128,256]{1,0:T(8,128)(2,1)S(1)} %add_convert_fusion), channel_id=1, source_target_pairs={{0,8},{1,9},{2,10},{3,11},{4,12},{5,13},{6,14},{7,15},{8,0},{9,1},... | collective-permute-start | bytes 196616 | tf_op jit(solution)/shard_map/ppermute | solution.py:405
  57.0 6.7 %collective-permute-start.12 = (bf16[128,256]{1,0:T(8,128)(2,1)S(1)}, bf16[128,256]{1,0:T(8,128)(2,1)S(1)}, u32[]{:S(2)}, u32[]{:S(2)}) collective-permute-start(bf16[128,256]{1,0:T(8,128)(2,1)S(1)} %add_convert_fusion), channel_id=1, source_target_pairs={{0,12},{1,13},{2,14},{3,15},{4,8},{5,9},{6,10},{7,11},{8,4},{9,5},... | collective-permute-start | bytes 196616 | tf_op jit(solution)/shard_map/ppermute | solution.py:405
  63.8 8.1 %collective-permute-start.15 = (bf16[512,256]{1,0:T(8,128)(2,1)S(1)}, bf16[512,256]{1,0:T(8,128)(2,1)S(1)}, u32[]{:S(2)}, u32[]{:S(2)}) collective-permute-start(bf16[512,256]{1,0:T(8,128)(2,1)S(1)} %bitcast.57), channel_id=1, source_target_pairs={{0,2},{1,3},{2,0},{3,1},{4,6},{5,7},{6,4},{7,5},{8,10},{9,11},{10,... | collective-permute-start | bytes 786440 | tf_op jit(solution)/shard_map/ppermute | solution.py:405
  70.9 4.9 %copy-start.1 = (bf16[256,256]{1,0:T(8,128)(2,1)S(1)}, bf16[256,256]{1,0:T(8,128)(2,1)}, u32[]{:S(2)}) copy-start(bf16[256,256]{1,0:T(8,128)(2,1)} %w_out.1) | copy-start | bytes 393220
  72.1 2.1 %collective-permute-start.16 = (bf16[1024,256]{1,0:T(8,128)(2,1)S(1)}, bf16[1024,256]{1,0:T(8,128)(2,1)}, u32[]{:S(2)}, u32[]{:S(2)}) collective-permute-start(bf16[1024,256]{1,0:T(8,128)(2,1)S(1)} %maximum_select_fusion.1), channel_id=1, source_target_pairs={{0,1},{1,0},{2,3},{3,2},{4,5},{5,4},{6,7},{7,6},{8,9},{9,8},{10,11... | collective-permute-start | bytes 1572872 | tf_op jit(solution)/shard_map/ppermute | solution.py:405

commit v4 on v3

--- a/solution.py
+++ b/solution.py
@@ -34,6 +34,10 @@
 CELL_ROW = 4
 POS_ROWS = 16
 VMEM = pltpu.VMEM
+
+
+def pinned(*values):
+    return [pltpu.with_memory_space_constraint(value, VMEM) for value in values]
 
 
 def horner(coefs, s):
@@ -133,7 +137,7 @@
         out_specs=[pl.BlockSpec(memory_space=pltpu.HBM), whole],
         out_shape=[
             pltpu.HBM((steps, 2, atoms, KTILE), BF16),
-            jax.ShapeDtypeStruct((steps * 2 * width, KTILE), F32),
+            VMEM((steps * 2 * width, KTILE), F32),
         ],
         scratch_shapes=[
             VMEM((steps, 2, atoms, KTILE), BF16),
@@ -146,7 +150,7 @@
             flops=24 * atoms * vectors * width, bytes_accessed=4 << 20, transcendentals=0
         ),
         name="factor",
-    )(pos, kidx, feat, wc)
+    )(*pinned(pos, kidx, feat, wc))
 
 
 def aggregate_row(slots, basis, near_feat, near_pos, own_pos, write):
@@ -320,7 +324,7 @@
         kernel,
         in_specs=[whole] * len(args),
         out_specs=whole,
-        out_shape=jax.ShapeDtypeStruct((cols, planes, rows, width), F32),
+        out_shape=VMEM((cols, planes, rows, width), F32),
         scratch_shapes=[VMEM((lines, rows, basis * width), BF16)],
         input_output_aliases=aliases,
         compiler_params=pltpu.CompilerParams(vmem_limit_bytes=16 << 20),
@@ -330,7 +334,7 @@
             transcendentals=lines * rows * 384 * (basis + 1),
         ),
         name=name,
-    )(*args)
+    )(*pinned(*args))
 
 
 def field_kernel(ph_all, weighted, w_out, base, pos, out, ph, rhs, held, in_sems, out_sems):
@@ -393,7 +397,7 @@
             flops=2 * atoms * tiles * KTILE * width, bytes_accessed=4 << 20, transcendentals=0
         ),
         name="field",
-    )(pltpu.with_memory_space_constraint(ph, pltpu.HBM), weighted, w_out, base, pos)
+    )(pltpu.with_memory_space_constraint(ph, pltpu.HBM), *pinned(weighted, w_out, base, pos))
 
 
 def my_index():
@@ -541,14 +545,13 @@
         ],
         axis=2,
     )
-    pos_before = from_before(pos, "gx", 0)
-    pos_after = from_after(pos, "gx", 0)
-
     ph, partial = factor_call(
         pos, k_index.T, feat.reshape(atoms, width), w_charge, grid_all, scale_all
     )
-    partial, before, pos_before, pos_after = tied(partial, before, pos_before, pos_after)
-    after = from_after(feat, "gx", 0)
+    partial, before, head, pos_late = tied(partial, before, feat[:1], pos)
+    after = from_after(head, "gx", 0)
+    pos_before = from_before(pos_late, "gx", 0)
+    pos_after = from_after(pos_late, "gx", 0)
 
     w_flat = w_short.reshape(basis * width, width)
     exchange = Exchange()
@@ -570,11 +573,12 @@
         return base
 
     value, _ = exchange.halve(partial, exchange.halved[0])
+    value, before, pos_before = tied(value, before, pos_before)
     value, base = exchange.halve(
         value, exchange.halved[1], plane_work(0, 1, 3, None, before, pos_before)
     )
     value, base = exchange.spread_sum(value, plane_work(0, 4, 3, base, before, pos_before))
-    value, base, after = tied(value, base, after)
+    value, base, after, pos_after = tied(value, base, after, pos_after)
     feat_planes = (before, feat, after)
     pos_planes = (pos_before, pos, pos_after)
     low = from_before(edge_rows(feat_planes, pos_planes, cols - 1), "gy", 1)

time: 84.8 us -> 77.3 us (0.912)
  local copies, waits for them, and re-layouts: 8.1 us -> 4.96 us
  Pallas kernels: 38.3 us -> 35.9 us
  waiting for transfers between devices: 14.1 us -> 12.4 us
    slice x2 -> x1, local copies, waits for them, and re-layouts: 2.88 us -> 0.01 us  [from_after(): head = lax.slice_in_dim(cells, 0, 1, axis=dim)]
    pallas_call x6, Pallas kernels: 21.7 us -> 19.3 us  [short_call(): pl.pallas_call(kernel, in_specs=[whole] * len(args), out_specs=whole, out...]
    slice x0 -> x1, local copies, waits for them, and re-layouts: none -> 2.36 us  [on_device(): partial, before, head, pos_late = tied(partial, before, feat[:1], pos)]
    ppermute x3, waiting for transfers between devices: 4.7 us -> 2.94 us  [from_before(): lax.ppermute(tail, axis, [(i, (i + 1) % count) for i in range(count)])]
    ppermute x11, starting transfers between devices: 13.9 us -> 12.2 us  [swap(): return lax.ppermute(value, AXES, [(i, i ^ mask) for i in range(count)])]
    ppermute x3, starting transfers between devices: 0.93 us -> 2.34 us  [from_after(): lax.ppermute(head, axis, [((i + 1) % count, i) for i in range(count)])]
    reshape x2, local copies, waits for them, and re-layouts: 1.35 us -> 0.37 us  [on_device(): jnp.transpose(fractions, (0, 1, 4, 2, 3)).reshape(planes, cols, 3, rows)]
    slice x3 -> x2, local copies, waits for them, and re-layouts: 1.87 us -> 0.91 us  [edge_rows(): parts.append(jnp.concatenate([f[:, y:y + 1], q], axis=2))]
  transfers between devices with their start and end apart: 17 -> 17, of which waited for: 8 -> 7; matrix products, arithmetic and copies ran while one was open for 7% -> 3% of each run, Pallas kernels for 36% -> 36%
where the time goes in v4:
time: 77.3 us; the launch traced here: 76.9 us
  Pallas kernels  35.9 us (46%)
  starting transfers between devices  19.8 us (26%)
  waiting for transfers between devices  12.4 us (16%)
  local copies, waits for them, and re-layouts  4.96 us (6%)
  other arithmetic  3.26 us (4%)
    pallas_call x6, Pallas kernels, short_call(): pl.pallas_call(kernel, in_specs=[whole] * len(args), out_specs=whole, out...  19.3 us
    ppermute x11, starting transfers between devices, swap(): return lax.ppermute(value, AXES, [(i, i ^ mask) for i in range(count)])  12.2 us
    ppermute x11, waiting for transfers between devices, swap(): return lax.ppermute(value, AXES, [(i, i ^ mask) for i in range(count)])  9.47 us
    pallas_call x1, Pallas kernels, factor_call(): pl.pallas_call(functools.partial(factor_kernel, grid_all, scale_all), in_...  8.33 us
    pallas_call x1, Pallas kernels, field_call(): pl.pallas_call(field_kernel, in_specs=[pl.BlockSpec(memory_space=pltpu.HB...  8.33 us
    ppermute x3, starting transfers between devices, from_before(): lax.ppermute(tail, axis, [(i, (i + 1) % count) for i in range(count)])  5.24 us
    ppermute x3, waiting for transfers between devices, from_before(): lax.ppermute(tail, axis, [(i, (i + 1) % count) for i in range(count)])  2.94 us
    slice x1, local copies, waits for them, and re-layouts, on_device(): partial, before, head, pos_late = tied(partial, before, feat[:1], pos)  2.36 us
  transfers between devices with their start and end apart: 17, of which 7 were waited for; matrix products, arithmetic and copies ran while one was open for 3% of the time, Pallas kernels for 36%

profile of v4, /device:TPU:0, one launch (start us, length us, event | category | flops | bytes accessed | tf_op | source)
XLA Modules:
  0.0 76.9 jit_solution(14210777873513892412)
XLA Ops:
  0.0 2.4 %slice_bitcast_fusion = (bf16[1,8,128,256]{3,2,1,0:T(8,128)(2,1)}, bf16[1,8,128,256]{3,2,1,0:T(8,128)(2,1)}) fusion(bf16[2,8,16,8,256]{4,3,2,1,0:T(8,128)(2,1)} %param.7), kind=kLoop, calls=%fused_computation.19 | loop fusion | bytes 2097152 | tf_op jit(solution)/shard_map/slice | solution.py:551
  2.4 3.0 %collective-permute-start = (bf16[1,8,128,256]{3,2,1,0:T(8,128)(2,1)}, bf16[1,8,128,256]{3,2,1,0:T(8,128)(2,1)}, u32[]{:S(2)}, u32[]{:S(2)}) collective-permute-start(bf16[1,8,128,256]{3,2,1,0:T(8,128)(2,1)} %get-tuple-element.146), channel_id=1, source_target_pairs={{0,16},{16,0},{1,17},{17,1},{2,18},{18,2},{3,19},{19,3},{4,20},{20... | collective-permute-start | bytes 1572872 | tf_op jit(solution)/shard_map/ppermute | solution.py:504
  6.3 8.3 %factor.1 = (bf16[4,2,2048,256]{3,2,1,0:T(8,128)(2,1)}, f32[2048,256]{1,0:T(8,128)S(1)}) custom-call(bf16[2,8,16,128]{3,2,1,0:T(8,128)(2,1)S(1)} %maximum_maximum_fusion.pos, s32[3,1024]{1,0:T(4,128)S(1)} %bitcast.53, bf16[2048,256]{1,0:T(8,128)(2,1)S(1)} %bitcast.39, bf16[256,256]{1,0:T(8,128)(2,1)S(1)} %copy-done.3), custom_call_target="tpu_custom_call" | custom-call | flops 12884901888 | bytes 4194304 | tf_op jit(solution)/shard_map/factor/pallas_call | solution.py:134
  14.6 2.9 %collective-permute-done.side_feat.before = bf16[1,8,128,256]{3,2,1,0:T(8,128)(2,1)} collective-permute-done((bf16[1,8,128,256]{3,2,1,0:T(8,128)(2,1)}, bf16[1,8,128,256]{3,2,1,0:T(8,128)(2,1)}, u32[]{:S(2)}, u32[]{:S(2)}) %collective-permute-start) | collective-permute-done | bytes 524320 | tf_op jit(solution)/shard_map/ppermute | solution.py:504
  18.5 1.8 %collective-permute-start.2 = (bf16[1,8,16,128]{3,2,1,0:T(8,128)(2,1)S(1)}, bf16[1,8,16,128]{3,2,1,0:T(8,128)(2,1)S(1)}, u32[]{:S(2)}, u32[]{:S(2)}) collective-permute-start(bf16[1,8,16,128]{3,2,1,0:T(8,128)(2,1)S(1)} %get-tuple-element.157), channel_id=1, source_target_pairs={{0,16},{16,0},{1,17},{17,1},{2,18},{18,2},{3,19},{19,3},{4,20},{20... | collective-permute-start | bytes 98312 | tf_op jit(solution)/shard_map/ppermute | solution.py:504
  20.5 1.7 %collective-permute-start.7 = (bf16[1,8,128,256]{3,2,1,0:T(8,128)(2,1)}, bf16[1,8,128,256]{3,2,1,0:T(8,128)(2,1)S(1)}, u32[]{:S(2)}, u32[]{:S(2)}) collective-permute-start(bf16[1,8,128,256]{3,2,1,0:T(8,128)(2,1)} %get-tuple-element.103), channel_id=1, source_target_pairs={{16,0},{0,16},{17,1},{1,17},{18,2},{2,18},{19,3},{3,19},{20,4},{4,... | collective-permute-start | bytes 1572872 | tf_op jit(solution)/shard_map/ppermute | solution.py:510
  23.5 1.6 %collective-permute-start.3 = (bf16[512,256]{1,0:T(8,128)(2,1)S(1)}, bf16[512,256]{1,0:T(8,128)(2,1)S(1)}, u32[]{:S(2)}, u32[]{:S(2)}) collective-permute-start(bf16[512,256]{1,0:T(8,128)(2,1)S(1)} %dynamic-slice_convert_fusion.1), channel_id=1, source_target_pairs={{0,2},{1,3},{2,0},{3,1},{4,6},{5,7},{6,4},{7,5},{8,10},{9,11},{10,... | collective-permute-start | bytes 786440 | tf_op jit(solution)/shard_map/ppermute | solution.py:409
  25.1 4.0 %plane.4.rest_0_ = f32[8,2,128,256]{3,2,1,0:T(8,128)S(1)} custom-call(bf16[2,8,128,256]{3,2,1,0:T(8,128)(2,1)S(1)} %bitcast.41, bf16[2,8,16,128]{3,2,1,0:T(8,128)(2,1)S(1)} %maximum_maximum_fusion.pos, bf16[1,8,128,256]{3,2,1,0:T(8,128)(2,1)} %collective-permute-done.side_feat.before, bf16[1,8,16,128]{3,2,1,0:T(8,128)(2,1)S(1)} %collective-permute-done.2.side_pos.pos_before, ...), custom_call_target="tpu_custom_call" | custom-call | flops 4026531840 | bytes 4194304 | tf_op jit(solution)/shard_map/plane/pallas_call | solution.py:323
  29.1 2.4 %collective-permute-done.3 = bf16[512,256]{1,0:T(8,128)(2,1)S(1)} collective-permute-done((bf16[512,256]{1,0:T(8,128)(2,1)S(1)}, bf16[512,256]{1,0:T(8,128)(2,1)S(1)}, u32[]{:S(2)}, u32[]{:S(2)}) %collective-permute-start.3) | collective-permute-done | bytes 262176 | tf_op jit(solution)/shard_map/ppermute | solution.py:409
  31.5 1.6 %collective-permute-start.4 = (bf16[128,256]{1,0:T(8,128)(2,1)S(1)}, bf16[128,256]{1,0:T(8,128)(2,1)S(1)}, u32[]{:S(2)}, u32[]{:S(2)}) collective-permute-start(bf16[128,256]{1,0:T(8,128)(2,1)S(1)} %get-tuple-element.90), channel_id=1, source_target_pairs={{0,4},{1,5},{2,6},{3,7},{4,0},{5,1},{6,2},{7,3},{8,12},{9,13},{10,... | collective-permute-start | bytes 196616 | tf_op jit(solution)/shard_map/ppermute | solution.py:409
  33.2 2.6 %collective-permute-start.5 = (bf16[128,256]{1,0:T(8,128)(2,1)S(1)}, bf16[128,256]{1,0:T(8,128)(2,1)S(1)}, u32[]{:S(2)}, u32[]{:S(2)}) collective-permute-start(bf16[128,256]{1,0:T(8,128)(2,1)S(1)} %get-tuple-element.91), channel_id=1, source_target_pairs={{0,8},{1,9},{2,10},{3,11},{4,12},{5,13},{6,14},{7,15},{8,0},{9,1},... | collective-permute-start | bytes 196616 | tf_op jit(solution)/shard_map/ppermute | solution.py:409
  36.0 4.0 %plane.5.rest_0_ = f32[8,2,128,256]{3,2,1,0:T(8,128)S(1)} custom-call(bf16[2,8,128,256]{3,2,1,0:T(8,128)(2,1)S(1)} %bitcast.42, bf16[2,8,16,128]{3,2,1,0:T(8,128)(2,1)S(1)} %maximum_maximum_fusion.pos, bf16[1,8,128,256]{3,2,1,0:T(8,128)(2,1)} %collective-permute-done.side_feat.before, ...), custom_call_target="tpu_custom_call", output_to_operand_aliasing={{}: (5, {})} | custom-call | flops 4026531840 | bytes 4194304 | tf_op jit(solution)/shard_map/plane/pallas_call | solution.py:323
  40.0 1.9 %collective-permute-done.6 = bf16[128,256]{1,0:T(8,128)(2,1)S(1)} collective-permute-done((bf16[128,256]{1,0:T(8,128)(2,1)S(1)}, bf16[128,256]{1,0:T(8,128)(2,1)S(1)}, u32[]{:S(2)}, u32[]{:S(2)}) %collective-permute-start.6) | collective-permute-done | bytes 65568 | tf_op jit(solution)/shard_map/ppermute | solution.py:409
  44.3 2.9 %plane.6.rest_0_ = f32[8,2,128,256]{3,2,1,0:T(8,128)S(1)} custom-call(bf16[2,8,128,256]{3,2,1,0:T(8,128)(2,1)S(1)} %bitcast.43, bf16[2,8,16,128]{3,2,1,0:T(8,128)(2,1)S(1)} %maximum_maximum_fusion.pos, bf16[1,8,128,256]{3,2,1,0:T(8,128)(2,1)S(1)} %collective-permute-done.7.side_feat.after, ...), custom_call_target="tpu_custom_call", output_to_operand_aliasing={{}: (5, {})} | custom-call | flops 4026531840 | bytes 4194304 | tf_op jit(solution)/shard_map/plane/pallas_call | solution.py:323
  47.2 1.3 %collective-permute-done.9 = bf16[128,256]{1,0:T(8,128)(2,1)S(1)} collective-permute-done((bf16[128,256]{1,0:T(8,128)(2,1)S(1)}, bf16[128,256]{1,0:T(8,128)(2,1)S(1)}, u32[]{:S(2)}, u32[]{:S(2)}) %collective-permute-start.9) | collective-permute-done | bytes 65568 | tf_op jit(solution)/shard_map/ppermute | solution.py:409
  48.6 2.3 %collective-permute-start.11 = (bf16[128,256]{1,0:T(8,128)(2,1)S(1)}, bf16[128,256]{1,0:T(8,128)(2,1)S(1)}, u32[]{:S(2)}, u32[]{:S(2)}) collective-permute-start(bf16[128,256]{1,0:T(8,128)(2,1)S(1)} %add_convert_fusion), channel_id=1, source_target_pairs={{0,8},{1,9},{2,10},{3,11},{4,12},{5,13},{6,14},{7,15},{8,0},{9,1},... | collective-permute-start | bytes 196616 | tf_op jit(solution)/shard_map/ppermute | solution.py:409
  50.9 2.1 %collective-permute-start.12 = (bf16[128,256]{1,0:T(8,128)(2,1)S(1)}, bf16[128,256]{1,0:T(8,128)(2,1)S(1)}, u32[]{:S(2)}, u32[]{:S(2)}) collective-permute-start(bf16[128,256]{1,0:T(8,128)(2,1)S(1)} %add_convert_fusion), channel_id=1, source_target_pairs={{0,12},{1,13},{2,14},{3,15},{4,8},{5,9},{6,10},{7,11},{8,4},{9,5},... | collective-permute-start | bytes 196616 | tf_op jit(solution)/shard_map/ppermute | solution.py:409
  53.0 2.9 %plane.7.rest_0_ = f32[8,2,128,256]{3,2,1,0:T(8,128)S(1)} custom-call(bf16[2,8,128,256]{3,2,1,0:T(8,128)(2,1)S(1)} %bitcast.44, bf16[2,8,16,128]{3,2,1,0:T(8,128)(2,1)S(1)} %maximum_maximum_fusion.pos, bf16[1,8,128,256]{3,2,1,0:T(8,128)(2,1)S(1)} %collective-permute-done.7.side_feat.after, ...), custom_call_target="tpu_custom_call", output_to_operand_aliasing={{}: (5, {})} | custom-call | flops 4026531840 | bytes 4194304 | tf_op jit(solution)/shard_map/plane/pallas_call | solution.py:323
  55.9 1.4 %collective-permute-done.11 = bf16[128,256]{1,0:T(8,128)(2,1)S(1)} collective-permute-done((bf16[128,256]{1,0:T(8,128)(2,1)S(1)}, bf16[128,256]{1,0:T(8,128)(2,1)S(1)}, u32[]{:S(2)}, u32[]{:S(2)}) %collective-permute-start.11) | collective-permute-done | bytes 65568 | tf_op jit(solution)/shard_map/ppermute | solution.py:409
  58.5 2.7 %low.1.rest_0_ = f32[8,2,128,256]{3,2,1,0:T(8,128)S(1)} custom-call(bf16[2,8,128,256]{3,2,1,0:T(8,128)(2,1)S(1)} %bitcast.45, bf16[2,8,16,128]{3,2,1,0:T(8,128)(2,1)S(1)} %maximum_maximum_fusion.pos, bf16[1,8,128,256]{3,2,1,0:T(8,128)(2,1)} %collective-permute-done.side_feat.before, ...), custom_call_target="tpu_custom_call", output_to_operand_aliasing={{}: (8, {})} | custom-call | flops 2684354560 | bytes 4194304 | tf_op jit(solution)/shard_map/low/pallas_call | solution.py:323
  61.3 2.7 %high.1.base = f32[8,2,128,256]{3,2,1,0:T(8,128)S(1)} custom-call(bf16[2,8,128,256]{3,2,1,0:T(8,128)(2,1)S(1)} %bitcast.46, bf16[2,8,16,128]{3,2,1,0:T(8,128)(2,1)S(1)} %maximum_maximum_fusion.pos, bf16[1,8,128,256]{3,2,1,0:T(8,128)(2,1)} %collective-permute-done.side_feat.before, ...), custom_call_target="tpu_custom_call", output_to_operand_aliasing={{}: (8, {})} | custom-call | flops 2684354560 | bytes 4194304 | tf_op jit(solution)/shard_map/high/pallas_call | solution.py:323
  64.9 2.0 %collective-permute-done.16 = bf16[1024,256]{1,0:T(8,128)(2,1)} collective-permute-done((bf16[1024,256]{1,0:T(8,128)(2,1)S(1)}, bf16[1024,256]{1,0:T(8,128)(2,1)}, u32[]{:S(2)}, u32[]{:S(2)}) %collective-permute-start.16) | collective-permute-done | bytes 524320 | tf_op jit(solution)/shard_map/ppermute | solution.py:409
  66.9 1.5 %maximum_select_fusion = bf16[2048,256]{1,0:T(8,128)(2,1)S(1)} fusion(bf16[1024,256]{1,0:T(8,128)(2,1)} %collective-permute-done.16, bf16[1024,256]{1,0:T(8,128)(2,1)S(1)} %maximum_select_fusion.1, pred[]{:T(512)S(6)} %eq.21), kind=kLoop, calls=%fused_computation | loop fusion | flops 4718592 | bytes 2097153 | tf_op jit(solution)/shard_map/jit(_where)/select_n | solution.py:476
  68.4 8.3 %field.1 = bf16[2048,256]{1,0:T(8,128)(2,1)} custom-call(bf16[4,2,2048,256]{3,2,1,0:T(8,128)(2,1)} %get-tuple-element.74.ph_all, bf16[8,256,256]{2,1,0:T(8,128)(2,1)S(1)} %bitcast.38, bf16[256,256]{1,0:T(8,128)(2,1)S(1)} %copy-done.1, f32[8,2,128,256]{3,2,1,0:T(8,128)S(1)} %high.1.base, bf16[2,8,16,128]{3,2,1,0:T(8,128)(2,1)S(1)} %maximum_maximum_fusion.pos), custom_call_target="tpu_custom_call" | custom-call | flops 2147483648 | bytes 4194304 | tf_op jit(solution)/shard_map/field/pallas_call | solution.py:383
  (64 shorter events, 8.0 us)
Async XLA Ops:
  0.0 6.2 %copy-start = (bf16[2,8,16,8,256]{4,3,2,1,0:T(8,128)(2,1)S(1)}, bf16[2,8,16,8,256]{4,3,2,1,0:T(8,128)(2,1)}, u32[]{:S(2)}) copy-start(bf16[2,8,16,8,256]{4,3,2,1,0:T(8,128)(2,1)} %param.7) | copy-start | bytes 3145732
  0.0 5.3 %copy-start.5 = (bf16[2,8,16,8,3]{2,3,4,1,0:T(8,128)(2,1)S(1)}, bf16[2,8,16,8,3]{2,3,4,1,0:T(8,128)(2,1)}, u32[]{:S(2)}) copy-start(bf16[2,8,16,8,3]{2,3,4,1,0:T(8,128)(2,1)} %param.8) | copy-start | bytes 36868
  0.0 5.7 %copy-start.6 = (s32[2,8,16]{2,1,0:T(8,128)S(1)}, s32[2,8,16]{2,1,0:T(8,128)}, u32[]{:S(2)}) copy-start(s32[2,8,16]{2,1,0:T(8,128)} %param.9) | copy-start | bytes 3076
  0.0 6.2 %copy-start.4 = (s32[1024,3]{0,1:T(4,128)S(1)}, s32[1024,3]{0,1:T(4,128)}, u32[]{:S(2)}) copy-start(s32[1024,3]{0,1:T(4,128)} %param.10) | copy-start | bytes 36868
  0.0 6.2 %copy-start.3 = (bf16[256,256]{1,0:T(8,128)(2,1)S(1)}, bf16[256,256]{1,0:T(8,128)(2,1)}, u32[]{:S(2)}) copy-start(bf16[256,256]{1,0:T(8,128)(2,1)} %wc.1) | copy-start | bytes 393220
  2.4 15.2 %collective-permute-start = (bf16[1,8,128,256]{3,2,1,0:T(8,128)(2,1)}, bf16[1,8,128,256]{3,2,1,0:T(8,128)(2,1)}, u32[]{:S(2)}, u32[]{:S(2)}) collective-permute-start(bf16[1,8,128,256]{3,2,1,0:T(8,128)(2,1)} %get-tuple-element.146), channel_id=1, source_target_pairs={{0,16},{16,0},{1,17},{17,1},{2,18},{18,2},{3,19},{19,3},{4,20},{20... | collective-permute-start | bytes 1572872 | tf_op jit(solution)/shard_map/ppermute | solution.py:504
  18.4 3.9 %collective-permute-start.1 = (bf16[1024,256]{1,0:T(8,128)(2,1)}, bf16[1024,256]{1,0:T(8,128)(2,1)}, u32[]{:S(2)}, u32[]{:S(2)}) collective-permute-start(bf16[1024,256]{1,0:T(8,128)(2,1)} %dynamic-slice_convert_fusion), channel_id=1, source_target_pairs={{0,1},{1,0},{2,3},{3,2},{4,5},{5,4},{6,7},{7,6},{8,9},{9,8},{10,11... | collective-permute-start | bytes 1572872 | tf_op jit(solution)/shard_map/ppermute | solution.py:409
  18.4 6.7 %copy-start.2 = (bf16[8,256,256]{2,1,0:T(8,128)(2,1)S(1)}, bf16[8,256,256]{2,1,0:T(8,128)(2,1)}, u32[]{:S(2)}) copy-start(bf16[8,256,256]{2,1,0:T(8,128)(2,1)} %param.11) | copy-start | bytes 3145732
  18.5 5.0 %collective-permute-start.2 = (bf16[1,8,16,128]{3,2,1,0:T(8,128)(2,1)S(1)}, bf16[1,8,16,128]{3,2,1,0:T(8,128)(2,1)S(1)}, u32[]{:S(2)}, u32[]{:S(2)}) collective-permute-start(bf16[1,8,16,128]{3,2,1,0:T(8,128)(2,1)S(1)} %get-tuple-element.157), channel_id=1, source_target_pairs={{0,16},{16,0},{1,17},{17,1},{2,18},{18,2},{3,19},{19,3},{4,20},{20... | collective-permute-start | bytes 98312 | tf_op jit(solution)/shard_map/ppermute | solution.py:504
  20.3 21.6 %collective-permute-start.8 = (bf16[1,8,16,128]{3,2,1,0:T(8,128)(2,1)S(1)}, bf16[1,8,16,128]{3,2,1,0:T(8,128)(2,1)S(1)}, u32[]{:S(2)}, u32[]{:S(2)}) collective-permute-start(bf16[1,8,16,128]{3,2,1,0:T(8,128)(2,1)S(1)} %get-tuple-element.156), channel_id=1, source_target_pairs={{16,0},{0,16},{17,1},{1,17},{18,2},{2,18},{19,3},{3,19},{20,4},{4,... | collective-permute-start | bytes 98312 | tf_op jit(solution)/shard_map/ppermute | solution.py:510
  20.5 21.3 %collective-permute-start.7 = (bf16[1,8,128,256]{3,2,1,0:T(8,128)(2,1)}, bf16[1,8,128,256]{3,2,1,0:T(8,128)(2,1)S(1)}, u32[]{:S(2)}, u32[]{:S(2)}) collective-permute-start(bf16[1,8,128,256]{3,2,1,0:T(8,128)(2,1)} %get-tuple-element.103), channel_id=1, source_target_pairs={{16,0},{0,16},{17,1},{1,17},{18,2},{2,18},{19,3},{3,19},{20,4},{4,... | collective-permute-start | bytes 1572872 | tf_op jit(solution)/shard_map/ppermute | solution.py:510
  23.5 7.9 %collective-permute-start.3 = (bf16[512,256]{1,0:T(8,128)(2,1)S(1)}, bf16[512,256]{1,0:T(8,128)(2,1)S(1)}, u32[]{:S(2)}, u32[]{:S(2)}) collective-permute-start(bf16[512,256]{1,0:T(8,128)(2,1)S(1)} %dynamic-slice_convert_fusion.1), channel_id=1, source_target_pairs={{0,2},{1,3},{2,0},{3,1},{4,6},{5,7},{6,4},{7,5},{8,10},{9,11},{10,... | collective-permute-start | bytes 786440 | tf_op jit(solution)/shard_map/ppermute | solution.py:409
  31.5 8.4 %collective-permute-start.4 = (bf16[128,256]{1,0:T(8,128)(2,1)S(1)}, bf16[128,256]{1,0:T(8,128)(2,1)S(1)}, u32[]{:S(2)}, u32[]{:S(2)}) collective-permute-start(bf16[128,256]{1,0:T(8,128)(2,1)S(1)} %get-tuple-element.90), channel_id=1, source_target_pairs={{0,4},{1,5},{2,6},{3,7},{4,0},{5,1},{6,2},{7,3},{8,12},{9,13},{10,... | collective-permute-start | bytes 196616 | tf_op jit(solution)/shard_map/ppermute | solution.py:409
  33.2 6.8 %collective-permute-start.5 = (bf16[128,256]{1,0:T(8,128)(2,1)S(1)}, bf16[128,256]{1,0:T(8,128)(2,1)S(1)}, u32[]{:S(2)}, u32[]{:S(2)}) collective-permute-start(bf16[128,256]{1,0:T(8,128)(2,1)S(1)} %get-tuple-element.91), channel_id=1, source_target_pairs={{0,8},{1,9},{2,10},{3,11},{4,12},{5,13},{6,14},{7,15},{8,0},{9,1},... | collective-permute-start | bytes 196616 | tf_op jit(solution)/shard_map/ppermute | solution.py:409
  35.8 6.1 %collective-permute-start.6 = (bf16[128,256]{1,0:T(8,128)(2,1)S(1)}, bf16[128,256]{1,0:T(8,128)(2,1)S(1)}, u32[]{:S(2)}, u32[]{:S(2)}) collective-permute-start(bf16[128,256]{1,0:T(8,128)(2,1)S(1)} %get-tuple-element.92), channel_id=1, source_target_pairs={{0,12},{1,13},{2,14},{3,15},{4,8},{5,9},{6,10},{7,11},{8,4},{9,5},... | collective-permute-start | bytes 196616 | tf_op jit(solution)/shard_map/ppermute | solution.py:409
  42.8 14.7 %collective-permute-start.14 = (bf16[4,1,144,256]{3,2,1,0:T(8,128)(2,1)S(1)}, bf16[4,1,144,256]{3,2,1,0:T(8,128)(2,1)S(1)}, u32[]{:S(2)}, u32[]{:S(2)}) collective-permute-start(bf16[4,1,144,256]{3,2,1,0:T(8,128)(2,1)S(1)} %fusion.21), channel_id=1, source_target_pairs={{1,0},{2,1},{3,2},{4,3},{5,4},{6,5},{7,6},{8,7},{9,8},{10,9},{11,1... | collective-permute-start | bytes 884744 | tf_op jit(solution)/shard_map/ppermute | solution.py:510
  43.2 14.3 %collective-permute-start.13 = (bf16[4,1,144,256]{3,2,1,0:T(8,128)(2,1)S(1)}, bf16[4,1,144,256]{3,2,1,0:T(8,128)(2,1)S(1)}, u32[]{:S(2)}, u32[]{:S(2)}) collective-permute-start(bf16[4,1,144,256]{3,2,1,0:T(8,128)(2,1)S(1)} %fusion.17), channel_id=1, source_target_pairs={{0,1},{1,2},{2,3},{3,4},{4,5},{5,6},{6,7},{7,8},{8,9},{9,10},{10,1... | collective-permute-start | bytes 884744 | tf_op jit(solution)/shard_map/ppermute | solution.py:504
  43.7 4.9 %collective-permute-start.9 = (bf16[128,256]{1,0:T(8,128)(2,1)S(1)}, bf16[128,256]{1,0:T(8,128)(2,1)S(1)}, u32[]{:S(2)}, u32[]{:S(2)}) collective-permute-start(bf16[128,256]{1,0:T(8,128)(2,1)S(1)} %convert_element_type.80), channel_id=1, source_target_pairs={{0,16},{1,17},{2,18},{3,19},{4,20},{5,21},{6,22},{7,23},{8,24},{9,... | collective-permute-start | bytes 196616 | tf_op jit(solution)/shard_map/ppermute | solution.py:409
  48.5 7.4 %collective-permute-start.10 = (bf16[128,256]{1,0:T(8,128)(2,1)S(1)}, bf16[128,256]{1,0:T(8,128)(2,1)S(1)}, u32[]{:S(2)}, u32[]{:S(2)}) collective-permute-start(bf16[128,256]{1,0:T(8,128)(2,1)S(1)} %add_convert_fusion), channel_id=1, source_target_pairs={{0,4},{1,5},{2,6},{3,7},{4,0},{5,1},{6,2},{7,3},{8,12},{9,13},{10,... | collective-permute-start | bytes 196616 | tf_op jit(solution)/shard_map/ppermute | solution.py:409
  48.6 8.7 %collective-permute-start.11 = (bf16[128,256]{1,0:T(8,128)(2,1)S(1)}, bf16[128,256]{1,0:T(8,128)(2,1)S(1)}, u32[]{:S(2)}, u32[]{:S(2)}) collective-permute-start(bf16[128,256]{1,0:T(8,128)(2,1)S(1)} %add_convert_fusion), channel_id=1, source_target_pairs={{0,8},{1,9},{2,10},{3,11},{4,12},{5,13},{6,14},{7,15},{8,0},{9,1},... | collective-permute-start | bytes 196616 | tf_op jit(solution)/shard_map/ppermute | solution.py:409
  50.9 6.4 %collective-permute-start.12 = (bf16[128,256]{1,0:T(8,128)(2,1)S(1)}, bf16[128,256]{1,0:T(8,128)(2,1)S(1)}, u32[]{:S(2)}, u32[]{:S(2)}) collective-permute-start(bf16[128,256]{1,0:T(8,128)(2,1)S(1)} %add_convert_fusion), channel_id=1, source_target_pairs={{0,12},{1,13},{2,14},{3,15},{4,8},{5,9},{6,10},{7,11},{8,4},{9,5},... | collective-permute-start | bytes 196616 | tf_op jit(solution)/shard_map/ppermute | solution.py:409
  57.5 7.0 %collective-permute-start.15 = (bf16[512,256]{1,0:T(8,128)(2,1)S(1)}, bf16[512,256]{1,0:T(8,128)(2,1)S(1)}, u32[]{:S(2)}, u32[]{:S(2)}) collective-permute-start(bf16[512,256]{1,0:T(8,128)(2,1)S(1)} %bitcast.57), channel_id=1, source_target_pairs={{0,2},{1,3},{2,0},{3,1},{4,6},{5,7},{6,4},{7,5},{8,10},{9,11},{10,... | collective-permute-start | bytes 786440 | tf_op jit(solution)/shard_map/ppermute | solution.py:409
  64.0 4.4 %copy-start.1 = (bf16[256,256]{1,0:T(8,128)(2,1)S(1)}, bf16[256,256]{1,0:T(8,128)(2,1)}, u32[]{:S(2)}) copy-start(bf16[256,256]{1,0:T(8,128)(2,1)} %w_out.1) | copy-start | bytes 393220
  64.8 2.1 %collective-permute-start.16 = (bf16[1024,256]{1,0:T(8,128)(2,1)S(1)}, bf16[1024,256]{1,0:T(8,128)(2,1)}, u32[]{:S(2)}, u32[]{:S(2)}) collective-permute-start(bf16[1024,256]{1,0:T(8,128)(2,1)S(1)} %maximum_select_fusion.1), channel_id=1, source_target_pairs={{0,1},{1,0},{2,3},{3,2},{4,5},{5,4},{6,7},{7,6},{8,9},{9,8},{10,11... | collective-permute-start | bytes 1572872 | tf_op jit(solution)/shard_map/ppermute | solution.py:409

commit v5 on v4

--- a/solution.py
+++ b/solution.py
@@ -47,9 +47,8 @@
     return value
 
 
-def factor_kernel(grid_all, scale_all, pos, kidx, feat, wc, ph_out, fac, ph, charges, where_at, sems):
+def factor_kernel(grid_all, scale_all, pos, kidx, feat, wc, ph_out, fac, head_out, ph, head, charges, where_at, sems):
     planes, cols, _, rows = pos.shape
-    copies = []
     steps = ph.shape[0]
     atoms, width = feat.shape
 
@@ -79,6 +78,12 @@
             tile = jnp.where(sub == CELL_ROW + 1, y0 + float(y), tile)
             tile = jnp.where(sub == CELL_ROW + 2, depth, tile)
             where_at[j : j + rows, :] = tile.T.astype(BF16)
+    for y in range(cols):
+        head[0, y, 0:rows, :] = feat[y * rows : (y + 1) * rows, :]
+        head[0, y, rows : rows + POS_ROWS, 0:rows] = pos[0, y]
+        head[0, y, rows : rows + POS_ROWS, rows:width] = pos[0, y]
+    copies = [pltpu.make_async_copy(head, head_out, sems.at[steps])]
+    copies[0].start()
     turned = wc[...].T
 
     size = 2 * rows
@@ -128,22 +133,28 @@
 
 def factor_call(pos, kidx, feat, wc, grid_all, scale_all):
     atoms, width = feat.shape
+    _, cols, _, rows = pos.shape
     vectors = kidx.shape[1]
     steps = vectors // KTILE
     whole = pl.BlockSpec(memory_space=VMEM)
+    in_hbm = pl.BlockSpec(memory_space=pltpu.HBM)
+    phases = (steps, 2, atoms, KTILE)
+    head = (1, cols, rows + POS_ROWS, width)
     return pl.pallas_call(
         functools.partial(factor_kernel, grid_all, scale_all),
         in_specs=[whole] * 4,
-        out_specs=[pl.BlockSpec(memory_space=pltpu.HBM), whole],
+        out_specs=[in_hbm, whole, in_hbm],
         out_shape=[
-            pltpu.HBM((steps, 2, atoms, KTILE), BF16),
+            pltpu.HBM(phases, BF16),
             VMEM((steps * 2 * width, KTILE), F32),
+            pltpu.HBM(head, BF16),
         ],
         scratch_shapes=[
-            VMEM((steps, 2, atoms, KTILE), BF16),
+            VMEM(phases, BF16),
+            VMEM(head, BF16),
             VMEM((width, atoms), BF16),
             VMEM((atoms, POS_ROWS), BF16),
-            pltpu.SemaphoreType.DMA((steps,)),
+            pltpu.SemaphoreType.DMA((steps + 1,)),
         ],
         compiler_params=pltpu.CompilerParams(vmem_limit_bytes=24 << 20),
         cost_estimate=pl.CostEstimate(
@@ -244,24 +255,34 @@
     return jnp.concatenate([value[128 - slots :], value[: 128 - slots]], axis=0)
 
 
-def plane_kernel(slots, basis, plane, first, count, feat, pos, side_feat, side_pos, w, *rest):
-    out, agg = rest[-2:]
+def plane_kernel(slots, basis, plane, first, count, fetch, feat, pos, w, *rest):
     planes, _, rows, width = feat.shape
-
-    def pick(ref, side, dx):
-        x = plane + dx
-        return (ref, x) if 0 <= x < planes else (side, 0)
+    sides = list(rest[: 2 if plane == 0 else 1])
+    if fetch:
+        out, held, agg, sem = rest[-4:]
+        copy = pltpu.make_async_copy(sides[0], held, sem)
+        copy.start()
+        copy.wait()
+        sides[0] = held
+    else:
+        out, agg = rest[-2:]
 
     def body(i, carry):
         y = first + i
 
         def near_feat(dx, dy, start, size):
-            ref, x = pick(feat, side_feat, dx)
-            return ref[x, y + dy, start : start + size, :]
+            x = plane + dx
+            if 0 <= x < planes:
+                return feat[x, y + dy, start : start + size, :]
+            return sides[0][0, y + dy, start : start + size, :]
 
         def near_pos(dx, dy):
-            ref, x = pick(pos, side_pos, dx)
-            return ref[x, y + dy]
+            x = plane + dx
+            if 0 <= x < planes:
+                return pos[x, y + dy]
+            if x < 0:
+                return sides[1][0, y + dy]
+            return sides[0][0, y + dy, rows : rows + POS_ROWS, 0:rows]
 
         def write(start, size, b, value):
             agg[i, start : start + size, width * b : width * (b + 1)] = value
@@ -279,7 +300,7 @@
 
 
 def edge_kernel(
-    slots, basis, y, halo_dy, feat, pos, before, pos_before, after, pos_after, halo, w, *rest
+    slots, basis, y, halo_dy, feat, pos, w, before, pos_before, after, halo, *rest
 ):
     out, agg = rest[-2:]
     planes, _, rows, width = feat.shape
@@ -299,7 +320,9 @@
                 return halo[x + 1, 0, rows : rows + POS_ROWS, 0:128]
             if 0 <= x < planes:
                 return pos[x, y + dy]
-            return (pos_before if x < 0 else pos_after)[0, y + dy]
+            if x < 0:
+                return pos_before[0, y + dy]
+            return after[0, y + dy, rows : rows + POS_ROWS, 0:rows]
 
         def write(start, size, b, value):
             agg[plane, start : start + size, width * b : width * (b + 1)] = value
@@ -313,19 +336,31 @@
         out[y, plane] = feat[plane, y].astype(F32) + turn(value[plane], slots)
 
 
-def short_call(kernel, name, lines, basis, args, base):
+def short_call(kernel, name, lines, basis, args, base, fetch=None):
     planes, cols, rows, width = args[0].shape
     whole = pl.BlockSpec(memory_space=VMEM)
+    in_specs = [whole] * len(args)
+    operands = pinned(*args)
+    out_specs = [whole]
+    out_shape = [VMEM((cols, planes, rows, width), F32)]
+    scratch = [VMEM((lines, rows, basis * width), BF16)]
     aliases = {}
+    if fetch is not None:
+        in_specs[fetch] = pl.BlockSpec(memory_space=pltpu.HBM)
+        operands[fetch] = pltpu.with_memory_space_constraint(args[fetch], pltpu.HBM)
+        out_specs.append(whole)
+        out_shape.append(VMEM(args[fetch].shape, BF16))
+        scratch.append(pltpu.SemaphoreType.DMA)
     if base is not None:
         aliases = {len(args): 0}
-        args = (*args, base)
+        in_specs.append(whole)
+        operands += pinned(base)
     return pl.pallas_call(
         kernel,
-        in_specs=[whole] * len(args),
-        out_specs=whole,
-        out_shape=VMEM((cols, planes, rows, width), F32),
-        scratch_shapes=[VMEM((lines, rows, basis * width), BF16)],
+        in_specs=in_specs,
+        out_specs=out_specs,
+        out_shape=out_shape,
+        scratch_shapes=scratch,
         input_output_aliases=aliases,
         compiler_params=pltpu.CompilerParams(vmem_limit_bytes=16 << 20),
         cost_estimate=pl.CostEstimate(
@@ -334,7 +369,7 @@
             transcendentals=lines * rows * 384 * (basis + 1),
         ),
         name=name,
-    )(*pinned(*args))
+    )(*operands)
 
 
 def field_kernel(ph_all, weighted, w_out, base, pos, out, ph, rhs, held, in_sems, out_sems):
@@ -510,12 +545,12 @@
     return lax.ppermute(head, axis, [((i + 1) % count, i) for i in range(count)])
 
 
-def edge_rows(feat_planes, pos_planes, y):
+def edge_rows(feat, pos, before, pos_before, after, y):
     parts = []
-    for f, q in zip(feat_planes, pos_planes):
+    for f, q in ((before, pos_before), (feat, pos)):
         q = jnp.pad(q[:, y : y + 1], ((0, 0), (0, 0), (0, 0), (0, f.shape[3] - q.shape[3])))
         parts.append(jnp.concatenate([f[:, y : y + 1], q], axis=2))
-    return jnp.concatenate(parts, axis=0)
+    return jnp.concatenate(parts + [after[:, y : y + 1]], axis=0)
 
 
 def on_device(features, fractions, counts, k_index, w_short, w_charge, w_out):
@@ -545,57 +580,67 @@
         ],
         axis=2,
     )
-    ph, partial = factor_call(
+    ph, partial, head = factor_call(
         pos, k_index.T, feat.reshape(atoms, width), w_charge, grid_all, scale_all
     )
-    partial, before, head, pos_late = tied(partial, before, feat[:1], pos)
+    partial, before, pos_late = tied(partial, before, pos)
     after = from_after(head, "gx", 0)
     pos_before = from_before(pos_late, "gx", 0)
-    pos_after = from_after(pos_late, "gx", 0)
 
     w_flat = w_short.reshape(basis * width, width)
     exchange = Exchange()
 
-    def plane_work(plane, first, count, base, *sides):
-        kernel = functools.partial(plane_kernel, slots, basis, plane, first, count)
-        call = lambda *args: short_call(
-            kernel, "plane", count, basis, args[:5], args[5] if len(args) > 5 else None
-        )
-        inputs = (feat, pos, *sides, w_flat) + (() if base is None else (base,))
-        return Work(call, *inputs)
+    own = (feat, pos, w_flat)
+
+    def plane_work(plane, first, count, fetch, base, *sides):
+        kernel = functools.partial(plane_kernel, slots, basis, plane, first, count, fetch)
+
+        def call(*args):
+            split = len(own) + len(sides)
+            return short_call(
+                kernel,
+                "plane",
+                count,
+                basis,
+                args[:split],
+                args[split] if args[split:] else None,
+                len(own) if fetch else None,
+            )
+
+        return Work(call, *own, *sides, *(() if base is None else (base,)))
 
     def edges(*args):
-        feat, pos, before, pos_before, after, pos_after, low, high, w, base = args
-        common = (feat, pos, before, pos_before, after, pos_after)
+        *common, low, high, base = args
         for name, y, dy, halo in (("low", 0, -1, low), ("high", cols - 1, 1, high)):
             kernel = functools.partial(edge_kernel, slots, basis, y, dy)
-            base = short_call(kernel, name, planes, basis, (*common, halo, w), base)
+            (base,) = short_call(kernel, name, planes, basis, (*common, halo), base)
         return base
 
     value, _ = exchange.halve(partial, exchange.halved[0])
     value, before, pos_before = tied(value, before, pos_before)
-    value, base = exchange.halve(
-        value, exchange.halved[1], plane_work(0, 1, 3, None, before, pos_before)
-    )
-    value, base = exchange.spread_sum(value, plane_work(0, 4, 3, base, before, pos_before))
-    value, base, after, pos_after = tied(value, base, after, pos_after)
-    feat_planes = (before, feat, after)
-    pos_planes = (pos_before, pos, pos_after)
-    low = from_before(edge_rows(feat_planes, pos_planes, cols - 1), "gy", 1)
-    high = from_after(edge_rows(feat_planes, pos_planes, 0), "gy", 1)
+    value, (base, before_held) = exchange.halve(
+        value, exchange.halved[1], plane_work(0, 1, 3, True, None, before, pos_before)
+    )
+    value, (base,) = exchange.spread_sum(
+        value, plane_work(0, 4, 3, False, base, before_held, pos_before)
+    )
+    value, base, after = tied(value, base, after)
+    near = (feat, pos, before, pos_before, after)
+    low = from_before(edge_rows(*near, cols - 1), "gy", 1)
+    high = from_after(edge_rows(*near, 0), "gy", 1)
     for i, bit in enumerate(exchange.whole):
         if i == 0:
-            value, base = exchange.whole_sum(
-                value, bit, plane_work(1, 1, 3, base, after, pos_after)
+            value, (base, after_held) = exchange.whole_sum(
+                value, bit, plane_work(1, 1, 3, True, base, after)
             )
         else:
             value, _ = exchange.whole_sum(value, bit)
     value = value.astype(BF16)
-    value, base = exchange.spread(value, plane_work(1, 4, 3, base, after, pos_after))
+    value, (base,) = exchange.spread(value, plane_work(1, 4, 3, False, base, after_held))
     value, base = exchange.double(
         value,
         exchange.halved[1],
-        Work(edges, feat, pos, before, pos_before, after, pos_after, low, high, w_flat, base),
+        Work(edges, *own, before_held, pos_before, after_held, low, high, base),
     )
     value, _ = exchange.double(value, exchange.halved[0])
     weighted = value.reshape(2 * vectors // KTILE, width, KTILE)

time: 77.3 us -> 92.1 us (1.19)
  waiting for transfers between devices: 12.4 us -> 22.9 us
  local copies, waits for them, and re-layouts: 4.96 us -> 9.87 us
  Pallas kernels: 35.9 us -> 33.9 us
  starting transfers between devices: 19.8 us -> 21 us
    ppermute x3, waiting for transfers between devices: 2.94 us -> 13.3 us  [from_before(): lax.ppermute(tail, axis, [(i, (i + 1) % count) for i in range(count)])]
    unnamed x14 -> x12, local copies, waits for them, and re-layouts: 0.03 us -> 2.85 us
    ppermute x3 -> x2, starting transfers between devices: 2.34 us -> 4.89 us  [from_after(): lax.ppermute(head, axis, [((i + 1) % count, i) for i in range(count)])]
    pallas_call x6, Pallas kernels: 19.3 us -> 17.2 us  [short_call(): pl.pallas_call(kernel, in_specs=in_specs, out_specs=out_specs, out_shape=...]
    ppermute x11, starting transfers between devices: 12.2 us -> 11.2 us  [swap(): return lax.ppermute(value, AXES, [(i, i ^ mask) for i in range(count)])]
    slice x2 -> x3, local copies, waits for them, and re-layouts: 2.37 us -> 2.89 us  [the longest x2 1.96 us: from_before(): tail = lax.slice_in_dim(cells, size - 1, size, axis=dim)]
  transfers between devices with their start and end apart: 17 -> 16, of which waited for: 7 -> 7; matrix products, arithmetic and copies ran while one was open for 3% -> 5% of each run, Pallas kernels for 36% -> 28%
where the time goes in v5:
time: 92.1 us; the launch traced here: 91.5 us
  Pallas kernels  33.9 us (37%)
  waiting for transfers between devices  22.9 us (25%)
  starting transfers between devices  21 us (23%)
  local copies, waits for them, and re-layouts  9.87 us (11%)
  other arithmetic  3.3 us (4%)
    pallas_call x6, Pallas kernels, short_call(): pl.pallas_call(kernel, in_specs=in_specs, out_specs=out_specs, out_shape=...  17.2 us
    ppermute x3, waiting for transfers between devices, from_before(): lax.ppermute(tail, axis, [(i, (i + 1) % count) for i in range(count)])  13.3 us
    ppermute x11, starting transfers between devices, swap(): return lax.ppermute(value, AXES, [(i, i ^ mask) for i in range(count)])  11.2 us
    ppermute x11, waiting for transfers between devices, swap(): return lax.ppermute(value, AXES, [(i, i ^ mask) for i in range(count)])  9.62 us
    pallas_call x1, Pallas kernels, factor_call(): pl.pallas_call(functools.partial(factor_kernel, grid_all, scale_all), in_...  8.37 us
    pallas_call x1, Pallas kernels, field_call(): pl.pallas_call(field_kernel, in_specs=[pl.BlockSpec(memory_space=pltpu.HB...  8.33 us
    ppermute x2, starting transfers between devices, from_after(): lax.ppermute(head, axis, [((i + 1) % count, i) for i in range(count)])  4.89 us
    ppermute x3, starting transfers between devices, from_before(): lax.ppermute(tail, axis, [(i, (i + 1) % count) for i in range(count)])  4.85 us
  transfers between devices with their start and end apart: 16, of which 7 were waited for; matrix products, arithmetic and copies ran while one was open for 5% of the time, Pallas kernels for 28%

profile of v5, /device:TPU:0, one launch (start us, length us, event | category | flops | bytes accessed | tf_op | source)
XLA Modules:
  0.0 91.5 jit_solution(13866215867130193244)
XLA Ops:
  0.0 2.0 %slice_bitcast_fusion = bf16[1,8,128,256]{3,2,1,0:T(8,128)(2,1)} fusion(bf16[2,8,16,8,256]{4,3,2,1,0:T(8,128)(2,1)} %param.7), kind=kLoop, calls=%fused_computation.15 | loop fusion | bytes 1048576 | tf_op jit(solution)/shard_map/slice | solution.py:538
  2.0 2.9 %collective-permute-start = (bf16[1,8,128,256]{3,2,1,0:T(8,128)(2,1)}, bf16[1,8,128,256]{3,2,1,0:T(8,128)(2,1)}, u32[]{:S(2)}, u32[]{:S(2)}) collective-permute-start(bf16[1,8,128,256]{3,2,1,0:T(8,128)(2,1)} %slice_bitcast_fusion), channel_id=1, source_target_pairs={{0,16},{16,0},{1,17},{17,1},{2,18},{18,2},{3,19},{19,3},{4,20},{20... | collective-permute-start | bytes 1572872 | tf_op jit(solution)/shard_map/ppermute | solution.py:539
  7.4 1.2 %copy-done = bf16[2,8,16,8,256]{4,3,2,1,0:T(8,128)(2,1)S(1)} copy-done((bf16[2,8,16,8,256]{4,3,2,1,0:T(8,128)(2,1)S(1)}, bf16[2,8,16,8,256]{4,3,2,1,0:T(8,128)(2,1)}, u32[]{:S(2)}) %copy-start) | copy-done | bytes 1048600
  10.2 8.4 %factor.1 = (bf16[4,2,2048,256]{3,2,1,0:T(8,128)(2,1)}, f32[2048,256]{1,0:T(8,128)S(1)}, bf16[1,8,144,256]{3,2,1,0:T(8,128)(2,1)}) custom-call(bf16[2,8,16,128]{3,2,1,0:T(8,128)(2,1)S(1)} %maximum_maximum_fusion.pos, s32[3,1024]{1,0:T(4,128)S(1)} %bitcast.51, bf16[2048,256]{1,0:T(8,128)(2,1)S(1)} %bitcast.37, bf16[256,256]{1,0:T(8,128)(2,1)S(1)} %copy-done.4), custom_call_target="tpu_custom_call" | custom-call | flops 12884901888 | bytes 4194304 | tf_op jit(solution)/shard_map/factor/pallas_call | solution.py:143
  19.8 1.9 %collective-permute-start.2 = (bf16[1,8,16,128]{3,2,1,0:T(8,128)(2,1)S(1)}, bf16[1,8,16,128]{3,2,1,0:T(8,128)(2,1)S(1)}, u32[]{:S(2)}, u32[]{:S(2)}) collective-permute-start(bf16[1,8,16,128]{3,2,1,0:T(8,128)(2,1)S(1)} %slice.41), channel_id=1, source_target_pairs={{0,16},{16,0},{1,17},{17,1},{2,18},{18,2},{3,19},{19,3},{4,20},{20... | collective-permute-start | bytes 98312 | tf_op jit(solution)/shard_map/ppermute | solution.py:539
  21.7 1.1 %convert_add_fusion = f32[1024,256]{1,0:T(8,128)S(1)} fusion(bf16[1024,256]{1,0:T(8,128)(2,1)} %collective-permute-done.1, f32[2048,256]{1,0:T(8,128)S(1)} %get-tuple-element.78, s32[]{:T(128)S(6)} %select_n.114), kind=kLoop, calls=%fused_computation.1 | loop fusion | flops 524288 | bytes 2621444 | tf_op jit(solution)/shard_map/add | solution.py:477
  22.9 13.3 %collective-permute-done.2.rest_1_.pos_before = bf16[1,8,16,128]{3,2,1,0:T(8,128)(2,1)S(1)} collective-permute-done((bf16[1,8,16,128]{3,2,1,0:T(8,128)(2,1)S(1)}, bf16[1,8,16,128]{3,2,1,0:T(8,128)(2,1)S(1)}, u32[]{:S(2)}, u32[]{:S(2)}) %collective-permute-start.2) | collective-permute-done | bytes 32800 | tf_op jit(solution)/shard_map/ppermute | solution.py:539
  36.2 1.6 %collective-permute-start.3 = (bf16[512,256]{1,0:T(8,128)(2,1)S(1)}, bf16[512,256]{1,0:T(8,128)(2,1)S(1)}, u32[]{:S(2)}, u32[]{:S(2)}) collective-permute-start(bf16[512,256]{1,0:T(8,128)(2,1)S(1)} %dynamic-slice_convert_fusion.1), channel_id=1, source_target_pairs={{0,2},{1,3},{2,0},{3,1},{4,6},{5,7},{6,4},{7,5},{8,10},{9,11},{10,... | collective-permute-start | bytes 786440 | tf_op jit(solution)/shard_map/ppermute | solution.py:444
  37.7 4.0 %plane.4 = (f32[8,2,128,256]{3,2,1,0:T(8,128)S(1)}, bf16[1,8,128,256]{3,2,1,0:T(8,128)(2,1)S(1)}) custom-call(bf16[2,8,128,256]{3,2,1,0:T(8,128)(2,1)S(1)} %bitcast.39, bf16[2,8,16,128]{3,2,1,0:T(8,128)(2,1)S(1)} %maximum_maximum_fusion.pos, bf16[2048,256]{1,0:T(8,128)(2,1)S(1)} %bitcast.45, bf16[1,8,128,256]{3,2,1,0:T(8,128)(2,1)} %collective-permute-done.rest_0_, ...), custom_call_target="tpu_custom_call" | custom-call | flops 4026531840 | bytes 4194304 | tf_op jit(solution)/shard_map/plane/pallas_call | solution.py:358
  42.6 1.6 %collective-permute-done.3 = bf16[512,256]{1,0:T(8,128)(2,1)S(1)} collective-permute-done((bf16[512,256]{1,0:T(8,128)(2,1)S(1)}, bf16[512,256]{1,0:T(8,128)(2,1)S(1)}, u32[]{:S(2)}, u32[]{:S(2)}) %collective-permute-start.3) | collective-permute-done | bytes 262176 | tf_op jit(solution)/shard_map/ppermute | solution.py:444
  44.4 1.6 %collective-permute-start.4 = (bf16[128,256]{1,0:T(8,128)(2,1)S(1)}, bf16[128,256]{1,0:T(8,128)(2,1)S(1)}, u32[]{:S(2)}, u32[]{:S(2)}) collective-permute-start(bf16[128,256]{1,0:T(8,128)(2,1)S(1)} %get-tuple-element.95), channel_id=1, source_target_pairs={{0,4},{1,5},{2,6},{3,7},{4,0},{5,1},{6,2},{7,3},{8,12},{9,13},{10,... | collective-permute-start | bytes 196616 | tf_op jit(solution)/shard_map/ppermute | solution.py:444
  46.0 2.6 %collective-permute-start.5 = (bf16[128,256]{1,0:T(8,128)(2,1)S(1)}, bf16[128,256]{1,0:T(8,128)(2,1)S(1)}, u32[]{:S(2)}, u32[]{:S(2)}) collective-permute-start(bf16[128,256]{1,0:T(8,128)(2,1)S(1)} %get-tuple-element.96), channel_id=1, source_target_pairs={{0,8},{1,9},{2,10},{3,11},{4,12},{5,13},{6,14},{7,15},{8,0},{9,1},... | collective-permute-start | bytes 196616 | tf_op jit(solution)/shard_map/ppermute | solution.py:444
  48.8 2.9 %plane.5.rest_1_ = f32[8,2,128,256]{3,2,1,0:T(8,128)S(1)} custom-call(bf16[2,8,128,256]{3,2,1,0:T(8,128)(2,1)S(1)} %bitcast.40, bf16[2,8,16,128]{3,2,1,0:T(8,128)(2,1)S(1)} %maximum_maximum_fusion.pos, bf16[2048,256]{1,0:T(8,128)(2,1)S(1)} %bitcast.46, ...), custom_call_target="tpu_custom_call", output_to_operand_aliasing={{}: (5, {})} | custom-call | flops 4026531840 | bytes 4194304 | tf_op jit(solution)/shard_map/plane/pallas_call | solution.py:358
  52.6 2.1 %collective-permute-done.6 = bf16[128,256]{1,0:T(8,128)(2,1)S(1)} collective-permute-done((bf16[128,256]{1,0:T(8,128)(2,1)S(1)}, bf16[128,256]{1,0:T(8,128)(2,1)S(1)}, u32[]{:S(2)}, u32[]{:S(2)}) %collective-permute-start.6) | collective-permute-done | bytes 65568 | tf_op jit(solution)/shard_map/ppermute | solution.py:444
  56.4 4.7 %collective-permute-start.13 = (bf16[4,1,144,256]{3,2,1,0:T(8,128)(2,1)S(1)}, bf16[4,1,144,256]{3,2,1,0:T(8,128)(2,1)S(1)}, u32[]{:S(2)}, u32[]{:S(2)}) collective-permute-start(bf16[4,1,144,256]{3,2,1,0:T(8,128)(2,1)S(1)} %fusion.16), channel_id=1, source_target_pairs={{1,0},{2,1},{3,2},{4,3},{5,4},{6,5},{7,6},{8,7},{9,8},{10,9},{11,1... | collective-permute-start | bytes 884744 | tf_op jit(solution)/shard_map/ppermute | solution.py:545
  61.0 4.0 %plane.6 = (f32[8,2,128,256]{3,2,1,0:T(8,128)S(1)}, bf16[1,8,144,256]{3,2,1,0:T(8,128)(2,1)S(1)}) custom-call(bf16[2,8,128,256]{3,2,1,0:T(8,128)(2,1)S(1)} %bitcast.41, bf16[2,8,16,128]{3,2,1,0:T(8,128)(2,1)S(1)} %maximum_maximum_fusion.pos, bf16[2048,256]{1,0:T(8,128)(2,1)S(1)} %bitcast.47, ...), custom_call_target="tpu_custom_call", output_to_operand_aliasing={{0}: (4, {})} | custom-call | flops 4026531840 | bytes 4194304 | tf_op jit(solution)/shard_map/plane/pallas_call | solution.py:358
  65.2 4.3 %collective-permute-start.11 = (bf16[128,256]{1,0:T(8,128)(2,1)S(1)}, bf16[128,256]{1,0:T(8,128)(2,1)S(1)}, u32[]{:S(2)}, u32[]{:S(2)}) collective-permute-start(bf16[128,256]{1,0:T(8,128)(2,1)S(1)} %add_convert_fusion), channel_id=1, source_target_pairs={{0,12},{1,13},{2,14},{3,15},{4,8},{5,9},{6,10},{7,11},{8,4},{9,5},... | collective-permute-start | bytes 196616 | tf_op jit(solution)/shard_map/ppermute | solution.py:444
  69.5 2.9 %plane.7.rest_0_ = f32[8,2,128,256]{3,2,1,0:T(8,128)S(1)} custom-call(bf16[2,8,128,256]{3,2,1,0:T(8,128)(2,1)S(1)} %bitcast.42, bf16[2,8,16,128]{3,2,1,0:T(8,128)(2,1)S(1)} %maximum_maximum_fusion.pos, bf16[2048,256]{1,0:T(8,128)(2,1)S(1)} %bitcast.48, bf16[1,8,144,256]{3,2,1,0:T(8,128)(2,1)S(1)} %get-tuple-element.141.rest_0_.after, ...), custom_call_target="tpu_custom_call", output_to_operand_aliasing={{}: (4, {})} | custom-call | flops 4026531840 | bytes 4194304 | tf_op jit(solution)/shard_map/plane/pallas_call | solution.py:358
  72.8 1.7 %low.1.rest_0_ = f32[8,2,128,256]{3,2,1,0:T(8,128)S(1)} custom-call(bf16[2,8,128,256]{3,2,1,0:T(8,128)(2,1)S(1)} %bitcast.43, bf16[2,8,16,128]{3,2,1,0:T(8,128)(2,1)S(1)} %maximum_maximum_fusion.pos, bf16[2048,256]{1,0:T(8,128)(2,1)S(1)} %bitcast.49, bf16[1,8,128,256]{3,2,1,0:T(8,128)(2,1)S(1)} %get-tuple-element.139.rest_0_.before, ...), custom_call_target="tpu_custom_call", output_to_operand_aliasing={{}: (7, {})} | custom-call | flops 2684354560 | bytes 4194304 | tf_op jit(solution)/shard_map/low/pallas_call | solution.py:358
  74.5 1.7 %high.1.base = f32[8,2,128,256]{3,2,1,0:T(8,128)S(1)} custom-call(bf16[2,8,128,256]{3,2,1,0:T(8,128)(2,1)S(1)} %bitcast.44, bf16[2,8,16,128]{3,2,1,0:T(8,128)(2,1)S(1)} %maximum_maximum_fusion.pos, bf16[2048,256]{1,0:T(8,128)(2,1)S(1)} %bitcast.50, bf16[1,8,128,256]{3,2,1,0:T(8,128)(2,1)S(1)} %get-tuple-element.139.rest_0_.before, ...), custom_call_target="tpu_custom_call", output_to_operand_aliasing={{}: (7, {})} | custom-call | flops 2684354560 | bytes 4194304 | tf_op jit(solution)/shard_map/high/pallas_call | solution.py:358
  76.2 2.9 %collective-permute-done.14 = bf16[512,256]{1,0:T(8,128)(2,1)S(1)} collective-permute-done((bf16[512,256]{1,0:T(8,128)(2,1)S(1)}, bf16[512,256]{1,0:T(8,128)(2,1)S(1)}, u32[]{:S(2)}, u32[]{:S(2)}) %collective-permute-start.14) | collective-permute-done | bytes 262176 | tf_op jit(solution)/shard_map/ppermute | solution.py:444
  79.4 2.0 %collective-permute-done.15 = bf16[1024,256]{1,0:T(8,128)(2,1)} collective-permute-done((bf16[1024,256]{1,0:T(8,128)(2,1)S(1)}, bf16[1024,256]{1,0:T(8,128)(2,1)}, u32[]{:S(2)}, u32[]{:S(2)}) %collective-permute-start.15) | collective-permute-done | bytes 524320 | tf_op jit(solution)/shard_map/ppermute | solution.py:444
  81.5 1.5 %maximum_select_fusion = bf16[2048,256]{1,0:T(8,128)(2,1)S(1)} fusion(bf16[1024,256]{1,0:T(8,128)(2,1)} %collective-permute-done.15, bf16[1024,256]{1,0:T(8,128)(2,1)S(1)} %maximum_select_fusion.1, pred[]{:T(512)S(6)} %eq.21), kind=kLoop, calls=%fused_computation | loop fusion | flops 4718592 | bytes 2097153 | tf_op jit(solution)/shard_map/jit(_where)/select_n | solution.py:511
  83.0 8.3 %field.1 = bf16[2048,256]{1,0:T(8,128)(2,1)} custom-call(bf16[4,2,2048,256]{3,2,1,0:T(8,128)(2,1)} %get-tuple-element.76.ph_all, bf16[8,256,256]{2,1,0:T(8,128)(2,1)S(1)} %bitcast.36, bf16[256,256]{1,0:T(8,128)(2,1)S(1)} %copy-done.2, f32[8,2,128,256]{3,2,1,0:T(8,128)S(1)} %high.1.base, bf16[2,8,16,128]{3,2,1,0:T(8,128)(2,1)S(1)} %maximum_maximum_fusion.pos), custom_call_target="tpu_custom_call" | custom-call | flops 2147483648 | bytes 4194304 | tf_op jit(solution)/shard_map/field/pallas_call | solution.py:418
  (61 shorter events, 9.7 us)
Async XLA Ops:
  2.0 16.7 %collective-permute-start = (bf16[1,8,128,256]{3,2,1,0:T(8,128)(2,1)}, bf16[1,8,128,256]{3,2,1,0:T(8,128)(2,1)}, u32[]{:S(2)}, u32[]{:S(2)}) collective-permute-start(bf16[1,8,128,256]{3,2,1,0:T(8,128)(2,1)} %slice_bitcast_fusion), channel_id=1, source_target_pairs={{0,16},{16,0},{1,17},{17,1},{2,18},{18,2},{3,19},{19,3},{4,20},{20... | collective-permute-start | bytes 1572872 | tf_op jit(solution)/shard_map/ppermute | solution.py:539
  7.4 1.2 %copy-start = (bf16[2,8,16,8,256]{4,3,2,1,0:T(8,128)(2,1)S(1)}, bf16[2,8,16,8,256]{4,3,2,1,0:T(8,128)(2,1)}, u32[]{:S(2)}) copy-start(bf16[2,8,16,8,256]{4,3,2,1,0:T(8,128)(2,1)} %param.7) | copy-start | bytes 3145732
  8.6 0.9 copy-start.4
  9.5 0.7 copy-start.5
  10.2 9.5 %copy-start.1 = (bf16[2,8,16,8,256]{4,3,2,1,0:T(8,128)(2,1)S(1)}, bf16[2,8,16,8,256]{4,3,2,1,0:T(8,128)(2,1)}, u32[]{:S(2)}) copy-start(bf16[2,8,16,8,256]{4,3,2,1,0:T(8,128)(2,1)} %param.7) | copy-start | bytes 3145732
  19.5 2.3 %collective-permute-start.1 = (bf16[1024,256]{1,0:T(8,128)(2,1)}, bf16[1024,256]{1,0:T(8,128)(2,1)}, u32[]{:S(2)}, u32[]{:S(2)}) collective-permute-start(bf16[1024,256]{1,0:T(8,128)(2,1)} %dynamic-slice_convert_fusion), channel_id=1, source_target_pairs={{0,1},{1,0},{2,3},{3,2},{4,5},{5,4},{6,7},{7,6},{8,9},{9,8},{10,11... | collective-permute-start | bytes 1572872 | tf_op jit(solution)/shard_map/ppermute | solution.py:444
  19.5 35.2 %collective-permute-start.7 = (bf16[1,8,144,256]{3,2,1,0:T(8,128)(2,1)}, bf16[1,8,144,256]{3,2,1,0:T(8,128)(2,1)}, u32[]{:S(2)}, u32[]{:S(2)}) collective-permute-start(bf16[1,8,144,256]{3,2,1,0:T(8,128)(2,1)} %get-tuple-element.108), channel_id=1, source_target_pairs={{16,0},{0,16},{17,1},{1,17},{18,2},{2,18},{19,3},{3,19},{20,4},{4,... | collective-permute-start | bytes 1769480 | tf_op jit(solution)/shard_map/ppermute | solution.py:545
  19.7 18.0 %copy-start.3 = (bf16[8,256,256]{2,1,0:T(8,128)(2,1)S(1)}, bf16[8,256,256]{2,1,0:T(8,128)(2,1)}, u32[]{:S(2)}) copy-start(bf16[8,256,256]{2,1,0:T(8,128)(2,1)} %param.11) | copy-start | bytes 3145732
  19.8 16.4 %collective-permute-start.2 = (bf16[1,8,16,128]{3,2,1,0:T(8,128)(2,1)S(1)}, bf16[1,8,16,128]{3,2,1,0:T(8,128)(2,1)S(1)}, u32[]{:S(2)}, u32[]{:S(2)}) collective-permute-start(bf16[1,8,16,128]{3,2,1,0:T(8,128)(2,1)S(1)} %slice.41), channel_id=1, source_target_pairs={{0,16},{16,0},{1,17},{17,1},{2,18},{18,2},{3,19},{19,3},{4,20},{20... | collective-permute-start | bytes 98312 | tf_op jit(solution)/shard_map/ppermute | solution.py:539
  36.2 8.1 %collective-permute-start.3 = (bf16[512,256]{1,0:T(8,128)(2,1)S(1)}, bf16[512,256]{1,0:T(8,128)(2,1)S(1)}, u32[]{:S(2)}, u32[]{:S(2)}) collective-permute-start(bf16[512,256]{1,0:T(8,128)(2,1)S(1)} %dynamic-slice_convert_fusion.1), channel_id=1, source_target_pairs={{0,2},{1,3},{2,0},{3,1},{4,6},{5,7},{6,4},{7,5},{8,10},{9,11},{10,... | collective-permute-start | bytes 786440 | tf_op jit(solution)/shard_map/ppermute | solution.py:444
  44.4 7.4 %collective-permute-start.4 = (bf16[128,256]{1,0:T(8,128)(2,1)S(1)}, bf16[128,256]{1,0:T(8,128)(2,1)S(1)}, u32[]{:S(2)}, u32[]{:S(2)}) collective-permute-start(bf16[128,256]{1,0:T(8,128)(2,1)S(1)} %get-tuple-element.95), channel_id=1, source_target_pairs={{0,4},{1,5},{2,6},{3,7},{4,0},{5,1},{6,2},{7,3},{8,12},{9,13},{10,... | collective-permute-start | bytes 196616 | tf_op jit(solution)/shard_map/ppermute | solution.py:444
  46.0 6.6 %collective-permute-start.5 = (bf16[128,256]{1,0:T(8,128)(2,1)S(1)}, bf16[128,256]{1,0:T(8,128)(2,1)S(1)}, u32[]{:S(2)}, u32[]{:S(2)}) collective-permute-start(bf16[128,256]{1,0:T(8,128)(2,1)S(1)} %get-tuple-element.96), channel_id=1, source_target_pairs={{0,8},{1,9},{2,10},{3,11},{4,12},{5,13},{6,14},{7,15},{8,0},{9,1},... | collective-permute-start | bytes 196616 | tf_op jit(solution)/shard_map/ppermute | solution.py:444
  48.6 6.1 %collective-permute-start.6 = (bf16[128,256]{1,0:T(8,128)(2,1)S(1)}, bf16[128,256]{1,0:T(8,128)(2,1)S(1)}, u32[]{:S(2)}, u32[]{:S(2)}) collective-permute-start(bf16[128,256]{1,0:T(8,128)(2,1)S(1)} %get-tuple-element.97), channel_id=1, source_target_pairs={{0,12},{1,13},{2,14},{3,15},{4,8},{5,9},{6,10},{7,11},{8,4},{9,5},... | collective-permute-start | bytes 196616 | tf_op jit(solution)/shard_map/ppermute | solution.py:444
  55.7 9.4 %collective-permute-start.8 = (bf16[128,256]{1,0:T(8,128)(2,1)S(1)}, bf16[128,256]{1,0:T(8,128)(2,1)S(1)}, u32[]{:S(2)}, u32[]{:S(2)}) collective-permute-start(bf16[128,256]{1,0:T(8,128)(2,1)S(1)} %convert_element_type.78), channel_id=1, source_target_pairs={{0,16},{1,17},{2,18},{3,19},{4,20},{5,21},{6,22},{7,23},{8,24},{9,... | collective-permute-start | bytes 196616 | tf_op jit(solution)/shard_map/ppermute | solution.py:444
  56.3 16.4 %collective-permute-start.12 = (bf16[4,1,144,256]{3,2,1,0:T(8,128)(2,1)S(1)}, bf16[4,1,144,256]{3,2,1,0:T(8,128)(2,1)S(1)}, u32[]{:S(2)}, u32[]{:S(2)}) collective-permute-start(bf16[4,1,144,256]{3,2,1,0:T(8,128)(2,1)S(1)} %fusion.12), channel_id=1, source_target_pairs={{0,1},{1,2},{2,3},{3,4},{4,5},{5,6},{6,7},{7,8},{8,9},{9,10},{10,1... | collective-permute-start | bytes 884744 | tf_op jit(solution)/shard_map/ppermute | solution.py:539
  56.4 16.3 %collective-permute-start.13 = (bf16[4,1,144,256]{3,2,1,0:T(8,128)(2,1)S(1)}, bf16[4,1,144,256]{3,2,1,0:T(8,128)(2,1)S(1)}, u32[]{:S(2)}, u32[]{:S(2)}) collective-permute-start(bf16[4,1,144,256]{3,2,1,0:T(8,128)(2,1)S(1)} %fusion.16), channel_id=1, source_target_pairs={{1,0},{2,1},{3,2},{4,3},{5,4},{6,5},{7,6},{8,7},{9,8},{10,9},{11,1... | collective-permute-start | bytes 884744 | tf_op jit(solution)/shard_map/ppermute | solution.py:545
  65.1 7.4 %collective-permute-start.9 = (bf16[128,256]{1,0:T(8,128)(2,1)S(1)}, bf16[128,256]{1,0:T(8,128)(2,1)S(1)}, u32[]{:S(2)}, u32[]{:S(2)}) collective-permute-start(bf16[128,256]{1,0:T(8,128)(2,1)S(1)} %add_convert_fusion), channel_id=1, source_target_pairs={{0,4},{1,5},{2,6},{3,7},{4,0},{5,1},{6,2},{7,3},{8,12},{9,13},{10,... | collective-permute-start | bytes 196616 | tf_op jit(solution)/shard_map/ppermute | solution.py:444
  65.2 7.3 %collective-permute-start.10 = (bf16[128,256]{1,0:T(8,128)(2,1)S(1)}, bf16[128,256]{1,0:T(8,128)(2,1)S(1)}, u32[]{:S(2)}, u32[]{:S(2)}) collective-permute-start(bf16[128,256]{1,0:T(8,128)(2,1)S(1)} %add_convert_fusion), channel_id=1, source_target_pairs={{0,8},{1,9},{2,10},{3,11},{4,12},{5,13},{6,14},{7,15},{8,0},{9,1},... | collective-permute-start | bytes 196616 | tf_op jit(solution)/shard_map/ppermute | solution.py:444
  65.2 7.3 %collective-permute-start.11 = (bf16[128,256]{1,0:T(8,128)(2,1)S(1)}, bf16[128,256]{1,0:T(8,128)(2,1)S(1)}, u32[]{:S(2)}, u32[]{:S(2)}) collective-permute-start(bf16[128,256]{1,0:T(8,128)(2,1)S(1)} %add_convert_fusion), channel_id=1, source_target_pairs={{0,12},{1,13},{2,14},{3,15},{4,8},{5,9},{6,10},{7,11},{8,4},{9,5},... | collective-permute-start | bytes 196616 | tf_op jit(solution)/shard_map/ppermute | solution.py:444
  72.7 6.4 %collective-permute-start.14 = (bf16[512,256]{1,0:T(8,128)(2,1)S(1)}, bf16[512,256]{1,0:T(8,128)(2,1)S(1)}, u32[]{:S(2)}, u32[]{:S(2)}) collective-permute-start(bf16[512,256]{1,0:T(8,128)(2,1)S(1)} %bitcast.55), channel_id=1, source_target_pairs={{0,2},{1,3},{2,0},{3,1},{4,6},{5,7},{6,4},{7,5},{8,10},{9,11},{10,... | collective-permute-start | bytes 786440 | tf_op jit(solution)/shard_map/ppermute | solution.py:444
  76.2 6.8 %copy-start.2 = (bf16[256,256]{1,0:T(8,128)(2,1)S(1)}, bf16[256,256]{1,0:T(8,128)(2,1)}, u32[]{:S(2)}) copy-start(bf16[256,256]{1,0:T(8,128)(2,1)} %w_out.1) | copy-start | bytes 393220
  79.4 2.1 %collective-permute-start.15 = (bf16[1024,256]{1,0:T(8,128)(2,1)S(1)}, bf16[1024,256]{1,0:T(8,128)(2,1)}, u32[]{:S(2)}, u32[]{:S(2)}) collective-permute-start(bf16[1024,256]{1,0:T(8,128)(2,1)S(1)} %maximum_select_fusion.1), channel_id=1, source_target_pairs={{0,1},{1,0},{2,3},{3,2},{4,5},{5,4},{6,7},{7,6},{8,9},{9,8},{10,11... | collective-permute-start | bytes 1572872 | tf_op jit(solution)/shard_map/ppermute | solution.py:444

commit v6 on v5

--- a/solution.py
+++ b/solution.py
@@ -584,8 +584,9 @@
         pos, k_index.T, feat.reshape(atoms, width), w_charge, grid_all, scale_all
     )
     partial, before, pos_late = tied(partial, before, pos)
+    pos_before = from_before(pos_late, "gx", 0)
+    head, pos_before = tied(head, pos_before)
     after = from_after(head, "gx", 0)
-    pos_before = from_before(pos_late, "gx", 0)
 
     w_flat = w_short.reshape(basis * width, width)
     exchange = Exchange()

time: 92.1 us -> 80.4 us (0.87)
  waiting for transfers between devices: 22.9 us -> 12.4 us
  local copies, waits for them, and re-layouts: 9.87 us -> 8.89 us
    ppermute x3, waiting for transfers between devices: 13.3 us -> 3.67 us  [from_before(): lax.ppermute(tail, axis, [(i, (i + 1) % count) for i in range(count)])]
    ppermute x3, starting transfers between devices: 4.85 us -> 3.3 us  [from_before(): lax.ppermute(tail, axis, [(i, (i + 1) % count) for i in range(count)])]
    ppermute x11, starting transfers between devices: 11.2 us -> 12.5 us  [swap(): return lax.ppermute(value, AXES, [(i, i ^ mask) for i in range(count)])]
    unnamed x12 -> x14, local copies, waits for them, and re-layouts: 2.85 us -> 2.86 us
  transfers between devices with their start and end apart: 16 -> 16, of which waited for: 7 -> 6; matrix products, arithmetic and copies ran while one was open for 5% -> 6% of each run, Pallas kernels for 28% -> 32%
where the time goes in v6:
time: 80.4 us; the launch traced here: 79.8 us
  Pallas kernels  33.9 us (42%)
  starting transfers between devices  20.7 us (26%)
  waiting for transfers between devices  12.4 us (15%)
  local copies, waits for them, and re-layouts  8.89 us (11%)
  other arithmetic  3.32 us (4%)
    pallas_call x6, Pallas kernels, short_call(): pl.pallas_call(kernel, in_specs=in_specs, out_specs=out_specs, out_shape=...  17.2 us
    ppermute x11, starting transfers between devices, swap(): return lax.ppermute(value, AXES, [(i, i ^ mask) for i in range(count)])  12.5 us
    ppermute x11, waiting for transfers between devices, swap(): return lax.ppermute(value, AXES, [(i, i ^ mask) for i in range(count)])  8.71 us
    pallas_call x1, Pallas kernels, factor_call(): pl.pallas_call(functools.partial(factor_kernel, grid_all, scale_all), in_...  8.36 us
    pallas_call x1, Pallas kernels, field_call(): pl.pallas_call(field_kernel, in_specs=[pl.BlockSpec(memory_space=pltpu.HB...  8.33 us
    ppermute x2, starting transfers between devices, from_after(): lax.ppermute(head, axis, [((i + 1) % count, i) for i in range(count)])  4.9 us
    ppermute x3, waiting for transfers between devices, from_before(): lax.ppermute(tail, axis, [(i, (i + 1) % count) for i in range(count)])  3.67 us
    ppermute x3, starting transfers between devices, from_before(): lax.ppermute(tail, axis, [(i, (i + 1) % count) for i in range(count)])  3.3 us
  transfers between devices with their start and end apart: 16, of which 6 were waited for; matrix products, arithmetic and copies ran while one was open for 6% of the time, Pallas kernels for 32%

profile of v6, /device:TPU:0, one launch (start us, length us, event | category | flops | bytes accessed | tf_op | source)
XLA Modules:
  0.0 79.8 jit_solution(12131352091058207988)
XLA Ops:
  0.0 1.9 %slice_bitcast_fusion = bf16[1,8,128,256]{3,2,1,0:T(8,128)(2,1)} fusion(bf16[2,8,16,8,256]{4,3,2,1,0:T(8,128)(2,1)} %param.7), kind=kLoop, calls=%fused_computation.15 | loop fusion | bytes 1048576 | tf_op jit(solution)/shard_map/slice | solution.py:538
  1.9 2.9 %collective-permute-start = (bf16[1,8,128,256]{3,2,1,0:T(8,128)(2,1)}, bf16[1,8,128,256]{3,2,1,0:T(8,128)(2,1)}, u32[]{:S(2)}, u32[]{:S(2)}) collective-permute-start(bf16[1,8,128,256]{3,2,1,0:T(8,128)(2,1)} %slice_bitcast_fusion), channel_id=1, source_target_pairs={{0,16},{16,0},{1,17},{17,1},{2,18},{18,2},{3,19},{19,3},{4,20},{20... | collective-permute-start | bytes 1572872 | tf_op jit(solution)/shard_map/ppermute | solution.py:539
  7.3 1.2 %copy-done = bf16[2,8,16,8,256]{4,3,2,1,0:T(8,128)(2,1)S(1)} copy-done((bf16[2,8,16,8,256]{4,3,2,1,0:T(8,128)(2,1)S(1)}, bf16[2,8,16,8,256]{4,3,2,1,0:T(8,128)(2,1)}, u32[]{:S(2)}) %copy-start) | copy-done | bytes 1048600
  10.1 8.4 %factor.1 = (bf16[4,2,2048,256]{3,2,1,0:T(8,128)(2,1)}, f32[2048,256]{1,0:T(8,128)S(1)}, bf16[1,8,144,256]{3,2,1,0:T(8,128)(2,1)}) custom-call(bf16[2,8,16,128]{3,2,1,0:T(8,128)(2,1)S(1)} %maximum_maximum_fusion.pos, s32[3,1024]{1,0:T(4,128)S(1)} %bitcast.51, bf16[2048,256]{1,0:T(8,128)(2,1)S(1)} %bitcast.37, bf16[256,256]{1,0:T(8,128)(2,1)S(1)} %copy-done.4), custom_call_target="tpu_custom_call" | custom-call | flops 12884901888 | bytes 4194304 | tf_op jit(solution)/shard_map/factor/pallas_call | solution.py:143
  19.7 3.7 %collective-permute-done.2.rest_1_.pos_before = bf16[1,8,16,128]{3,2,1,0:T(8,128)(2,1)S(1)} collective-permute-done((bf16[1,8,16,128]{3,2,1,0:T(8,128)(2,1)S(1)}, bf16[1,8,16,128]{3,2,1,0:T(8,128)(2,1)S(1)}, u32[]{:S(2)}, u32[]{:S(2)}) %collective-permute-start.2) | collective-permute-done | bytes 32800 | tf_op jit(solution)/shard_map/ppermute | solution.py:539
  23.7 1.2 %convert_add_fusion = f32[1024,256]{1,0:T(8,128)S(1)} fusion(bf16[1024,256]{1,0:T(8,128)(2,1)} %collective-permute-done.1, f32[2048,256]{1,0:T(8,128)S(1)} %get-tuple-element.80, s32[]{:T(128)S(6)} %select_n.114), kind=kLoop, calls=%fused_computation.1 | loop fusion | flops 524288 | bytes 2621444 | tf_op jit(solution)/shard_map/add | solution.py:477
  24.9 1.9 %collective-permute-start.3 = (bf16[512,256]{1,0:T(8,128)(2,1)S(1)}, bf16[512,256]{1,0:T(8,128)(2,1)S(1)}, u32[]{:S(2)}, u32[]{:S(2)}) collective-permute-start(bf16[512,256]{1,0:T(8,128)(2,1)S(1)} %dynamic-slice_convert_fusion.1), channel_id=1, source_target_pairs={{0,2},{1,3},{2,0},{3,1},{4,6},{5,7},{6,4},{7,5},{8,10},{9,11},{10,... | collective-permute-start | bytes 786440 | tf_op jit(solution)/shard_map/ppermute | solution.py:444
  26.8 4.0 %plane.4 = (f32[8,2,128,256]{3,2,1,0:T(8,128)S(1)}, bf16[1,8,128,256]{3,2,1,0:T(8,128)(2,1)S(1)}) custom-call(bf16[2,8,128,256]{3,2,1,0:T(8,128)(2,1)S(1)} %bitcast.39, bf16[2,8,16,128]{3,2,1,0:T(8,128)(2,1)S(1)} %maximum_maximum_fusion.pos, bf16[2048,256]{1,0:T(8,128)(2,1)S(1)} %bitcast.45, bf16[1,8,128,256]{3,2,1,0:T(8,128)(2,1)} %collective-permute-done.rest_0_, ...), custom_call_target="tpu_custom_call" | custom-call | flops 4026531840 | bytes 4194304 | tf_op jit(solution)/shard_map/plane/pallas_call | solution.py:358
  32.4 1.9 %collective-permute-start.4 = (bf16[128,256]{1,0:T(8,128)(2,1)S(1)}, bf16[128,256]{1,0:T(8,128)(2,1)S(1)}, u32[]{:S(2)}, u32[]{:S(2)}) collective-permute-start(bf16[128,256]{1,0:T(8,128)(2,1)S(1)} %get-tuple-element.99), channel_id=1, source_target_pairs={{0,4},{1,5},{2,6},{3,7},{4,0},{5,1},{6,2},{7,3},{8,12},{9,13},{10,... | collective-permute-start | bytes 196616 | tf_op jit(solution)/shard_map/ppermute | solution.py:444
  34.3 2.6 %collective-permute-start.5 = (bf16[128,256]{1,0:T(8,128)(2,1)S(1)}, bf16[128,256]{1,0:T(8,128)(2,1)S(1)}, u32[]{:S(2)}, u32[]{:S(2)}) collective-permute-start(bf16[128,256]{1,0:T(8,128)(2,1)S(1)} %get-tuple-element.100), channel_id=1, source_target_pairs={{0,8},{1,9},{2,10},{3,11},{4,12},{5,13},{6,14},{7,15},{8,0},{9,1},... | collective-permute-start | bytes 196616 | tf_op jit(solution)/shard_map/ppermute | solution.py:444
  36.9 2.9 %plane.5.rest_1_ = f32[8,2,128,256]{3,2,1,0:T(8,128)S(1)} custom-call(bf16[2,8,128,256]{3,2,1,0:T(8,128)(2,1)S(1)} %bitcast.40, bf16[2,8,16,128]{3,2,1,0:T(8,128)(2,1)S(1)} %maximum_maximum_fusion.pos, bf16[2048,256]{1,0:T(8,128)(2,1)S(1)} %bitcast.46, ...), custom_call_target="tpu_custom_call", output_to_operand_aliasing={{}: (5, {})} | custom-call | flops 4026531840 | bytes 4194304 | tf_op jit(solution)/shard_map/plane/pallas_call | solution.py:358
  39.8 1.0 %collective-permute-done.5 = bf16[128,256]{1,0:T(8,128)(2,1)S(1)} collective-permute-done((bf16[128,256]{1,0:T(8,128)(2,1)S(1)}, bf16[128,256]{1,0:T(8,128)(2,1)S(1)}, u32[]{:S(2)}, u32[]{:S(2)}) %collective-permute-start.5) | collective-permute-done | bytes 65568 | tf_op jit(solution)/shard_map/ppermute | solution.py:444
  40.9 2.1 %collective-permute-done.6 = bf16[128,256]{1,0:T(8,128)(2,1)S(1)} collective-permute-done((bf16[128,256]{1,0:T(8,128)(2,1)S(1)}, bf16[128,256]{1,0:T(8,128)(2,1)S(1)}, u32[]{:S(2)}, u32[]{:S(2)}) %collective-permute-start.6) | collective-permute-done | bytes 65568 | tf_op jit(solution)/shard_map/ppermute | solution.py:444
  43.0 1.6 %collective-permute-start.8 = (bf16[128,256]{1,0:T(8,128)(2,1)S(1)}, bf16[128,256]{1,0:T(8,128)(2,1)S(1)}, u32[]{:S(2)}, u32[]{:S(2)}) collective-permute-start(bf16[128,256]{1,0:T(8,128)(2,1)S(1)} %convert_element_type.78), channel_id=1, source_target_pairs={{0,16},{1,17},{2,18},{3,19},{4,20},{5,21},{6,22},{7,23},{8,24},{9,... | collective-permute-start | bytes 196616 | tf_op jit(solution)/shard_map/ppermute | solution.py:444
  44.7 4.7 %collective-permute-start.13 = (bf16[4,1,144,256]{3,2,1,0:T(8,128)(2,1)S(1)}, bf16[4,1,144,256]{3,2,1,0:T(8,128)(2,1)S(1)}, u32[]{:S(2)}, u32[]{:S(2)}) collective-permute-start(bf16[4,1,144,256]{3,2,1,0:T(8,128)(2,1)S(1)} %fusion.16), channel_id=1, source_target_pairs={{1,0},{2,1},{3,2},{4,3},{5,4},{6,5},{7,6},{8,7},{9,8},{10,9},{11,1... | collective-permute-start | bytes 884744 | tf_op jit(solution)/shard_map/ppermute | solution.py:545
  49.4 4.0 %plane.6 = (f32[8,2,128,256]{3,2,1,0:T(8,128)S(1)}, bf16[1,8,144,256]{3,2,1,0:T(8,128)(2,1)S(1)}) custom-call(bf16[2,8,128,256]{3,2,1,0:T(8,128)(2,1)S(1)} %bitcast.41, bf16[2,8,16,128]{3,2,1,0:T(8,128)(2,1)S(1)} %maximum_maximum_fusion.pos, bf16[2048,256]{1,0:T(8,128)(2,1)S(1)} %bitcast.47, ...), custom_call_target="tpu_custom_call", output_to_operand_aliasing={{0}: (4, {})} | custom-call | flops 4026531840 | bytes 4194304 | tf_op jit(solution)/shard_map/plane/pallas_call | solution.py:358
  53.6 4.3 %collective-permute-start.11 = (bf16[128,256]{1,0:T(8,128)(2,1)S(1)}, bf16[128,256]{1,0:T(8,128)(2,1)S(1)}, u32[]{:S(2)}, u32[]{:S(2)}) collective-permute-start(bf16[128,256]{1,0:T(8,128)(2,1)S(1)} %add_convert_fusion), channel_id=1, source_target_pairs={{0,12},{1,13},{2,14},{3,15},{4,8},{5,9},{6,10},{7,11},{8,4},{9,5},... | collective-permute-start | bytes 196616 | tf_op jit(solution)/shard_map/ppermute | solution.py:444
  57.9 2.9 %plane.7.rest_0_ = f32[8,2,128,256]{3,2,1,0:T(8,128)S(1)} custom-call(bf16[2,8,128,256]{3,2,1,0:T(8,128)(2,1)S(1)} %bitcast.42, bf16[2,8,16,128]{3,2,1,0:T(8,128)(2,1)S(1)} %maximum_maximum_fusion.pos, bf16[2048,256]{1,0:T(8,128)(2,1)S(1)} %bitcast.48, bf16[1,8,144,256]{3,2,1,0:T(8,128)(2,1)S(1)} %get-tuple-element.145.rest_0_.after, ...), custom_call_target="tpu_custom_call", output_to_operand_aliasing={{}: (4, {})} | custom-call | flops 4026531840 | bytes 4194304 | tf_op jit(solution)/shard_map/plane/pallas_call | solution.py:358
  61.1 1.7 %low.1.rest_0_ = f32[8,2,128,256]{3,2,1,0:T(8,128)S(1)} custom-call(bf16[2,8,128,256]{3,2,1,0:T(8,128)(2,1)S(1)} %bitcast.43, bf16[2,8,16,128]{3,2,1,0:T(8,128)(2,1)S(1)} %maximum_maximum_fusion.pos, bf16[2048,256]{1,0:T(8,128)(2,1)S(1)} %bitcast.49, bf16[1,8,128,256]{3,2,1,0:T(8,128)(2,1)S(1)} %get-tuple-element.143.rest_0_.before, ...), custom_call_target="tpu_custom_call", output_to_operand_aliasing={{}: (7, {})} | custom-call | flops 2684354560 | bytes 4194304 | tf_op jit(solution)/shard_map/low/pallas_call | solution.py:358
  62.9 1.7 %high.1.base = f32[8,2,128,256]{3,2,1,0:T(8,128)S(1)} custom-call(bf16[2,8,128,256]{3,2,1,0:T(8,128)(2,1)S(1)} %bitcast.44, bf16[2,8,16,128]{3,2,1,0:T(8,128)(2,1)S(1)} %maximum_maximum_fusion.pos, bf16[2048,256]{1,0:T(8,128)(2,1)S(1)} %bitcast.50, bf16[1,8,128,256]{3,2,1,0:T(8,128)(2,1)S(1)} %get-tuple-element.143.rest_0_.before, ...), custom_call_target="tpu_custom_call", output_to_operand_aliasing={{}: (7, {})} | custom-call | flops 2684354560 | bytes 4194304 | tf_op jit(solution)/shard_map/high/pallas_call | solution.py:358
  64.6 2.9 %collective-permute-done.14 = bf16[512,256]{1,0:T(8,128)(2,1)S(1)} collective-permute-done((bf16[512,256]{1,0:T(8,128)(2,1)S(1)}, bf16[512,256]{1,0:T(8,128)(2,1)S(1)}, u32[]{:S(2)}, u32[]{:S(2)}) %collective-permute-start.14) | collective-permute-done | bytes 262176 | tf_op jit(solution)/shard_map/ppermute | solution.py:444
  67.8 2.0 %collective-permute-done.15 = bf16[1024,256]{1,0:T(8,128)(2,1)} collective-permute-done((bf16[1024,256]{1,0:T(8,128)(2,1)S(1)}, bf16[1024,256]{1,0:T(8,128)(2,1)}, u32[]{:S(2)}, u32[]{:S(2)}) %collective-permute-start.15) | collective-permute-done | bytes 524320 | tf_op jit(solution)/shard_map/ppermute | solution.py:444
  69.8 1.5 %maximum_select_fusion = bf16[2048,256]{1,0:T(8,128)(2,1)S(1)} fusion(bf16[1024,256]{1,0:T(8,128)(2,1)} %collective-permute-done.15, bf16[1024,256]{1,0:T(8,128)(2,1)S(1)} %maximum_select_fusion.1, pred[]{:T(512)S(6)} %eq.21), kind=kLoop, calls=%fused_computation | loop fusion | flops 4718592 | bytes 2097153 | tf_op jit(solution)/shard_map/jit(_where)/select_n | solution.py:511
  71.3 8.3 %field.1 = bf16[2048,256]{1,0:T(8,128)(2,1)} custom-call(bf16[4,2,2048,256]{3,2,1,0:T(8,128)(2,1)} %get-tuple-element.78.ph_all, bf16[8,256,256]{2,1,0:T(8,128)(2,1)S(1)} %bitcast.36, bf16[256,256]{1,0:T(8,128)(2,1)S(1)} %copy-done.2, f32[8,2,128,256]{3,2,1,0:T(8,128)S(1)} %high.1.base, bf16[2,8,16,128]{3,2,1,0:T(8,128)(2,1)S(1)} %maximum_maximum_fusion.pos), custom_call_target="tpu_custom_call" | custom-call | flops 2147483648 | bytes 4194304 | tf_op jit(solution)/shard_map/field/pallas_call | solution.py:418
  (63 shorter events, 8.1 us)
Async XLA Ops:
  1.9 16.7 %collective-permute-start = (bf16[1,8,128,256]{3,2,1,0:T(8,128)(2,1)}, bf16[1,8,128,256]{3,2,1,0:T(8,128)(2,1)}, u32[]{:S(2)}, u32[]{:S(2)}) collective-permute-start(bf16[1,8,128,256]{3,2,1,0:T(8,128)(2,1)} %slice_bitcast_fusion), channel_id=1, source_target_pairs={{0,16},{16,0},{1,17},{17,1},{2,18},{18,2},{3,19},{19,3},{4,20},{20... | collective-permute-start | bytes 1572872 | tf_op jit(solution)/shard_map/ppermute | solution.py:539
  7.3 1.2 %copy-start = (bf16[2,8,16,8,256]{4,3,2,1,0:T(8,128)(2,1)S(1)}, bf16[2,8,16,8,256]{4,3,2,1,0:T(8,128)(2,1)}, u32[]{:S(2)}) copy-start(bf16[2,8,16,8,256]{4,3,2,1,0:T(8,128)(2,1)} %param.7) | copy-start | bytes 3145732
  8.5 0.9 %copy-start.4 = (bf16[256,256]{1,0:T(8,128)(2,1)S(1)}, bf16[256,256]{1,0:T(8,128)(2,1)}, u32[]{:S(2)}) copy-start(bf16[256,256]{1,0:T(8,128)(2,1)} %wc.1) | copy-start | bytes 393220
  9.4 0.7 copy-start.5
  10.1 9.3 %copy-start.1 = (bf16[2,8,16,8,256]{4,3,2,1,0:T(8,128)(2,1)S(1)}, bf16[2,8,16,8,256]{4,3,2,1,0:T(8,128)(2,1)}, u32[]{:S(2)}) copy-start(bf16[2,8,16,8,256]{4,3,2,1,0:T(8,128)(2,1)} %param.7) | copy-start | bytes 3145732
  19.4 4.3 %collective-permute-start.1 = (bf16[1024,256]{1,0:T(8,128)(2,1)}, bf16[1024,256]{1,0:T(8,128)(2,1)}, u32[]{:S(2)}, u32[]{:S(2)}) collective-permute-start(bf16[1024,256]{1,0:T(8,128)(2,1)} %dynamic-slice_convert_fusion), channel_id=1, source_target_pairs={{0,1},{1,0},{2,3},{3,2},{4,5},{5,4},{6,7},{7,6},{8,9},{9,8},{10,11... | collective-permute-start | bytes 1572872 | tf_op jit(solution)/shard_map/ppermute | solution.py:444
  19.4 4.0 %collective-permute-start.2 = (bf16[1,8,16,128]{3,2,1,0:T(8,128)(2,1)S(1)}, bf16[1,8,16,128]{3,2,1,0:T(8,128)(2,1)S(1)}, u32[]{:S(2)}, u32[]{:S(2)}) collective-permute-start(bf16[1,8,16,128]{3,2,1,0:T(8,128)(2,1)S(1)} %slice.41), channel_id=1, source_target_pairs={{0,16},{16,0},{1,17},{17,1},{2,18},{18,2},{3,19},{19,3},{4,20},{20... | collective-permute-start | bytes 98312 | tf_op jit(solution)/shard_map/ppermute | solution.py:539
  19.7 7.0 %copy-start.3 = (bf16[8,256,256]{2,1,0:T(8,128)(2,1)S(1)}, bf16[8,256,256]{2,1,0:T(8,128)(2,1)}, u32[]{:S(2)}) copy-start(bf16[8,256,256]{2,1,0:T(8,128)(2,1)} %param.11) | copy-start | bytes 3145732
  23.4 19.6 %collective-permute-start.7 = (bf16[1,8,144,256]{3,2,1,0:T(8,128)(2,1)}, bf16[1,8,144,256]{3,2,1,0:T(8,128)(2,1)S(1)}, u32[]{:S(2)}, u32[]{:S(2)}) collective-permute-start(bf16[1,8,144,256]{3,2,1,0:T(8,128)(2,1)} %get-tuple-element.112), channel_id=1, source_target_pairs={{16,0},{0,16},{17,1},{1,17},{18,2},{2,18},{19,3},{3,19},{20,4},{4,... | collective-permute-start | bytes 1769480 | tf_op jit(solution)/shard_map/ppermute | solution.py:545
  24.9 7.4 %collective-permute-start.3 = (bf16[512,256]{1,0:T(8,128)(2,1)S(1)}, bf16[512,256]{1,0:T(8,128)(2,1)S(1)}, u32[]{:S(2)}, u32[]{:S(2)}) collective-permute-start(bf16[512,256]{1,0:T(8,128)(2,1)S(1)} %dynamic-slice_convert_fusion.1), channel_id=1, source_target_pairs={{0,2},{1,3},{2,0},{3,1},{4,6},{5,7},{6,4},{7,5},{8,10},{9,11},{10,... | collective-permute-start | bytes 786440 | tf_op jit(solution)/shard_map/ppermute | solution.py:444
  32.4 7.4 %collective-permute-start.4 = (bf16[128,256]{1,0:T(8,128)(2,1)S(1)}, bf16[128,256]{1,0:T(8,128)(2,1)S(1)}, u32[]{:S(2)}, u32[]{:S(2)}) collective-permute-start(bf16[128,256]{1,0:T(8,128)(2,1)S(1)} %get-tuple-element.99), channel_id=1, source_target_pairs={{0,4},{1,5},{2,6},{3,7},{4,0},{5,1},{6,2},{7,3},{8,12},{9,13},{10,... | collective-permute-start | bytes 196616 | tf_op jit(solution)/shard_map/ppermute | solution.py:444
  34.3 6.6 %collective-permute-start.5 = (bf16[128,256]{1,0:T(8,128)(2,1)S(1)}, bf16[128,256]{1,0:T(8,128)(2,1)S(1)}, u32[]{:S(2)}, u32[]{:S(2)}) collective-permute-start(bf16[128,256]{1,0:T(8,128)(2,1)S(1)} %get-tuple-element.100), channel_id=1, source_target_pairs={{0,8},{1,9},{2,10},{3,11},{4,12},{5,13},{6,14},{7,15},{8,0},{9,1},... | collective-permute-start | bytes 196616 | tf_op jit(solution)/shard_map/ppermute | solution.py:444
  36.9 6.1 %collective-permute-start.6 = (bf16[128,256]{1,0:T(8,128)(2,1)S(1)}, bf16[128,256]{1,0:T(8,128)(2,1)S(1)}, u32[]{:S(2)}, u32[]{:S(2)}) collective-permute-start(bf16[128,256]{1,0:T(8,128)(2,1)S(1)} %get-tuple-element.101), channel_id=1, source_target_pairs={{0,12},{1,13},{2,14},{3,15},{4,8},{5,9},{6,10},{7,11},{8,4},{9,5},... | collective-permute-start | bytes 196616 | tf_op jit(solution)/shard_map/ppermute | solution.py:444
  43.0 6.4 %copy-start.6 = (bf16[1,8,144,256]{3,2,1,0:T(8,128)(2,1)}, bf16[1,8,144,256]{3,2,1,0:T(8,128)(2,1)S(1)}, u32[]{:S(2)}) copy-start(bf16[1,8,144,256]{3,2,1,0:T(8,128)(2,1)S(1)} %collective-permute-done.7.rest_0_) | copy-start | bytes 1769476
  43.0 10.4 %collective-permute-start.8 = (bf16[128,256]{1,0:T(8,128)(2,1)S(1)}, bf16[128,256]{1,0:T(8,128)(2,1)S(1)}, u32[]{:S(2)}, u32[]{:S(2)}) collective-permute-start(bf16[128,256]{1,0:T(8,128)(2,1)S(1)} %convert_element_type.78), channel_id=1, source_target_pairs={{0,16},{1,17},{2,18},{3,19},{4,20},{5,21},{6,22},{7,23},{8,24},{9,... | collective-permute-start | bytes 196616 | tf_op jit(solution)/shard_map/ppermute | solution.py:444
  44.6 16.4 %collective-permute-start.12 = (bf16[4,1,144,256]{3,2,1,0:T(8,128)(2,1)S(1)}, bf16[4,1,144,256]{3,2,1,0:T(8,128)(2,1)S(1)}, u32[]{:S(2)}, u32[]{:S(2)}) collective-permute-start(bf16[4,1,144,256]{3,2,1,0:T(8,128)(2,1)S(1)} %fusion.12), channel_id=1, source_target_pairs={{0,1},{1,2},{2,3},{3,4},{4,5},{5,6},{6,7},{7,8},{8,9},{9,10},{10,1... | collective-permute-start | bytes 884744 | tf_op jit(solution)/shard_map/ppermute | solution.py:539
  44.7 16.3 %collective-permute-start.13 = (bf16[4,1,144,256]{3,2,1,0:T(8,128)(2,1)S(1)}, bf16[4,1,144,256]{3,2,1,0:T(8,128)(2,1)S(1)}, u32[]{:S(2)}, u32[]{:S(2)}) collective-permute-start(bf16[4,1,144,256]{3,2,1,0:T(8,128)(2,1)S(1)} %fusion.16), channel_id=1, source_target_pairs={{1,0},{2,1},{3,2},{4,3},{5,4},{6,5},{7,6},{8,7},{9,8},{10,9},{11,1... | collective-permute-start | bytes 884744 | tf_op jit(solution)/shard_map/ppermute | solution.py:545
  53.4 7.4 %collective-permute-start.9 = (bf16[128,256]{1,0:T(8,128)(2,1)S(1)}, bf16[128,256]{1,0:T(8,128)(2,1)S(1)}, u32[]{:S(2)}, u32[]{:S(2)}) collective-permute-start(bf16[128,256]{1,0:T(8,128)(2,1)S(1)} %add_convert_fusion), channel_id=1, source_target_pairs={{0,4},{1,5},{2,6},{3,7},{4,0},{5,1},{6,2},{7,3},{8,12},{9,13},{10,... | collective-permute-start | bytes 196616 | tf_op jit(solution)/shard_map/ppermute | solution.py:444
  53.5 7.3 %collective-permute-start.10 = (bf16[128,256]{1,0:T(8,128)(2,1)S(1)}, bf16[128,256]{1,0:T(8,128)(2,1)S(1)}, u32[]{:S(2)}, u32[]{:S(2)}) collective-permute-start(bf16[128,256]{1,0:T(8,128)(2,1)S(1)} %add_convert_fusion), channel_id=1, source_target_pairs={{0,8},{1,9},{2,10},{3,11},{4,12},{5,13},{6,14},{7,15},{8,0},{9,1},... | collective-permute-start | bytes 196616 | tf_op jit(solution)/shard_map/ppermute | solution.py:444
  53.6 7.3 %collective-permute-start.11 = (bf16[128,256]{1,0:T(8,128)(2,1)S(1)}, bf16[128,256]{1,0:T(8,128)(2,1)S(1)}, u32[]{:S(2)}, u32[]{:S(2)}) collective-permute-start(bf16[128,256]{1,0:T(8,128)(2,1)S(1)} %add_convert_fusion), channel_id=1, source_target_pairs={{0,12},{1,13},{2,14},{3,15},{4,8},{5,9},{6,10},{7,11},{8,4},{9,5},... | collective-permute-start | bytes 196616 | tf_op jit(solution)/shard_map/ppermute | solution.py:444
  61.0 6.4 %collective-permute-start.14 = (bf16[512,256]{1,0:T(8,128)(2,1)S(1)}, bf16[512,256]{1,0:T(8,128)(2,1)S(1)}, u32[]{:S(2)}, u32[]{:S(2)}) collective-permute-start(bf16[512,256]{1,0:T(8,128)(2,1)S(1)} %bitcast.55), channel_id=1, source_target_pairs={{0,2},{1,3},{2,0},{3,1},{4,6},{5,7},{6,4},{7,5},{8,10},{9,11},{10,... | collective-permute-start | bytes 786440 | tf_op jit(solution)/shard_map/ppermute | solution.py:444
  64.6 6.7 %copy-start.2 = (bf16[256,256]{1,0:T(8,128)(2,1)S(1)}, bf16[256,256]{1,0:T(8,128)(2,1)}, u32[]{:S(2)}) copy-start(bf16[256,256]{1,0:T(8,128)(2,1)} %w_out.1) | copy-start | bytes 393220
  67.7 2.1 %collective-permute-start.15 = (bf16[1024,256]{1,0:T(8,128)(2,1)S(1)}, bf16[1024,256]{1,0:T(8,128)(2,1)}, u32[]{:S(2)}, u32[]{:S(2)}) collective-permute-start(bf16[1024,256]{1,0:T(8,128)(2,1)S(1)} %maximum_select_fusion.1), channel_id=1, source_target_pairs={{0,1},{1,0},{2,3},{3,2},{4,5},{5,4},{6,7},{7,6},{8,9},{9,8},{10,11... | collective-permute-start | bytes 1572872 | tf_op jit(solution)/shard_map/ppermute | solution.py:444

commit v7 on v5

--- a/solution.py
+++ b/solution.py
@@ -47,11 +47,34 @@
     return value
 
 
-def factor_kernel(grid_all, scale_all, pos, kidx, feat, wc, ph_out, fac, head_out, ph, head, charges, where_at, sems):
+def factor_kernel(grid_all, scale_all, pos, kidx_in, feat_in, wc_in, ph_out, fac, head_out, kidx, feat, wc, ph, head, charges, where_at, sems):
     planes, cols, _, rows = pos.shape
     steps = ph.shape[0]
     atoms, width = feat.shape
-
+    loads = [
+        pltpu.make_async_copy(kidx_in, kidx, sems.at[steps + 2]),
+        pltpu.make_async_copy(feat_in, feat, sems.at[steps + 3]),
+        pltpu.make_async_copy(wc_in, wc, sems.at[steps + 4]),
+    ]
+    for load in loads:
+        load.start()
+
+    for y in range(cols):
+        head[0, y, :, 0:rows] = pos[0, y]
+        head[0, y, :, rows:width] = pos[0, y]
+    sub = lax.broadcasted_iota(jnp.int32, (POS_ROWS, rows), 0)
+    depth = (lax.broadcasted_iota(jnp.int32, (POS_ROWS, rows), 1) // 8).astype(F32)
+    x0 = (lax.axis_index("gx") * planes).astype(F32)
+    y0 = (lax.axis_index("gy") * cols).astype(F32)
+    for x in range(planes):
+        for y in range(cols):
+            j = (x * cols + y) * rows
+            tile = pos[x, y].astype(F32)
+            tile = jnp.where(sub == CELL_ROW, x0 + float(x), tile)
+            tile = jnp.where(sub == CELL_ROW + 1, y0 + float(y), tile)
+            tile = jnp.where(sub == CELL_ROW + 2, depth, tile)
+            where_at[j : j + rows, :] = tile.T.astype(BF16)
+    loads[0].wait()
     sub = lax.broadcasted_iota(jnp.int32, (POS_ROWS, KTILE), 0)
     kmat, screened = [], []
     for step in range(steps):
@@ -66,24 +89,21 @@
         screened.append(jnp.exp(-k_sq / (4.0 * SCREEN)) / k_sq)
     total = sum(jnp.sum(part, axis=1, keepdims=True) for part in screened)
 
-    sub = lax.broadcasted_iota(jnp.int32, (POS_ROWS, rows), 0)
-    depth = (lax.broadcasted_iota(jnp.int32, (POS_ROWS, rows), 1) // 8).astype(F32)
-    x0 = (lax.axis_index("gx") * planes).astype(F32)
-    y0 = (lax.axis_index("gy") * cols).astype(F32)
-    for x in range(planes):
-        for y in range(cols):
-            j = (x * cols + y) * rows
-            tile = pos[x, y].astype(F32)
-            tile = jnp.where(sub == CELL_ROW, x0 + float(x), tile)
-            tile = jnp.where(sub == CELL_ROW + 1, y0 + float(y), tile)
-            tile = jnp.where(sub == CELL_ROW + 2, depth, tile)
-            where_at[j : j + rows, :] = tile.T.astype(BF16)
+    loads[1].wait()
+    loads[2].wait()
+    copies = [
+        pltpu.make_async_copy(head, head_out.at[:, :, pl.ds(rows, POS_ROWS), :], sems.at[steps]),
+    ]
     for y in range(cols):
-        head[0, y, 0:rows, :] = feat[y * rows : (y + 1) * rows, :]
-        head[0, y, rows : rows + POS_ROWS, 0:rows] = pos[0, y]
-        head[0, y, rows : rows + POS_ROWS, rows:width] = pos[0, y]
-    copies = [pltpu.make_async_copy(head, head_out, sems.at[steps])]
-    copies[0].start()
+        copies.append(
+            pltpu.make_async_copy(
+                feat.at[pl.ds(y * rows, rows), :],
+                head_out.at[0, y, pl.ds(0, rows), :],
+                sems.at[steps + 5 + y],
+            )
+        )
+    for copy in copies:
+        copy.start()
     turned = wc[...].T
 
     size = 2 * rows
@@ -142,7 +162,7 @@
     head = (1, cols, rows + POS_ROWS, width)
     return pl.pallas_call(
         functools.partial(factor_kernel, grid_all, scale_all),
-        in_specs=[whole] * 4,
+        in_specs=[whole] + [in_hbm] * 3,
         out_specs=[in_hbm, whole, in_hbm],
         out_shape=[
             pltpu.HBM(phases, BF16),
@@ -150,18 +170,24 @@
             pltpu.HBM(head, BF16),
         ],
         scratch_shapes=[
+            VMEM(kidx.shape, jnp.int32),
+            VMEM(feat.shape, BF16),
+            VMEM(wc.shape, BF16),
             VMEM(phases, BF16),
-            VMEM(head, BF16),
+            VMEM((1, cols, POS_ROWS, width), BF16),
             VMEM((width, atoms), BF16),
             VMEM((atoms, POS_ROWS), BF16),
-            pltpu.SemaphoreType.DMA((steps + 1,)),
+            pltpu.SemaphoreType.DMA((steps + 5 + cols,)),
         ],
         compiler_params=pltpu.CompilerParams(vmem_limit_bytes=24 << 20),
         cost_estimate=pl.CostEstimate(
             flops=24 * atoms * vectors * width, bytes_accessed=4 << 20, transcendentals=0
         ),
         name="factor",
-    )(*pinned(pos, kidx, feat, wc))
+    )(
+        *pinned(pos),
+        *[pltpu.with_memory_space_constraint(value, pltpu.HBM) for value in (kidx, feat, wc)],
+    )
 
 
 def aggregate_row(slots, basis, near_feat, near_pos, own_pos, write):
@@ -580,12 +606,13 @@
         ],
         axis=2,
     )
+    pos_before = from_before(pos, "gx", 0)
+
     ph, partial, head = factor_call(
         pos, k_index.T, feat.reshape(atoms, width), w_charge, grid_all, scale_all
     )
-    partial, before, pos_late = tied(partial, before, pos)
+    partial, before, pos_before = tied(partial, before, pos_before)
     after = from_after(head, "gx", 0)
-    pos_before = from_before(pos_late, "gx", 0)
 
     w_flat = w_short.reshape(basis * width, width)
     exchange = Exchange()

time: 92.1 us -> 79.3 us (0.86)
  waiting for transfers between devices: 22.9 us -> 10.9 us
  local copies, waits for them, and re-layouts: 9.87 us -> 7.04 us
  Pallas kernels: 33.9 us -> 35.2 us
    ppermute x3, waiting for transfers between devices: 13.3 us -> 0.64 us  [from_before(): lax.ppermute(tail, axis, [(i, (i + 1) % count) for i in range(count)])]
    unnamed x12 -> x6, local copies, waits for them, and re-layouts: 2.85 us -> 0.02 us
    ppermute x3, starting transfers between devices: 4.85 us -> 3.07 us  [from_before(): lax.ppermute(tail, axis, [(i, (i + 1) % count) for i in range(count)])]
    ppermute x2, starting transfers between devices: 4.89 us -> 6.4 us  [from_after(): lax.ppermute(head, axis, [((i + 1) % count, i) for i in range(count)])]
    ppermute x11, starting transfers between devices: 11.2 us -> 12.4 us  [swap(): return lax.ppermute(value, AXES, [(i, i ^ mask) for i in range(count)])]
    pallas_call x1, Pallas kernels: 8.37 us -> 9.59 us  [factor_call(): pl.pallas_call(functools.partial(factor_kernel, grid_all, scale_all), in_...]
  transfers between devices with their start and end apart: 16 -> 16, of which waited for: 7 -> 7; matrix products, arithmetic and copies ran while one was open for 5% -> 6% of each run, Pallas kernels for 28% -> 34%
where the time goes in v7:
time: 79.3 us; the launch traced here: 78.8 us
  Pallas kernels  35.2 us (44%)
  starting transfers between devices  21.9 us (28%)
  waiting for transfers between devices  10.9 us (14%)
  local copies, waits for them, and re-layouts  7.04 us (9%)
  other arithmetic  3.26 us (4%)
    pallas_call x6, Pallas kernels, short_call(): pl.pallas_call(kernel, in_specs=in_specs, out_specs=out_specs, out_shape=...  17.2 us
    ppermute x11, starting transfers between devices, swap(): return lax.ppermute(value, AXES, [(i, i ^ mask) for i in range(count)])  12.4 us
    ppermute x11, waiting for transfers between devices, swap(): return lax.ppermute(value, AXES, [(i, i ^ mask) for i in range(count)])  10.3 us
    pallas_call x1, Pallas kernels, factor_call(): pl.pallas_call(functools.partial(factor_kernel, grid_all, scale_all), in_...  9.59 us
    pallas_call x1, Pallas kernels, field_call(): pl.pallas_call(field_kernel, in_specs=[pl.BlockSpec(memory_space=pltpu.HB...  8.33 us
    ppermute x2, starting transfers between devices, from_after(): lax.ppermute(head, axis, [((i + 1) % count, i) for i in range(count)])  6.4 us
    ppermute x3, starting transfers between devices, from_before(): lax.ppermute(tail, axis, [(i, (i + 1) % count) for i in range(count)])  3.07 us
    slice x2, local copies, waits for them, and re-layouts, from_before(): tail = lax.slice_in_dim(cells, size - 1, size, axis=dim)  1.95 us
  transfers between devices with their start and end apart: 16, of which 7 were waited for; matrix products, arithmetic and copies ran while one was open for 6% of the time, Pallas kernels for 34%

profile of v7, /device:TPU:0, one launch (start us, length us, event | category | flops | bytes accessed | tf_op | source)
XLA Modules:
  0.0 78.8 jit_solution(4414605142427826587)
XLA Ops:
  0.0 1.9 %slice_bitcast_fusion = bf16[1,8,128,256]{3,2,1,0:T(8,128)(2,1)} fusion(bf16[2,8,16,8,256]{4,3,2,1,0:T(8,128)(2,1)} %param.7), kind=kLoop, calls=%fused_computation.15 | loop fusion | bytes 1048576 | tf_op jit(solution)/shard_map/slice | solution.py:564
  1.9 2.9 %collective-permute-start = (bf16[1,8,128,256]{3,2,1,0:T(8,128)(2,1)}, bf16[1,8,128,256]{3,2,1,0:T(8,128)(2,1)}, u32[]{:S(2)}, u32[]{:S(2)}) collective-permute-start(bf16[1,8,128,256]{3,2,1,0:T(8,128)(2,1)} %slice_bitcast_fusion), channel_id=1, source_target_pairs={{0,16},{16,0},{1,17},{17,1},{2,18},{18,2},{3,19},{19,3},{4,20},{20... | collective-permute-start | bytes 1572872 | tf_op jit(solution)/shard_map/ppermute | solution.py:565
  7.5 9.6 %factor.1 = (bf16[4,2,2048,256]{3,2,1,0:T(8,128)(2,1)}, f32[2048,256]{1,0:T(8,128)S(1)}, bf16[1,8,144,256]{3,2,1,0:T(8,128)(2,1)}) custom-call(bf16[2,8,16,128]{3,2,1,0:T(8,128)(2,1)S(1)} %maximum_maximum_fusion.pos, s32[3,1024]{1,0:T(4,128)} %bitcast.63, bf16[2048,256]{1,0:T(8,128)(2,1)} %bitcast.37, bf16[256,256]{1,0:T(8,128)(2,1)} %wc_in.1), custom_call_target="tpu_custom_call" | custom-call | flops 12884901888 | bytes 4194304 | tf_op jit(solution)/shard_map/factor/pallas_call | solution.py:163
  18.6 1.7 %collective-permute-start.7 = (bf16[1,8,144,256]{3,2,1,0:T(8,128)(2,1)}, bf16[1,8,144,256]{3,2,1,0:T(8,128)(2,1)}, u32[]{:S(2)}, u32[]{:S(2)}) collective-permute-start(bf16[1,8,144,256]{3,2,1,0:T(8,128)(2,1)} %get-tuple-element.108), channel_id=1, source_target_pairs={{16,0},{0,16},{17,1},{1,17},{18,2},{2,18},{19,3},{3,19},{20,4},{4,... | collective-permute-start | bytes 1769480 | tf_op jit(solution)/shard_map/ppermute | solution.py:571
  20.8 1.1 %convert_add_fusion = f32[1024,256]{1,0:T(8,128)S(1)} fusion(bf16[1024,256]{1,0:T(8,128)(2,1)} %collective-permute-done.2, f32[2048,256]{1,0:T(8,128)S(1)} %get-tuple-element.78, s32[]{:T(128)S(6)} %select_n.114), kind=kLoop, calls=%fused_computation.1 | loop fusion | flops 524288 | bytes 2621444 | tf_op jit(solution)/shard_map/add | solution.py:503
  22.0 1.8 %collective-permute-start.3 = (bf16[512,256]{1,0:T(8,128)(2,1)S(1)}, bf16[512,256]{1,0:T(8,128)(2,1)S(1)}, u32[]{:S(2)}, u32[]{:S(2)}) collective-permute-start(bf16[512,256]{1,0:T(8,128)(2,1)S(1)} %dynamic-slice_convert_fusion.1), channel_id=1, source_target_pairs={{0,2},{1,3},{2,0},{3,1},{4,6},{5,7},{6,4},{7,5},{8,10},{9,11},{10,... | collective-permute-start | bytes 786440 | tf_op jit(solution)/shard_map/ppermute | solution.py:470
  23.8 4.0 %plane.4 = (f32[8,2,128,256]{3,2,1,0:T(8,128)S(1)}, bf16[1,8,128,256]{3,2,1,0:T(8,128)(2,1)S(1)}) custom-call(bf16[2,8,128,256]{3,2,1,0:T(8,128)(2,1)S(1)} %bitcast.39, bf16[2,8,16,128]{3,2,1,0:T(8,128)(2,1)S(1)} %maximum_maximum_fusion.pos, bf16[2048,256]{1,0:T(8,128)(2,1)S(1)} %bitcast.45, bf16[1,8,128,256]{3,2,1,0:T(8,128)(2,1)} %collective-permute-done.rest_0_, ...), custom_call_target="tpu_custom_call" | custom-call | flops 4026531840 | bytes 4194304 | tf_op jit(solution)/shard_map/plane/pallas_call | solution.py:384
  28.7 1.7 %collective-permute-done.3 = bf16[512,256]{1,0:T(8,128)(2,1)S(1)} collective-permute-done((bf16[512,256]{1,0:T(8,128)(2,1)S(1)}, bf16[512,256]{1,0:T(8,128)(2,1)S(1)}, u32[]{:S(2)}, u32[]{:S(2)}) %collective-permute-start.3) | collective-permute-done | bytes 262176 | tf_op jit(solution)/shard_map/ppermute | solution.py:470
  30.5 1.9 %collective-permute-start.4 = (bf16[128,256]{1,0:T(8,128)(2,1)S(1)}, bf16[128,256]{1,0:T(8,128)(2,1)S(1)}, u32[]{:S(2)}, u32[]{:S(2)}) collective-permute-start(bf16[128,256]{1,0:T(8,128)(2,1)S(1)} %get-tuple-element.95), channel_id=1, source_target_pairs={{0,4},{1,5},{2,6},{3,7},{4,0},{5,1},{6,2},{7,3},{8,12},{9,13},{10,... | collective-permute-start | bytes 196616 | tf_op jit(solution)/shard_map/ppermute | solution.py:470
  32.4 2.6 %collective-permute-start.5 = (bf16[128,256]{1,0:T(8,128)(2,1)S(1)}, bf16[128,256]{1,0:T(8,128)(2,1)S(1)}, u32[]{:S(2)}, u32[]{:S(2)}) collective-permute-start(bf16[128,256]{1,0:T(8,128)(2,1)S(1)} %get-tuple-element.96), channel_id=1, source_target_pairs={{0,8},{1,9},{2,10},{3,11},{4,12},{5,13},{6,14},{7,15},{8,0},{9,1},... | collective-permute-start | bytes 196616 | tf_op jit(solution)/shard_map/ppermute | solution.py:470
  35.0 2.9 %plane.5.rest_1_ = f32[8,2,128,256]{3,2,1,0:T(8,128)S(1)} custom-call(bf16[2,8,128,256]{3,2,1,0:T(8,128)(2,1)S(1)} %bitcast.40, bf16[2,8,16,128]{3,2,1,0:T(8,128)(2,1)S(1)} %maximum_maximum_fusion.pos, bf16[2048,256]{1,0:T(8,128)(2,1)S(1)} %bitcast.46, ...), custom_call_target="tpu_custom_call", output_to_operand_aliasing={{}: (5, {})} | custom-call | flops 4026531840 | bytes 4194304 | tf_op jit(solution)/shard_map/plane/pallas_call | solution.py:384
  37.9 1.3 %collective-permute-done.5 = bf16[128,256]{1,0:T(8,128)(2,1)S(1)} collective-permute-done((bf16[128,256]{1,0:T(8,128)(2,1)S(1)}, bf16[128,256]{1,0:T(8,128)(2,1)S(1)}, u32[]{:S(2)}, u32[]{:S(2)}) %collective-permute-start.5) | collective-permute-done | bytes 65568 | tf_op jit(solution)/shard_map/ppermute | solution.py:470
  39.3 1.8 %collective-permute-done.6 = bf16[128,256]{1,0:T(8,128)(2,1)S(1)} collective-permute-done((bf16[128,256]{1,0:T(8,128)(2,1)S(1)}, bf16[128,256]{1,0:T(8,128)(2,1)S(1)}, u32[]{:S(2)}, u32[]{:S(2)}) %collective-permute-start.6) | collective-permute-done | bytes 65568 | tf_op jit(solution)/shard_map/ppermute | solution.py:470
  42.1 1.6 %collective-permute-start.8 = (bf16[128,256]{1,0:T(8,128)(2,1)S(1)}, bf16[128,256]{1,0:T(8,128)(2,1)S(1)}, u32[]{:S(2)}, u32[]{:S(2)}) collective-permute-start(bf16[128,256]{1,0:T(8,128)(2,1)S(1)} %convert_element_type.78), channel_id=1, source_target_pairs={{0,16},{1,17},{2,18},{3,19},{4,20},{5,21},{6,22},{7,23},{8,24},{9,... | collective-permute-start | bytes 196616 | tf_op jit(solution)/shard_map/ppermute | solution.py:470
  43.7 4.7 %collective-permute-start.13 = (bf16[4,1,144,256]{3,2,1,0:T(8,128)(2,1)S(1)}, bf16[4,1,144,256]{3,2,1,0:T(8,128)(2,1)S(1)}, u32[]{:S(2)}, u32[]{:S(2)}) collective-permute-start(bf16[4,1,144,256]{3,2,1,0:T(8,128)(2,1)S(1)} %fusion.16), channel_id=1, source_target_pairs={{1,0},{2,1},{3,2},{4,3},{5,4},{6,5},{7,6},{8,7},{9,8},{10,9},{11,1... | collective-permute-start | bytes 884744 | tf_op jit(solution)/shard_map/ppermute | solution.py:571
  48.4 4.0 %plane.6 = (f32[8,2,128,256]{3,2,1,0:T(8,128)S(1)}, bf16[1,8,144,256]{3,2,1,0:T(8,128)(2,1)S(1)}) custom-call(bf16[2,8,128,256]{3,2,1,0:T(8,128)(2,1)S(1)} %bitcast.41, bf16[2,8,16,128]{3,2,1,0:T(8,128)(2,1)S(1)} %maximum_maximum_fusion.pos, bf16[2048,256]{1,0:T(8,128)(2,1)S(1)} %bitcast.47, ...), custom_call_target="tpu_custom_call", output_to_operand_aliasing={{0}: (4, {})} | custom-call | flops 4026531840 | bytes 4194304 | tf_op jit(solution)/shard_map/plane/pallas_call | solution.py:384
  52.6 4.3 %collective-permute-start.11 = (bf16[128,256]{1,0:T(8,128)(2,1)S(1)}, bf16[128,256]{1,0:T(8,128)(2,1)S(1)}, u32[]{:S(2)}, u32[]{:S(2)}) collective-permute-start(bf16[128,256]{1,0:T(8,128)(2,1)S(1)} %add_convert_fusion), channel_id=1, source_target_pairs={{0,12},{1,13},{2,14},{3,15},{4,8},{5,9},{6,10},{7,11},{8,4},{9,5},... | collective-permute-start | bytes 196616 | tf_op jit(solution)/shard_map/ppermute | solution.py:470
  56.9 2.9 %plane.7.rest_0_ = f32[8,2,128,256]{3,2,1,0:T(8,128)S(1)} custom-call(bf16[2,8,128,256]{3,2,1,0:T(8,128)(2,1)S(1)} %bitcast.42, bf16[2,8,16,128]{3,2,1,0:T(8,128)(2,1)S(1)} %maximum_maximum_fusion.pos, bf16[2048,256]{1,0:T(8,128)(2,1)S(1)} %bitcast.48, bf16[1,8,144,256]{3,2,1,0:T(8,128)(2,1)S(1)} %get-tuple-element.141.rest_0_.after, ...), custom_call_target="tpu_custom_call", output_to_operand_aliasing={{}: (4, {})} | custom-call | flops 4026531840 | bytes 4194304 | tf_op jit(solution)/shard_map/plane/pallas_call | solution.py:384
  60.1 1.7 %low.1.rest_0_ = f32[8,2,128,256]{3,2,1,0:T(8,128)S(1)} custom-call(bf16[2,8,128,256]{3,2,1,0:T(8,128)(2,1)S(1)} %bitcast.43, bf16[2,8,16,128]{3,2,1,0:T(8,128)(2,1)S(1)} %maximum_maximum_fusion.pos, bf16[2048,256]{1,0:T(8,128)(2,1)S(1)} %bitcast.49, bf16[1,8,128,256]{3,2,1,0:T(8,128)(2,1)S(1)} %get-tuple-element.139.rest_0_.before, ...), custom_call_target="tpu_custom_call", output_to_operand_aliasing={{}: (7, {})} | custom-call | flops 2684354560 | bytes 4194304 | tf_op jit(solution)/shard_map/low/pallas_call | solution.py:384
  61.8 1.7 %high.1.base = f32[8,2,128,256]{3,2,1,0:T(8,128)S(1)} custom-call(bf16[2,8,128,256]{3,2,1,0:T(8,128)(2,1)S(1)} %bitcast.44, bf16[2,8,16,128]{3,2,1,0:T(8,128)(2,1)S(1)} %maximum_maximum_fusion.pos, bf16[2048,256]{1,0:T(8,128)(2,1)S(1)} %bitcast.50, bf16[1,8,128,256]{3,2,1,0:T(8,128)(2,1)S(1)} %get-tuple-element.139.rest_0_.before, ...), custom_call_target="tpu_custom_call", output_to_operand_aliasing={{}: (7, {})} | custom-call | flops 2684354560 | bytes 4194304 | tf_op jit(solution)/shard_map/high/pallas_call | solution.py:384
  63.6 2.9 %collective-permute-done.14 = bf16[512,256]{1,0:T(8,128)(2,1)S(1)} collective-permute-done((bf16[512,256]{1,0:T(8,128)(2,1)S(1)}, bf16[512,256]{1,0:T(8,128)(2,1)S(1)}, u32[]{:S(2)}, u32[]{:S(2)}) %collective-permute-start.14) | collective-permute-done | bytes 262176 | tf_op jit(solution)/shard_map/ppermute | solution.py:470
  66.8 2.0 %collective-permute-done.15 = bf16[1024,256]{1,0:T(8,128)(2,1)} collective-permute-done((bf16[1024,256]{1,0:T(8,128)(2,1)S(1)}, bf16[1024,256]{1,0:T(8,128)(2,1)}, u32[]{:S(2)}, u32[]{:S(2)}) %collective-permute-start.15) | collective-permute-done | bytes 524320 | tf_op jit(solution)/shard_map/ppermute | solution.py:470
  68.8 1.5 %maximum_select_fusion = bf16[2048,256]{1,0:T(8,128)(2,1)S(1)} fusion(bf16[1024,256]{1,0:T(8,128)(2,1)} %collective-permute-done.15, bf16[1024,256]{1,0:T(8,128)(2,1)S(1)} %maximum_select_fusion.1, pred[]{:T(512)S(6)} %eq.21), kind=kLoop, calls=%fused_computation | loop fusion | flops 4718592 | bytes 2097153 | tf_op jit(solution)/shard_map/jit(_where)/select_n | solution.py:537
  70.3 8.3 %field.1 = bf16[2048,256]{1,0:T(8,128)(2,1)} custom-call(bf16[4,2,2048,256]{3,2,1,0:T(8,128)(2,1)} %get-tuple-element.76.ph_all, bf16[8,256,256]{2,1,0:T(8,128)(2,1)S(1)} %bitcast.36, bf16[256,256]{1,0:T(8,128)(2,1)S(1)} %copy-done.1, f32[8,2,128,256]{3,2,1,0:T(8,128)S(1)} %high.1.base, bf16[2,8,16,128]{3,2,1,0:T(8,128)(2,1)S(1)} %maximum_maximum_fusion.pos), custom_call_target="tpu_custom_call" | custom-call | flops 2147483648 | bytes 4194304 | tf_op jit(solution)/shard_map/field/pallas_call | solution.py:444
  (55 shorter events, 7.3 us)
Async XLA Ops:
  1.9 15.8 %collective-permute-start = (bf16[1,8,128,256]{3,2,1,0:T(8,128)(2,1)}, bf16[1,8,128,256]{3,2,1,0:T(8,128)(2,1)}, u32[]{:S(2)}, u32[]{:S(2)}) collective-permute-start(bf16[1,8,128,256]{3,2,1,0:T(8,128)(2,1)} %slice_bitcast_fusion), channel_id=1, source_target_pairs={{0,16},{16,0},{1,17},{17,1},{2,18},{18,2},{3,19},{19,3},{4,20},{20... | collective-permute-start | bytes 1572872 | tf_op jit(solution)/shard_map/ppermute | solution.py:565
  7.4 10.3 %collective-permute-start.1 = (bf16[1,8,16,128]{3,2,1,0:T(8,128)(2,1)S(1)}, bf16[1,8,16,128]{3,2,1,0:T(8,128)(2,1)S(1)}, u32[]{:S(2)}, u32[]{:S(2)}) collective-permute-start(bf16[1,8,16,128]{3,2,1,0:T(8,128)(2,1)S(1)} %slice.52), channel_id=1, source_target_pairs={{0,16},{16,0},{1,17},{17,1},{2,18},{18,2},{3,19},{19,3},{4,20},{20... | collective-permute-start | bytes 98312 | tf_op jit(solution)/shard_map/ppermute | solution.py:565
  7.4 12.9 %copy-start = (bf16[2,8,16,8,256]{4,3,2,1,0:T(8,128)(2,1)S(1)}, bf16[2,8,16,8,256]{4,3,2,1,0:T(8,128)(2,1)}, u32[]{:S(2)}) copy-start(bf16[2,8,16,8,256]{4,3,2,1,0:T(8,128)(2,1)} %param.7) | copy-start | bytes 3145732
  18.6 2.3 %collective-permute-start.2 = (bf16[1024,256]{1,0:T(8,128)(2,1)}, bf16[1024,256]{1,0:T(8,128)(2,1)}, u32[]{:S(2)}, u32[]{:S(2)}) collective-permute-start(bf16[1024,256]{1,0:T(8,128)(2,1)} %dynamic-slice_convert_fusion), channel_id=1, source_target_pairs={{0,1},{1,0},{2,3},{3,2},{4,5},{5,4},{6,7},{7,6},{8,9},{9,8},{10,11... | collective-permute-start | bytes 1572872 | tf_op jit(solution)/shard_map/ppermute | solution.py:470
  18.6 22.5 %collective-permute-start.7 = (bf16[1,8,144,256]{3,2,1,0:T(8,128)(2,1)}, bf16[1,8,144,256]{3,2,1,0:T(8,128)(2,1)}, u32[]{:S(2)}, u32[]{:S(2)}) collective-permute-start(bf16[1,8,144,256]{3,2,1,0:T(8,128)(2,1)} %get-tuple-element.108), channel_id=1, source_target_pairs={{16,0},{0,16},{17,1},{1,17},{18,2},{2,18},{19,3},{3,19},{20,4},{4,... | collective-permute-start | bytes 1769480 | tf_op jit(solution)/shard_map/ppermute | solution.py:571
  20.3 3.5 %copy-start.2 = (bf16[8,256,256]{2,1,0:T(8,128)(2,1)S(1)}, bf16[8,256,256]{2,1,0:T(8,128)(2,1)}, u32[]{:S(2)}) copy-start(bf16[8,256,256]{2,1,0:T(8,128)(2,1)} %param.11) | copy-start | bytes 3145732
  22.0 8.4 %collective-permute-start.3 = (bf16[512,256]{1,0:T(8,128)(2,1)S(1)}, bf16[512,256]{1,0:T(8,128)(2,1)S(1)}, u32[]{:S(2)}, u32[]{:S(2)}) collective-permute-start(bf16[512,256]{1,0:T(8,128)(2,1)S(1)} %dynamic-slice_convert_fusion.1), channel_id=1, source_target_pairs={{0,2},{1,3},{2,0},{3,1},{4,6},{5,7},{6,4},{7,5},{8,10},{9,11},{10,... | collective-permute-start | bytes 786440 | tf_op jit(solution)/shard_map/ppermute | solution.py:470
  30.5 7.4 %collective-permute-start.4 = (bf16[128,256]{1,0:T(8,128)(2,1)S(1)}, bf16[128,256]{1,0:T(8,128)(2,1)S(1)}, u32[]{:S(2)}, u32[]{:S(2)}) collective-permute-start(bf16[128,256]{1,0:T(8,128)(2,1)S(1)} %get-tuple-element.95), channel_id=1, source_target_pairs={{0,4},{1,5},{2,6},{3,7},{4,0},{5,1},{6,2},{7,3},{8,12},{9,13},{10,... | collective-permute-start | bytes 196616 | tf_op jit(solution)/shard_map/ppermute | solution.py:470
  32.4 6.8 %collective-permute-start.5 = (bf16[128,256]{1,0:T(8,128)(2,1)S(1)}, bf16[128,256]{1,0:T(8,128)(2,1)S(1)}, u32[]{:S(2)}, u32[]{:S(2)}) collective-permute-start(bf16[128,256]{1,0:T(8,128)(2,1)S(1)} %get-tuple-element.96), channel_id=1, source_target_pairs={{0,8},{1,9},{2,10},{3,11},{4,12},{5,13},{6,14},{7,15},{8,0},{9,1},... | collective-permute-start | bytes 196616 | tf_op jit(solution)/shard_map/ppermute | solution.py:470
  35.0 6.1 %collective-permute-start.6 = (bf16[128,256]{1,0:T(8,128)(2,1)S(1)}, bf16[128,256]{1,0:T(8,128)(2,1)S(1)}, u32[]{:S(2)}, u32[]{:S(2)}) collective-permute-start(bf16[128,256]{1,0:T(8,128)(2,1)S(1)} %get-tuple-element.97), channel_id=1, source_target_pairs={{0,12},{1,13},{2,14},{3,15},{4,8},{5,9},{6,10},{7,11},{8,4},{9,5},... | collective-permute-start | bytes 196616 | tf_op jit(solution)/shard_map/ppermute | solution.py:470
  42.1 10.4 %collective-permute-start.8 = (bf16[128,256]{1,0:T(8,128)(2,1)S(1)}, bf16[128,256]{1,0:T(8,128)(2,1)S(1)}, u32[]{:S(2)}, u32[]{:S(2)}) collective-permute-start(bf16[128,256]{1,0:T(8,128)(2,1)S(1)} %convert_element_type.78), channel_id=1, source_target_pairs={{0,16},{1,17},{2,18},{3,19},{4,20},{5,21},{6,22},{7,23},{8,24},{9,... | collective-permute-start | bytes 196616 | tf_op jit(solution)/shard_map/ppermute | solution.py:470
  43.6 16.4 %collective-permute-start.12 = (bf16[4,1,144,256]{3,2,1,0:T(8,128)(2,1)S(1)}, bf16[4,1,144,256]{3,2,1,0:T(8,128)(2,1)S(1)}, u32[]{:S(2)}, u32[]{:S(2)}) collective-permute-start(bf16[4,1,144,256]{3,2,1,0:T(8,128)(2,1)S(1)} %fusion.12), channel_id=1, source_target_pairs={{0,1},{1,2},{2,3},{3,4},{4,5},{5,6},{6,7},{7,8},{8,9},{9,10},{10,1... | collective-permute-start | bytes 884744 | tf_op jit(solution)/shard_map/ppermute | solution.py:565
  43.7 16.3 %collective-permute-start.13 = (bf16[4,1,144,256]{3,2,1,0:T(8,128)(2,1)S(1)}, bf16[4,1,144,256]{3,2,1,0:T(8,128)(2,1)S(1)}, u32[]{:S(2)}, u32[]{:S(2)}) collective-permute-start(bf16[4,1,144,256]{3,2,1,0:T(8,128)(2,1)S(1)} %fusion.16), channel_id=1, source_target_pairs={{1,0},{2,1},{3,2},{4,3},{5,4},{6,5},{7,6},{8,7},{9,8},{10,9},{11,1... | collective-permute-start | bytes 884744 | tf_op jit(solution)/shard_map/ppermute | solution.py:571
  52.4 7.4 %collective-permute-start.9 = (bf16[128,256]{1,0:T(8,128)(2,1)S(1)}, bf16[128,256]{1,0:T(8,128)(2,1)S(1)}, u32[]{:S(2)}, u32[]{:S(2)}) collective-permute-start(bf16[128,256]{1,0:T(8,128)(2,1)S(1)} %add_convert_fusion), channel_id=1, source_target_pairs={{0,4},{1,5},{2,6},{3,7},{4,0},{5,1},{6,2},{7,3},{8,12},{9,13},{10,... | collective-permute-start | bytes 196616 | tf_op jit(solution)/shard_map/ppermute | solution.py:470
  52.5 7.3 %collective-permute-start.10 = (bf16[128,256]{1,0:T(8,128)(2,1)S(1)}, bf16[128,256]{1,0:T(8,128)(2,1)S(1)}, u32[]{:S(2)}, u32[]{:S(2)}) collective-permute-start(bf16[128,256]{1,0:T(8,128)(2,1)S(1)} %add_convert_fusion), channel_id=1, source_target_pairs={{0,8},{1,9},{2,10},{3,11},{4,12},{5,13},{6,14},{7,15},{8,0},{9,1},... | collective-permute-start | bytes 196616 | tf_op jit(solution)/shard_map/ppermute | solution.py:470
  52.6 7.2 %collective-permute-start.11 = (bf16[128,256]{1,0:T(8,128)(2,1)S(1)}, bf16[128,256]{1,0:T(8,128)(2,1)S(1)}, u32[]{:S(2)}, u32[]{:S(2)}) collective-permute-start(bf16[128,256]{1,0:T(8,128)(2,1)S(1)} %add_convert_fusion), channel_id=1, source_target_pairs={{0,12},{1,13},{2,14},{3,15},{4,8},{5,9},{6,10},{7,11},{8,4},{9,5},... | collective-permute-start | bytes 196616 | tf_op jit(solution)/shard_map/ppermute | solution.py:470
  60.0 6.4 %collective-permute-start.14 = (bf16[512,256]{1,0:T(8,128)(2,1)S(1)}, bf16[512,256]{1,0:T(8,128)(2,1)S(1)}, u32[]{:S(2)}, u32[]{:S(2)}) collective-permute-start(bf16[512,256]{1,0:T(8,128)(2,1)S(1)} %bitcast.54), channel_id=1, source_target_pairs={{0,2},{1,3},{2,0},{3,1},{4,6},{5,7},{6,4},{7,5},{8,10},{9,11},{10,... | collective-permute-start | bytes 786440 | tf_op jit(solution)/shard_map/ppermute | solution.py:470
  63.6 6.8 %copy-start.1 = (bf16[256,256]{1,0:T(8,128)(2,1)S(1)}, bf16[256,256]{1,0:T(8,128)(2,1)}, u32[]{:S(2)}) copy-start(bf16[256,256]{1,0:T(8,128)(2,1)} %w_out.1) | copy-start | bytes 393220
  66.7 2.1 %collective-permute-start.15 = (bf16[1024,256]{1,0:T(8,128)(2,1)S(1)}, bf16[1024,256]{1,0:T(8,128)(2,1)}, u32[]{:S(2)}, u32[]{:S(2)}) collective-permute-start(bf16[1024,256]{1,0:T(8,128)(2,1)S(1)} %maximum_select_fusion.1), channel_id=1, source_target_pairs={{0,1},{1,0},{2,3},{3,2},{4,5},{5,4},{6,7},{7,6},{8,9},{9,8},{10,11... | collective-permute-start | bytes 1572872 | tf_op jit(solution)/shard_map/ppermute | solution.py:470

commit v8 on v4

--- a/solution.py
+++ b/solution.py
@@ -337,33 +337,58 @@
     )(*pinned(*args))
 
 
-def field_kernel(ph_all, weighted, w_out, base, pos, out, ph, rhs, held, in_sems, out_sems):
-    tiles, width, _ = weighted.shape
-    cols, planes, rows, _ = base.shape
-    count, size, _ = held.shape
-    lines = size // rows
+def phase_loads(ph_all, ph, sems, half, lines):
+    size = ph.shape[2] // lines
     loads = []
-    for i in range(count):
+    for i in range(lines):
         part = pl.ds(size * i, size)
         load = pltpu.make_async_copy(
-            ph_all.at[:, :, part, :], ph.at[:, :, part, :], in_sems.at[i]
+            ph_all.at[pl.ds(half * ph.shape[0], ph.shape[0]), :, part, :],
+            ph.at[:, :, part, :],
+            sems.at[i],
         )
         load.start()
         loads.append(load)
+    return loads
+
+
+def half_field(ph, rhs, tiles, part):
+    lhs = jnp.concatenate([ph[t // 2, t % 2, part, :] for t in range(tiles)], axis=1)
+    return jnp.dot(lhs, rhs[...], preferred_element_type=F32)
+
+
+def near_field_kernel(lines, ph_all, weighted, out, ph, rhs, in_sems):
+    tiles = weighted.shape[0]
+    loads = phase_loads(ph_all, ph, in_sems, lax.rem(lax.axis_index("gy"), 2), lines)
+    for t in range(tiles):
+        rhs[t * KTILE : (t + 1) * KTILE, :] = weighted[t].T
+    size = ph.shape[2] // lines
+    for i in range(lines):
+        loads[i].wait()
+        part = slice(size * i, size * (i + 1))
+        out[part, :] = half_field(ph, rhs, tiles, part)
+
+
+def far_field_kernel(
+    lines, ph_all, weighted, partial, w_out, base, pos, out, ph, rhs, held, in_sems, out_sems
+):
+    tiles, width, _ = weighted.shape
+    cols, planes, rows, _ = base.shape
+    loads = phase_loads(ph_all, ph, in_sems, 1 - lax.rem(lax.axis_index("gy"), 2), lines)
     for t in range(tiles):
         rhs[t * KTILE : (t + 1) * KTILE, :] = weighted[t].T
     sub = lax.broadcasted_iota(jnp.int32, (POS_ROWS, width), 0)
     select = jnp.where(sub == OCC_ROW, 1.0, 0.0).astype(BF16)
+    size = ph.shape[2] // lines
+    each = size // rows
     stores = []
-    for i in range(count):
+    for i in range(lines):
         loads[i].wait()
-        lhs = jnp.concatenate(
-            [ph[t // 2, t % 2, size * i : size * (i + 1), :] for t in range(tiles)], axis=1
-        )
-        recip = jnp.dot(lhs, rhs[...], preferred_element_type=F32)
+        part = slice(size * i, size * (i + 1))
+        recip = partial[part, :] + half_field(ph, rhs, tiles, part)
         far = jnp.dot(recip.astype(BF16), w_out[...], preferred_element_type=F32)
-        for j in range(lines):
-            x, y = divmod(lines * i + j, cols)
+        for j in range(each):
+            x, y = divmod(each * i + j, cols)
             occ = lax.dot_general(pos[x, y], select, TN, preferred_element_type=F32)
             value = base[y, x] + far[rows * j : rows * (j + 1)]
             held[i, rows * j : rows * (j + 1), :] = jnp.where(occ > 0.0, value, 0.0).astype(BF16)
@@ -374,30 +399,29 @@
         store.wait()
 
 
-def field_call(ph, weighted, w_out, base, pos, lines=4):
-    atoms = ph.shape[2]
+def field_call(kernel, name, out_shape, extra, ph, weighted, *args, lines=4):
+    steps, _, atoms, _ = ph.shape
     tiles, width, _ = weighted.shape
-    cols, planes, rows, _ = base.shape
-    count = planes * cols // lines
     whole = pl.BlockSpec(memory_space=VMEM)
+    in_hbm = pl.BlockSpec(memory_space=pltpu.HBM)
     return pl.pallas_call(
-        field_kernel,
-        in_specs=[pl.BlockSpec(memory_space=pltpu.HBM)] + [whole] * 4,
-        out_specs=pl.BlockSpec(memory_space=pltpu.HBM),
-        out_shape=jax.ShapeDtypeStruct((atoms, width), BF16),
+        functools.partial(kernel, lines),
+        in_specs=[in_hbm] + [whole] * (1 + len(args)),
+        out_specs=in_hbm if extra else whole,
+        out_shape=out_shape,
         scratch_shapes=[
-            VMEM(ph.shape, BF16),
+            VMEM((steps // 2,) + ph.shape[1:], BF16),
             VMEM((tiles * KTILE, width), BF16),
-            VMEM((count, lines * rows, width), BF16),
-            pltpu.SemaphoreType.DMA((count,)),
-            pltpu.SemaphoreType.DMA((count,)),
+            *([VMEM((lines, atoms // lines, width), BF16)] if extra else []),
+            pltpu.SemaphoreType.DMA((lines,)),
+            *([pltpu.SemaphoreType.DMA((lines,))] if extra else []),
         ],
-        compiler_params=pltpu.CompilerParams(vmem_limit_bytes=24 << 20),
+        compiler_params=pltpu.CompilerParams(vmem_limit_bytes=16 << 20),
         cost_estimate=pl.CostEstimate(
-            flops=2 * atoms * tiles * KTILE * width, bytes_accessed=4 << 20, transcendentals=0
+            flops=4 * atoms * tiles * KTILE * width, bytes_accessed=4 << 20, transcendentals=0
         ),
-        name="field",
-    )(pltpu.with_memory_space_constraint(ph, pltpu.HBM), *pinned(weighted, w_out, base, pos))
+        name=name,
+    )(pltpu.with_memory_space_constraint(ph, pltpu.HBM), *pinned(weighted, *args))
 
 
 def my_index():
@@ -597,9 +621,27 @@
         exchange.halved[1],
         Work(edges, feat, pos, before, pos_before, after, pos_after, low, high, w_flat, base),
     )
-    value, _ = exchange.double(value, exchange.halved[0])
-    weighted = value.reshape(2 * vectors // KTILE, width, KTILE)
-    out = field_call(ph, weighted, w_out, base, pos)
+    assert exchange.halved[0] == 1 and (vectors // KTILE) % 2 == 0
+    half = (vectors // KTILE, width, KTILE)
+
+    def near_field(ph, value):
+        return field_call(
+            near_field_kernel, "near", VMEM((atoms, width), F32), False, ph, value.reshape(half)
+        )
+
+    (other,), partial = run_under([value], [exchange.halved[0]], Work(near_field, ph, value))
+    out = field_call(
+        far_field_kernel,
+        "far",
+        jax.ShapeDtypeStruct((atoms, width), BF16),
+        True,
+        ph,
+        other.reshape(half),
+        partial,
+        w_out,
+        base,
+        pos,
+    )
     return out.reshape(features.shape)
 
 

time: 77.3 us -> 75.4 us (0.975)
  waiting for transfers between devices: 12.4 us -> 10.4 us
  Pallas kernels: 35.9 us -> 37.5 us
  other arithmetic: 3.26 us -> 1.76 us
    ppermute x11, waiting for transfers between devices: 9.47 us -> 7.46 us  [swap(): return lax.ppermute(value, AXES, [(i, i ^ mask) for i in range(count)])]
    pallas_call x1 -> x2, Pallas kernels: 8.33 us -> 9.89 us  [field_call(): pl.pallas_call(functools.partial(kernel, lines), in_specs=[in_hbm] + [who...]
    select_n x2 -> x1, other arithmetic: 1.72 us -> 0.23 us  [double(): jnp.where(mine == 0, jnp.concatenate([value, other]), jnp.concatenate([ot...]
  transfers between devices with their start and end apart: 17 -> 17, of which waited for: 7 -> 6; matrix products, arithmetic and copies ran while one was open for 3% -> 3% of each run, Pallas kernels for 36% -> 42%
where the time goes in v8:
time: 75.4 us; the launch traced here: 74.9 us
  Pallas kernels  37.5 us (50%)
  starting transfers between devices  19.8 us (26%)
  waiting for transfers between devices  10.4 us (14%)
  local copies, waits for them, and re-layouts  4.96 us (7%)
  other arithmetic  1.76 us (2%)
    pallas_call x6, Pallas kernels, short_call(): pl.pallas_call(kernel, in_specs=[whole] * len(args), out_specs=whole, out...  19.3 us
    ppermute x11, starting transfers between devices, swap(): return lax.ppermute(value, AXES, [(i, i ^ mask) for i in range(count)])  12.2 us
    pallas_call x2, Pallas kernels, field_call(): pl.pallas_call(functools.partial(kernel, lines), in_specs=[in_hbm] + [who...  9.89 us
    pallas_call x1, Pallas kernels, factor_call(): pl.pallas_call(functools.partial(factor_kernel, grid_all, scale_all), in_...  8.33 us
    ppermute x11, waiting for transfers between devices, swap(): return lax.ppermute(value, AXES, [(i, i ^ mask) for i in range(count)])  7.46 us
    ppermute x3, starting transfers between devices, from_before(): lax.ppermute(tail, axis, [(i, (i + 1) % count) for i in range(count)])  5.24 us
    ppermute x3, waiting for transfers between devices, from_before(): lax.ppermute(tail, axis, [(i, (i + 1) % count) for i in range(count)])  2.94 us
    slice x1, local copies, waits for them, and re-layouts, on_device(): partial, before, head, pos_late = tied(partial, before, feat[:1], pos)  2.36 us
  transfers between devices with their start and end apart: 17, of which 6 were waited for; matrix products, arithmetic and copies ran while one was open for 3% of the time, Pallas kernels for 42%

profile of v8, /device:TPU:0, one launch (start us, length us, event | category | flops | bytes accessed | tf_op | source)
XLA Modules:
  0.0 74.9 jit_solution(8371795370857324516)
XLA Ops:
  0.0 2.4 %slice_bitcast_fusion = (bf16[1,8,128,256]{3,2,1,0:T(8,128)(2,1)}, bf16[1,8,128,256]{3,2,1,0:T(8,128)(2,1)}) fusion(bf16[2,8,16,8,256]{4,3,2,1,0:T(8,128)(2,1)} %param.7), kind=kLoop, calls=%fused_computation.18 | loop fusion | bytes 2097152 | tf_op jit(solution)/shard_map/slice | solution.py:575
  2.4 3.0 %collective-permute-start = (bf16[1,8,128,256]{3,2,1,0:T(8,128)(2,1)}, bf16[1,8,128,256]{3,2,1,0:T(8,128)(2,1)}, u32[]{:S(2)}, u32[]{:S(2)}) collective-permute-start(bf16[1,8,128,256]{3,2,1,0:T(8,128)(2,1)} %get-tuple-element.156), channel_id=1, source_target_pairs={{0,16},{16,0},{1,17},{17,1},{2,18},{18,2},{3,19},{19,3},{4,20},{20... | collective-permute-start | bytes 1572872 | tf_op jit(solution)/shard_map/ppermute | solution.py:528
  6.3 8.3 %factor.1 = (bf16[4,2,2048,256]{3,2,1,0:T(8,128)(2,1)}, f32[2048,256]{1,0:T(8,128)S(1)}) custom-call(bf16[2,8,16,128]{3,2,1,0:T(8,128)(2,1)S(1)} %maximum_maximum_fusion.pos, s32[3,1024]{1,0:T(4,128)S(1)} %bitcast.55, bf16[2048,256]{1,0:T(8,128)(2,1)S(1)} %bitcast.40, bf16[256,256]{1,0:T(8,128)(2,1)S(1)} %copy-done.3), custom_call_target="tpu_custom_call" | custom-call | flops 12884901888 | bytes 4194304 | tf_op jit(solution)/shard_map/factor/pallas_call | solution.py:134
  14.6 2.9 %collective-permute-done.side_feat.before = bf16[1,8,128,256]{3,2,1,0:T(8,128)(2,1)} collective-permute-done((bf16[1,8,128,256]{3,2,1,0:T(8,128)(2,1)}, bf16[1,8,128,256]{3,2,1,0:T(8,128)(2,1)}, u32[]{:S(2)}, u32[]{:S(2)}) %collective-permute-start) | collective-permute-done | bytes 524320 | tf_op jit(solution)/shard_map/ppermute | solution.py:528
  18.5 1.8 %collective-permute-start.2 = (bf16[1,8,16,128]{3,2,1,0:T(8,128)(2,1)S(1)}, bf16[1,8,16,128]{3,2,1,0:T(8,128)(2,1)S(1)}, u32[]{:S(2)}, u32[]{:S(2)}) collective-permute-start(bf16[1,8,16,128]{3,2,1,0:T(8,128)(2,1)S(1)} %get-tuple-element.167), channel_id=1, source_target_pairs={{0,16},{16,0},{1,17},{17,1},{2,18},{18,2},{3,19},{19,3},{4,20},{20... | collective-permute-start | bytes 98312 | tf_op jit(solution)/shard_map/ppermute | solution.py:528
  20.5 1.7 %collective-permute-start.7 = (bf16[1,8,128,256]{3,2,1,0:T(8,128)(2,1)}, bf16[1,8,128,256]{3,2,1,0:T(8,128)(2,1)S(1)}, u32[]{:S(2)}, u32[]{:S(2)}) collective-permute-start(bf16[1,8,128,256]{3,2,1,0:T(8,128)(2,1)} %get-tuple-element.108), channel_id=1, source_target_pairs={{16,0},{0,16},{17,1},{1,17},{18,2},{2,18},{19,3},{3,19},{20,4},{4,... | collective-permute-start | bytes 1572872 | tf_op jit(solution)/shard_map/ppermute | solution.py:534
  22.3 1.1 %convert_add_fusion = f32[1024,256]{1,0:T(8,128)S(1)} fusion(bf16[1024,256]{1,0:T(8,128)(2,1)} %collective-permute-done.1, f32[2048,256]{1,0:T(8,128)S(1)} %get-tuple-element.81, s32[]{:T(128)S(6)} %select_n.98), kind=kLoop, calls=%fused_computation | loop fusion | flops 524288 | bytes 2621444 | tf_op jit(solution)/shard_map/add | solution.py:466
  23.5 1.6 %collective-permute-start.3 = (bf16[512,256]{1,0:T(8,128)(2,1)S(1)}, bf16[512,256]{1,0:T(8,128)(2,1)S(1)}, u32[]{:S(2)}, u32[]{:S(2)}) collective-permute-start(bf16[512,256]{1,0:T(8,128)(2,1)S(1)} %dynamic-slice_convert_fusion.1), channel_id=1, source_target_pairs={{0,2},{1,3},{2,0},{3,1},{4,6},{5,7},{6,4},{7,5},{8,10},{9,11},{10,... | collective-permute-start | bytes 786440 | tf_op jit(solution)/shard_map/ppermute | solution.py:433
  25.1 4.0 %plane.4.rest_0_ = f32[8,2,128,256]{3,2,1,0:T(8,128)S(1)} custom-call(bf16[2,8,128,256]{3,2,1,0:T(8,128)(2,1)S(1)} %bitcast.42, bf16[2,8,16,128]{3,2,1,0:T(8,128)(2,1)S(1)} %maximum_maximum_fusion.pos, bf16[1,8,128,256]{3,2,1,0:T(8,128)(2,1)} %collective-permute-done.side_feat.before, bf16[1,8,16,128]{3,2,1,0:T(8,128)(2,1)S(1)} %collective-permute-done.2.side_pos.pos_before, ...), custom_call_target="tpu_custom_call" | custom-call | flops 4026531840 | bytes 4194304 | tf_op jit(solution)/shard_map/plane/pallas_call | solution.py:323
  29.1 2.4 %collective-permute-done.3 = bf16[512,256]{1,0:T(8,128)(2,1)S(1)} collective-permute-done((bf16[512,256]{1,0:T(8,128)(2,1)S(1)}, bf16[512,256]{1,0:T(8,128)(2,1)S(1)}, u32[]{:S(2)}, u32[]{:S(2)}) %collective-permute-start.3) | collective-permute-done | bytes 262176 | tf_op jit(solution)/shard_map/ppermute | solution.py:433
  31.5 1.6 %collective-permute-start.4 = (bf16[128,256]{1,0:T(8,128)(2,1)S(1)}, bf16[128,256]{1,0:T(8,128)(2,1)S(1)}, u32[]{:S(2)}, u32[]{:S(2)}) collective-permute-start(bf16[128,256]{1,0:T(8,128)(2,1)S(1)} %get-tuple-element.95), channel_id=1, source_target_pairs={{0,4},{1,5},{2,6},{3,7},{4,0},{5,1},{6,2},{7,3},{8,12},{9,13},{10,... | collective-permute-start | bytes 196616 | tf_op jit(solution)/shard_map/ppermute | solution.py:433
  33.2 2.6 %collective-permute-start.5 = (bf16[128,256]{1,0:T(8,128)(2,1)S(1)}, bf16[128,256]{1,0:T(8,128)(2,1)S(1)}, u32[]{:S(2)}, u32[]{:S(2)}) collective-permute-start(bf16[128,256]{1,0:T(8,128)(2,1)S(1)} %get-tuple-element.96), channel_id=1, source_target_pairs={{0,8},{1,9},{2,10},{3,11},{4,12},{5,13},{6,14},{7,15},{8,0},{9,1},... | collective-permute-start | bytes 196616 | tf_op jit(solution)/shard_map/ppermute | solution.py:433
  36.0 4.0 %plane.5.rest_0_ = f32[8,2,128,256]{3,2,1,0:T(8,128)S(1)} custom-call(bf16[2,8,128,256]{3,2,1,0:T(8,128)(2,1)S(1)} %bitcast.43, bf16[2,8,16,128]{3,2,1,0:T(8,128)(2,1)S(1)} %maximum_maximum_fusion.pos, bf16[1,8,128,256]{3,2,1,0:T(8,128)(2,1)} %collective-permute-done.side_feat.before, ...), custom_call_target="tpu_custom_call", output_to_operand_aliasing={{}: (5, {})} | custom-call | flops 4026531840 | bytes 4194304 | tf_op jit(solution)/shard_map/plane/pallas_call | solution.py:323
  40.0 1.9 %collective-permute-done.6 = bf16[128,256]{1,0:T(8,128)(2,1)S(1)} collective-permute-done((bf16[128,256]{1,0:T(8,128)(2,1)S(1)}, bf16[128,256]{1,0:T(8,128)(2,1)S(1)}, u32[]{:S(2)}, u32[]{:S(2)}) %collective-permute-start.6) | collective-permute-done | bytes 65568 | tf_op jit(solution)/shard_map/ppermute | solution.py:433
  44.3 2.9 %plane.6.rest_0_ = f32[8,2,128,256]{3,2,1,0:T(8,128)S(1)} custom-call(bf16[2,8,128,256]{3,2,1,0:T(8,128)(2,1)S(1)} %bitcast.44, bf16[2,8,16,128]{3,2,1,0:T(8,128)(2,1)S(1)} %maximum_maximum_fusion.pos, bf16[1,8,128,256]{3,2,1,0:T(8,128)(2,1)S(1)} %collective-permute-done.7.side_feat.after, ...), custom_call_target="tpu_custom_call", output_to_operand_aliasing={{}: (5, {})} | custom-call | flops 4026531840 | bytes 4194304 | tf_op jit(solution)/shard_map/plane/pallas_call | solution.py:323
  47.2 1.3 %collective-permute-done.9 = bf16[128,256]{1,0:T(8,128)(2,1)S(1)} collective-permute-done((bf16[128,256]{1,0:T(8,128)(2,1)S(1)}, bf16[128,256]{1,0:T(8,128)(2,1)S(1)}, u32[]{:S(2)}, u32[]{:S(2)}) %collective-permute-start.9) | collective-permute-done | bytes 65568 | tf_op jit(solution)/shard_map/ppermute | solution.py:433
  48.6 2.3 %collective-permute-start.11 = (bf16[128,256]{1,0:T(8,128)(2,1)S(1)}, bf16[128,256]{1,0:T(8,128)(2,1)S(1)}, u32[]{:S(2)}, u32[]{:S(2)}) collective-permute-start(bf16[128,256]{1,0:T(8,128)(2,1)S(1)} %add_convert_fusion), channel_id=1, source_target_pairs={{0,8},{1,9},{2,10},{3,11},{4,12},{5,13},{6,14},{7,15},{8,0},{9,1},... | collective-permute-start | bytes 196616 | tf_op jit(solution)/shard_map/ppermute | solution.py:433
  50.9 2.1 %collective-permute-start.12 = (bf16[128,256]{1,0:T(8,128)(2,1)S(1)}, bf16[128,256]{1,0:T(8,128)(2,1)S(1)}, u32[]{:S(2)}, u32[]{:S(2)}) collective-permute-start(bf16[128,256]{1,0:T(8,128)(2,1)S(1)} %add_convert_fusion), channel_id=1, source_target_pairs={{0,12},{1,13},{2,14},{3,15},{4,8},{5,9},{6,10},{7,11},{8,4},{9,5},... | collective-permute-start | bytes 196616 | tf_op jit(solution)/shard_map/ppermute | solution.py:433
  53.0 2.9 %plane.7.rest_0_ = f32[8,2,128,256]{3,2,1,0:T(8,128)S(1)} custom-call(bf16[2,8,128,256]{3,2,1,0:T(8,128)(2,1)S(1)} %bitcast.45, bf16[2,8,16,128]{3,2,1,0:T(8,128)(2,1)S(1)} %maximum_maximum_fusion.pos, bf16[1,8,128,256]{3,2,1,0:T(8,128)(2,1)S(1)} %collective-permute-done.7.side_feat.after, ...), custom_call_target="tpu_custom_call", output_to_operand_aliasing={{}: (5, {})} | custom-call | flops 4026531840 | bytes 4194304 | tf_op jit(solution)/shard_map/plane/pallas_call | solution.py:323
  55.9 1.4 %collective-permute-done.11 = bf16[128,256]{1,0:T(8,128)(2,1)S(1)} collective-permute-done((bf16[128,256]{1,0:T(8,128)(2,1)S(1)}, bf16[128,256]{1,0:T(8,128)(2,1)S(1)}, u32[]{:S(2)}, u32[]{:S(2)}) %collective-permute-start.11) | collective-permute-done | bytes 65568 | tf_op jit(solution)/shard_map/ppermute | solution.py:433
  58.5 2.7 %low.1.rest_0_ = f32[8,2,128,256]{3,2,1,0:T(8,128)S(1)} custom-call(bf16[2,8,128,256]{3,2,1,0:T(8,128)(2,1)S(1)} %bitcast.46, bf16[2,8,16,128]{3,2,1,0:T(8,128)(2,1)S(1)} %maximum_maximum_fusion.pos, bf16[1,8,128,256]{3,2,1,0:T(8,128)(2,1)} %collective-permute-done.side_feat.before, ...), custom_call_target="tpu_custom_call", output_to_operand_aliasing={{}: (8, {})} | custom-call | flops 2684354560 | bytes 4194304 | tf_op jit(solution)/shard_map/low/pallas_call | solution.py:323
  61.3 2.7 %high.1.base = f32[8,2,128,256]{3,2,1,0:T(8,128)S(1)} custom-call(bf16[2,8,128,256]{3,2,1,0:T(8,128)(2,1)S(1)} %bitcast.47, bf16[2,8,16,128]{3,2,1,0:T(8,128)(2,1)S(1)} %maximum_maximum_fusion.pos, bf16[1,8,128,256]{3,2,1,0:T(8,128)(2,1)} %collective-permute-done.side_feat.before, ...), custom_call_target="tpu_custom_call", output_to_operand_aliasing={{}: (8, {})} | custom-call | flops 2684354560 | bytes 4194304 | tf_op jit(solution)/shard_map/high/pallas_call | solution.py:323
  64.9 4.1 %near.1.partial = f32[2048,256]{1,0:T(8,128)S(1)} custom-call(bf16[4,2,2048,256]{3,2,1,0:T(8,128)(2,1)} %get-tuple-element.148.ph_all, bf16[4,256,256]{2,1,0:T(8,128)(2,1)S(1)} %bitcast.39), custom_call_target="tpu_custom_call" | custom-call | flops 2147483648 | bytes 4194304 | tf_op jit(solution)/shard_map/near/pallas_call | solution.py:407
  69.0 5.8 %far.1 = bf16[2048,256]{1,0:T(8,128)(2,1)} custom-call(bf16[4,2,2048,256]{3,2,1,0:T(8,128)(2,1)} %get-tuple-element.148.ph_all, bf16[4,256,256]{2,1,0:T(8,128)(2,1)S(1)} %bitcast.48, f32[2048,256]{1,0:T(8,128)S(1)} %near.1.partial, bf16[256,256]{1,0:T(8,128)(2,1)S(1)} %copy-done.1, f32[8,2,128,256]{3,2,1,0:T(8,128)S(1)} %high.1.base, ...), custom_call_target="tpu_custom_call" | custom-call | flops 2147483648 | bytes 4194304 | tf_op jit(solution)/shard_map/far/pallas_call | solution.py:407
  (64 shorter events, 6.9 us)
Async XLA Ops:
  0.0 6.2 %copy-start = (bf16[2,8,16,8,256]{4,3,2,1,0:T(8,128)(2,1)S(1)}, bf16[2,8,16,8,256]{4,3,2,1,0:T(8,128)(2,1)}, u32[]{:S(2)}) copy-start(bf16[2,8,16,8,256]{4,3,2,1,0:T(8,128)(2,1)} %param.7) | copy-start | bytes 3145732
  0.0 5.3 %copy-start.5 = (bf16[2,8,16,8,3]{2,3,4,1,0:T(8,128)(2,1)S(1)}, bf16[2,8,16,8,3]{2,3,4,1,0:T(8,128)(2,1)}, u32[]{:S(2)}) copy-start(bf16[2,8,16,8,3]{2,3,4,1,0:T(8,128)(2,1)} %param.8) | copy-start | bytes 36868
  0.0 5.7 %copy-start.6 = (s32[2,8,16]{2,1,0:T(8,128)S(1)}, s32[2,8,16]{2,1,0:T(8,128)}, u32[]{:S(2)}) copy-start(s32[2,8,16]{2,1,0:T(8,128)} %param.9) | copy-start | bytes 3076
  0.0 6.2 %copy-start.4 = (s32[1024,3]{0,1:T(4,128)S(1)}, s32[1024,3]{0,1:T(4,128)}, u32[]{:S(2)}) copy-start(s32[1024,3]{0,1:T(4,128)} %param.10) | copy-start | bytes 36868
  0.0 6.2 %copy-start.3 = (bf16[256,256]{1,0:T(8,128)(2,1)S(1)}, bf16[256,256]{1,0:T(8,128)(2,1)}, u32[]{:S(2)}) copy-start(bf16[256,256]{1,0:T(8,128)(2,1)} %wc.1) | copy-start | bytes 393220
  2.4 15.2 %collective-permute-start = (bf16[1,8,128,256]{3,2,1,0:T(8,128)(2,1)}, bf16[1,8,128,256]{3,2,1,0:T(8,128)(2,1)}, u32[]{:S(2)}, u32[]{:S(2)}) collective-permute-start(bf16[1,8,128,256]{3,2,1,0:T(8,128)(2,1)} %get-tuple-element.156), channel_id=1, source_target_pairs={{0,16},{16,0},{1,17},{17,1},{2,18},{18,2},{3,19},{19,3},{4,20},{20... | collective-permute-start | bytes 1572872 | tf_op jit(solution)/shard_map/ppermute | solution.py:528
  18.4 3.9 %collective-permute-start.1 = (bf16[1024,256]{1,0:T(8,128)(2,1)}, bf16[1024,256]{1,0:T(8,128)(2,1)}, u32[]{:S(2)}, u32[]{:S(2)}) collective-permute-start(bf16[1024,256]{1,0:T(8,128)(2,1)} %dynamic-slice_convert_fusion), channel_id=1, source_target_pairs={{0,1},{1,0},{2,3},{3,2},{4,5},{5,4},{6,7},{7,6},{8,9},{9,8},{10,11... | collective-permute-start | bytes 1572872 | tf_op jit(solution)/shard_map/ppermute | solution.py:433
  18.4 6.7 %copy-start.2 = (bf16[8,256,256]{2,1,0:T(8,128)(2,1)S(1)}, bf16[8,256,256]{2,1,0:T(8,128)(2,1)}, u32[]{:S(2)}) copy-start(bf16[8,256,256]{2,1,0:T(8,128)(2,1)} %param.11) | copy-start | bytes 3145732
  18.5 5.0 %collective-permute-start.2 = (bf16[1,8,16,128]{3,2,1,0:T(8,128)(2,1)S(1)}, bf16[1,8,16,128]{3,2,1,0:T(8,128)(2,1)S(1)}, u32[]{:S(2)}, u32[]{:S(2)}) collective-permute-start(bf16[1,8,16,128]{3,2,1,0:T(8,128)(2,1)S(1)} %get-tuple-element.167), channel_id=1, source_target_pairs={{0,16},{16,0},{1,17},{17,1},{2,18},{18,2},{3,19},{19,3},{4,20},{20... | collective-permute-start | bytes 98312 | tf_op jit(solution)/shard_map/ppermute | solution.py:528
  20.3 21.6 %collective-permute-start.8 = (bf16[1,8,16,128]{3,2,1,0:T(8,128)(2,1)S(1)}, bf16[1,8,16,128]{3,2,1,0:T(8,128)(2,1)S(1)}, u32[]{:S(2)}, u32[]{:S(2)}) collective-permute-start(bf16[1,8,16,128]{3,2,1,0:T(8,128)(2,1)S(1)} %get-tuple-element.166), channel_id=1, source_target_pairs={{16,0},{0,16},{17,1},{1,17},{18,2},{2,18},{19,3},{3,19},{20,4},{4,... | collective-permute-start | bytes 98312 | tf_op jit(solution)/shard_map/ppermute | solution.py:534
  20.5 21.3 %collective-permute-start.7 = (bf16[1,8,128,256]{3,2,1,0:T(8,128)(2,1)}, bf16[1,8,128,256]{3,2,1,0:T(8,128)(2,1)S(1)}, u32[]{:S(2)}, u32[]{:S(2)}) collective-permute-start(bf16[1,8,128,256]{3,2,1,0:T(8,128)(2,1)} %get-tuple-element.108), channel_id=1, source_target_pairs={{16,0},{0,16},{17,1},{1,17},{18,2},{2,18},{19,3},{3,19},{20,4},{4,... | collective-permute-start | bytes 1572872 | tf_op jit(solution)/shard_map/ppermute | solution.py:534
  23.5 7.9 %collective-permute-start.3 = (bf16[512,256]{1,0:T(8,128)(2,1)S(1)}, bf16[512,256]{1,0:T(8,128)(2,1)S(1)}, u32[]{:S(2)}, u32[]{:S(2)}) collective-permute-start(bf16[512,256]{1,0:T(8,128)(2,1)S(1)} %dynamic-slice_convert_fusion.1), channel_id=1, source_target_pairs={{0,2},{1,3},{2,0},{3,1},{4,6},{5,7},{6,4},{7,5},{8,10},{9,11},{10,... | collective-permute-start | bytes 786440 | tf_op jit(solution)/shard_map/ppermute | solution.py:433
  31.5 8.4 %collective-permute-start.4 = (bf16[128,256]{1,0:T(8,128)(2,1)S(1)}, bf16[128,256]{1,0:T(8,128)(2,1)S(1)}, u32[]{:S(2)}, u32[]{:S(2)}) collective-permute-start(bf16[128,256]{1,0:T(8,128)(2,1)S(1)} %get-tuple-element.95), channel_id=1, source_target_pairs={{0,4},{1,5},{2,6},{3,7},{4,0},{5,1},{6,2},{7,3},{8,12},{9,13},{10,... | collective-permute-start | bytes 196616 | tf_op jit(solution)/shard_map/ppermute | solution.py:433
  33.2 6.8 %collective-permute-start.5 = (bf16[128,256]{1,0:T(8,128)(2,1)S(1)}, bf16[128,256]{1,0:T(8,128)(2,1)S(1)}, u32[]{:S(2)}, u32[]{:S(2)}) collective-permute-start(bf16[128,256]{1,0:T(8,128)(2,1)S(1)} %get-tuple-element.96), channel_id=1, source_target_pairs={{0,8},{1,9},{2,10},{3,11},{4,12},{5,13},{6,14},{7,15},{8,0},{9,1},... | collective-permute-start | bytes 196616 | tf_op jit(solution)/shard_map/ppermute | solution.py:433
  35.8 6.1 %collective-permute-start.6 = (bf16[128,256]{1,0:T(8,128)(2,1)S(1)}, bf16[128,256]{1,0:T(8,128)(2,1)S(1)}, u32[]{:S(2)}, u32[]{:S(2)}) collective-permute-start(bf16[128,256]{1,0:T(8,128)(2,1)S(1)} %get-tuple-element.97), channel_id=1, source_target_pairs={{0,12},{1,13},{2,14},{3,15},{4,8},{5,9},{6,10},{7,11},{8,4},{9,5},... | collective-permute-start | bytes 196616 | tf_op jit(solution)/shard_map/ppermute | solution.py:433
  42.8 14.7 %collective-permute-start.14 = (bf16[4,1,144,256]{3,2,1,0:T(8,128)(2,1)S(1)}, bf16[4,1,144,256]{3,2,1,0:T(8,128)(2,1)S(1)}, u32[]{:S(2)}, u32[]{:S(2)}) collective-permute-start(bf16[4,1,144,256]{3,2,1,0:T(8,128)(2,1)S(1)} %fusion.21), channel_id=1, source_target_pairs={{1,0},{2,1},{3,2},{4,3},{5,4},{6,5},{7,6},{8,7},{9,8},{10,9},{11,1... | collective-permute-start | bytes 884744 | tf_op jit(solution)/shard_map/ppermute | solution.py:534
  43.2 14.3 %collective-permute-start.13 = (bf16[4,1,144,256]{3,2,1,0:T(8,128)(2,1)S(1)}, bf16[4,1,144,256]{3,2,1,0:T(8,128)(2,1)S(1)}, u32[]{:S(2)}, u32[]{:S(2)}) collective-permute-start(bf16[4,1,144,256]{3,2,1,0:T(8,128)(2,1)S(1)} %fusion.17), channel_id=1, source_target_pairs={{0,1},{1,2},{2,3},{3,4},{4,5},{5,6},{6,7},{7,8},{8,9},{9,10},{10,1... | collective-permute-start | bytes 884744 | tf_op jit(solution)/shard_map/ppermute | solution.py:528
  43.7 4.9 %collective-permute-start.9 = (bf16[128,256]{1,0:T(8,128)(2,1)S(1)}, bf16[128,256]{1,0:T(8,128)(2,1)S(1)}, u32[]{:S(2)}, u32[]{:S(2)}) collective-permute-start(bf16[128,256]{1,0:T(8,128)(2,1)S(1)} %convert_element_type.80), channel_id=1, source_target_pairs={{0,16},{1,17},{2,18},{3,19},{4,20},{5,21},{6,22},{7,23},{8,24},{9,... | collective-permute-start | bytes 196616 | tf_op jit(solution)/shard_map/ppermute | solution.py:433
  48.5 7.4 %collective-permute-start.10 = (bf16[128,256]{1,0:T(8,128)(2,1)S(1)}, bf16[128,256]{1,0:T(8,128)(2,1)S(1)}, u32[]{:S(2)}, u32[]{:S(2)}) collective-permute-start(bf16[128,256]{1,0:T(8,128)(2,1)S(1)} %add_convert_fusion), channel_id=1, source_target_pairs={{0,4},{1,5},{2,6},{3,7},{4,0},{5,1},{6,2},{7,3},{8,12},{9,13},{10,... | collective-permute-start | bytes 196616 | tf_op jit(solution)/shard_map/ppermute | solution.py:433
  48.6 8.7 %collective-permute-start.11 = (bf16[128,256]{1,0:T(8,128)(2,1)S(1)}, bf16[128,256]{1,0:T(8,128)(2,1)S(1)}, u32[]{:S(2)}, u32[]{:S(2)}) collective-permute-start(bf16[128,256]{1,0:T(8,128)(2,1)S(1)} %add_convert_fusion), channel_id=1, source_target_pairs={{0,8},{1,9},{2,10},{3,11},{4,12},{5,13},{6,14},{7,15},{8,0},{9,1},... | collective-permute-start | bytes 196616 | tf_op jit(solution)/shard_map/ppermute | solution.py:433
  50.9 6.4 %collective-permute-start.12 = (bf16[128,256]{1,0:T(8,128)(2,1)S(1)}, bf16[128,256]{1,0:T(8,128)(2,1)S(1)}, u32[]{:S(2)}, u32[]{:S(2)}) collective-permute-start(bf16[128,256]{1,0:T(8,128)(2,1)S(1)} %add_convert_fusion), channel_id=1, source_target_pairs={{0,12},{1,13},{2,14},{3,15},{4,8},{5,9},{6,10},{7,11},{8,4},{9,5},... | collective-permute-start | bytes 196616 | tf_op jit(solution)/shard_map/ppermute | solution.py:433
  57.5 7.0 %collective-permute-start.15 = (bf16[512,256]{1,0:T(8,128)(2,1)S(1)}, bf16[512,256]{1,0:T(8,128)(2,1)S(1)}, u32[]{:S(2)}, u32[]{:S(2)}) collective-permute-start(bf16[512,256]{1,0:T(8,128)(2,1)S(1)} %bitcast.59), channel_id=1, source_target_pairs={{0,2},{1,3},{2,0},{3,1},{4,6},{5,7},{6,4},{7,5},{8,10},{9,11},{10,... | collective-permute-start | bytes 786440 | tf_op jit(solution)/shard_map/ppermute | solution.py:433
  64.8 4.2 %collective-permute-start.16 = (bf16[1024,256]{1,0:T(8,128)(2,1)S(1)}, bf16[1024,256]{1,0:T(8,128)(2,1)S(1)}, u32[]{:S(2)}, u32[]{:S(2)}) collective-permute-start(bf16[1024,256]{1,0:T(8,128)(2,1)S(1)} %maximum_select_fusion), channel_id=1, source_target_pairs={{0,1},{1,0},{2,3},{3,2},{4,5},{5,4},{6,7},{7,6},{8,9},{9,8},{10,11... | collective-permute-start | bytes 1572872 | tf_op jit(solution)/shard_map/ppermute | solution.py:433
  64.9 4.1 %copy-start.1 = (bf16[256,256]{1,0:T(8,128)(2,1)S(1)}, bf16[256,256]{1,0:T(8,128)(2,1)}, u32[]{:S(2)}) copy-start(bf16[256,256]{1,0:T(8,128)(2,1)} %w_out.1) | copy-start | bytes 393220

commit v9 on v8

--- a/solution.py
+++ b/solution.py
@@ -572,7 +572,7 @@
     ph, partial = factor_call(
         pos, k_index.T, feat.reshape(atoms, width), w_charge, grid_all, scale_all
     )
-    partial, before, head, pos_late = tied(partial, before, feat[:1], pos)
+    partial, head, pos_late = tied(partial, feat[:1], pos)
     after = from_after(head, "gx", 0)
     pos_before = from_before(pos_late, "gx", 0)
     pos_after = from_after(pos_late, "gx", 0)
@@ -596,7 +596,9 @@
             base = short_call(kernel, name, planes, basis, (*common, halo, w), base)
         return base
 
-    value, _ = exchange.halve(partial, exchange.halved[0])
+    value, before = exchange.halve(
+        partial, exchange.halved[0], Work(lambda plane: plane, before)
+    )
     value, before, pos_before = tied(value, before, pos_before)
     value, base = exchange.halve(
         value, exchange.halved[1], plane_work(0, 1, 3, None, before, pos_before)

time: 75.4 us -> 76 us (level)
  waiting for transfers between devices: 10.4 us -> 7.54 us
  Pallas kernels: 37.5 us -> 39.9 us
  starting transfers between devices: 19.8 us -> 20.6 us
    pallas_call x6, Pallas kernels: 19.3 us -> 21.6 us  [short_call(): pl.pallas_call(kernel, in_specs=[whole] * len(args), out_specs=whole, out...]
    ppermute x11, waiting for transfers between devices: 7.46 us -> 5.44 us  [swap(): return lax.ppermute(value, AXES, [(i, i ^ mask) for i in range(count)])]
    ppermute x3, waiting for transfers between devices: 2.94 us -> 2.09 us  [from_before(): lax.ppermute(tail, axis, [(i, (i + 1) % count) for i in range(count)])]
    ppermute x11, starting transfers between devices: 12.2 us -> 13 us  [swap(): return lax.ppermute(value, AXES, [(i, i ^ mask) for i in range(count)])]
  transfers between devices with their start and end apart: 17 -> 17, of which waited for: 6 -> 6; matrix products, arithmetic and copies ran while one was open for 3% -> 4% of each run, Pallas kernels for 42% -> 45%
where the time goes in v9:
time: 76 us; the launch traced here: 75.5 us
  Pallas kernels  39.9 us (52%)
  starting transfers between devices  20.6 us (27%)
  waiting for transfers between devices  7.54 us (10%)
  local copies, waits for them, and re-layouts  5.1 us (7%)
  other arithmetic  1.85 us (2%)
    pallas_call x6, Pallas kernels, short_call(): pl.pallas_call(kernel, in_specs=[whole] * len(args), out_specs=whole, out...  21.6 us
    ppermute x11, starting transfers between devices, swap(): return lax.ppermute(value, AXES, [(i, i ^ mask) for i in range(count)])  13 us
    pallas_call x2, Pallas kernels, field_call(): pl.pallas_call(functools.partial(kernel, lines), in_specs=[in_hbm] + [who...  9.89 us
    pallas_call x1, Pallas kernels, factor_call(): pl.pallas_call(functools.partial(factor_kernel, grid_all, scale_all), in_...  8.33 us
    ppermute x11, waiting for transfers between devices, swap(): return lax.ppermute(value, AXES, [(i, i ^ mask) for i in range(count)])  5.44 us
    ppermute x3, starting transfers between devices, from_before(): lax.ppermute(tail, axis, [(i, (i + 1) % count) for i in range(count)])  5.21 us
    slice x1, local copies, waits for them, and re-layouts, from_before(): tail = lax.slice_in_dim(cells, size - 1, size, axis=dim)  2.43 us
    ppermute x3, starting transfers between devices, from_after(): lax.ppermute(head, axis, [((i + 1) % count, i) for i in range(count)])  2.37 us
  transfers between devices with their start and end apart: 17, of which 6 were waited for; matrix products, arithmetic and copies ran while one was open for 4% of the time, Pallas kernels for 45%

profile of v9, /device:TPU:0, one launch (start us, length us, event | category | flops | bytes accessed | tf_op | source)
XLA Modules:
  0.0 75.5 jit_solution(12353758120175678477)
XLA Ops:
  0.0 2.4 %slice_bitcast_fusion = (bf16[1,8,128,256]{3,2,1,0:T(8,128)(2,1)}, bf16[1,8,128,256]{3,2,1,0:T(8,128)(2,1)}) fusion(bf16[2,8,16,8,256]{4,3,2,1,0:T(8,128)(2,1)} %param.7), kind=kLoop, calls=%fused_computation.18 | loop fusion | bytes 2097152 | tf_op jit(solution)/shard_map/slice | solution.py:527
  2.4 3.0 %collective-permute-start = (bf16[1,8,128,256]{3,2,1,0:T(8,128)(2,1)}, bf16[1,8,128,256]{3,2,1,0:T(8,128)(2,1)}, u32[]{:S(2)}, u32[]{:S(2)}) collective-permute-start(bf16[1,8,128,256]{3,2,1,0:T(8,128)(2,1)} %get-tuple-element.161), channel_id=1, source_target_pairs={{0,16},{16,0},{1,17},{17,1},{2,18},{18,2},{3,19},{19,3},{4,20},{20... | collective-permute-start | bytes 1572872 | tf_op jit(solution)/shard_map/ppermute | solution.py:528
  6.3 8.3 %factor.1 = (bf16[4,2,2048,256]{3,2,1,0:T(8,128)(2,1)}, f32[2048,256]{1,0:T(8,128)S(1)}) custom-call(bf16[2,8,16,128]{3,2,1,0:T(8,128)(2,1)S(1)} %maximum_maximum_fusion.pos, s32[3,1024]{1,0:T(4,128)S(1)} %bitcast.55, bf16[2048,256]{1,0:T(8,128)(2,1)S(1)} %bitcast.40, bf16[256,256]{1,0:T(8,128)(2,1)S(1)} %copy-done.3), custom_call_target="tpu_custom_call" | custom-call | flops 12884901888 | bytes 4194304 | tf_op jit(solution)/shard_map/factor/pallas_call | solution.py:134
  15.5 2.1 %collective-permute-done.side_feat.before = bf16[1,8,128,256]{3,2,1,0:T(8,128)(2,1)} collective-permute-done((bf16[1,8,128,256]{3,2,1,0:T(8,128)(2,1)}, bf16[1,8,128,256]{3,2,1,0:T(8,128)(2,1)}, u32[]{:S(2)}, u32[]{:S(2)}) %collective-permute-start) | collective-permute-done | bytes 524320 | tf_op jit(solution)/shard_map/ppermute | solution.py:528
  17.6 1.8 %collective-permute-start.2 = (bf16[1,8,16,128]{3,2,1,0:T(8,128)(2,1)S(1)}, bf16[1,8,16,128]{3,2,1,0:T(8,128)(2,1)S(1)}, u32[]{:S(2)}, u32[]{:S(2)}) collective-permute-start(bf16[1,8,16,128]{3,2,1,0:T(8,128)(2,1)S(1)} %get-tuple-element.173), channel_id=1, source_target_pairs={{0,16},{16,0},{1,17},{17,1},{2,18},{18,2},{3,19},{19,3},{4,20},{20... | collective-permute-start | bytes 98312 | tf_op jit(solution)/shard_map/ppermute | solution.py:528
  19.7 1.7 %collective-permute-start.7 = (bf16[1,8,128,256]{3,2,1,0:T(8,128)(2,1)}, bf16[1,8,128,256]{3,2,1,0:T(8,128)(2,1)}, u32[]{:S(2)}, u32[]{:S(2)}) collective-permute-start(bf16[1,8,128,256]{3,2,1,0:T(8,128)(2,1)} %get-tuple-element.114), channel_id=1, source_target_pairs={{16,0},{0,16},{17,1},{1,17},{18,2},{2,18},{19,3},{3,19},{20,4},{4,... | collective-permute-start | bytes 1572872 | tf_op jit(solution)/shard_map/ppermute | solution.py:534
  21.5 1.2 %convert_add_fusion = f32[1024,256]{1,0:T(8,128)S(1)} fusion(bf16[1024,256]{1,0:T(8,128)(2,1)} %collective-permute-done.1, f32[2048,256]{1,0:T(8,128)S(1)} %get-tuple-element.84, s32[]{:T(128)S(6)} %select_n.98), kind=kLoop, calls=%fused_computation | loop fusion | flops 524288 | bytes 2621444 | tf_op jit(solution)/shard_map/add | solution.py:466
  22.8 1.6 %collective-permute-start.3 = (bf16[512,256]{1,0:T(8,128)(2,1)S(1)}, bf16[512,256]{1,0:T(8,128)(2,1)S(1)}, u32[]{:S(2)}, u32[]{:S(2)}) collective-permute-start(bf16[512,256]{1,0:T(8,128)(2,1)S(1)} %dynamic-slice_convert_fusion.1), channel_id=1, source_target_pairs={{0,2},{1,3},{2,0},{3,1},{4,6},{5,7},{6,4},{7,5},{8,10},{9,11},{10,... | collective-permute-start | bytes 786440 | tf_op jit(solution)/shard_map/ppermute | solution.py:433
  24.4 4.0 %plane.4.rest_0_ = f32[8,2,128,256]{3,2,1,0:T(8,128)S(1)} custom-call(bf16[2,8,128,256]{3,2,1,0:T(8,128)(2,1)S(1)} %bitcast.42, bf16[2,8,16,128]{3,2,1,0:T(8,128)(2,1)S(1)} %maximum_maximum_fusion.pos, bf16[1,8,128,256]{3,2,1,0:T(8,128)(2,1)} %collective-permute-done.side_feat.before, bf16[1,8,16,128]{3,2,1,0:T(8,128)(2,1)S(1)} %collective-permute-done.2.side_pos.pos_before, ...), custom_call_target="tpu_custom_call" | custom-call | flops 4026531840 | bytes 4194304 | tf_op jit(solution)/shard_map/plane/pallas_call | solution.py:323
  28.4 2.3 %collective-permute-done.3 = bf16[512,256]{1,0:T(8,128)(2,1)S(1)} collective-permute-done((bf16[512,256]{1,0:T(8,128)(2,1)S(1)}, bf16[512,256]{1,0:T(8,128)(2,1)S(1)}, u32[]{:S(2)}, u32[]{:S(2)}) %collective-permute-start.3) | collective-permute-done | bytes 262176 | tf_op jit(solution)/shard_map/ppermute | solution.py:433
  30.8 1.6 %collective-permute-start.4 = (bf16[128,256]{1,0:T(8,128)(2,1)S(1)}, bf16[128,256]{1,0:T(8,128)(2,1)S(1)}, u32[]{:S(2)}, u32[]{:S(2)}) collective-permute-start(bf16[128,256]{1,0:T(8,128)(2,1)S(1)} %get-tuple-element.101), channel_id=1, source_target_pairs={{0,4},{1,5},{2,6},{3,7},{4,0},{5,1},{6,2},{7,3},{8,12},{9,13},{10,... | collective-permute-start | bytes 196616 | tf_op jit(solution)/shard_map/ppermute | solution.py:433
  32.4 2.6 %collective-permute-start.5 = (bf16[128,256]{1,0:T(8,128)(2,1)S(1)}, bf16[128,256]{1,0:T(8,128)(2,1)S(1)}, u32[]{:S(2)}, u32[]{:S(2)}) collective-permute-start(bf16[128,256]{1,0:T(8,128)(2,1)S(1)} %get-tuple-element.102), channel_id=1, source_target_pairs={{0,8},{1,9},{2,10},{3,11},{4,12},{5,13},{6,14},{7,15},{8,0},{9,1},... | collective-permute-start | bytes 196616 | tf_op jit(solution)/shard_map/ppermute | solution.py:433
  35.2 4.0 %plane.5.rest_0_ = f32[8,2,128,256]{3,2,1,0:T(8,128)S(1)} custom-call(bf16[2,8,128,256]{3,2,1,0:T(8,128)(2,1)S(1)} %bitcast.43, bf16[2,8,16,128]{3,2,1,0:T(8,128)(2,1)S(1)} %maximum_maximum_fusion.pos, bf16[1,8,128,256]{3,2,1,0:T(8,128)(2,1)} %collective-permute-done.side_feat.before, ...), custom_call_target="tpu_custom_call", output_to_operand_aliasing={{}: (5, {})} | custom-call | flops 4026531840 | bytes 4194304 | tf_op jit(solution)/shard_map/plane/pallas_call | solution.py:323
  39.2 1.9 %collective-permute-done.6 = bf16[128,256]{1,0:T(8,128)(2,1)S(1)} collective-permute-done((bf16[128,256]{1,0:T(8,128)(2,1)S(1)}, bf16[128,256]{1,0:T(8,128)(2,1)S(1)}, u32[]{:S(2)}, u32[]{:S(2)}) %collective-permute-start.6) | collective-permute-done | bytes 65568 | tf_op jit(solution)/shard_map/ppermute | solution.py:433
  41.1 1.0 %fusion.33 = (bf16[1,1,128,256]{3,2,1,0:T(8,128)(2,1)S(1)}, bf16[1,1,128,256]{3,2,1,0:T(8,128)(2,1)S(1)}, bf16[1,1,128,256]{3,2,1,0:T(8,128)(2,1)S(1)}, bf16[1,1,128,256]{3,2,1,0:T(8,128)(2,1)S(1)}) fusion(bf16[1,8,128,256]{3,2,1,0:T(8,128)(2,1)} %collective-permute-done.side_feat.before, bf16[1,8,128,256]{3,2,1,0:T(8,128)(2,1)} %collective-permute-done.7.side_feat.after), kind=kLoop, calls=%fused_computation.55 | loop fusion | bytes 524288 | tf_op jit(solution)/shard_map/slice | solution.py:541
  43.7 4.0 %plane.6.rest_0_ = f32[8,2,128,256]{3,2,1,0:T(8,128)S(1)} custom-call(bf16[2,8,128,256]{3,2,1,0:T(8,128)(2,1)S(1)} %bitcast.44, bf16[2,8,16,128]{3,2,1,0:T(8,128)(2,1)S(1)} %maximum_maximum_fusion.pos, bf16[1,8,128,256]{3,2,1,0:T(8,128)(2,1)} %collective-permute-done.7.side_feat.after, ...), custom_call_target="tpu_custom_call", output_to_operand_aliasing={{}: (5, {})} | custom-call | flops 4026531840 | bytes 4194304 | tf_op jit(solution)/shard_map/plane/pallas_call | solution.py:323
  47.9 2.3 %collective-permute-start.11 = (bf16[128,256]{1,0:T(8,128)(2,1)S(1)}, bf16[128,256]{1,0:T(8,128)(2,1)S(1)}, u32[]{:S(2)}, u32[]{:S(2)}) collective-permute-start(bf16[128,256]{1,0:T(8,128)(2,1)S(1)} %add_convert_fusion), channel_id=1, source_target_pairs={{0,8},{1,9},{2,10},{3,11},{4,12},{5,13},{6,14},{7,15},{8,0},{9,1},... | collective-permute-start | bytes 196616 | tf_op jit(solution)/shard_map/ppermute | solution.py:433
  50.2 2.1 %collective-permute-start.12 = (bf16[128,256]{1,0:T(8,128)(2,1)S(1)}, bf16[128,256]{1,0:T(8,128)(2,1)S(1)}, u32[]{:S(2)}, u32[]{:S(2)}) collective-permute-start(bf16[128,256]{1,0:T(8,128)(2,1)S(1)} %add_convert_fusion), channel_id=1, source_target_pairs={{0,12},{1,13},{2,14},{3,15},{4,8},{5,9},{6,10},{7,11},{8,4},{9,5},... | collective-permute-start | bytes 196616 | tf_op jit(solution)/shard_map/ppermute | solution.py:433
  52.3 4.0 %plane.7.rest_0_ = f32[8,2,128,256]{3,2,1,0:T(8,128)S(1)} custom-call(bf16[2,8,128,256]{3,2,1,0:T(8,128)(2,1)S(1)} %bitcast.45, bf16[2,8,16,128]{3,2,1,0:T(8,128)(2,1)S(1)} %maximum_maximum_fusion.pos, bf16[1,8,128,256]{3,2,1,0:T(8,128)(2,1)} %collective-permute-done.7.side_feat.after, ...), custom_call_target="tpu_custom_call", output_to_operand_aliasing={{}: (5, {})} | custom-call | flops 4026531840 | bytes 4194304 | tf_op jit(solution)/shard_map/plane/pallas_call | solution.py:323
  56.9 1.8 %collective-permute-start.15 = (bf16[512,256]{1,0:T(8,128)(2,1)S(1)}, bf16[512,256]{1,0:T(8,128)(2,1)S(1)}, u32[]{:S(2)}, u32[]{:S(2)}) collective-permute-start(bf16[512,256]{1,0:T(8,128)(2,1)S(1)} %bitcast.59), channel_id=1, source_target_pairs={{0,2},{1,3},{2,0},{3,1},{4,6},{5,7},{6,4},{7,5},{8,10},{9,11},{10,... | collective-permute-start | bytes 786440 | tf_op jit(solution)/shard_map/ppermute | solution.py:433
  58.6 2.9 %low.1.rest_0_ = f32[8,2,128,256]{3,2,1,0:T(8,128)S(1)} custom-call(bf16[2,8,128,256]{3,2,1,0:T(8,128)(2,1)S(1)} %bitcast.46, bf16[2,8,16,128]{3,2,1,0:T(8,128)(2,1)S(1)} %maximum_maximum_fusion.pos, bf16[1,8,128,256]{3,2,1,0:T(8,128)(2,1)} %collective-permute-done.side_feat.before, ...), custom_call_target="tpu_custom_call", output_to_operand_aliasing={{}: (8, {})} | custom-call | flops 2684354560 | bytes 4194304 | tf_op jit(solution)/shard_map/low/pallas_call | solution.py:323
  61.5 2.9 %high.1.base = f32[8,2,128,256]{3,2,1,0:T(8,128)S(1)} custom-call(bf16[2,8,128,256]{3,2,1,0:T(8,128)(2,1)S(1)} %bitcast.47, bf16[2,8,16,128]{3,2,1,0:T(8,128)(2,1)S(1)} %maximum_maximum_fusion.pos, bf16[1,8,128,256]{3,2,1,0:T(8,128)(2,1)} %collective-permute-done.side_feat.before, ...), custom_call_target="tpu_custom_call", output_to_operand_aliasing={{}: (8, {})} | custom-call | flops 2684354560 | bytes 4194304 | tf_op jit(solution)/shard_map/high/pallas_call | solution.py:323
  65.4 4.1 %near.1.partial = f32[2048,256]{1,0:T(8,128)S(1)} custom-call(bf16[4,2,2048,256]{3,2,1,0:T(8,128)(2,1)} %get-tuple-element.154.ph_all, bf16[4,256,256]{2,1,0:T(8,128)(2,1)S(1)} %bitcast.39), custom_call_target="tpu_custom_call" | custom-call | flops 2147483648 | bytes 4194304 | tf_op jit(solution)/shard_map/near/pallas_call | solution.py:407
  69.5 5.8 %far.1 = bf16[2048,256]{1,0:T(8,128)(2,1)} custom-call(bf16[4,2,2048,256]{3,2,1,0:T(8,128)(2,1)} %get-tuple-element.154.ph_all, bf16[4,256,256]{2,1,0:T(8,128)(2,1)S(1)} %bitcast.48, f32[2048,256]{1,0:T(8,128)S(1)} %near.1.partial, bf16[256,256]{1,0:T(8,128)(2,1)S(1)} %copy-done.1, f32[8,2,128,256]{3,2,1,0:T(8,128)S(1)} %high.1.base, ...), custom_call_target="tpu_custom_call" | custom-call | flops 2147483648 | bytes 4194304 | tf_op jit(solution)/shard_map/far/pallas_call | solution.py:407
  (64 shorter events, 5.8 us)
Async XLA Ops:
  0.0 6.3 %copy-start = (bf16[2,8,16,8,256]{4,3,2,1,0:T(8,128)(2,1)S(1)}, bf16[2,8,16,8,256]{4,3,2,1,0:T(8,128)(2,1)}, u32[]{:S(2)}) copy-start(bf16[2,8,16,8,256]{4,3,2,1,0:T(8,128)(2,1)} %param.7) | copy-start | bytes 3145732
  0.0 5.4 %copy-start.5 = (bf16[2,8,16,8,3]{2,3,4,1,0:T(8,128)(2,1)S(1)}, bf16[2,8,16,8,3]{2,3,4,1,0:T(8,128)(2,1)}, u32[]{:S(2)}) copy-start(bf16[2,8,16,8,3]{2,3,4,1,0:T(8,128)(2,1)} %param.8) | copy-start | bytes 36868
  0.0 5.8 %copy-start.6 = (s32[2,8,16]{2,1,0:T(8,128)S(1)}, s32[2,8,16]{2,1,0:T(8,128)}, u32[]{:S(2)}) copy-start(s32[2,8,16]{2,1,0:T(8,128)} %param.9) | copy-start | bytes 3076
  0.0 6.3 %copy-start.4 = (s32[1024,3]{0,1:T(4,128)S(1)}, s32[1024,3]{0,1:T(4,128)}, u32[]{:S(2)}) copy-start(s32[1024,3]{0,1:T(4,128)} %param.10) | copy-start | bytes 36868
  0.0 6.3 %copy-start.3 = (bf16[256,256]{1,0:T(8,128)(2,1)S(1)}, bf16[256,256]{1,0:T(8,128)(2,1)}, u32[]{:S(2)}) copy-start(bf16[256,256]{1,0:T(8,128)(2,1)} %wc.1) | copy-start | bytes 393220
  2.4 15.2 %collective-permute-start = (bf16[1,8,128,256]{3,2,1,0:T(8,128)(2,1)}, bf16[1,8,128,256]{3,2,1,0:T(8,128)(2,1)}, u32[]{:S(2)}, u32[]{:S(2)}) collective-permute-start(bf16[1,8,128,256]{3,2,1,0:T(8,128)(2,1)} %get-tuple-element.161), channel_id=1, source_target_pairs={{0,16},{16,0},{1,17},{17,1},{2,18},{18,2},{3,19},{19,3},{4,20},{20... | collective-permute-start | bytes 1572872 | tf_op jit(solution)/shard_map/ppermute | solution.py:528
  17.6 3.9 %collective-permute-start.1 = (bf16[1024,256]{1,0:T(8,128)(2,1)}, bf16[1024,256]{1,0:T(8,128)(2,1)}, u32[]{:S(2)}, u32[]{:S(2)}) collective-permute-start(bf16[1024,256]{1,0:T(8,128)(2,1)} %dynamic-slice_convert_fusion), channel_id=1, source_target_pairs={{0,1},{1,0},{2,3},{3,2},{4,5},{5,4},{6,7},{7,6},{8,9},{9,8},{10,11... | collective-permute-start | bytes 1572872 | tf_op jit(solution)/shard_map/ppermute | solution.py:433
  17.6 5.1 %collective-permute-start.2 = (bf16[1,8,16,128]{3,2,1,0:T(8,128)(2,1)S(1)}, bf16[1,8,16,128]{3,2,1,0:T(8,128)(2,1)S(1)}, u32[]{:S(2)}, u32[]{:S(2)}) collective-permute-start(bf16[1,8,16,128]{3,2,1,0:T(8,128)(2,1)S(1)} %get-tuple-element.173), channel_id=1, source_target_pairs={{0,16},{16,0},{1,17},{17,1},{2,18},{18,2},{3,19},{19,3},{4,20},{20... | collective-permute-start | bytes 98312 | tf_op jit(solution)/shard_map/ppermute | solution.py:528
  19.5 21.7 %collective-permute-start.8 = (bf16[1,8,16,128]{3,2,1,0:T(8,128)(2,1)S(1)}, bf16[1,8,16,128]{3,2,1,0:T(8,128)(2,1)S(1)}, u32[]{:S(2)}, u32[]{:S(2)}) collective-permute-start(bf16[1,8,16,128]{3,2,1,0:T(8,128)(2,1)S(1)} %get-tuple-element.172), channel_id=1, source_target_pairs={{16,0},{0,16},{17,1},{1,17},{18,2},{2,18},{19,3},{3,19},{20,4},{4,... | collective-permute-start | bytes 98312 | tf_op jit(solution)/shard_map/ppermute | solution.py:534
  19.7 21.4 %collective-permute-start.7 = (bf16[1,8,128,256]{3,2,1,0:T(8,128)(2,1)}, bf16[1,8,128,256]{3,2,1,0:T(8,128)(2,1)}, u32[]{:S(2)}, u32[]{:S(2)}) collective-permute-start(bf16[1,8,128,256]{3,2,1,0:T(8,128)(2,1)} %get-tuple-element.114), channel_id=1, source_target_pairs={{16,0},{0,16},{17,1},{1,17},{18,2},{2,18},{19,3},{3,19},{20,4},{4,... | collective-permute-start | bytes 1572872 | tf_op jit(solution)/shard_map/ppermute | solution.py:534
  21.5 2.9 %copy-start.2 = (bf16[8,256,256]{2,1,0:T(8,128)(2,1)S(1)}, bf16[8,256,256]{2,1,0:T(8,128)(2,1)}, u32[]{:S(2)}) copy-start(bf16[8,256,256]{2,1,0:T(8,128)(2,1)} %param.11) | copy-start | bytes 3145732
  22.8 7.9 %collective-permute-start.3 = (bf16[512,256]{1,0:T(8,128)(2,1)S(1)}, bf16[512,256]{1,0:T(8,128)(2,1)S(1)}, u32[]{:S(2)}, u32[]{:S(2)}) collective-permute-start(bf16[512,256]{1,0:T(8,128)(2,1)S(1)} %dynamic-slice_convert_fusion.1), channel_id=1, source_target_pairs={{0,2},{1,3},{2,0},{3,1},{4,6},{5,7},{6,4},{7,5},{8,10},{9,11},{10,... | collective-permute-start | bytes 786440 | tf_op jit(solution)/shard_map/ppermute | solution.py:433
  30.8 8.4 %collective-permute-start.4 = (bf16[128,256]{1,0:T(8,128)(2,1)S(1)}, bf16[128,256]{1,0:T(8,128)(2,1)S(1)}, u32[]{:S(2)}, u32[]{:S(2)}) collective-permute-start(bf16[128,256]{1,0:T(8,128)(2,1)S(1)} %get-tuple-element.101), channel_id=1, source_target_pairs={{0,4},{1,5},{2,6},{3,7},{4,0},{5,1},{6,2},{7,3},{8,12},{9,13},{10,... | collective-permute-start | bytes 196616 | tf_op jit(solution)/shard_map/ppermute | solution.py:433
  32.4 6.8 %collective-permute-start.5 = (bf16[128,256]{1,0:T(8,128)(2,1)S(1)}, bf16[128,256]{1,0:T(8,128)(2,1)S(1)}, u32[]{:S(2)}, u32[]{:S(2)}) collective-permute-start(bf16[128,256]{1,0:T(8,128)(2,1)S(1)} %get-tuple-element.102), channel_id=1, source_target_pairs={{0,8},{1,9},{2,10},{3,11},{4,12},{5,13},{6,14},{7,15},{8,0},{9,1},... | collective-permute-start | bytes 196616 | tf_op jit(solution)/shard_map/ppermute | solution.py:433
  35.0 6.1 %collective-permute-start.6 = (bf16[128,256]{1,0:T(8,128)(2,1)S(1)}, bf16[128,256]{1,0:T(8,128)(2,1)S(1)}, u32[]{:S(2)}, u32[]{:S(2)}) collective-permute-start(bf16[128,256]{1,0:T(8,128)(2,1)S(1)} %get-tuple-element.103), channel_id=1, source_target_pairs={{0,12},{1,13},{2,14},{3,15},{4,8},{5,9},{6,10},{7,11},{8,4},{9,5},... | collective-permute-start | bytes 196616 | tf_op jit(solution)/shard_map/ppermute | solution.py:433
  42.1 14.7 %collective-permute-start.14 = (bf16[4,1,144,256]{3,2,1,0:T(8,128)(2,1)S(1)}, bf16[4,1,144,256]{3,2,1,0:T(8,128)(2,1)S(1)}, u32[]{:S(2)}, u32[]{:S(2)}) collective-permute-start(bf16[4,1,144,256]{3,2,1,0:T(8,128)(2,1)S(1)} %fusion.21), channel_id=1, source_target_pairs={{1,0},{2,1},{3,2},{4,3},{5,4},{6,5},{7,6},{8,7},{9,8},{10,9},{11,1... | collective-permute-start | bytes 884744 | tf_op jit(solution)/shard_map/ppermute | solution.py:534
  42.5 14.4 %collective-permute-start.13 = (bf16[4,1,144,256]{3,2,1,0:T(8,128)(2,1)S(1)}, bf16[4,1,144,256]{3,2,1,0:T(8,128)(2,1)S(1)}, u32[]{:S(2)}, u32[]{:S(2)}) collective-permute-start(bf16[4,1,144,256]{3,2,1,0:T(8,128)(2,1)S(1)} %fusion.17), channel_id=1, source_target_pairs={{0,1},{1,2},{2,3},{3,4},{4,5},{5,6},{6,7},{7,8},{8,9},{9,10},{10,1... | collective-permute-start | bytes 884744 | tf_op jit(solution)/shard_map/ppermute | solution.py:528
  43.0 4.9 %collective-permute-start.9 = (bf16[128,256]{1,0:T(8,128)(2,1)S(1)}, bf16[128,256]{1,0:T(8,128)(2,1)S(1)}, u32[]{:S(2)}, u32[]{:S(2)}) collective-permute-start(bf16[128,256]{1,0:T(8,128)(2,1)S(1)} %convert_element_type.80), channel_id=1, source_target_pairs={{0,16},{1,17},{2,18},{3,19},{4,20},{5,21},{6,22},{7,23},{8,24},{9,... | collective-permute-start | bytes 196616 | tf_op jit(solution)/shard_map/ppermute | solution.py:433
  47.8 8.4 %collective-permute-start.10 = (bf16[128,256]{1,0:T(8,128)(2,1)S(1)}, bf16[128,256]{1,0:T(8,128)(2,1)S(1)}, u32[]{:S(2)}, u32[]{:S(2)}) collective-permute-start(bf16[128,256]{1,0:T(8,128)(2,1)S(1)} %add_convert_fusion), channel_id=1, source_target_pairs={{0,4},{1,5},{2,6},{3,7},{4,0},{5,1},{6,2},{7,3},{8,12},{9,13},{10,... | collective-permute-start | bytes 196616 | tf_op jit(solution)/shard_map/ppermute | solution.py:433
  47.9 8.8 %collective-permute-start.11 = (bf16[128,256]{1,0:T(8,128)(2,1)S(1)}, bf16[128,256]{1,0:T(8,128)(2,1)S(1)}, u32[]{:S(2)}, u32[]{:S(2)}) collective-permute-start(bf16[128,256]{1,0:T(8,128)(2,1)S(1)} %add_convert_fusion), channel_id=1, source_target_pairs={{0,8},{1,9},{2,10},{3,11},{4,12},{5,13},{6,14},{7,15},{8,0},{9,1},... | collective-permute-start | bytes 196616 | tf_op jit(solution)/shard_map/ppermute | solution.py:433
  50.2 6.5 %collective-permute-start.12 = (bf16[128,256]{1,0:T(8,128)(2,1)S(1)}, bf16[128,256]{1,0:T(8,128)(2,1)S(1)}, u32[]{:S(2)}, u32[]{:S(2)}) collective-permute-start(bf16[128,256]{1,0:T(8,128)(2,1)S(1)} %add_convert_fusion), channel_id=1, source_target_pairs={{0,12},{1,13},{2,14},{3,15},{4,8},{5,9},{6,10},{7,11},{8,4},{9,5},... | collective-permute-start | bytes 196616 | tf_op jit(solution)/shard_map/ppermute | solution.py:433
  56.9 8.2 %collective-permute-start.15 = (bf16[512,256]{1,0:T(8,128)(2,1)S(1)}, bf16[512,256]{1,0:T(8,128)(2,1)S(1)}, u32[]{:S(2)}, u32[]{:S(2)}) collective-permute-start(bf16[512,256]{1,0:T(8,128)(2,1)S(1)} %bitcast.59), channel_id=1, source_target_pairs={{0,2},{1,3},{2,0},{3,1},{4,6},{5,7},{6,4},{7,5},{8,10},{9,11},{10,... | collective-permute-start | bytes 786440 | tf_op jit(solution)/shard_map/ppermute | solution.py:433
  65.3 4.2 %collective-permute-start.16 = (bf16[1024,256]{1,0:T(8,128)(2,1)S(1)}, bf16[1024,256]{1,0:T(8,128)(2,1)S(1)}, u32[]{:S(2)}, u32[]{:S(2)}) collective-permute-start(bf16[1024,256]{1,0:T(8,128)(2,1)S(1)} %maximum_select_fusion), channel_id=1, source_target_pairs={{0,1},{1,0},{2,3},{3,2},{4,5},{5,4},{6,7},{7,6},{8,9},{9,8},{10,11... | collective-permute-start | bytes 1572872 | tf_op jit(solution)/shard_map/ppermute | solution.py:433
  65.4 4.1 %copy-start.1 = (bf16[256,256]{1,0:T(8,128)(2,1)S(1)}, bf16[256,256]{1,0:T(8,128)(2,1)}, u32[]{:S(2)}) copy-start(bf16[256,256]{1,0:T(8,128)(2,1)} %w_out.1) | copy-start | bytes 393220

commit v10 on v9

--- a/solution.py
+++ b/solution.py
@@ -572,8 +572,7 @@
     ph, partial = factor_call(
         pos, k_index.T, feat.reshape(atoms, width), w_charge, grid_all, scale_all
     )
-    partial, head, pos_late = tied(partial, feat[:1], pos)
-    after = from_after(head, "gx", 0)
+    partial, pos_late = tied(partial, pos)
     pos_before = from_before(pos_late, "gx", 0)
     pos_after = from_after(pos_late, "gx", 0)
 
@@ -599,7 +598,8 @@
     value, before = exchange.halve(
         partial, exchange.halved[0], Work(lambda plane: plane, before)
     )
-    value, before, pos_before = tied(value, before, pos_before)
+    value, before, pos_before, head = tied(value, before, pos_before, feat[:1])
+    after = from_after(head, "gx", 0)
     value, base = exchange.halve(
         value, exchange.halved[1], plane_work(0, 1, 3, None, before, pos_before)
     )

time: 76 us -> 73.7 us (0.970)
  Pallas kernels: 39.9 us -> 37.5 us
    pallas_call x6, Pallas kernels: 21.6 us -> 19.3 us  [short_call(): pl.pallas_call(kernel, in_specs=[whole] * len(args), out_specs=whole, out...]
  transfers between devices with their start and end apart: 17 -> 17, of which waited for: 6 -> 7; matrix products, arithmetic and copies ran while one was open for 4% -> 6% of each run, Pallas kernels for 45% -> 43%
where the time goes in v10:
time: 73.7 us; the launch traced here: 73.2 us
  Pallas kernels  37.5 us (51%)
  starting transfers between devices  20.9 us (28%)
  waiting for transfers between devices  7.46 us (10%)
  local copies, waits for them, and re-layouts  4.99 us (7%)
  other arithmetic  1.85 us (3%)
    pallas_call x6, Pallas kernels, short_call(): pl.pallas_call(kernel, in_specs=[whole] * len(args), out_specs=whole, out...  19.3 us
    ppermute x11, starting transfers between devices, swap(): return lax.ppermute(value, AXES, [(i, i ^ mask) for i in range(count)])  13.4 us
    pallas_call x2, Pallas kernels, field_call(): pl.pallas_call(functools.partial(kernel, lines), in_specs=[in_hbm] + [who...  9.89 us
    pallas_call x1, Pallas kernels, factor_call(): pl.pallas_call(functools.partial(factor_kernel, grid_all, scale_all), in_...  8.34 us
    ppermute x3, starting transfers between devices, from_before(): lax.ppermute(tail, axis, [(i, (i + 1) % count) for i in range(count)])  5.48 us
    ppermute x11, waiting for transfers between devices, swap(): return lax.ppermute(value, AXES, [(i, i ^ mask) for i in range(count)])  4.87 us
    ppermute x3, waiting for transfers between devices, from_before(): lax.ppermute(tail, axis, [(i, (i + 1) % count) for i in range(count)])  2.58 us
    slice x1, local copies, waits for them, and re-layouts, on_device(): value, before, pos_before, head = tied(value, before, pos_before, feat[:1])  2.38 us
  transfers between devices with their start and end apart: 17, of which 7 were waited for; matrix products, arithmetic and copies ran while one was open for 6% of the time, Pallas kernels for 43%

profile of v10, /device:TPU:0, one launch (start us, length us, event | category | flops | bytes accessed | tf_op | source)
XLA Modules:
  0.0 73.2 jit_solution(17751128393059647462)
XLA Ops:
  0.0 2.4 %slice_bitcast_fusion = (bf16[1,8,128,256]{3,2,1,0:T(8,128)(2,1)}, bf16[1,8,128,256]{3,2,1,0:T(8,128)(2,1)}) fusion(bf16[2,8,16,8,256]{4,3,2,1,0:T(8,128)(2,1)} %param.7), kind=kLoop, calls=%fused_computation.18 | loop fusion | bytes 2097152 | tf_op jit(solution)/shard_map/slice | solution.py:601
  2.4 3.0 %collective-permute-start = (bf16[1,8,128,256]{3,2,1,0:T(8,128)(2,1)}, bf16[1,8,128,256]{3,2,1,0:T(8,128)(2,1)}, u32[]{:S(2)}, u32[]{:S(2)}) collective-permute-start(bf16[1,8,128,256]{3,2,1,0:T(8,128)(2,1)} %get-tuple-element.162), channel_id=1, source_target_pairs={{0,16},{16,0},{1,17},{17,1},{2,18},{18,2},{3,19},{19,3},{4,20},{20... | collective-permute-start | bytes 1572872 | tf_op jit(solution)/shard_map/ppermute | solution.py:528
  6.3 8.3 %factor.1 = (bf16[4,2,2048,256]{3,2,1,0:T(8,128)(2,1)}, f32[2048,256]{1,0:T(8,128)S(1)}) custom-call(bf16[2,8,16,128]{3,2,1,0:T(8,128)(2,1)S(1)} %maximum_maximum_fusion.pos, s32[3,1024]{1,0:T(4,128)S(1)} %bitcast.55, bf16[2048,256]{1,0:T(8,128)(2,1)S(1)} %bitcast.40, bf16[256,256]{1,0:T(8,128)(2,1)S(1)} %copy-done.3), custom_call_target="tpu_custom_call" | custom-call | flops 12884901888 | bytes 4194304 | tf_op jit(solution)/shard_map/factor/pallas_call | solution.py:134
  15.5 2.1 %collective-permute-done.side_feat.before = bf16[1,8,128,256]{3,2,1,0:T(8,128)(2,1)} collective-permute-done((bf16[1,8,128,256]{3,2,1,0:T(8,128)(2,1)}, bf16[1,8,128,256]{3,2,1,0:T(8,128)(2,1)}, u32[]{:S(2)}, u32[]{:S(2)}) %collective-permute-start) | collective-permute-done | bytes 524320 | tf_op jit(solution)/shard_map/ppermute | solution.py:528
  17.6 1.8 %collective-permute-start.2 = (bf16[1,8,16,128]{3,2,1,0:T(8,128)(2,1)S(1)}, bf16[1,8,16,128]{3,2,1,0:T(8,128)(2,1)S(1)}, u32[]{:S(2)}, u32[]{:S(2)}) collective-permute-start(bf16[1,8,16,128]{3,2,1,0:T(8,128)(2,1)S(1)} %get-tuple-element.173), channel_id=1, source_target_pairs={{0,16},{16,0},{1,17},{17,1},{2,18},{18,2},{3,19},{19,3},{4,20},{20... | collective-permute-start | bytes 98312 | tf_op jit(solution)/shard_map/ppermute | solution.py:528
  19.8 1.2 %convert_add_fusion = f32[1024,256]{1,0:T(8,128)S(1)} fusion(bf16[1024,256]{1,0:T(8,128)(2,1)} %collective-permute-done.1, f32[2048,256]{1,0:T(8,128)S(1)} %get-tuple-element.84, s32[]{:T(128)S(6)} %select_n.98), kind=kLoop, calls=%fused_computation | loop fusion | flops 524288 | bytes 2621444 | tf_op jit(solution)/shard_map/add | solution.py:466
  21.6 1.8 %collective-permute-start.3 = (bf16[512,256]{1,0:T(8,128)(2,1)S(1)}, bf16[512,256]{1,0:T(8,128)(2,1)S(1)}, u32[]{:S(2)}, u32[]{:S(2)}) collective-permute-start(bf16[512,256]{1,0:T(8,128)(2,1)S(1)} %dynamic-slice_convert_fusion.1), channel_id=1, source_target_pairs={{0,2},{1,3},{2,0},{3,1},{4,6},{5,7},{6,4},{7,5},{8,10},{9,11},{10,... | collective-permute-start | bytes 786440 | tf_op jit(solution)/shard_map/ppermute | solution.py:433
  23.4 1.7 %collective-permute-start.7 = (bf16[1,8,128,256]{3,2,1,0:T(8,128)(2,1)S(1)}, bf16[1,8,128,256]{3,2,1,0:T(8,128)(2,1)S(1)}, u32[]{:S(2)}, u32[]{:S(2)}) collective-permute-start(bf16[1,8,128,256]{3,2,1,0:T(8,128)(2,1)S(1)} %copy-done.5), channel_id=1, source_target_pairs={{16,0},{0,16},{17,1},{1,17},{18,2},{2,18},{19,3},{3,19},{20,4},{4,... | collective-permute-start | bytes 1572872 | tf_op jit(solution)/shard_map/ppermute | solution.py:534
  25.1 4.0 %plane.4.rest_0_ = f32[8,2,128,256]{3,2,1,0:T(8,128)S(1)} custom-call(bf16[2,8,128,256]{3,2,1,0:T(8,128)(2,1)S(1)} %bitcast.42, bf16[2,8,16,128]{3,2,1,0:T(8,128)(2,1)S(1)} %maximum_maximum_fusion.pos, bf16[1,8,128,256]{3,2,1,0:T(8,128)(2,1)} %collective-permute-done.side_feat.before, bf16[1,8,16,128]{3,2,1,0:T(8,128)(2,1)S(1)} %collective-permute-done.2.side_pos.pos_before, ...), custom_call_target="tpu_custom_call" | custom-call | flops 4026531840 | bytes 4194304 | tf_op jit(solution)/shard_map/plane/pallas_call | solution.py:323
  30.1 1.6 %collective-permute-start.4 = (bf16[128,256]{1,0:T(8,128)(2,1)S(1)}, bf16[128,256]{1,0:T(8,128)(2,1)S(1)}, u32[]{:S(2)}, u32[]{:S(2)}) collective-permute-start(bf16[128,256]{1,0:T(8,128)(2,1)S(1)} %get-tuple-element.101), channel_id=1, source_target_pairs={{0,4},{1,5},{2,6},{3,7},{4,0},{5,1},{6,2},{7,3},{8,12},{9,13},{10,... | collective-permute-start | bytes 196616 | tf_op jit(solution)/shard_map/ppermute | solution.py:433
  31.7 2.6 %collective-permute-start.5 = (bf16[128,256]{1,0:T(8,128)(2,1)S(1)}, bf16[128,256]{1,0:T(8,128)(2,1)S(1)}, u32[]{:S(2)}, u32[]{:S(2)}) collective-permute-start(bf16[128,256]{1,0:T(8,128)(2,1)S(1)} %get-tuple-element.102), channel_id=1, source_target_pairs={{0,8},{1,9},{2,10},{3,11},{4,12},{5,13},{6,14},{7,15},{8,0},{9,1},... | collective-permute-start | bytes 196616 | tf_op jit(solution)/shard_map/ppermute | solution.py:433
  34.5 4.0 %plane.5.rest_0_ = f32[8,2,128,256]{3,2,1,0:T(8,128)S(1)} custom-call(bf16[2,8,128,256]{3,2,1,0:T(8,128)(2,1)S(1)} %bitcast.43, bf16[2,8,16,128]{3,2,1,0:T(8,128)(2,1)S(1)} %maximum_maximum_fusion.pos, bf16[1,8,128,256]{3,2,1,0:T(8,128)(2,1)} %collective-permute-done.side_feat.before, ...), custom_call_target="tpu_custom_call", output_to_operand_aliasing={{}: (5, {})} | custom-call | flops 4026531840 | bytes 4194304 | tf_op jit(solution)/shard_map/plane/pallas_call | solution.py:323
  38.5 1.9 %collective-permute-done.6 = bf16[128,256]{1,0:T(8,128)(2,1)S(1)} collective-permute-done((bf16[128,256]{1,0:T(8,128)(2,1)S(1)}, bf16[128,256]{1,0:T(8,128)(2,1)S(1)}, u32[]{:S(2)}, u32[]{:S(2)}) %collective-permute-start.6) | collective-permute-done | bytes 65568 | tf_op jit(solution)/shard_map/ppermute | solution.py:433
  41.3 1.3 %collective-permute-start.9 = (bf16[128,256]{1,0:T(8,128)(2,1)S(1)}, bf16[128,256]{1,0:T(8,128)(2,1)S(1)}, u32[]{:S(2)}, u32[]{:S(2)}) collective-permute-start(bf16[128,256]{1,0:T(8,128)(2,1)S(1)} %convert_element_type.80), channel_id=1, source_target_pairs={{0,16},{1,17},{2,18},{3,19},{4,20},{5,21},{6,22},{7,23},{8,24},{9,... | collective-permute-start | bytes 196616 | tf_op jit(solution)/shard_map/ppermute | solution.py:433
  42.7 2.9 %plane.6.rest_0_ = f32[8,2,128,256]{3,2,1,0:T(8,128)S(1)} custom-call(bf16[2,8,128,256]{3,2,1,0:T(8,128)(2,1)S(1)} %bitcast.44, bf16[2,8,16,128]{3,2,1,0:T(8,128)(2,1)S(1)} %maximum_maximum_fusion.pos, bf16[1,8,128,256]{3,2,1,0:T(8,128)(2,1)S(1)} %collective-permute-done.7.side_feat.after, ...), custom_call_target="tpu_custom_call", output_to_operand_aliasing={{}: (5, {})} | custom-call | flops 4026531840 | bytes 4194304 | tf_op jit(solution)/shard_map/plane/pallas_call | solution.py:323
  46.4 2.3 %collective-permute-start.11 = (bf16[128,256]{1,0:T(8,128)(2,1)S(1)}, bf16[128,256]{1,0:T(8,128)(2,1)S(1)}, u32[]{:S(2)}, u32[]{:S(2)}) collective-permute-start(bf16[128,256]{1,0:T(8,128)(2,1)S(1)} %add_convert_fusion), channel_id=1, source_target_pairs={{0,8},{1,9},{2,10},{3,11},{4,12},{5,13},{6,14},{7,15},{8,0},{9,1},... | collective-permute-start | bytes 196616 | tf_op jit(solution)/shard_map/ppermute | solution.py:433
  48.7 2.1 %collective-permute-start.12 = (bf16[128,256]{1,0:T(8,128)(2,1)S(1)}, bf16[128,256]{1,0:T(8,128)(2,1)S(1)}, u32[]{:S(2)}, u32[]{:S(2)}) collective-permute-start(bf16[128,256]{1,0:T(8,128)(2,1)S(1)} %add_convert_fusion), channel_id=1, source_target_pairs={{0,12},{1,13},{2,14},{3,15},{4,8},{5,9},{6,10},{7,11},{8,4},{9,5},... | collective-permute-start | bytes 196616 | tf_op jit(solution)/shard_map/ppermute | solution.py:433
  50.8 2.9 %plane.7.rest_0_ = f32[8,2,128,256]{3,2,1,0:T(8,128)S(1)} custom-call(bf16[2,8,128,256]{3,2,1,0:T(8,128)(2,1)S(1)} %bitcast.45, bf16[2,8,16,128]{3,2,1,0:T(8,128)(2,1)S(1)} %maximum_maximum_fusion.pos, bf16[1,8,128,256]{3,2,1,0:T(8,128)(2,1)S(1)} %collective-permute-done.7.side_feat.after, ...), custom_call_target="tpu_custom_call", output_to_operand_aliasing={{}: (5, {})} | custom-call | flops 4026531840 | bytes 4194304 | tf_op jit(solution)/shard_map/plane/pallas_call | solution.py:323
  53.7 1.3 %collective-permute-done.11 = bf16[128,256]{1,0:T(8,128)(2,1)S(1)} collective-permute-done((bf16[128,256]{1,0:T(8,128)(2,1)S(1)}, bf16[128,256]{1,0:T(8,128)(2,1)S(1)}, u32[]{:S(2)}, u32[]{:S(2)}) %collective-permute-start.11) | collective-permute-done | bytes 65568 | tf_op jit(solution)/shard_map/ppermute | solution.py:433
  55.2 1.3 %collective-permute-start.15 = (bf16[512,256]{1,0:T(8,128)(2,1)S(1)}, bf16[512,256]{1,0:T(8,128)(2,1)S(1)}, u32[]{:S(2)}, u32[]{:S(2)}) collective-permute-start(bf16[512,256]{1,0:T(8,128)(2,1)S(1)} %bitcast.59), channel_id=1, source_target_pairs={{0,2},{1,3},{2,0},{3,1},{4,6},{5,7},{6,4},{7,5},{8,10},{9,11},{10,... | collective-permute-start | bytes 786440 | tf_op jit(solution)/shard_map/ppermute | solution.py:433
  56.5 2.7 %low.1.rest_0_ = f32[8,2,128,256]{3,2,1,0:T(8,128)S(1)} custom-call(bf16[2,8,128,256]{3,2,1,0:T(8,128)(2,1)S(1)} %bitcast.46, bf16[2,8,16,128]{3,2,1,0:T(8,128)(2,1)S(1)} %maximum_maximum_fusion.pos, bf16[1,8,128,256]{3,2,1,0:T(8,128)(2,1)} %collective-permute-done.side_feat.before, ...), custom_call_target="tpu_custom_call", output_to_operand_aliasing={{}: (8, {})} | custom-call | flops 2684354560 | bytes 4194304 | tf_op jit(solution)/shard_map/low/pallas_call | solution.py:323
  59.2 2.7 %high.1.base = f32[8,2,128,256]{3,2,1,0:T(8,128)S(1)} custom-call(bf16[2,8,128,256]{3,2,1,0:T(8,128)(2,1)S(1)} %bitcast.47, bf16[2,8,16,128]{3,2,1,0:T(8,128)(2,1)S(1)} %maximum_maximum_fusion.pos, bf16[1,8,128,256]{3,2,1,0:T(8,128)(2,1)} %collective-permute-done.side_feat.before, ...), custom_call_target="tpu_custom_call", output_to_operand_aliasing={{}: (8, {})} | custom-call | flops 2684354560 | bytes 4194304 | tf_op jit(solution)/shard_map/high/pallas_call | solution.py:323
  63.2 4.1 %near.1.partial = f32[2048,256]{1,0:T(8,128)S(1)} custom-call(bf16[4,2,2048,256]{3,2,1,0:T(8,128)(2,1)} %get-tuple-element.154.ph_all, bf16[4,256,256]{2,1,0:T(8,128)(2,1)S(1)} %bitcast.39), custom_call_target="tpu_custom_call" | custom-call | flops 2147483648 | bytes 4194304 | tf_op jit(solution)/shard_map/near/pallas_call | solution.py:407
  67.3 5.8 %far.1 = bf16[2048,256]{1,0:T(8,128)(2,1)} custom-call(bf16[4,2,2048,256]{3,2,1,0:T(8,128)(2,1)} %get-tuple-element.154.ph_all, bf16[4,256,256]{2,1,0:T(8,128)(2,1)S(1)} %bitcast.48, f32[2048,256]{1,0:T(8,128)S(1)} %near.1.partial, bf16[256,256]{1,0:T(8,128)(2,1)S(1)} %copy-done.1, f32[8,2,128,256]{3,2,1,0:T(8,128)S(1)} %high.1.base, ...), custom_call_target="tpu_custom_call" | custom-call | flops 2147483648 | bytes 4194304 | tf_op jit(solution)/shard_map/far/pallas_call | solution.py:407
  (68 shorter events, 6.9 us)
Async XLA Ops:
  0.0 6.3 %copy-start = (bf16[2,8,16,8,256]{4,3,2,1,0:T(8,128)(2,1)S(1)}, bf16[2,8,16,8,256]{4,3,2,1,0:T(8,128)(2,1)}, u32[]{:S(2)}) copy-start(bf16[2,8,16,8,256]{4,3,2,1,0:T(8,128)(2,1)} %param.7) | copy-start | bytes 3145732
  0.0 5.3 %copy-start.6 = (bf16[2,8,16,8,3]{2,3,4,1,0:T(8,128)(2,1)S(1)}, bf16[2,8,16,8,3]{2,3,4,1,0:T(8,128)(2,1)}, u32[]{:S(2)}) copy-start(bf16[2,8,16,8,3]{2,3,4,1,0:T(8,128)(2,1)} %param.8) | copy-start | bytes 36868
  0.0 5.7 %copy-start.7 = (s32[2,8,16]{2,1,0:T(8,128)S(1)}, s32[2,8,16]{2,1,0:T(8,128)}, u32[]{:S(2)}) copy-start(s32[2,8,16]{2,1,0:T(8,128)} %param.9) | copy-start | bytes 3076
  0.0 6.3 %copy-start.4 = (s32[1024,3]{0,1:T(4,128)S(1)}, s32[1024,3]{0,1:T(4,128)}, u32[]{:S(2)}) copy-start(s32[1024,3]{0,1:T(4,128)} %param.10) | copy-start | bytes 36868
  0.0 6.3 %copy-start.3 = (bf16[256,256]{1,0:T(8,128)(2,1)S(1)}, bf16[256,256]{1,0:T(8,128)(2,1)}, u32[]{:S(2)}) copy-start(bf16[256,256]{1,0:T(8,128)(2,1)} %wc.1) | copy-start | bytes 393220
  2.4 15.2 %collective-permute-start = (bf16[1,8,128,256]{3,2,1,0:T(8,128)(2,1)}, bf16[1,8,128,256]{3,2,1,0:T(8,128)(2,1)}, u32[]{:S(2)}, u32[]{:S(2)}) collective-permute-start(bf16[1,8,128,256]{3,2,1,0:T(8,128)(2,1)} %get-tuple-element.162), channel_id=1, source_target_pairs={{0,16},{16,0},{1,17},{17,1},{2,18},{18,2},{3,19},{19,3},{4,20},{20... | collective-permute-start | bytes 1572872 | tf_op jit(solution)/shard_map/ppermute | solution.py:528
  17.6 2.3 %collective-permute-start.1 = (bf16[1024,256]{1,0:T(8,128)(2,1)}, bf16[1024,256]{1,0:T(8,128)(2,1)}, u32[]{:S(2)}, u32[]{:S(2)}) collective-permute-start(bf16[1024,256]{1,0:T(8,128)(2,1)} %dynamic-slice_convert_fusion), channel_id=1, source_target_pairs={{0,1},{1,0},{2,3},{3,2},{4,5},{5,4},{6,7},{7,6},{8,9},{9,8},{10,11... | collective-permute-start | bytes 1572872 | tf_op jit(solution)/shard_map/ppermute | solution.py:433
  17.6 4.0 %collective-permute-start.2 = (bf16[1,8,16,128]{3,2,1,0:T(8,128)(2,1)S(1)}, bf16[1,8,16,128]{3,2,1,0:T(8,128)(2,1)S(1)}, u32[]{:S(2)}, u32[]{:S(2)}) collective-permute-start(bf16[1,8,16,128]{3,2,1,0:T(8,128)(2,1)S(1)} %get-tuple-element.173), channel_id=1, source_target_pairs={{0,16},{16,0},{1,17},{17,1},{2,18},{18,2},{3,19},{19,3},{4,20},{20... | collective-permute-start | bytes 98312 | tf_op jit(solution)/shard_map/ppermute | solution.py:528
  19.4 21.0 %collective-permute-start.8 = (bf16[1,8,16,128]{3,2,1,0:T(8,128)(2,1)S(1)}, bf16[1,8,16,128]{3,2,1,0:T(8,128)(2,1)S(1)}, u32[]{:S(2)}, u32[]{:S(2)}) collective-permute-start(bf16[1,8,16,128]{3,2,1,0:T(8,128)(2,1)S(1)} %get-tuple-element.172), channel_id=1, source_target_pairs={{16,0},{0,16},{17,1},{1,17},{18,2},{2,18},{19,3},{3,19},{20,4},{4,... | collective-permute-start | bytes 98312 | tf_op jit(solution)/shard_map/ppermute | solution.py:534
  19.7 5.4 %copy-start.2 = (bf16[8,256,256]{2,1,0:T(8,128)(2,1)S(1)}, bf16[8,256,256]{2,1,0:T(8,128)(2,1)}, u32[]{:S(2)}) copy-start(bf16[8,256,256]{2,1,0:T(8,128)(2,1)} %param.11) | copy-start | bytes 3145732
  21.6 8.4 %collective-permute-start.3 = (bf16[512,256]{1,0:T(8,128)(2,1)S(1)}, bf16[512,256]{1,0:T(8,128)(2,1)S(1)}, u32[]{:S(2)}, u32[]{:S(2)}) collective-permute-start(bf16[512,256]{1,0:T(8,128)(2,1)S(1)} %dynamic-slice_convert_fusion.1), channel_id=1, source_target_pairs={{0,2},{1,3},{2,0},{3,1},{4,6},{5,7},{6,4},{7,5},{8,10},{9,11},{10,... | collective-permute-start | bytes 786440 | tf_op jit(solution)/shard_map/ppermute | solution.py:433
  23.4 17.0 %collective-permute-start.7 = (bf16[1,8,128,256]{3,2,1,0:T(8,128)(2,1)S(1)}, bf16[1,8,128,256]{3,2,1,0:T(8,128)(2,1)S(1)}, u32[]{:S(2)}, u32[]{:S(2)}) collective-permute-start(bf16[1,8,128,256]{3,2,1,0:T(8,128)(2,1)S(1)} %copy-done.5), channel_id=1, source_target_pairs={{16,0},{0,16},{17,1},{1,17},{18,2},{2,18},{19,3},{3,19},{20,4},{4,... | collective-permute-start | bytes 1572872 | tf_op jit(solution)/shard_map/ppermute | solution.py:534
  30.1 8.4 %collective-permute-start.4 = (bf16[128,256]{1,0:T(8,128)(2,1)S(1)}, bf16[128,256]{1,0:T(8,128)(2,1)S(1)}, u32[]{:S(2)}, u32[]{:S(2)}) collective-permute-start(bf16[128,256]{1,0:T(8,128)(2,1)S(1)} %get-tuple-element.101), channel_id=1, source_target_pairs={{0,4},{1,5},{2,6},{3,7},{4,0},{5,1},{6,2},{7,3},{8,12},{9,13},{10,... | collective-permute-start | bytes 196616 | tf_op jit(solution)/shard_map/ppermute | solution.py:433
  31.7 6.8 %collective-permute-start.5 = (bf16[128,256]{1,0:T(8,128)(2,1)S(1)}, bf16[128,256]{1,0:T(8,128)(2,1)S(1)}, u32[]{:S(2)}, u32[]{:S(2)}) collective-permute-start(bf16[128,256]{1,0:T(8,128)(2,1)S(1)} %get-tuple-element.102), channel_id=1, source_target_pairs={{0,8},{1,9},{2,10},{3,11},{4,12},{5,13},{6,14},{7,15},{8,0},{9,1},... | collective-permute-start | bytes 196616 | tf_op jit(solution)/shard_map/ppermute | solution.py:433
  34.3 6.1 %collective-permute-start.6 = (bf16[128,256]{1,0:T(8,128)(2,1)S(1)}, bf16[128,256]{1,0:T(8,128)(2,1)S(1)}, u32[]{:S(2)}, u32[]{:S(2)}) collective-permute-start(bf16[128,256]{1,0:T(8,128)(2,1)S(1)} %get-tuple-element.103), channel_id=1, source_target_pairs={{0,12},{1,13},{2,14},{3,15},{4,8},{5,9},{6,10},{7,11},{8,4},{9,5},... | collective-permute-start | bytes 196616 | tf_op jit(solution)/shard_map/ppermute | solution.py:433
  40.5 14.7 %collective-permute-start.14 = (bf16[4,1,144,256]{3,2,1,0:T(8,128)(2,1)S(1)}, bf16[4,1,144,256]{3,2,1,0:T(8,128)(2,1)S(1)}, u32[]{:S(2)}, u32[]{:S(2)}) collective-permute-start(bf16[4,1,144,256]{3,2,1,0:T(8,128)(2,1)S(1)} %fusion.21), channel_id=1, source_target_pairs={{1,0},{2,1},{3,2},{4,3},{5,4},{6,5},{7,6},{8,7},{9,8},{10,9},{11,1... | collective-permute-start | bytes 884744 | tf_op jit(solution)/shard_map/ppermute | solution.py:534
  40.6 14.6 %collective-permute-start.13 = (bf16[4,1,144,256]{3,2,1,0:T(8,128)(2,1)S(1)}, bf16[4,1,144,256]{3,2,1,0:T(8,128)(2,1)S(1)}, u32[]{:S(2)}, u32[]{:S(2)}) collective-permute-start(bf16[4,1,144,256]{3,2,1,0:T(8,128)(2,1)S(1)} %fusion.17), channel_id=1, source_target_pairs={{0,1},{1,2},{2,3},{3,4},{4,5},{5,6},{6,7},{7,8},{8,9},{9,10},{10,1... | collective-permute-start | bytes 884744 | tf_op jit(solution)/shard_map/ppermute | solution.py:528
  41.3 5.0 %collective-permute-start.9 = (bf16[128,256]{1,0:T(8,128)(2,1)S(1)}, bf16[128,256]{1,0:T(8,128)(2,1)S(1)}, u32[]{:S(2)}, u32[]{:S(2)}) collective-permute-start(bf16[128,256]{1,0:T(8,128)(2,1)S(1)} %convert_element_type.80), channel_id=1, source_target_pairs={{0,16},{1,17},{2,18},{3,19},{4,20},{5,21},{6,22},{7,23},{8,24},{9,... | collective-permute-start | bytes 196616 | tf_op jit(solution)/shard_map/ppermute | solution.py:433
  46.3 7.4 %collective-permute-start.10 = (bf16[128,256]{1,0:T(8,128)(2,1)S(1)}, bf16[128,256]{1,0:T(8,128)(2,1)S(1)}, u32[]{:S(2)}, u32[]{:S(2)}) collective-permute-start(bf16[128,256]{1,0:T(8,128)(2,1)S(1)} %add_convert_fusion), channel_id=1, source_target_pairs={{0,4},{1,5},{2,6},{3,7},{4,0},{5,1},{6,2},{7,3},{8,12},{9,13},{10,... | collective-permute-start | bytes 196616 | tf_op jit(solution)/shard_map/ppermute | solution.py:433
  46.4 8.6 %collective-permute-start.11 = (bf16[128,256]{1,0:T(8,128)(2,1)S(1)}, bf16[128,256]{1,0:T(8,128)(2,1)S(1)}, u32[]{:S(2)}, u32[]{:S(2)}) collective-permute-start(bf16[128,256]{1,0:T(8,128)(2,1)S(1)} %add_convert_fusion), channel_id=1, source_target_pairs={{0,8},{1,9},{2,10},{3,11},{4,12},{5,13},{6,14},{7,15},{8,0},{9,1},... | collective-permute-start | bytes 196616 | tf_op jit(solution)/shard_map/ppermute | solution.py:433
  48.7 6.3 %collective-permute-start.12 = (bf16[128,256]{1,0:T(8,128)(2,1)S(1)}, bf16[128,256]{1,0:T(8,128)(2,1)S(1)}, u32[]{:S(2)}, u32[]{:S(2)}) collective-permute-start(bf16[128,256]{1,0:T(8,128)(2,1)S(1)} %add_convert_fusion), channel_id=1, source_target_pairs={{0,12},{1,13},{2,14},{3,15},{4,8},{5,9},{6,10},{7,11},{8,4},{9,5},... | collective-permute-start | bytes 196616 | tf_op jit(solution)/shard_map/ppermute | solution.py:433
  55.2 7.6 %collective-permute-start.15 = (bf16[512,256]{1,0:T(8,128)(2,1)S(1)}, bf16[512,256]{1,0:T(8,128)(2,1)S(1)}, u32[]{:S(2)}, u32[]{:S(2)}) collective-permute-start(bf16[512,256]{1,0:T(8,128)(2,1)S(1)} %bitcast.59), channel_id=1, source_target_pairs={{0,2},{1,3},{2,0},{3,1},{4,6},{5,7},{6,4},{7,5},{8,10},{9,11},{10,... | collective-permute-start | bytes 786440 | tf_op jit(solution)/shard_map/ppermute | solution.py:433
  63.1 4.2 %collective-permute-start.16 = (bf16[1024,256]{1,0:T(8,128)(2,1)S(1)}, bf16[1024,256]{1,0:T(8,128)(2,1)S(1)}, u32[]{:S(2)}, u32[]{:S(2)}) collective-permute-start(bf16[1024,256]{1,0:T(8,128)(2,1)S(1)} %maximum_select_fusion), channel_id=1, source_target_pairs={{0,1},{1,0},{2,3},{3,2},{4,5},{5,4},{6,7},{7,6},{8,9},{9,8},{10,11... | collective-permute-start | bytes 1572872 | tf_op jit(solution)/shard_map/ppermute | solution.py:433
  63.2 4.1 %copy-start.1 = (bf16[256,256]{1,0:T(8,128)(2,1)S(1)}, bf16[256,256]{1,0:T(8,128)(2,1)}, u32[]{:S(2)}) copy-start(bf16[256,256]{1,0:T(8,128)(2,1)} %w_out.1) | copy-start | bytes 393220
  (1 other events, 3.8 us)
